TPU v7x, 128 devices: a whole 4x4x4 slice. The times are simulated.
128 devices in a mesh: dp: 8 (over y, x_hi), expert: 16 (over z, x_lo, core).
Axes of the slice: x: 4 (x_hi: 2, x_lo: 2; x = x_hi * 2 + x_lo), y: 4, z: 4, core: 2. Of those that a mesh axis runs over, the one named last changes fastest.
Arguments:
- tokens: bfloat16 [401408, 768], P(('dp', 'expert')), may hold values from -120 to 120
- router: bfloat16 [768, 16], replicated, may hold values from -1 to 1
- w_in: bfloat16 [16, 768, 3072], P('expert'), may hold values from -0.21875 to 0.21875
- w_out: bfloat16 [16, 3072, 768], P('expert'), may hold values from -0.109375 to 0.109375
- g_outputs: bfloat16 [401408, 768], P(('dp', 'expert')), may hold values from -6 to 6
Outputs:
- g_tokens: bfloat16 [401408, 768], P(('dp', 'expert'))
- g_router: float32 [768, 16], replicated
- g_w_in: float32 [16, 768, 3072], P('expert', 'dp')
- g_w_out: float32 [16, 3072, 768], P('expert', 'dp')
All inputs are finite; a program needn't handle non-finite values.
Results may differ from a plain program's by a relative error of at most 0.02.
Values may be sent and summed in bfloat16 or wider, within the bound.
No kernel may reach another device: no remote copies, remote signals or barrier semaphores. Data moves between devices by JAX's collectives and lax.ppermute only.
A program may use at most 192 MiB of HBM per device.

v0:
```python
import jax
import jax.numpy as jnp
from jax import lax
from jax.sharding import PartitionSpec as P

PATCHES = 196


def contract(left, right, left_dim, right_dim):
    return lax.dot_general(
        left, right, (((left_dim,), (right_dim,)), ((), ())), preferred_element_type=jnp.float32
    )


def on_device(tokens, router, w_in, w_out, g_outputs):
    feat_width = tokens.shape[1]
    img_count = tokens.shape[0] // PATCHES
    experts = router.shape[1]
    tok_grid = tokens.reshape(img_count, PATCHES, feat_width)
    out_grid = g_outputs.reshape(img_count, PATCHES, feat_width)
    logits = jnp.dot(tokens, router, preferred_element_type=jnp.float32).reshape(
        img_count, PATCHES, experts
    )
    dispatch = jax.nn.softmax(logits, axis=1)
    combine = jax.nn.softmax(logits, axis=2)
    dispatch_low = dispatch.astype(jnp.bfloat16)
    combine_low = combine.astype(jnp.bfloat16)
    slot_in = jnp.einsum(
        "bpe,bpd->bed", dispatch_low, tok_grid, preferred_element_type=jnp.float32
    ).astype(jnp.bfloat16)
    arrived = lax.all_to_all(slot_in, "expert", split_axis=1, concat_axis=0, tiled=True)
    rows_in = arrived.reshape(-1, feat_width)
    w_first = w_in[0]
    w_second = w_out[0]
    pre_act = jnp.dot(rows_in, w_first, preferred_element_type=jnp.float32)
    activated = jax.nn.gelu(pre_act).astype(jnp.bfloat16)
    rows_out = jnp.dot(activated, w_second, preferred_element_type=jnp.float32).astype(jnp.bfloat16)
    returned = lax.all_to_all(
        rows_out.reshape(-1, 1, feat_width), "expert", split_axis=0, concat_axis=1, tiled=True
    )
    grad_comb = jnp.einsum("bpd,bed->bpe", out_grid, returned, preferred_element_type=jnp.float32)
    grad_slot_out = jnp.einsum(
        "bpe,bpd->bed", combine_low, out_grid, preferred_element_type=jnp.float32
    ).astype(jnp.bfloat16)
    comb_part = combine * (grad_comb - jnp.sum(combine * grad_comb, axis=2, keepdims=True))
    arrived_grads = lax.all_to_all(grad_slot_out, "expert", split_axis=1, concat_axis=0, tiled=True)
    rows_grad = arrived_grads.reshape(-1, feat_width)
    unused, gelu_back = jax.vjp(jax.nn.gelu, pre_act)
    grad_act = contract(rows_grad, w_second, 1, 1)
    grad_pre = gelu_back(grad_act)[0].astype(jnp.bfloat16)
    picked = rows_in
    grad_first = lax.psum_scatter(
        contract(picked, grad_pre, 0, 0).astype(jnp.bfloat16), "dp", scatter_dimension=0, tiled=True
    ).astype(jnp.float32)
    picked = activated
    grad_second = lax.psum_scatter(
        contract(picked, rows_grad, 0, 0).astype(jnp.bfloat16),
        "dp",
        scatter_dimension=0,
        tiled=True,
    ).astype(jnp.float32)
    grad_rows = contract(grad_pre, w_first, 1, 1).astype(jnp.bfloat16)
    grad_slot_in = lax.all_to_all(
        grad_rows.reshape(-1, 1, feat_width), "expert", split_axis=0, concat_axis=1, tiled=True
    )
    grad_disp = jnp.einsum(
        "bpd,bed->bpe", tok_grid, grad_slot_in, preferred_element_type=jnp.float32
    )
    disp_part = dispatch * (grad_disp - jnp.sum(dispatch * grad_disp, axis=1, keepdims=True))
    grad_logits = (comb_part + disp_part).astype(jnp.bfloat16).reshape(-1, experts)
    grad_tok = jnp.einsum(
        "bpe,bed->bpd", dispatch_low, grad_slot_in, preferred_element_type=jnp.float32
    ).reshape(-1, feat_width)
    grad_tok = grad_tok + contract(grad_logits, router, 1, 1)
    router_term = contract(tokens, grad_logits, 0, 0)
    grad_router = lax.psum(router_term, ("dp", "expert"))
    return (grad_tok.astype(jnp.bfloat16), grad_router, grad_first[None], grad_second[None])


def solution(mesh):
    return jax.shard_map(
        on_device,
        mesh=mesh,
        in_specs=(
            P(("dp", "expert"), None),
            P(),
            P("expert", None, None),
            P("expert", None, None),
            P(("dp", "expert"), None),
        ),
        out_specs=(
            P(("dp", "expert"), None),
            P(),
            P("expert", "dp", None),
            P("expert", "dp", None),
        ),
        check_vma=False,
    )
```

profile of v0, /device:TPU:0, one launch (start us, length us, event | category | flops | bytes accessed | tf_op | source)
XLA Modules:
  0.0 258.6 jit_solution(1749364280197828076)
XLA Ops:
  7.2 7.2 %reshape.52 = bf16[16,196,768]{2,1,0:T(8,128)(2,1)} reshape(bf16[3136,768]{1,0:T(8,128)(2,1)} %param.5) | data formatting | bytes 9633792 | tf_op jit(solution)/shard_map/reshape | solution.py:19
  14.4 3.7 %fusion.54 = (f32[3136]{0:T(1024)S(1)}, f32[3136,16]{0,1:T(8,128)S(1)}) fusion(bf16[3136,768]{1,0:T(8,128)(2,1)} %param.5, bf16[768,16]{0,1:T(8,128)(2,1)S(1)} %copy-done), kind=kOutput, calls=%fused_computation.59 | convolution fusion | flops 77117376 | bytes 5054720 | tf_op jit(solution)/shard_map/dot_general | solution.py:21
  18.9 3.3 %convolution_convert_fusion.2 = bf16[16,16,768]{2,1,0:T(8,128)(2,1)S(1)} fusion(bf16[16,196,768]{2,1,0:T(8,128)(2,1)} %reshape.52, f32[16,196,16]{1,0,2:T(8,128)S(1)} %reshape.49, f32[16,16]{1,0:T(8,128)S(1)} %fusion.47, f32[16,16]{1,0:T(8,128)S(1)} %copy.28), kind=kOutput, calls=%fused_computation.25 | convolution fusion | flops 77417472 | bytes 5412864 | tf_op jit(solution)/shard_map/bpe,bpd->bed/dot_general | solution.py:28
  23.1 6.4 %all-to-all-start.1 = ((bf16[16,16,768]{2,0,1:T(8,128)(2,1)}), bf16[16,16,768]{2,0,1:T(8,128)(2,1)S(1)}, u32[]{:S(2)}, u32[]{:S(2)}) async-start(bf16[16,16,768]{2,0,1:T(8,128)(2,1)} %copy.32), calls=%async_computation.1 | async-start | bytes 786432 | tf_op jit(solution)/shard_map/all_to_all | solution.py:31
  29.8 7.2 %reshape.50 = bf16[16,196,768]{2,1,0:T(8,128)(2,1)} reshape(bf16[3136,768]{1,0:T(8,128)(2,1)} %param.9) | data formatting | bytes 9633792 | tf_op jit(solution)/shard_map/reshape | solution.py:20
  37.0 3.4 %convolution_convert_fusion.3 = bf16[16,16,768]{2,1,0:T(8,128)(2,1)S(1)} fusion(bf16[16,196,768]{2,1,0:T(8,128)(2,1)} %reshape.50, f32[16,196,16]{1,0,2:T(8,128)S(1)} %reshape.49, f32[16,196]{1,0:T(8,128)S(1)} %div.20, f32[16,196]{1,0:T(8,128)S(1)} %sub.44), kind=kOutput, calls=%fused_computation.26 | convolution fusion | flops 77417472 | bytes 5435904 | tf_op jit(solution)/shard_map/bpe,bpd->bed/dot_general | solution.py:42
  41.2 5.7 %all-to-all-start = ((bf16[16,16,768]{2,0,1:T(8,128)(2,1)}), bf16[16,16,768]{2,0,1:T(8,128)(2,1)S(1)}, u32[]{:S(2)}, u32[]{:S(2)}) async-start(bf16[16,16,768]{2,0,1:T(8,128)(2,1)} %copy.31), calls=%async_computation | async-start | bytes 786432 | tf_op jit(solution)/shard_map/all_to_all | solution.py:46
  47.0 5.4 %fusion.4 = f32[256,3072]{1,0:T(8,128)} fusion(bf16[256,768]{1,0:T(8,128)(2,1)S(1)} %bitcast.84, bf16[1,768,3072]{2,1,0:T(8,128)(2,1)} %param.7), kind=kOutput, calls=%fused_computation.7 | convolution fusion | flops 1207959552 | bytes 8257536 | tf_op jit(solution)/shard_map/dot_general | solution.py:35
  52.4 4.0 %all-to-all-done = bf16[16,16,768]{2,0,1:T(8,128)(2,1)S(1)} async-done(((bf16[16,16,768]{2,0,1:T(8,128)(2,1)}), bf16[16,16,768]{2,0,1:T(8,128)(2,1)S(1)}, u32[]{:S(2)}, u32[]{:S(2)}) %all-to-all-start) | async-done | bytes 393248 | tf_op jit(solution)/shard_map/all_to_all | solution.py:46
  56.4 6.3 %convolution_convert_fusion = bf16[3072,768]{1,0:T(8,128)(2,1)} fusion(bf16[256,768]{1,0:T(8,128)(2,1)S(1)} %bitcast.87, f32[256,3072]{1,0:T(8,128)} %fusion.4), kind=kOutput, calls=%fused_computation.3 | convolution fusion | flops 1217396736 | bytes 8257536 | tf_op jit(solution)/shard_map/dot_general | solution.py:10
  62.9 6.6 %fusion.16 = bf16[256,3072]{1,0:T(8,128)(2,1)S(1)} fusion(f32[256,3072]{1,0:T(8,128)} %fusion.4, bf16[256,768]{1,0:T(8,128)(2,1)S(1)} %bitcast.88, bf16[1,3072,768]{2,1,0:T(8,128)(2,1)} %param.8), kind=kOutput, calls=%fused_computation.21 | convolution fusion | flops 1223688192 | bytes 9830400 | tf_op jit(solution)/shard_map/dot_general | solution.py:10
  69.6 3.6 %convolution_convert_fusion.1 = bf16[768,3072]{1,0:T(8,128)(2,1)} fusion(bf16[256,768]{1,0:T(8,128)(2,1)S(1)} %bitcast.85, bf16[256,3072]{1,0:T(8,128)(2,1)S(1)} %fusion.16), kind=kOutput, calls=%fused_computation.4 | convolution fusion | flops 1210318848 | bytes 6684672 | tf_op jit(solution)/shard_map/dot_general | solution.py:10
  73.2 5.2 %fusion.28 = bf16[256,1,768]{2,0,1:T(8,128)(2,1)S(1)} fusion(bf16[1,3072,768]{2,1,0:T(8,128)(2,1)} %param.8, f32[256,3072]{1,0:T(8,128)} %fusion.4), kind=kOutput, calls=%fused_computation.28 | convolution fusion | flops 1215234048 | bytes 8257536 | tf_op jit(solution)/shard_map/dot_general | solution.py:37
  80.7 3.6 %all-to-all-start.3 = ((bf16[16,2,6144]{2,1,0:T(2,128)(2,1)}), bf16[16,2,6144]{2,1,0:T(2,128)(2,1)S(1)}, u32[]{:S(2)}, u32[]{:S(2)}) async-start(bf16[16,2,6144]{2,1,0:T(2,128)(2,1)} %reshape.62), calls=%async_computation.3 | async-start | bytes 786432 | tf_op jit(solution)/shard_map/all_to_all | solution.py:38
  84.2 3.8 %fusion.25 = bf16[256,1,768]{2,0,1:T(8,128)(2,1)S(1)} fusion(bf16[256,3072]{1,0:T(8,128)(2,1)S(1)} %fusion.16, bf16[1,768,3072]{2,1,0:T(8,128)(2,1)} %param.7), kind=kOutput, calls=%fused_computation.27 | convolution fusion | flops 1208156160 | bytes 6684672 | tf_op jit(solution)/shard_map/dot_general | solution.py:10
  89.8 6.9 %all-to-all-done.3 = bf16[16,2,6144]{2,1,0:T(2,128)(2,1)S(1)} async-done(((bf16[16,2,6144]{2,1,0:T(2,128)(2,1)}), bf16[16,2,6144]{2,1,0:T(2,128)(2,1)S(1)}, u32[]{:S(2)}, u32[]{:S(2)}) %all-to-all-start.3) | async-done | bytes 393248 | tf_op jit(solution)/shard_map/all_to_all | solution.py:38
  96.8 3.6 %all-to-all-start.2 = ((bf16[16,2,6144]{2,1,0:T(2,128)(2,1)}), bf16[16,2,6144]{2,1,0:T(2,128)(2,1)S(1)}, u32[]{:S(2)}, u32[]{:S(2)}) async-start(bf16[16,2,6144]{2,1,0:T(2,128)(2,1)} %reshape.60), calls=%async_computation.2 | async-start | bytes 786432 | tf_op jit(solution)/shard_map/all_to_all | solution.py:63
  100.8 12.1 %all-to-all-done.2 = bf16[16,2,6144]{2,1,0:T(2,128)(2,1)S(1)} async-done(((bf16[16,2,6144]{2,1,0:T(2,128)(2,1)}), bf16[16,2,6144]{2,1,0:T(2,128)(2,1)S(1)}, u32[]{:S(2)}, u32[]{:S(2)}) %all-to-all-start.2) | async-done | bytes 393248 | tf_op jit(solution)/shard_map/all_to_all | solution.py:63
  113.3 3.9 %convolution_bitcast_fusion = f32[16,196,16]{1,2,0:T(8,128)S(1)} fusion(bf16[16,196,768]{2,1,0:T(8,128)(2,1)} %reshape.52, bf16[16,16,1,768]{3,1,0,2:T(8,128)(2,1)S(1)} %bitcast.82), kind=kOutput, calls=%fused_computation.34 | convolution fusion | flops 77070336 | bytes 5410816 | tf_op jit(solution)/shard_map/bpd,bed->bpe/dot_general | solution.py:66
  121.7 5.5 %fusion.39 = f32[16,196,768]{2,1,0:T(8,128)} fusion(bf16[16,16,1,768]{3,1,0,2:T(8,128)(2,1)S(1)} %bitcast.83, f32[16,196,16]{1,0,2:T(8,128)S(1)} %reshape.49, f32[16,16]{1,0:T(8,128)S(1)} %fusion.47, f32[16,16]{1,0:T(8,128)S(1)} %copy.28), kind=kOutput, calls=%fused_computation.42 | convolution fusion | flops 77220864 | bytes 10229760 | tf_op jit(solution)/shard_map/bpe,bed->bpd/dot_general | solution.py:71
  127.1 9.9 %reshape.55 = f32[3136,768]{1,0:T(8,128)} reshape(f32[16,196,768]{2,1,0:T(8,128)} %fusion.39) | data formatting | bytes 19267584 | tf_op jit(solution)/shard_map/reshape | solution.py:73
  140.1 69.2 %psum.7 = f32[768,16]{0,1:T(8,128)} all-reduce(f32[768,16]{0,1:T(8,128)S(1)} %convolution_bitcast_fusion.2), channel_id=1, replica_groups=mesh['dp'=8,'expert'=16] {'dp','expert'}, use_global_device_ids=true, to_apply=%region_6.0 | all-reduce | flops 12288 | bytes 98304 | tf_op jit(solution)/shard_map/psum | solution.py:76
  209.3 7.5 %add_convert_fusion = bf16[3136,768]{1,0:T(8,128)(2,1)} fusion(f32[3136,768]{1,0:T(8,128)} %reshape.55, bf16[3136,16]{0,1:T(8,128)(2,1)S(1)} %reshape.57, bf16[768,16]{0,1:T(8,128)(2,1)S(1)} %copy-done), kind=kOutput, calls=%fused_computation.2 | convolution fusion | flops 81887232 | bytes 14575616 | tf_op jit(solution)/shard_map/dot_general | solution.py:10
  219.0 30.6 %reduce-scatter.3.cloned.1.call-done = bf16[96,3072]{1,0:T(8,128)(2,1)} async-done(((bf16[768,3072]{1,0:T(8,128)(2,1)}), bf16[96,3072]{1,0:T(8,128)(2,1)}) %reduce-scatter.3.cloned.1.call-update) | async-done | bytes 589840 | tf_op jit(solution)/shard_map/reduce_scatter | solution.py:52
  (39 shorter events, 19.8 us)
Async XLA Ops:
  7.2 7.2 %copy-start = (bf16[768,16]{0,1:T(8,128)(2,1)S(1)}, bf16[768,16]{0,1:T(8,128)(2,1)}, u32[]{:S(2)}) copy-start(bf16[768,16]{0,1:T(8,128)(2,1)} %param.6) | copy-start | bytes 73732
  23.1 18.1 %all-to-all-start.1 = ((bf16[16,16,768]{2,0,1:T(8,128)(2,1)}), bf16[16,16,768]{2,0,1:T(8,128)(2,1)S(1)}, u32[]{:S(2)}, u32[]{:S(2)}) async-start(bf16[16,16,768]{2,0,1:T(8,128)(2,1)} %copy.32), calls=%async_computation.1 | async-start | bytes 786432 | tf_op jit(solution)/shard_map/all_to_all | solution.py:31
  41.2 15.2 %all-to-all-start = ((bf16[16,16,768]{2,0,1:T(8,128)(2,1)}), bf16[16,16,768]{2,0,1:T(8,128)(2,1)S(1)}, u32[]{:S(2)}, u32[]{:S(2)}) async-start(bf16[16,16,768]{2,0,1:T(8,128)(2,1)} %copy.31), calls=%async_computation | async-start | bytes 786432 | tf_op jit(solution)/shard_map/all_to_all | solution.py:46
  46.9 169.9 %reduce-scatter.5.cloned.1.call-start = ((), (), s32[]{:S(2)}) async-start(), calls=%async_computation.7 | async-start | bytes 5308416 | tf_op jit(solution)/shard_map/reduce_scatter | solution.py:56
  62.7 186.9 %reduce-scatter.3.cloned.1.call-start = ((), (), s32[]{:S(2)}) async-start(), calls=%async_computation.6 | async-start | bytes 5308416 | tf_op jit(solution)/shard_map/reduce_scatter | solution.py:52
  80.7 16.1 %all-to-all-start.3 = ((bf16[16,2,6144]{2,1,0:T(2,128)(2,1)}), bf16[16,2,6144]{2,1,0:T(2,128)(2,1)S(1)}, u32[]{:S(2)}, u32[]{:S(2)}) async-start(bf16[16,2,6144]{2,1,0:T(2,128)(2,1)} %reshape.62), calls=%async_computation.3 | async-start | bytes 786432 | tf_op jit(solution)/shard_map/all_to_all | solution.py:38
  96.8 16.1 %all-to-all-start.2 = ((bf16[16,2,6144]{2,1,0:T(2,128)(2,1)}), bf16[16,2,6144]{2,1,0:T(2,128)(2,1)S(1)}, u32[]{:S(2)}, u32[]{:S(2)}) async-start(bf16[16,2,6144]{2,1,0:T(2,128)(2,1)} %reshape.60), calls=%async_computation.2 | async-start | bytes 786432 | tf_op jit(solution)/shard_map/all_to_all | solution.py:63
  113.2 6.6 %slice-start = ((s8[4915200]{0:T(1024)(128)(4,1)}), s8[4194304]{0:T(1024)(128)(4,1)S(1)}, s32[]{:S(2)}) async-start(s8[4915200]{0:T(1024)(128)(4,1)} %bitcast.80), calls=%async_computation.8 | async-start | bytes 8388608
  113.3 6.5 %slice-start.1 = ((s8[4915200]{0:T(1024)(128)(4,1)}), s8[720896]{0:T(1024)(128)(4,1)S(1)}, s32[]{:S(2)}) async-start(s8[4915200]{0:T(1024)(128)(4,1)} %bitcast.80), calls=%async_computation.9 | async-start | bytes 1441792
Sparse Core Ops, SparseCore 0:
  62.8 96.0 reduce-scatter.4
  162.8 86.7 reduce-scatter.2
where the time goes:
time: 260 us; the launch traced here: 259 us
  blocking collectives  69.2 us (27%)
  matrix products  62.7 us (24%)
  waiting for transfers between devices  53.6 us (21%)
  local copies, waits for them, and re-layouts  30 us (12%)
  starting transfers between devices  19.5 us (8%)
  between operations  14.2 us (5%)
  other arithmetic  9.39 us (4%)
    psum x1, blocking collectives, on_device(): grad_router = lax.psum(router_term, ('dp', 'expert'))  69.2 us
    dot_general x6, matrix products, contract(): lax.dot_general(left, right, (((left_dim,), (right_dim,)), ((), ())), pre...  30.9 us
    reduce_scatter x1, waiting for transfers between devices, on_device(): lax.psum_scatter(contract(picked, grad_pre, 0, 0).astype(jnp.bfloat16), '...  30.6 us
    all_to_all x1, waiting for transfers between devices, on_device(): lax.all_to_all(grad_rows.reshape(-1, 1, feat_width), 'expert', split_axis...  12.1 us
    reshape x1, local copies, waits for them, and re-layouts, on_device(): grad_tok = jnp.einsum('bpe,bed->bpd', dispatch_low, grad_slot_in, preferr...  9.88 us
    reshape x1, local copies, waits for them, and re-layouts, on_device(): tok_grid = tokens.reshape(img_count, PATCHES, feat_width)  7.22 us
    reshape x1, local copies, waits for them, and re-layouts, on_device(): out_grid = g_outputs.reshape(img_count, PATCHES, feat_width)  7.2 us
    all_to_all x1, waiting for transfers between devices, on_device(): lax.all_to_all(rows_out.reshape(-1, 1, feat_width), 'expert', split_axis=...  6.94 us
  transfers between devices with their start and end apart: 6, of which 4 were waited for; matrix products, arithmetic and copies ran while one was open for 30% of the time, Pallas kernels for 0%

commit v1 on v0

v1 whole, which is shorter than its diff:
```python
import jax
import jax.numpy as jnp
from jax import lax
from jax.experimental import pallas as pl
from jax.experimental.pallas import tpu as pltpu
from jax.sharding import Mesh, PartitionSpec as P

PATCHES = 196
GROUP = 4
XH = 2
VMEM_BYTES = 56 * 1024 * 1024
GELU_C = 0.7978845608028654
GELU_A = 0.044715

f32 = jnp.float32
bf16 = jnp.bfloat16


def contract(left, right, left_dim, right_dim):
    return lax.dot_general(
        left, right, (((left_dim,), (right_dim,)), ((), ())), preferred_element_type=f32
    )


def params():
    return pltpu.CompilerParams(
        dimension_semantics=("arbitrary",), vmem_limit_bytes=VMEM_BYTES
    )


def lane_images(width):
    lane = lax.broadcasted_iota(jnp.int32, (1, width), 1)
    image = jnp.zeros_like(lane)
    for i in range(1, width // PATCHES):
        image = image + (lane >= i * PATCHES).astype(jnp.int32)
    return image


def per_image(values, image, count, reduce, start):
    out = jnp.zeros_like(values)
    for i in range(count):
        own = reduce(jnp.where(image == i, values, start), axis=1, keepdims=True)
        out = jnp.where(image == i, own, out)
    return out


def gelu_parts(x):
    x2 = x * x
    th = jnp.tanh(GELU_C * x * (1.0 + GELU_A * x2))
    cdf = 0.5 + 0.5 * th
    slope = cdf + (0.5 * GELU_C) * x * (1.0 - th * th) * (1.0 + (3.0 * GELU_A) * x2)
    return x * cdf, slope


def token_forward_body(router_ref, x_ref, g_ref, slots_ref, disp_ref, comb_ref, rt, acc_x, acc_g):
    step = pl.program_id(0)
    experts, images, _ = slots_ref.shape
    feat = x_ref.shape[1]
    width = x_ref.shape[0]

    @pl.when(step == 0)
    def _():
        rt[...] = router_ref[...].astype(f32).T.astype(bf16)
        acc_x[...] = jnp.zeros_like(acc_x)
        acc_g[...] = jnp.zeros_like(acc_g)

    x = x_ref[...]
    logits = contract(rt[...], x, 1, 1)
    image = lane_images(width)
    top = per_image(logits, image, GROUP, jnp.max, -jnp.inf)
    raised = jnp.exp(logits - top)
    dispatch = raised / per_image(raised, image, GROUP, jnp.sum, 0.0)
    raised_e = jnp.exp(logits - jnp.max(logits, axis=0, keepdims=True))
    combine = raised_e / jnp.sum(raised_e, axis=0, keepdims=True)
    disp_ref[0] = dispatch
    comb_ref[0] = combine
    row = lax.broadcasted_iota(jnp.int32, (1, images, 1), 1)
    own = row == (image + step * GROUP)[None]
    spread_d = jnp.where(own, dispatch[:, None, :], 0.0).astype(bf16)
    spread_c = jnp.where(own, combine[:, None, :], 0.0).astype(bf16)
    acc_x[...] += jnp.dot(
        spread_d.reshape(experts * images, width), x, preferred_element_type=f32
    )
    acc_g[...] += jnp.dot(
        spread_c.reshape(experts * images, width), g_ref[...], preferred_element_type=f32
    )

    @pl.when(step == pl.num_programs(0) - 1)
    def _():
        slots_ref[:, :, :feat] = acc_x[...].astype(bf16).reshape(experts, images, feat)
        slots_ref[:, :, feat:] = acc_g[...].astype(bf16).reshape(experts, images, feat)


def token_forward(tokens, router, g_outputs):
    rows, feat = tokens.shape
    experts = router.shape[1]
    images = rows // PATCHES
    width = GROUP * PATCHES
    steps = rows // width
    return pl.pallas_call(
        token_forward_body,
        grid=(steps,),
        in_specs=[
            pl.BlockSpec((feat, experts), lambda i: (0, 0)),
            pl.BlockSpec((width, feat), lambda i: (i, 0)),
            pl.BlockSpec((width, feat), lambda i: (i, 0)),
        ],
        out_specs=[
            pl.BlockSpec((experts, images, 2 * feat), lambda i: (0, 0, 0)),
            pl.BlockSpec((1, experts, width), lambda i: (i, 0, 0)),
            pl.BlockSpec((1, experts, width), lambda i: (i, 0, 0)),
        ],
        out_shape=[
            jax.ShapeDtypeStruct((experts, images, 2 * feat), bf16),
            jax.ShapeDtypeStruct((steps, experts, width), f32),
            jax.ShapeDtypeStruct((steps, experts, width), f32),
        ],
        scratch_shapes=[
            pltpu.VMEM((experts, feat), bf16),
            pltpu.VMEM((experts * images, feat), f32),
            pltpu.VMEM((experts * images, feat), f32),
        ],
        compiler_params=params(),
        name="token_forward",
    )(router, tokens, g_outputs)


def expert_body(rows_ref, w1_ref, w2_ref, out_ref, acc_o, acc_g):
    step = pl.program_id(0)
    feat = w1_ref.shape[0]

    @pl.when(step == 0)
    def _():
        acc_o[...] = jnp.zeros_like(acc_o)
        acc_g[...] = jnp.zeros_like(acc_g)

    rows = rows_ref[:, :feat]
    grads = rows_ref[:, feat:]
    w1 = w1_ref[...]
    w2 = w2_ref[...]
    pre = jnp.dot(rows, w1, preferred_element_type=f32)
    act, slope = gelu_parts(pre)
    acc_o[...] += jnp.dot(act.astype(bf16), w2, preferred_element_type=f32)
    grad_pre = (contract(grads, w2, 1, 1) * slope).astype(bf16)
    acc_g[...] += contract(grad_pre, w1, 1, 1)

    @pl.when(step == pl.num_programs(0) - 1)
    def _():
        out_ref[:, :feat] = acc_o[...].astype(bf16)
        out_ref[:, feat:] = acc_g[...].astype(bf16)


def expert_rows(rows, w_in, w_out):
    count, double = rows.shape
    feat = double // 2
    hidden = w_in.shape[2]
    tile = 512
    return pl.pallas_call(
        expert_body,
        grid=(hidden // tile,),
        in_specs=[
            pl.BlockSpec((count, double), lambda i: (0, 0)),
            pl.BlockSpec((None, feat, tile), lambda i: (0, 0, i)),
            pl.BlockSpec((None, tile, feat), lambda i: (0, i, 0)),
        ],
        out_specs=pl.BlockSpec((count, double), lambda i: (0, 0)),
        out_shape=jax.ShapeDtypeStruct((count, double), bf16),
        scratch_shapes=[pltpu.VMEM((count, feat), f32), pltpu.VMEM((count, feat), f32)],
        compiler_params=params(),
        name="expert_rows",
    )(rows, w_in, w_out)


def weight_grad_body(
    pos_ref, p0, p1, p2, p3, p4, w1_ref, w2_ref, keep_in, send_in, keep_out, send_out, acc
):
    feat = w1_ref.shape[0]
    xh = pos_ref[1]
    step = pl.program_id(0)
    w1 = w1_ref[...]
    w2 = w2_ref[...]
    total_in = None
    total_out = None
    for piece in (p0, p1, p2, p3, p4):
        rows = piece[:, :feat]
        grads = piece[:, feat:]
        act, slope = gelu_parts(jnp.dot(rows, w1, preferred_element_type=f32))
        grad_pre = (contract(grads, w2, 1, 1) * slope).astype(bf16)
        part_out = contract(act.astype(bf16), grads, 0, 0)
        part_in = contract(rows, grad_pre, 0, 0)
        total_out = part_out if total_out is None else total_out + part_out
        total_in = part_in if total_in is None else total_in + part_in
    acc[...] = total_in.reshape(acc.shape)
    keep_in[...] = acc[:, pl.ds(xh, 1)].reshape(keep_in.shape)
    send_in[...] = acc[:, pl.ds(1 - xh, 1)].reshape(send_in.shape).astype(bf16)

    @pl.when(step == 0)
    def _():
        send_out[...] = total_out.astype(bf16)

    @pl.when(step == 1)
    def _():
        keep_out[...] = total_out


def weight_grads(pos, pieces, w_in, w_out, parts):
    feat = w_in.shape[1]
    hidden = w_in.shape[2]
    tile = hidden // (parts * XH)
    own = feat // (parts * XH)

    def half(i, pos):
        return XH * pos[0] + jnp.where(i == 0, 1 - pos[1], pos[1])

    def tile_at(i, pos):
        return jnp.where(i == 0, 1 - pos[1], pos[1])

    return pl.pallas_call(
        weight_grad_body,
        grid_spec=pltpu.PrefetchScalarGridSpec(
            num_scalar_prefetch=1,
            grid=(XH,),
            in_specs=[pl.BlockSpec(p.shape, lambda i, pos: (0, 0)) for p in pieces]
            + [
                pl.BlockSpec((None, feat, tile), lambda i, pos: (0, 0, half(i, pos))),
                pl.BlockSpec((None, tile, feat), lambda i, pos: (0, half(i, pos), 0)),
            ],
            out_specs=[
                pl.BlockSpec((parts, own, tile), lambda i, pos: (0, 0, tile_at(i, pos))),
                pl.BlockSpec((parts, own, tile), lambda i, pos: (0, 0, tile_at(i, pos))),
                pl.BlockSpec((tile, feat), lambda i, pos: (0, 0)),
                pl.BlockSpec((tile, feat), lambda i, pos: (0, 0)),
            ],
            scratch_shapes=[pltpu.VMEM((parts, XH, own, tile), f32)],
        ),
        out_shape=[
            jax.ShapeDtypeStruct((parts, own, XH * tile), f32),
            jax.ShapeDtypeStruct((parts, own, XH * tile), bf16),
            jax.ShapeDtypeStruct((tile, feat), f32),
            jax.ShapeDtypeStruct((tile, feat), bf16),
        ],
        compiler_params=params(),
        name="weight_grads",
    )(pos, *pieces, w_in, w_out)


def token_logits_body(back_ref, x_ref, g_ref, disp_ref, comb_ref, gl_ref, slots_ref, router_ref, mix):
    step = pl.program_id(0)
    experts, images, double = back_ref.shape
    feat = double // 2
    width = x_ref.shape[0]
    total = experts * images

    @pl.when(step == 0)
    def _():
        out_row = lax.broadcasted_iota(jnp.int32, (total, total), 0)
        in_row = lax.broadcasted_iota(jnp.int32, (total, total), 1)
        wanted = (out_row % experts) * images + out_row // experts
        swap = (in_row == wanted).astype(f32).astype(bf16)
        mix[...] = jnp.dot(
            swap, back_ref[...].reshape(total, double), preferred_element_type=f32
        ).astype(bf16)
        router_ref[...] = jnp.zeros_like(router_ref)

    x = x_ref[...]
    block = mix[pl.ds(pl.multiple_of(step * (GROUP * experts), GROUP * experts), GROUP * experts), :]
    slots_ref[0] = block[:, feat:]
    image = lane_images(width)

    def picked(both):
        out = jnp.zeros((experts, width), f32)
        for i in range(GROUP):
            out = jnp.where(image == i, both[i * experts : (i + 1) * experts], out)
        return out

    grad_comb = picked(contract(block[:, :feat], g_ref[...], 1, 1))
    grad_disp = picked(contract(block[:, feat:], x, 1, 1))
    dispatch = disp_ref[0]
    combine = comb_ref[0]
    comb_part = combine * (grad_comb - jnp.sum(combine * grad_comb, axis=0, keepdims=True))
    disp_part = dispatch * (
        grad_disp - per_image(dispatch * grad_disp, image, GROUP, jnp.sum, 0.0)
    )
    grad_logits = (comb_part + disp_part).astype(bf16)
    gl_ref[0] = grad_logits
    router_ref[...] += jnp.dot(grad_logits, x, preferred_element_type=f32)


def token_logits(back, tokens, g_outputs, dispatch, combine):
    experts, images, double = back.shape
    rows, feat = tokens.shape
    steps, _, width = dispatch.shape
    return pl.pallas_call(
        token_logits_body,
        grid=(steps,),
        in_specs=[
            pl.BlockSpec((experts, images, double), lambda i: (0, 0, 0)),
            pl.BlockSpec((width, feat), lambda i: (i, 0)),
            pl.BlockSpec((width, feat), lambda i: (i, 0)),
            pl.BlockSpec((1, experts, width), lambda i: (i, 0, 0)),
            pl.BlockSpec((1, experts, width), lambda i: (i, 0, 0)),
        ],
        out_specs=[
            pl.BlockSpec((1, experts, width), lambda i: (i, 0, 0)),
            pl.BlockSpec((1, GROUP * experts, feat), lambda i: (i, 0, 0)),
            pl.BlockSpec((experts, feat), lambda i: (0, 0)),
        ],
        out_shape=[
            jax.ShapeDtypeStruct((steps, experts, width), bf16),
            jax.ShapeDtypeStruct((steps, GROUP * experts, feat), bf16),
            jax.ShapeDtypeStruct((experts, feat), f32),
        ],
        scratch_shapes=[pltpu.VMEM((experts * images, double), bf16)],
        compiler_params=params(),
        name="token_logits",
    )(back, tokens, g_outputs, dispatch, combine)


def token_grads_body(gl_ref, slots_ref, disp_ref, router_ref, out_ref, rt):
    experts = gl_ref.shape[1]
    width = gl_ref.shape[2]

    @pl.when(pl.program_id(0) == 0)
    def _():
        rt[...] = router_ref[...].astype(f32).T.astype(bf16)

    image = lane_images(width)
    dispatch = disp_ref[0]
    left = jnp.concatenate(
        [jnp.where(image == i, dispatch, 0.0) for i in range(GROUP)], axis=0
    ).astype(bf16)
    left = jnp.concatenate([left, gl_ref[0]], axis=0)
    right = jnp.concatenate([slots_ref[0], rt[...]], axis=0)
    out_ref[...] = contract(left, right, 0, 0).astype(bf16)


def token_grads(grad_logits, slots, dispatch, router):
    steps, experts, width = grad_logits.shape
    feat = slots.shape[2]
    return pl.pallas_call(
        token_grads_body,
        grid=(steps,),
        in_specs=[
            pl.BlockSpec((1, experts, width), lambda i: (i, 0, 0)),
            pl.BlockSpec((1, GROUP * experts, feat), lambda i: (i, 0, 0)),
            pl.BlockSpec((1, experts, width), lambda i: (i, 0, 0)),
            pl.BlockSpec((feat, experts), lambda i: (0, 0)),
        ],
        out_specs=pl.BlockSpec((width, feat), lambda i: (i, 0)),
        out_shape=jax.ShapeDtypeStruct((steps * width, feat), bf16),
        scratch_shapes=[pltpu.VMEM((experts, feat), bf16)],
        compiler_params=params(),
        name="token_grads",
    )(grad_logits, slots, dispatch, router)


def shift(value, axis, by, count):
    return lax.ppermute(value, axis, [(i, (i + by) % count) for i in range(count)])


def everywhere_sum(value, sizes):
    for axis, count in sizes:
        value = sum([shift(value, axis, by, count) for by in range(1, count)], value)
    return value


def solution(mesh):
    dp, experts = mesh.shape["dp"], mesh.shape["expert"]
    ny = dp // XH
    inner = (("core", 2), ("xl", 2), ("z", experts // 4))
    fine = Mesh(
        mesh.devices.reshape(ny, XH, experts // 4, 2, 2), ("y", "xh", "z", "xl", "core")
    )
    dp_axes = ("y", "xh")
    ex_axes = ("z", "xl", "core")
    sizes = inner + (("y", ny), ("xh", XH))

    def on_device(tokens, router, w_in, w_out, g_outputs):
        feat = tokens.shape[1]
        slots, dispatch, combine = token_forward(tokens, router, g_outputs)
        arrived = lax.all_to_all(slots, ex_axes, split_axis=0, concat_axis=0, tiled=True)
        rows = arrived.reshape(-1, 2 * feat)
        half = rows.shape[0] // 2
        right = shift(rows, "y", 1, ny)
        left = shift(rows, "y", ny - 1, ny)
        far_a = shift(right[:half], "y", 1, ny)
        far_b = shift(left[half:], "y", ny - 1, ny)
        results = expert_rows(rows, w_in, w_out)
        back = lax.all_to_all(
            results.reshape(slots.shape), ex_axes, split_axis=0, concat_axis=0, tiled=True
        )
        pos = jnp.stack([lax.axis_index("y"), lax.axis_index("xh")]).astype(jnp.int32)
        keep_in, send_in, keep_out, send_out = weight_grads(
            pos, (rows, right, left, far_a, far_b), w_in, w_out, ny
        )
        came_in = shift(send_in, "xh", 1, XH)
        came_out = shift(send_out, "xh", 1, XH)
        part_in = (keep_in + came_in.astype(f32)).astype(bf16)
        spread = lax.all_to_all(part_in, "y", split_axis=0, concat_axis=0, tiled=True)
        grad_first = jnp.transpose(spread, (1, 0, 2)).reshape(spread.shape[1], -1).astype(f32)
        grad_second = keep_out + came_out.astype(f32)
        grad_logits, slot_grads, router_term = token_logits(
            back, tokens, g_outputs, dispatch, combine
        )
        grad_router = everywhere_sum(router_term, sizes).T
        grad_tok = token_grads(grad_logits, slot_grads, dispatch, router)
        return grad_tok, grad_router, grad_first[None], grad_second[None]

    return jax.shard_map(
        on_device,
        mesh=fine,
        in_specs=(
            P(dp_axes + ex_axes, None),
            P(),
            P(ex_axes, None, None),
            P(ex_axes, None, None),
            P(dp_axes + ex_axes, None),
        ),
        out_specs=(
            P(dp_axes + ex_axes, None),
            P(),
            P(ex_axes, dp_axes, None),
            P(ex_axes, dp_axes, None),
        ),
        check_vma=False,
    )
```

time: 260 us -> 131 us (0.50)
  matrix products: 62.7 us -> 0 us
  blocking collectives: 69.2 us -> 20.1 us
  Pallas kernels: 0 us -> 46.5 us
  waiting for transfers between devices: 53.6 us -> 22.3 us
  local copies, waits for them, and re-layouts: 30 us -> 7.23 us
  between operations: 14.2 us -> 0.75 us
  starting transfers between devices: 19.5 us -> 28.5 us
  other arithmetic: 9.39 us -> 4.19 us
    psum x1 -> x0, blocking collectives: 69.2 us -> none  [on_device(): grad_router = lax.psum(router_term, ('dp', 'expert'))]
    dot_general x14 -> x0, matrix products: 62.7 us -> none  [the longest x6 30.9 us: contract(): lax.dot_general(left, right, (((left_dim,), (right_dim,)), ((), ())), pre...]
    pallas_call x0 -> x5, Pallas kernels: none -> 46.5 us  [the longest x1 12.4 us: weight_grads(): pl.pallas_call(weight_grad_body, grid_spec=pltpu.PrefetchScalarGridSpec(n...]
    reduce_scatter x2 -> x0, waiting for transfers between devices: 30.6 us -> none  [the longest x1 30.6 us: on_device(): lax.psum_scatter(contract(picked, grad_pre, 0, 0).astype(jnp.bfloat16), '...]
    reshape x6 -> x0, local copies, waits for them, and re-layouts: 25.3 us -> none  [the longest x1 9.88 us: on_device(): grad_tok = jnp.einsum('bpe,bed->bpd', dispatch_low, grad_slot_in, preferr...]
    ppermute x0 -> x15, starting transfers between devices: none -> 20.9 us  [shift(): lax.ppermute(value, axis, [(i, (i + by) % count) for i in range(count)])]
    all_to_all x0 -> x1, blocking collectives: none -> 20.1 us  [on_device(): lax.all_to_all(slots, ex_axes, split_axis=0, concat_axis=0, tiled=True)]
    all_to_all x4 -> x2, waiting for transfers between devices: 23 us -> 6.77 us  [the longest x1 6.76 us: on_device(): lax.all_to_all(results.reshape(slots.shape), ex_axes, split_axis=0, conca...]
  transfers between devices with their start and end apart: 6 -> 17, of which waited for: 4 -> 7; matrix products, arithmetic and copies ran while one was open for 30% -> 4% of each run, Pallas kernels for 0% -> 29%
where the time goes in v1:
time: 131 us; the launch traced here: 130 us
  Pallas kernels  46.5 us (35%)
  starting transfers between devices  28.5 us (22%)
  waiting for transfers between devices  22.3 us (17%)
  blocking collectives  20.1 us (15%)
  local copies, waits for them, and re-layouts  7.23 us (6%)
  other arithmetic  4.19 us (3%)
    ppermute x15, starting transfers between devices, shift(): lax.ppermute(value, axis, [(i, (i + by) % count) for i in range(count)])  20.9 us
    all_to_all x1, blocking collectives, on_device(): lax.all_to_all(slots, ex_axes, split_axis=0, concat_axis=0, tiled=True)  20.1 us
    ppermute x15, waiting for transfers between devices, shift(): lax.ppermute(value, axis, [(i, (i + by) % count) for i in range(count)])  15.5 us
    pallas_call x1, Pallas kernels, weight_grads(): pl.pallas_call(weight_grad_body, grid_spec=pltpu.PrefetchScalarGridSpec(n...  12.4 us
    pallas_call x1, Pallas kernels, expert_rows(): pl.pallas_call(expert_body, grid=(hidden // tile,), in_specs=[pl.BlockSpe...  10.6 us
    pallas_call x1, Pallas kernels, token_forward(): pl.pallas_call(token_forward_body, grid=(steps,), in_specs=[pl.BlockSpec(...  9.34 us
    pallas_call x1, Pallas kernels, token_logits(): pl.pallas_call(token_logits_body, grid=(steps,), in_specs=[pl.BlockSpec((...  8.87 us
    all_to_all x1, waiting for transfers between devices, on_device(): lax.all_to_all(results.reshape(slots.shape), ex_axes, split_axis=0, conca...  6.76 us
  transfers between devices with their start and end apart: 17, of which 7 were waited for; matrix products, arithmetic and copies ran while one was open for 4% of the time, Pallas kernels for 29%

profile of v1, /device:TPU:0, one launch (start us, length us, event | category | flops | bytes accessed | tf_op | source)
XLA Modules:
  0.0 129.5 jit_solution(10451361015479404211)
XLA Ops:
  0.6 1.6 %copy.11.router_ref = bf16[768,16]{1,0:T(8,128)(2,1)} copy(bf16[768,16]{0,1:T(8,128)(2,1)} %param.6) | data formatting | bytes 49152 | tf_op args[1]
  2.2 9.3 %token_forward.1 = (bf16[16,16,1536]{2,1,0:T(8,128)(2,1)}, f32[4,16,784]{2,1,0:T(8,128)}, f32[4,16,784]{2,1,0:T(8,128)}) custom-call(bf16[768,16]{1,0:T(8,128)(2,1)} %copy.11.router_ref, bf16[3136,768]{1,0:T(8,128)(2,1)} %x_ref.3, bf16[3136,768]{1,0:T(8,128)(2,1)} %g_ref.3), custom_call_target="tpu_custom_call" | custom-call | tf_op jit(solution)/shard_map/token_forward/pallas_call | solution.py:100
  11.6 20.1 %all_to_all.15 = bf16[16,16,1536]{2,1,0:T(8,128)(2,1)S(1)} all-to-all(bf16[16,16,1536]{2,1,0:T(8,128)(2,1)} %get-tuple-element.14), channel_id=1, replica_groups=mesh['y'=4,'xh'=2,'z'=4,'xl'=2,'core'=2] {'z','xl','core'}, dimensions={0} | all-to-all | bytes 1572864 | tf_op jit(solution)/shard_map/all_to_all | solution.py:381
  31.7 3.0 %collective-permute-start.10 = (bf16[256,1536]{1,0:T(8,128)(2,1)S(1)}, bf16[256,1536]{1,0:T(8,128)(2,1)S(1)}, u32[]{:S(2)}, u32[]{:S(2)}) collective-permute-start(bf16[256,1536]{1,0:T(8,128)(2,1)S(1)} %bitcast.10), channel_id=1, source_target_pairs={{0,96},{32,0},{64,32},{96,64},{1,97},{33,1},{65,33},{97,65},{2,98}... | collective-permute-start | bytes 2359304 | tf_op jit(solution)/shard_map/ppermute | solution.py:358
  34.7 10.6 %expert_rows.1 = bf16[256,1536]{1,0:T(8,128)(2,1)} custom-call(bf16[256,1536]{1,0:T(8,128)(2,1)} %bitcast.12, bf16[1,768,3072]{2,1,0:T(8,128)(2,1)} %w1_ref.3, bf16[1,3072,768]{2,1,0:T(8,128)(2,1)} %w2_ref.3), custom_call_target="tpu_custom_call" | custom-call | tf_op jit(solution)/shard_map/expert_rows/pallas_call | solution.py:158
  45.3 3.6 %all-to-all-start.1 = ((bf16[16,16,1536]{2,1,0:T(8,128)(2,1)}), bf16[16,16,1536]{2,1,0:T(8,128)(2,1)S(1)}, u32[]{:S(2)}, u32[]{:S(2)}) async-start(bf16[16,16,1536]{2,1,0:T(8,128)(2,1)} %bitcast.14), calls=%async_computation.1 | async-start | bytes 1572864 | tf_op jit(solution)/shard_map/all_to_all | solution.py:389
  48.9 2.3 %collective-permute-done.10.p2 = bf16[256,1536]{1,0:T(8,128)(2,1)S(1)} collective-permute-done((bf16[256,1536]{1,0:T(8,128)(2,1)S(1)}, bf16[256,1536]{1,0:T(8,128)(2,1)S(1)}, u32[]{:S(2)}, u32[]{:S(2)}) %collective-permute-start.10) | collective-permute-done | bytes 786464 | tf_op jit(solution)/shard_map/ppermute | solution.py:358
  52.0 3.7 %collective-permute-start.12 = (bf16[128,1536]{1,0:T(8,128)(2,1)}, bf16[128,1536]{1,0:T(8,128)(2,1)S(1)}, u32[]{:S(2)}, u32[]{:S(2)}) collective-permute-start(bf16[128,1536]{1,0:T(8,128)(2,1)} %slice.9), channel_id=1, source_target_pairs={{0,96},{32,0},{64,32},{96,64},{1,97},{33,1},{65,33},{97,65},{2,98}... | collective-permute-start | bytes 1179656 | tf_op jit(solution)/shard_map/ppermute | solution.py:358
  55.8 6.8 %all-to-all-done.1.back_ref = bf16[16,16,1536]{2,1,0:T(8,128)(2,1)S(1)} async-done(((bf16[16,16,1536]{2,1,0:T(8,128)(2,1)}), bf16[16,16,1536]{2,1,0:T(8,128)(2,1)S(1)}, u32[]{:S(2)}, u32[]{:S(2)}) %all-to-all-start.1) | async-done | bytes 786464 | tf_op jit(solution)/shard_map/all_to_all | solution.py:389
  63.5 8.9 %token_logits.1 = (bf16[4,16,784]{2,1,0:T(8,128)(2,1)}, bf16[4,64,768]{2,1,0:T(8,128)(2,1)}, f32[16,768]{1,0:T(8,128)}) custom-call(bf16[16,16,1536]{2,1,0:T(8,128)(2,1)} %copy-done.1, bf16[3136,768]{1,0:T(8,128)(2,1)} %x_ref.3, bf16[3136,768]{1,0:T(8,128)(2,1)} %g_ref.3, f32[4,16,784]{2,1,0:T(8,128)} %get-tuple-element.15.disp_ref, ...), custom_call_target="tpu_custom_call" | custom-call | tf_op jit(solution)/shard_map/token_logits/pallas_call | solution.py:293
  72.5 1.4 %collective-permute-done = f32[16,768]{1,0:T(8,128)S(1)} collective-permute-done((f32[16,768]{1,0:T(8,128)}, f32[16,768]{1,0:T(8,128)S(1)}, u32[]{:S(2)}, u32[]{:S(2)}) %collective-permute-start) | collective-permute-done | bytes 49184 | tf_op jit(solution)/shard_map/ppermute | solution.py:358
  77.5 12.4 %weight_grads.1 = (f32[4,96,768]{2,1,0:T(8,128)}, bf16[4,96,768]{2,1,0:T(8,128)(2,1)}, f32[384,768]{1,0:T(8,128)}, bf16[384,768]{1,0:T(8,128)(2,1)}) custom-call(s32[2]{0:T(128)} %pad_add_fusion.pos_ref, bf16[256,1536]{1,0:T(8,128)(2,1)} %bitcast.13, bf16[256,1536]{1,0:T(8,128)(2,1)} %copy-done.3, bf16[256,1536]{1,0:T(8,128)(2,1)} %copy-done.2, ...), custom_call_target="tpu_custom_call" | custom-call | tf_op jit(solution)/shard_map/weight_grads/pallas_call | solution.py:218
  89.9 2.8 %collective-permute-start.13 = (bf16[4,96,768]{2,1,0:T(8,128)(2,1)}, bf16[4,96,768]{2,1,0:T(8,128)(2,1)S(1)}, u32[]{:S(2)}, u32[]{:S(2)}) collective-permute-start(bf16[4,96,768]{2,1,0:T(8,128)(2,1)} %get-tuple-element.21), channel_id=1, source_target_pairs={{0,16},{16,0},{1,17},{17,1},{2,18},{18,2},{3,19},{19,3},{4,20},{20... | collective-permute-start | bytes 1769480 | tf_op jit(solution)/shard_map/ppermute | solution.py:358
  93.2 1.5 %collective-permute-start.3 = (f32[16,768]{1,0:T(8,128)S(1)}, f32[16,768]{1,0:T(8,128)S(1)}, u32[]{:S(2)}, u32[]{:S(2)}) collective-permute-start(f32[16,768]{1,0:T(8,128)S(1)} %add.34), channel_id=1, source_target_pairs={{0,8},{4,12},{8,0},{12,4},{1,9},{5,13},{9,1},{13,5},{2,10},{6,14},... | collective-permute-start | bytes 147464 | tf_op jit(solution)/shard_map/ppermute | solution.py:358
  95.2 1.6 %collective-permute-done.4 = f32[16,768]{1,0:T(8,128)S(1)} collective-permute-done((f32[16,768]{1,0:T(8,128)S(1)}, f32[16,768]{1,0:T(8,128)S(1)}, u32[]{:S(2)}, u32[]{:S(2)}) %collective-permute-start.4) | collective-permute-done | bytes 49184 | tf_op jit(solution)/shard_map/ppermute | solution.py:358
  96.9 2.1 %collective-permute-done.3 = f32[16,768]{1,0:T(8,128)S(1)} collective-permute-done((f32[16,768]{1,0:T(8,128)S(1)}, f32[16,768]{1,0:T(8,128)S(1)}, u32[]{:S(2)}, u32[]{:S(2)}) %collective-permute-start.3) | collective-permute-done | bytes 49184 | tf_op jit(solution)/shard_map/ppermute | solution.py:358
  99.0 1.0 collective-permute-done.2
  100.0 3.5 %collective-permute-start.7 = (f32[16,768]{1,0:T(8,128)S(1)}, f32[16,768]{1,0:T(8,128)S(1)}, u32[]{:S(2)}, u32[]{:S(2)}) collective-permute-start(f32[16,768]{1,0:T(8,128)S(1)} %add_add_fusion.1), channel_id=1, source_target_pairs={{0,96},{32,0},{64,32},{96,64},{1,97},{33,1},{65,33},{97,65},{2,98}... | collective-permute-start | bytes 147464 | tf_op jit(solution)/shard_map/ppermute | solution.py:358
  104.4 5.3 %token_grads.1 = bf16[3136,768]{1,0:T(8,128)(2,1)} custom-call(bf16[4,16,784]{2,1,0:T(8,128)(2,1)} %get-tuple-element.17.gl_ref, bf16[4,64,768]{2,1,0:T(8,128)(2,1)} %get-tuple-element.18.slots_ref, f32[4,16,784]{2,1,0:T(8,128)} %get-tuple-element.15.disp_ref, bf16[768,16]{1,0:T(8,128)(2,1)} %copy.11.router_ref), custom_call_target="tpu_custom_call" | custom-call | tf_op jit(solution)/shard_map/token_grads/pallas_call | solution.py:340
  110.5 2.8 %collective-permute-start.8 = (f32[16,768]{1,0:T(8,128)S(1)}, f32[16,768]{1,0:T(8,128)S(1)}, u32[]{:S(2)}, u32[]{:S(2)}) collective-permute-start(f32[16,768]{1,0:T(8,128)S(1)} %add_add_fusion), channel_id=1, source_target_pairs={{0,16},{16,0},{1,17},{17,1},{2,18},{18,2},{3,19},{19,3},{4,20},{20... | collective-permute-start | bytes 147464 | tf_op jit(solution)/shard_map/ppermute | solution.py:358
  114.3 4.0 %all-to-all-start.2 = ((bf16[4,96,768]{2,1,0:T(8,128)(2,1)}), bf16[4,96,768]{2,1,0:T(8,128)(2,1)S(1)}, u32[]{:S(2)}, u32[]{:S(2)}) async-start(bf16[4,96,768]{2,1,0:T(8,128)(2,1)} %add_convert_fusion), calls=%async_computation.2 | async-start | bytes 1179648 | tf_op jit(solution)/shard_map/all_to_all | solution.py:399
  118.3 7.0 %collective-permute-done.8 = f32[16,768]{1,0:T(8,128)S(1)} collective-permute-done((f32[16,768]{1,0:T(8,128)S(1)}, f32[16,768]{1,0:T(8,128)S(1)}, u32[]{:S(2)}, u32[]{:S(2)}) %collective-permute-start.8) | collective-permute-done | bytes 49184 | tf_op jit(solution)/shard_map/ppermute | solution.py:358
  125.9 1.1 add_bitcast_fusion
  127.9 1.6 %reshape.29 = f32[1,96,3072]{2,1,0:T(8,128)} reshape(f32[96,4,768]{2,1,0:T(4,128)S(1)} %copy.13) | data formatting | bytes 2359296 | tf_op jit(solution)/shard_map/convert_element_type | solution.py:400
  (48 shorter events, 10.8 us)
Async XLA Ops:
  31.7 3.0 %copy-start = (bf16[16,16,1536]{2,1,0:T(8,128)(2,1)}, bf16[16,16,1536]{2,1,0:T(8,128)(2,1)S(1)}, u32[]{:S(2)}) copy-start(bf16[16,16,1536]{2,1,0:T(8,128)(2,1)S(1)} %all_to_all.15) | copy-start | bytes 2359300
  31.7 19.5 %collective-permute-start.10 = (bf16[256,1536]{1,0:T(8,128)(2,1)S(1)}, bf16[256,1536]{1,0:T(8,128)(2,1)S(1)}, u32[]{:S(2)}, u32[]{:S(2)}) collective-permute-start(bf16[256,1536]{1,0:T(8,128)(2,1)S(1)} %bitcast.10), channel_id=1, source_target_pairs={{0,96},{32,0},{64,32},{96,64},{1,97},{33,1},{65,33},{97,65},{2,98}... | collective-permute-start | bytes 2359304 | tf_op jit(solution)/shard_map/ppermute | solution.py:358
  34.7 21.0 %collective-permute-start.9 = (bf16[256,1536]{1,0:T(8,128)(2,1)S(1)}, bf16[256,1536]{1,0:T(8,128)(2,1)S(1)}, u32[]{:S(2)}, u32[]{:S(2)}) collective-permute-start(bf16[256,1536]{1,0:T(8,128)(2,1)S(1)} %bitcast.11), channel_id=1, source_target_pairs={{0,32},{32,64},{64,96},{96,0},{1,33},{33,65},{65,97},{97,1},{2,34}... | collective-permute-start | bytes 2359304 | tf_op jit(solution)/shard_map/ppermute | solution.py:358
  45.3 17.3 %all-to-all-start.1 = ((bf16[16,16,1536]{2,1,0:T(8,128)(2,1)}), bf16[16,16,1536]{2,1,0:T(8,128)(2,1)S(1)}, u32[]{:S(2)}, u32[]{:S(2)}) async-start(bf16[16,16,1536]{2,1,0:T(8,128)(2,1)} %bitcast.14), calls=%async_computation.1 | async-start | bytes 1572864 | tf_op jit(solution)/shard_map/all_to_all | solution.py:389
  51.2 21.2 %copy-start.2 = (bf16[256,1536]{1,0:T(8,128)(2,1)}, bf16[256,1536]{1,0:T(8,128)(2,1)S(1)}, u32[]{:S(2)}) copy-start(bf16[256,1536]{1,0:T(8,128)(2,1)S(1)} %collective-permute-done.10.p2) | copy-start | bytes 2359300
  52.0 23.9 %collective-permute-start.12 = (bf16[128,1536]{1,0:T(8,128)(2,1)}, bf16[128,1536]{1,0:T(8,128)(2,1)S(1)}, u32[]{:S(2)}, u32[]{:S(2)}) collective-permute-start(bf16[128,1536]{1,0:T(8,128)(2,1)} %slice.9), channel_id=1, source_target_pairs={{0,96},{32,0},{64,32},{96,64},{1,97},{33,1},{65,33},{97,65},{2,98}... | collective-permute-start | bytes 1179656 | tf_op jit(solution)/shard_map/ppermute | solution.py:358
  55.7 16.6 %copy-start.3 = (bf16[256,1536]{1,0:T(8,128)(2,1)}, bf16[256,1536]{1,0:T(8,128)(2,1)S(1)}, u32[]{:S(2)}) copy-start(bf16[256,1536]{1,0:T(8,128)(2,1)S(1)} %collective-permute-done.9.p1) | copy-start | bytes 2359300
  55.8 20.2 %collective-permute-start.11 = (bf16[128,1536]{1,0:T(8,128)(2,1)S(1)}, bf16[128,1536]{1,0:T(8,128)(2,1)S(1)}, u32[]{:S(2)}, u32[]{:S(2)}) collective-permute-start(bf16[128,1536]{1,0:T(8,128)(2,1)S(1)} %slice.8), channel_id=1, source_target_pairs={{0,32},{32,64},{64,96},{96,0},{1,33},{33,65},{65,97},{97,1},{2,34}... | collective-permute-start | bytes 1179656 | tf_op jit(solution)/shard_map/ppermute | solution.py:358
  62.6 0.9 copy-start.1
  72.4 1.5 %collective-permute-start = (f32[16,768]{1,0:T(8,128)}, f32[16,768]{1,0:T(8,128)S(1)}, u32[]{:S(2)}, u32[]{:S(2)}) collective-permute-start(f32[16,768]{1,0:T(8,128)} %get-tuple-element.19), channel_id=1, source_target_pairs={{0,1},{1,0},{2,3},{3,2},{4,5},{5,4},{6,7},{7,6},{8,9},{9,8},{10,11... | collective-permute-start | bytes 147464 | tf_op jit(solution)/shard_map/ppermute | solution.py:358
  74.7 18.0 %collective-permute-start.1 = (f32[16,768]{1,0:T(8,128)S(1)}, f32[16,768]{1,0:T(8,128)S(1)}, u32[]{:S(2)}, u32[]{:S(2)}) collective-permute-start(f32[16,768]{1,0:T(8,128)S(1)} %add.33), channel_id=1, source_target_pairs={{0,2},{2,0},{1,3},{3,1},{4,6},{6,4},{5,7},{7,5},{8,10},{10,8},{9,1... | collective-permute-start | bytes 147464 | tf_op jit(solution)/shard_map/ppermute | solution.py:358
  89.9 23.4 %collective-permute-start.13 = (bf16[4,96,768]{2,1,0:T(8,128)(2,1)}, bf16[4,96,768]{2,1,0:T(8,128)(2,1)S(1)}, u32[]{:S(2)}, u32[]{:S(2)}) collective-permute-start(bf16[4,96,768]{2,1,0:T(8,128)(2,1)} %get-tuple-element.21), channel_id=1, source_target_pairs={{0,16},{16,0},{1,17},{17,1},{2,18},{18,2},{3,19},{19,3},{4,20},{20... | collective-permute-start | bytes 1769480 | tf_op jit(solution)/shard_map/ppermute | solution.py:358
  92.7 4.2 %collective-permute-start.4 = (f32[16,768]{1,0:T(8,128)S(1)}, f32[16,768]{1,0:T(8,128)S(1)}, u32[]{:S(2)}, u32[]{:S(2)}) collective-permute-start(f32[16,768]{1,0:T(8,128)S(1)} %add.34), channel_id=1, source_target_pairs={{0,12},{4,0},{8,4},{12,8},{1,13},{5,1},{9,5},{13,9},{2,14},{6,2},{... | collective-permute-start | bytes 147464 | tf_op jit(solution)/shard_map/ppermute | solution.py:358
  93.2 5.8 %collective-permute-start.3 = (f32[16,768]{1,0:T(8,128)S(1)}, f32[16,768]{1,0:T(8,128)S(1)}, u32[]{:S(2)}, u32[]{:S(2)}) collective-permute-start(f32[16,768]{1,0:T(8,128)S(1)} %add.34), channel_id=1, source_target_pairs={{0,8},{4,12},{8,0},{12,4},{1,9},{5,13},{9,1},{13,5},{2,10},{6,14},... | collective-permute-start | bytes 147464 | tf_op jit(solution)/shard_map/ppermute | solution.py:358
  94.7 5.3 %collective-permute-start.2 = (f32[16,768]{1,0:T(8,128)S(1)}, f32[16,768]{1,0:T(8,128)S(1)}, u32[]{:S(2)}, u32[]{:S(2)}) collective-permute-start(f32[16,768]{1,0:T(8,128)S(1)} %add.34), channel_id=1, source_target_pairs={{0,4},{4,8},{8,12},{12,0},{1,5},{5,9},{9,13},{13,1},{2,6},{6,10},{... | collective-permute-start | bytes 147464 | tf_op jit(solution)/shard_map/ppermute | solution.py:358
  100.0 10.5 %collective-permute-start.7 = (f32[16,768]{1,0:T(8,128)S(1)}, f32[16,768]{1,0:T(8,128)S(1)}, u32[]{:S(2)}, u32[]{:S(2)}) collective-permute-start(f32[16,768]{1,0:T(8,128)S(1)} %add_add_fusion.1), channel_id=1, source_target_pairs={{0,96},{32,0},{64,32},{96,64},{1,97},{33,1},{65,33},{97,65},{2,98}... | collective-permute-start | bytes 147464 | tf_op jit(solution)/shard_map/ppermute | solution.py:358
  103.4 7.1 %collective-permute-start.6 = (f32[16,768]{1,0:T(8,128)S(1)}, f32[16,768]{1,0:T(8,128)S(1)}, u32[]{:S(2)}, u32[]{:S(2)}) collective-permute-start(f32[16,768]{1,0:T(8,128)S(1)} %add_add_fusion.1), channel_id=1, source_target_pairs={{0,64},{32,96},{64,0},{96,32},{1,65},{33,97},{65,1},{97,33},{2,66}... | collective-permute-start | bytes 147464 | tf_op jit(solution)/shard_map/ppermute | solution.py:358
  103.5 7.1 %collective-permute-start.5 = (f32[16,768]{1,0:T(8,128)S(1)}, f32[16,768]{1,0:T(8,128)S(1)}, u32[]{:S(2)}, u32[]{:S(2)}) collective-permute-start(f32[16,768]{1,0:T(8,128)S(1)} %add_add_fusion.1), channel_id=1, source_target_pairs={{0,32},{32,64},{64,96},{96,0},{1,33},{33,65},{65,97},{97,1},{2,34}... | collective-permute-start | bytes 147464 | tf_op jit(solution)/shard_map/ppermute | solution.py:358
  104.4 5.3 %copy-start.8 = (bf16[384,768]{1,0:T(8,128)(2,1)S(1)}, bf16[384,768]{1,0:T(8,128)(2,1)}, u32[]{:S(2)}) copy-start(bf16[384,768]{1,0:T(8,128)(2,1)} %get-tuple-element.23) | copy-start | bytes 1769476
  104.4 8.9 %copy-start.4 = (f32[4,96,768]{2,1,0:T(8,128)S(1)}, f32[4,96,768]{2,1,0:T(8,128)}, u32[]{:S(2)}) copy-start(f32[4,96,768]{2,1,0:T(8,128)} %get-tuple-element.20) | copy-start | bytes 3538948
  109.7 16.2 %collective-permute-start.14 = (bf16[384,768]{1,0:T(8,128)(2,1)S(1)}, bf16[384,768]{1,0:T(8,128)(2,1)S(1)}, u32[]{:S(2)}, u32[]{:S(2)}) collective-permute-start(bf16[384,768]{1,0:T(8,128)(2,1)S(1)} %copy-done.8), channel_id=1, source_target_pairs={{0,16},{16,0},{1,17},{17,1},{2,18},{18,2},{3,19},{19,3},{4,20},{20... | collective-permute-start | bytes 1769480 | tf_op jit(solution)/shard_map/ppermute | solution.py:358
  110.5 14.7 %collective-permute-start.8 = (f32[16,768]{1,0:T(8,128)S(1)}, f32[16,768]{1,0:T(8,128)S(1)}, u32[]{:S(2)}, u32[]{:S(2)}) collective-permute-start(f32[16,768]{1,0:T(8,128)S(1)} %add_add_fusion), channel_id=1, source_target_pairs={{0,16},{16,0},{1,17},{17,1},{2,18},{18,2},{3,19},{19,3},{4,20},{20... | collective-permute-start | bytes 147464 | tf_op jit(solution)/shard_map/ppermute | solution.py:358
  114.3 11.6 %copy-start.5 = (f32[384,768]{1,0:T(8,128)S(1)}, f32[384,768]{1,0:T(8,128)}, u32[]{:S(2)}) copy-start(f32[384,768]{1,0:T(8,128)} %get-tuple-element.22) | copy-start | bytes 3538948
  114.3 12.8 %all-to-all-start.2 = ((bf16[4,96,768]{2,1,0:T(8,128)(2,1)}), bf16[4,96,768]{2,1,0:T(8,128)(2,1)S(1)}, u32[]{:S(2)}, u32[]{:S(2)}) async-start(bf16[4,96,768]{2,1,0:T(8,128)(2,1)} %add_convert_fusion), calls=%async_computation.2 | async-start | bytes 1179648 | tf_op jit(solution)/shard_map/all_to_all | solution.py:399
  (2 other events, 1.5 us)

commit v2 on v0

v2 whole, which is shorter than its diff:
```python
import functools

import jax
import jax.numpy as jnp
from jax import lax
from jax.experimental import pallas as pl
from jax.experimental.pallas import tpu as pltpu
from jax.sharding import Mesh, PartitionSpec as P

PATCHES = 196
GROUP = 4
XH = 2
MIB = 1024 * 1024
GELU_C = 0.7978845608028654
GELU_A = 0.044715

f32 = jnp.float32
bf16 = jnp.bfloat16


def contract(left, right, left_dim, right_dim):
    return lax.dot_general(
        left, right, (((left_dim,), (right_dim,)), ((), ())), preferred_element_type=f32
    )


def params(mib):
    return pltpu.CompilerParams(vmem_limit_bytes=mib * MIB)


def pinned(value):
    return pltpu.with_memory_space_constraint(value, pltpu.HBM)


IN_VMEM = pl.BlockSpec(memory_space=pltpu.VMEM)
IN_PLACE = pl.BlockSpec(memory_space=pltpu.HBM)


def gelu_parts(x):
    x2 = x * x
    th = jnp.tanh(GELU_C * x * (1.0 + GELU_A * x2))
    cdf = 0.5 + 0.5 * th
    slope = cdf + (0.5 * GELU_C) * x * (1.0 - th * th) * (1.0 + (3.0 * GELU_A) * x2)
    return x * cdf, slope


def lane_images(width):
    lane = lax.broadcasted_iota(jnp.int32, (1, width), 1)
    image = jnp.zeros_like(lane)
    for i in range(1, width // PATCHES):
        image = image + (lane >= i * PATCHES).astype(jnp.int32)
    return image


def per_image(values, image, reduce, start):
    width = values.shape[1]
    out = jnp.zeros_like(values)
    for i in range(GROUP):
        low = i * PATCHES // 128 * 128
        high = min(-(-(i + 1) * PATCHES // 128) * 128, width)
        part = jnp.where(image[:, low:high] == i, values[:, low:high], start)
        own = reduce(part, axis=1, keepdims=True)
        out = jnp.where(image == i, own, out)
    return out


def per_slot_rows(weights, image):
    return jnp.concatenate(
        [jnp.where(image == i, weights, 0.0) for i in range(GROUP)], axis=0
    ).astype(bf16)


def swap_matrix(total, inner):
    outer = total // inner
    out_row = lax.broadcasted_iota(jnp.int32, (total, total), 0)
    in_row = lax.broadcasted_iota(jnp.int32, (total, total), 1)
    wanted = (out_row % outer) * inner + out_row // outer
    return (in_row == wanted).astype(f32).astype(bf16)


def block_copies(src, dst, sem):
    width = GROUP * PATCHES
    return [
        pltpu.make_async_copy(
            src.at[pl.ds(b * width, width)], dst.at[pl.ds(b * width, width)], sem.at[b]
        )
        for b in range(src.shape[0] // width)
    ]


def token_forward_body(
    rt_ref, x_hbm, g_hbm, slots_ref, disp_ref, comb_ref, x_ref, g_ref, acc, x_sem, g_sem
):
    experts, images, double = slots_ref.shape
    feat = double // 2
    width = GROUP * PATCHES
    steps = images // GROUP
    rows = GROUP * experts
    total = experts * images

    x_copies = block_copies(x_hbm, x_ref, x_sem)
    g_copies = block_copies(g_hbm, g_ref, g_sem)
    for copy in x_copies + g_copies:
        copy.start()
    image = lane_images(width)
    rt = rt_ref[...]
    spread = []
    for b in range(steps):
        x_copies[b].wait()
        x = x_ref[b * width : (b + 1) * width, :]
        logits = contract(rt, x, 1, 1)
        top = per_image(logits, image, jnp.max, -jnp.inf)
        raised = jnp.exp(logits - top)
        dispatch = raised / per_image(raised, image, jnp.sum, 0.0)
        raised_e = jnp.exp(logits - jnp.max(logits, axis=0, keepdims=True))
        combine = raised_e / jnp.sum(raised_e, axis=0, keepdims=True)
        disp_ref[b] = dispatch
        comb_ref[b] = combine
        spread.append(per_slot_rows(combine, image))
        acc[b * rows : (b + 1) * rows, :feat] = jnp.dot(
            per_slot_rows(dispatch, image), x, preferred_element_type=f32
        ).astype(bf16)
    for b in range(steps):
        g_copies[b].wait()
        acc[b * rows : (b + 1) * rows, feat:] = jnp.dot(
            spread[b], g_ref[b * width : (b + 1) * width, :], preferred_element_type=f32
        ).astype(bf16)
    slots_ref[...] = (
        jnp.dot(swap_matrix(total, experts), acc[...], preferred_element_type=f32)
        .astype(bf16)
        .reshape(experts, images, double)
    )


def token_forward(tokens, rt, g_outputs):
    rows, feat = tokens.shape
    experts = rt.shape[0]
    images = rows // PATCHES
    width = GROUP * PATCHES
    steps = rows // width
    return pl.pallas_call(
        token_forward_body,
        in_specs=[IN_VMEM, IN_PLACE, IN_PLACE],
        out_specs=[IN_VMEM, IN_VMEM, IN_VMEM],
        out_shape=[
            jax.ShapeDtypeStruct((experts, images, 2 * feat), bf16),
            jax.ShapeDtypeStruct((steps, experts, width), f32),
            jax.ShapeDtypeStruct((steps, experts, width), f32),
        ],
        scratch_shapes=[
            pltpu.VMEM((rows, feat), bf16),
            pltpu.VMEM((rows, feat), bf16),
            pltpu.VMEM((experts * images, 2 * feat), bf16),
            pltpu.SemaphoreType.DMA((steps,)),
            pltpu.SemaphoreType.DMA((steps,)),
        ],
        compiler_params=params(20),
        name="token_forward",
    )(rt, pinned(tokens), pinned(g_outputs))


def expert_body(rows_ref, w1_ref, w2_ref, out_ref):
    feat = w1_ref.shape[1]
    hidden = w1_ref.shape[2]
    tile = 768
    rows = rows_ref[:, :feat]
    grads = rows_ref[:, feat:]
    made, back = None, None
    for low in range(0, hidden, tile):
        w1 = w1_ref[0, :, low : low + tile]
        w2 = w2_ref[0, low : low + tile, :]
        act, slope = gelu_parts(jnp.dot(rows, w1, preferred_element_type=f32))
        part = jnp.dot(act.astype(bf16), w2, preferred_element_type=f32)
        made = part if made is None else made + part
        grad_pre = (contract(grads, w2, 1, 1) * slope).astype(bf16)
        part = contract(grad_pre, w1, 1, 1)
        back = part if back is None else back + part
    out_ref[:, :feat] = made.astype(bf16)
    out_ref[:, feat:] = back.astype(bf16)


def expert_rows(rows, w_in, w_out):
    return pl.pallas_call(
        expert_body,
        in_specs=[IN_VMEM] * 3,
        out_specs=IN_VMEM,
        out_shape=jax.ShapeDtypeStruct(rows.shape, bf16),
        compiler_params=params(12),
        name="expert_rows",
    )(rows, w_in, w_out)


def slice_grads(piece_refs, w1_hbm, w2_hbm, low, tile, both, act_all, pre_all, w1, w2, sem):
    feat = w1.shape[0]
    low = pl.multiple_of(low, tile)
    first = pltpu.make_async_copy(w1_hbm.at[0, :, pl.ds(low, tile)], w1, sem.at[0])
    second = pltpu.make_async_copy(w2_hbm.at[0, pl.ds(low, tile), :], w2, sem.at[1])
    first.start()
    second.start()
    at = 0
    for piece in piece_refs:
        both[at : at + piece.shape[0], :] = piece[...]
        at += piece.shape[0]
    rows = both[:, :feat]
    grads = both[:, feat:]
    first.wait()
    act, slope = gelu_parts(jnp.dot(rows, w1[...], preferred_element_type=f32))
    act_all[...] = act.astype(bf16)
    second.wait()
    pre_all[...] = (contract(grads, w2[...], 1, 1) * slope).astype(bf16)
    return contract(rows, pre_all[...], 0, 0), contract(act_all[...], grads, 0, 0)


def grads_body(count, first, *refs):
    pieces, (w1_ref, w2_ref) = refs[:count], refs[count : count + 2]
    refs = refs[count + 2 :]
    sums, refs = (None, refs) if first else (refs[:2], refs[2:])
    out_in, out_out, *scratch = refs
    tile = out_in.shape[1]
    low = lax.axis_index("y") * tile
    part_in, part_out = slice_grads(pieces, w1_ref, w2_ref, low, tile, *scratch)
    out_in[...] = part_in if first else sums[0][...] + part_in
    out_out[...] = part_out if first else sums[1][...] + part_out


def last_grads_body(count, *refs):
    pieces, (w1_ref, w2_ref, sum_in, sum_out) = refs[:count], refs[count : count + 4]
    keep_in, send_in, keep_out, send_out, acc_in, acc_out, *scratch = refs[count + 4 :]
    tile = sum_in.shape[1]
    low = lax.axis_index("y") * tile
    xh = lax.axis_index("xh")
    part_in, part_out = slice_grads(pieces, w1_ref, w2_ref, low, tile, *scratch)
    acc_in[...] = (sum_in[...] + part_in).reshape(acc_in.shape)
    acc_out[...] = (sum_out[...] + part_out).reshape(acc_out.shape)
    keep_in[...] = acc_in[:, pl.ds(xh, 1)].reshape(keep_in.shape)
    send_in[...] = acc_in[:, pl.ds(1 - xh, 1)].reshape(send_in.shape).astype(bf16)
    keep_out[...] = acc_out[xh]
    send_out[...] = acc_out[1 - xh].astype(bf16)


def piece_scratch(pieces, tile):
    count = sum(p.shape[0] for p in pieces)
    feat = pieces[0].shape[1] // 2
    return [
        pltpu.VMEM((count, 2 * feat), bf16),
        pltpu.VMEM((count, tile), bf16),
        pltpu.VMEM((count, tile), bf16),
        pltpu.VMEM((feat, tile), bf16),
        pltpu.VMEM((tile, feat), bf16),
        pltpu.SemaphoreType.DMA((2,)),
    ]


def weight_grads(pieces, w_in, w_out, sums, parts, name):
    feat, hidden = w_in.shape[1:]
    tile = hidden // parts
    count = sum(p.shape[0] for p in pieces)
    return pl.pallas_call(
        functools.partial(grads_body, len(pieces), not sums),
        in_specs=[IN_VMEM] * len(pieces) + [IN_PLACE] * 2 + [IN_VMEM] * len(sums),
        out_specs=[IN_VMEM] * 2,
        out_shape=[
            jax.ShapeDtypeStruct((feat, tile), f32),
            jax.ShapeDtypeStruct((tile, feat), f32),
        ],
        scratch_shapes=piece_scratch(pieces, tile),
        compiler_params=params(16),
        name=name,
    )(*pieces, pinned(w_in), pinned(w_out), *sums)


def last_weight_grads(pieces, w_in, w_out, sums, parts):
    feat, hidden = w_in.shape[1:]
    tile = hidden // parts
    own = feat // (parts * XH)
    count = sum(p.shape[0] for p in pieces)
    return pl.pallas_call(
        functools.partial(last_grads_body, len(pieces)),
        in_specs=[IN_VMEM] * len(pieces) + [IN_PLACE] * 2 + [IN_VMEM] * 2,
        out_specs=[IN_VMEM] * 4,
        out_shape=[
            jax.ShapeDtypeStruct((parts, own, tile), f32),
            jax.ShapeDtypeStruct((parts, own, tile), bf16),
            jax.ShapeDtypeStruct((tile // XH, feat), f32),
            jax.ShapeDtypeStruct((tile // XH, feat), bf16),
        ],
        scratch_shapes=[
            pltpu.VMEM((parts, XH, own, tile), f32),
            pltpu.VMEM((XH, tile // XH, feat), f32),
        ]
        + piece_scratch(pieces, tile),
        compiler_params=params(20),
        name="far_grads",
    )(*pieces, pinned(w_in), pinned(w_out), *sums)


def widen_body(in_ref, out_ref):
    parts, _, tile = in_ref.shape
    for i in range(parts):
        out_ref[0, :, i * tile : (i + 1) * tile] = in_ref[i].astype(f32)


def widen(spread):
    parts, own, tile = spread.shape
    return pl.pallas_call(
        widen_body,
        in_specs=[IN_VMEM],
        out_specs=IN_VMEM,
        out_shape=jax.ShapeDtypeStruct((1, own, parts * tile), f32),
        compiler_params=params(4),
        name="widen",
    )(spread)


def token_logits_body(
    back_ref, x_hbm, g_hbm, disp_ref, comb_ref, gl_ref, slots_ref, router_ref,
    mix, x_ref, g_ref, x_sem, g_sem
):
    experts, images, double = back_ref.shape
    feat = double // 2
    width = GROUP * PATCHES
    rows = GROUP * experts
    total = experts * images
    x_copies = block_copies(x_hbm, x_ref, x_sem)
    g_copies = block_copies(g_hbm, g_ref, g_sem)
    for x_copy, g_copy in zip(x_copies, g_copies):
        g_copy.start()
        x_copy.start()
    mix[...] = jnp.dot(
        swap_matrix(total, images),
        back_ref[...].reshape(total, double),
        preferred_element_type=f32,
    ).astype(bf16)
    image = lane_images(width)

    def picked(both):
        out = jnp.zeros((experts, width), f32)
        for i in range(GROUP):
            out = jnp.where(image == i, both[i * experts : (i + 1) * experts], out)
        return out

    router_sum = None
    for b in range(images // GROUP):
        g_copies[b].wait()
        x_copies[b].wait()
        x = x_ref[b * width : (b + 1) * width, :]
        g = g_ref[b * width : (b + 1) * width, :]
        block = mix[b * rows : (b + 1) * rows, :]
        slots_ref[b] = block[:, feat:]
        grad_comb = picked(contract(block[:, :feat], g, 1, 1))
        grad_disp = picked(contract(block[:, feat:], x, 1, 1))
        dispatch = disp_ref[b]
        combine = comb_ref[b]
        comb_part = combine * (grad_comb - jnp.sum(combine * grad_comb, axis=0, keepdims=True))
        disp_part = dispatch * (
            grad_disp - per_image(dispatch * grad_disp, image, jnp.sum, 0.0)
        )
        grad_logits = (comb_part + disp_part).astype(bf16)
        gl_ref[b] = grad_logits
        part = jnp.dot(grad_logits, x, preferred_element_type=f32)
        router_sum = part if router_sum is None else router_sum + part
    router_ref[...] = router_sum


def token_logits(back, tokens, g_outputs, dispatch, combine):
    experts, images, double = back.shape
    rows, feat = tokens.shape
    steps, _, width = dispatch.shape
    return pl.pallas_call(
        token_logits_body,
        in_specs=[IN_VMEM, IN_PLACE, IN_PLACE, IN_VMEM, IN_VMEM],
        out_specs=[IN_VMEM] * 3,
        out_shape=[
            jax.ShapeDtypeStruct((steps, experts, width), bf16),
            jax.ShapeDtypeStruct((steps, GROUP * experts, feat), bf16),
            jax.ShapeDtypeStruct((experts, feat), f32),
        ],
        scratch_shapes=[
            pltpu.VMEM((experts * images, double), bf16),
            pltpu.VMEM((rows, feat), bf16),
            pltpu.VMEM((rows, feat), bf16),
            pltpu.SemaphoreType.DMA((steps,)),
            pltpu.SemaphoreType.DMA((steps,)),
        ],
        compiler_params=params(20),
        name="token_logits",
    )(back, pinned(tokens), pinned(g_outputs), dispatch, combine)


def token_grads_body(gl_ref, slots_ref, disp_ref, rt_ref, out_ref):
    image = lane_images(gl_ref.shape[2])
    left = jnp.concatenate([per_slot_rows(disp_ref[0], image), gl_ref[0]], axis=0)
    right = jnp.concatenate([slots_ref[0], rt_ref[...]], axis=0)
    out_ref[...] = contract(left, right, 0, 0).astype(bf16)


def token_grads(grad_logits, slots, dispatch, rt):
    steps, experts, width = grad_logits.shape
    feat = slots.shape[2]
    return pl.pallas_call(
        token_grads_body,
        grid=(steps,),
        in_specs=[
            pl.BlockSpec((1, experts, width), lambda i: (i, 0, 0)),
            pl.BlockSpec((1, GROUP * experts, feat), lambda i: (i, 0, 0)),
            pl.BlockSpec((1, experts, width), lambda i: (i, 0, 0)),
            pl.BlockSpec((experts, feat), lambda i: (0, 0)),
        ],
        out_specs=pl.BlockSpec((width, feat), lambda i: (i, 0)),
        out_shape=jax.ShapeDtypeStruct((steps * width, feat), bf16),
        compiler_params=params(12),
        name="token_grads",
    )(grad_logits, slots, dispatch, rt)


def shift(value, axis, by, count):
    return lax.ppermute(value, axis, [(i, (i + by) % count) for i in range(count)])


def everywhere_sum(value, sizes):
    for axis, count in sizes:
        value = sum([shift(value, axis, by, count) for by in range(1, count)], value)
    return value


def solution(mesh):
    dp, experts = mesh.shape["dp"], mesh.shape["expert"]
    ny = dp // XH
    inner = (("core", 2), ("xl", 2), ("z", experts // 4))
    fine = Mesh(
        mesh.devices.reshape(ny, XH, experts // 4, 2, 2), ("y", "xh", "z", "xl", "core")
    )
    dp_axes = ("y", "xh")
    ex_axes = ("z", "xl", "core")
    sizes = inner + (("y", ny), ("xh", XH))

    def over_experts(value):
        return lax.all_to_all(value, ex_axes, split_axis=0, concat_axis=0, tiled=True)

    def on_device(tokens, router, w_in, w_out, g_outputs):
        rt = router.T
        slots, dispatch, combine = token_forward(tokens, rt, g_outputs)
        rows = over_experts(slots).reshape(-1, slots.shape[2])
        mid = rows.shape[0] // 2
        right = shift(rows, "y", 1, ny)
        left = shift(rows, "y", ny - 1, ny)
        results = expert_rows(rows, w_in, w_out)
        back = over_experts(results.reshape(slots.shape))
        own_sums = weight_grads((rows,), w_in, w_out, (), ny, "own_grads")
        far_a = shift(right[:mid], "y", 1, ny)
        far_b = shift(left[mid:], "y", ny - 1, ny)
        near_sums = weight_grads((right, left), w_in, w_out, tuple(own_sums), ny, "near_grads")
        back, near_sums = lax.optimization_barrier((back, tuple(near_sums)))
        grad_logits, slot_grads, router_term = token_logits(
            back, tokens, g_outputs, dispatch, combine
        )
        keep_in, send_in, keep_out, send_out = last_weight_grads(
            (far_a, far_b), w_in, w_out, near_sums, ny
        )
        came_in = shift(send_in, "xh", 1, XH)
        came_out = shift(send_out, "xh", 1, XH)
        part_in = (keep_in + came_in.astype(f32)).astype(bf16)
        spread = lax.all_to_all(part_in, "y", split_axis=0, concat_axis=0, tiled=True)
        grad_first = widen(spread)
        grad_second = keep_out + came_out.astype(f32)
        grad_router = everywhere_sum(router_term, sizes).T
        grad_tok = token_grads(grad_logits, slot_grads, dispatch, rt)
        return grad_tok, grad_router, grad_first, grad_second[None]

    return jax.shard_map(
        on_device,
        mesh=fine,
        in_specs=(
            P(dp_axes + ex_axes, None),
            P(),
            P(ex_axes, None, None),
            P(ex_axes, None, None),
            P(dp_axes + ex_axes, None),
        ),
        out_specs=(
            P(dp_axes + ex_axes, None),
            P(),
            P(ex_axes, dp_axes, None),
            P(ex_axes, dp_axes, None),
        ),
        check_vma=False,
    )
```

time: 260 us -> 117 us (0.45)
  matrix products: 62.7 us -> 0 us
  blocking collectives: 69.2 us -> 19.9 us
  Pallas kernels: 0 us -> 39.7 us
  waiting for transfers between devices: 53.6 us -> 17.7 us
  local copies, waits for them, and re-layouts: 30 us -> 5.29 us
  between operations: 14.2 us -> 0.8 us
  starting transfers between devices: 19.5 us -> 29.1 us
  other arithmetic: 9.39 us -> 4.18 us
    psum x1 -> x0, blocking collectives: 69.2 us -> none  [on_device(): grad_router = lax.psum(router_term, ('dp', 'expert'))]
    dot_general x14 -> x0, matrix products: 62.7 us -> none  [the longest x6 30.9 us: contract(): lax.dot_general(left, right, (((left_dim,), (right_dim,)), ((), ())), pre...]
    pallas_call x0 -> x8, Pallas kernels: none -> 39.7 us  [the longest x2 8.25 us: weight_grads(): pl.pallas_call(functools.partial(grads_body, len(pieces), not sums), in_s...]
    reduce_scatter x2 -> x0, waiting for transfers between devices: 30.6 us -> none  [the longest x1 30.6 us: on_device(): lax.psum_scatter(contract(picked, grad_pre, 0, 0).astype(jnp.bfloat16), '...]
    reshape x6 -> x0, local copies, waits for them, and re-layouts: 25.3 us -> none  [the longest x1 9.88 us: on_device(): grad_tok = jnp.einsum('bpe,bed->bpd', dispatch_low, grad_slot_in, preferr...]
    all_to_all x4 -> x2, waiting for transfers between devices: 23 us -> 0.01 us  [the longest x1 0.01 us: on_device(): lax.all_to_all(part_in, 'y', split_axis=0, concat_axis=0, tiled=True)]
    ppermute x0 -> x15, starting transfers between devices: none -> 21.4 us  [shift(): lax.ppermute(value, axis, [(i, (i + by) % count) for i in range(count)])]
    all_to_all x0 -> x1, blocking collectives: none -> 19.9 us  [over_experts(): lax.all_to_all(value, ex_axes, split_axis=0, concat_axis=0, tiled=True)]
  transfers between devices with their start and end apart: 6 -> 17, of which waited for: 4 -> 6; matrix products, arithmetic and copies ran while one was open for 30% -> 5% of each run, Pallas kernels for 0% -> 26%
where the time goes in v2:
time: 117 us
  Pallas kernels  39.7 us (34%)
  starting transfers between devices  29.1 us (25%)
  blocking collectives  19.9 us (17%)
  waiting for transfers between devices  17.7 us (15%)
  local copies, waits for them, and re-layouts  5.29 us (5%)
  other arithmetic  4.18 us (4%)
    ppermute x15, starting transfers between devices, shift(): lax.ppermute(value, axis, [(i, (i + by) % count) for i in range(count)])  21.4 us
    all_to_all x1, blocking collectives, over_experts(): lax.all_to_all(value, ex_axes, split_axis=0, concat_axis=0, tiled=True)  19.9 us
    ppermute x15, waiting for transfers between devices, shift(): lax.ppermute(value, axis, [(i, (i + by) % count) for i in range(count)])  17.7 us
    pallas_call x2, Pallas kernels, weight_grads(): pl.pallas_call(functools.partial(grads_body, len(pieces), not sums), in_s...  8.25 us
    pallas_call x1, Pallas kernels, token_forward(): pl.pallas_call(token_forward_body, in_specs=[IN_VMEM, IN_PLACE, IN_PLACE]...  7.89 us
    pallas_call x1, Pallas kernels, token_logits(): pl.pallas_call(token_logits_body, in_specs=[IN_VMEM, IN_PLACE, IN_PLACE,...  6.9 us
    pallas_call x1, Pallas kernels, expert_rows(): pl.pallas_call(expert_body, in_specs=[IN_VMEM] * 3, out_specs=IN_VMEM, ou...  6.47 us
    pallas_call x1, Pallas kernels, last_weight_grads(): pl.pallas_call(functools.partial(last_grads_body, len(pieces)), in_specs=...  5.46 us
  transfers between devices with their start and end apart: 17, of which 6 were waited for; matrix products, arithmetic and copies ran while one was open for 5% of the time, Pallas kernels for 26%

profile of v2, /device:TPU:0, one launch (start us, length us, event | category | flops | bytes accessed | tf_op | source)
XLA Modules:
  0.0 116.7 jit_solution(196582394956086649)
XLA Ops:
  1.5 7.9 %token_forward.1 = (bf16[16,16,1536]{2,1,0:T(8,128)(2,1)S(1)}, f32[4,16,784]{2,1,0:T(8,128)S(1)}, f32[4,16,784]{2,1,0:T(8,128)S(1)}) custom-call(bf16[16,768]{1,0:T(8,128)(2,1)S(1)} %bitcast.13, bf16[3136,768]{1,0:T(8,128)(2,1)} %x_hbm.3, bf16[3136,768]{1,0:T(8,128)(2,1)} %g_hbm.3), custom_call_target="tpu_custom_call" | custom-call | tf_op jit(solution)/shard_map/token_forward/pallas_call | solution.py:141
  9.4 19.9 %all_to_all.15 = bf16[16,16,1536]{2,1,0:T(8,128)(2,1)S(1)} all-to-all(bf16[16,16,1536]{2,1,0:T(8,128)(2,1)S(1)} %get-tuple-element.21), channel_id=1, replica_groups=mesh['y'=4,'xh'=2,'z'=4,'xl'=2,'core'=2] {'z','xl','core'}, dimensions={0} | all-to-all | bytes 1572864 | tf_op jit(solution)/shard_map/all_to_all | solution.py:438
  29.4 1.6 %collective-permute-start = (bf16[256,1536]{1,0:T(8,128)(2,1)S(1)}, bf16[256,1536]{1,0:T(8,128)(2,1)S(1)}, u32[]{:S(2)}, u32[]{:S(2)}) collective-permute-start(bf16[256,1536]{1,0:T(8,128)(2,1)S(1)} %bitcast.9), channel_id=1, source_target_pairs={{0,32},{32,64},{64,96},{96,0},{1,33},{33,65},{65,97},{97,1},{2,34}... | collective-permute-start | bytes 2359304 | tf_op jit(solution)/shard_map/ppermute | solution.py:417
  30.9 1.7 %collective-permute-start.1 = (bf16[256,1536]{1,0:T(8,128)(2,1)S(1)}, bf16[256,1536]{1,0:T(8,128)(2,1)S(1)}, u32[]{:S(2)}, u32[]{:S(2)}) collective-permute-start(bf16[256,1536]{1,0:T(8,128)(2,1)S(1)} %bitcast.10), channel_id=1, source_target_pairs={{0,96},{32,0},{64,32},{96,64},{1,97},{33,1},{65,33},{97,65},{2,98}... | collective-permute-start | bytes 2359304 | tf_op jit(solution)/shard_map/ppermute | solution.py:417
  32.6 6.5 %expert_rows.1 = bf16[256,1536]{1,0:T(8,128)(2,1)} custom-call(bf16[256,1536]{1,0:T(8,128)(2,1)S(1)} %bitcast.11, bf16[1,768,3072]{2,1,0:T(8,128)(2,1)S(1)} %bitcast.8, bf16[1,3072,768]{2,1,0:T(8,128)(2,1)S(1)} %copy-done), custom_call_target="tpu_custom_call" | custom-call | tf_op jit(solution)/shard_map/expert_rows/pallas_call | solution.py:183
  39.1 3.6 %all-to-all-start.1 = ((bf16[16,16,1536]{2,1,0:T(8,128)(2,1)}), bf16[16,16,1536]{2,1,0:T(8,128)(2,1)S(1)}, u32[]{:S(2)}, u32[]{:S(2)}) async-start(bf16[16,16,1536]{2,1,0:T(8,128)(2,1)} %bitcast.2), calls=%async_computation.1 | async-start | bytes 1572864 | tf_op jit(solution)/shard_map/all_to_all | solution.py:438
  42.7 6.9 %collective-permute-done.refs_0_ = bf16[256,1536]{1,0:T(8,128)(2,1)S(1)} collective-permute-done((bf16[256,1536]{1,0:T(8,128)(2,1)S(1)}, bf16[256,1536]{1,0:T(8,128)(2,1)S(1)}, u32[]{:S(2)}, u32[]{:S(2)}) %collective-permute-start) | collective-permute-done | bytes 786464 | tf_op jit(solution)/shard_map/ppermute | solution.py:417
  51.5 2.9 %collective-permute-start.12 = (bf16[128,1536]{1,0:T(8,128)(2,1)}, bf16[128,1536]{1,0:T(8,128)(2,1)}, u32[]{:S(2)}, u32[]{:S(2)}) collective-permute-start(bf16[128,1536]{1,0:T(8,128)(2,1)} %slice.9), channel_id=1, source_target_pairs={{0,96},{32,0},{64,32},{96,64},{1,97},{33,1},{65,33},{97,65},{2,98}... | collective-permute-start | bytes 1179656 | tf_op jit(solution)/shard_map/ppermute | solution.py:417
  54.4 3.3 %own_grads.1 = (f32[768,768]{1,0:T(8,128)S(1)}, f32[768,768]{1,0:T(8,128)S(1)}) custom-call(bf16[256,1536]{1,0:T(8,128)(2,1)S(1)} %bitcast.12, bf16[1,768,3072]{2,1,0:T(8,128)(2,1)} %refs_2_.5, bf16[1,3072,768]{2,1,0:T(8,128)(2,1)} %refs_3_.3), custom_call_target="tpu_custom_call" | custom-call | tf_op jit(solution)/shard_map/own_grads/pallas_call | solution.py:258
  57.7 5.0 %near_grads.1 = (f32[768,768]{1,0:T(8,128)S(1)}, f32[768,768]{1,0:T(8,128)S(1)}) custom-call(bf16[256,1536]{1,0:T(8,128)(2,1)S(1)} %collective-permute-done.refs_0_, bf16[256,1536]{1,0:T(8,128)(2,1)S(1)} %collective-permute-done.1.refs_1_, bf16[1,768,3072]{2,1,0:T(8,128)(2,1)} %refs_2_.5, bf16[1,3072,768]{2,1,0:T(8,128)(2,1)} %refs_3_.3, ...), custom_call_target="tpu_custom_call" | custom-call | tf_op jit(solution)/shard_map/near_grads/pallas_call | solution.py:258
  64.1 1.4 %copy-done.3 = f32[768,768]{1,0:T(8,128)} copy-done((f32[768,768]{1,0:T(8,128)}, f32[768,768]{1,0:T(8,128)S(1)}, u32[]{:S(2)}) %copy-start.3) | copy-done | bytes 2359320
  65.5 6.9 %token_logits.1 = (bf16[4,16,784]{2,1,0:T(8,128)(2,1)S(1)}, bf16[4,64,768]{2,1,0:T(8,128)(2,1)S(1)}, f32[16,768]{1,0:T(8,128)S(1)}) custom-call(bf16[16,16,1536]{2,1,0:T(8,128)(2,1)S(1)} %all-to-all-done.1.back_ref, bf16[3136,768]{1,0:T(8,128)(2,1)} %x_hbm.3, bf16[3136,768]{1,0:T(8,128)(2,1)} %g_hbm.3, f32[4,16,784]{2,1,0:T(8,128)S(1)} %get-tuple-element.27.disp_ref, ...), custom_call_target="tpu_custom_call" | custom-call | tf_op jit(solution)/shard_map/token_logits/pallas_call | solution.py:369
  73.7 1.5 %collective-permute-start.3 = (f32[16,768]{1,0:T(8,128)S(1)}, f32[16,768]{1,0:T(8,128)S(1)}, u32[]{:S(2)}, u32[]{:S(2)}) collective-permute-start(f32[16,768]{1,0:T(8,128)S(1)} %add.33), channel_id=1, source_target_pairs={{0,2},{2,0},{1,3},{3,1},{4,6},{6,4},{5,7},{7,5},{8,10},{10,8},{9,1... | collective-permute-start | bytes 147464 | tf_op jit(solution)/shard_map/ppermute | solution.py:417
  75.2 5.5 %far_grads.1 = (f32[4,96,768]{2,1,0:T(8,128)S(1)}, bf16[4,96,768]{2,1,0:T(8,128)(2,1)S(1)}, f32[384,768]{1,0:T(8,128)S(1)}, bf16[384,768]{1,0:T(8,128)(2,1)S(1)}) custom-call(bf16[128,1536]{1,0:T(8,128)(2,1)} %collective-permute-done.11.refs_0_, bf16[128,1536]{1,0:T(8,128)(2,1)} %collective-permute-done.12.refs_1_, bf16[1,768,3072]{2,1,0:T(8,128)(2,1)} %refs_2_.5, ...), custom_call_target="tpu_custom_call" | custom-call | tf_op jit(solution)/shard_map/far_grads/pallas_call | solution.py:277
  80.7 2.9 %collective-permute-start.13 = (bf16[4,96,768]{2,1,0:T(8,128)(2,1)S(1)}, bf16[4,96,768]{2,1,0:T(8,128)(2,1)S(1)}, u32[]{:S(2)}, u32[]{:S(2)}) collective-permute-start(bf16[4,96,768]{2,1,0:T(8,128)(2,1)S(1)} %get-tuple-element.35), channel_id=1, source_target_pairs={{0,16},{16,0},{1,17},{17,1},{2,18},{18,2},{3,19},{19,3},{4,20},{20... | collective-permute-start | bytes 1769480 | tf_op jit(solution)/shard_map/ppermute | solution.py:417
  83.7 2.0 %collective-permute-start.5 = (f32[16,768]{1,0:T(8,128)S(1)}, f32[16,768]{1,0:T(8,128)S(1)}, u32[]{:S(2)}, u32[]{:S(2)}) collective-permute-start(f32[16,768]{1,0:T(8,128)S(1)} %add.34), channel_id=1, source_target_pairs={{0,8},{4,12},{8,0},{12,4},{1,9},{5,13},{9,1},{13,5},{2,10},{6,14},... | collective-permute-start | bytes 147464 | tf_op jit(solution)/shard_map/ppermute | solution.py:417
  85.7 1.5 %collective-permute-start.6 = (f32[16,768]{1,0:T(8,128)S(1)}, f32[16,768]{1,0:T(8,128)S(1)}, u32[]{:S(2)}, u32[]{:S(2)}) collective-permute-start(f32[16,768]{1,0:T(8,128)S(1)} %add.34), channel_id=1, source_target_pairs={{0,12},{4,0},{8,4},{12,8},{1,13},{5,1},{9,5},{13,9},{2,14},{6,2},{... | collective-permute-start | bytes 147464 | tf_op jit(solution)/shard_map/ppermute | solution.py:417
  87.2 1.7 %collective-permute-done.4 = f32[16,768]{1,0:T(8,128)S(1)} collective-permute-done((f32[16,768]{1,0:T(8,128)S(1)}, f32[16,768]{1,0:T(8,128)S(1)}, u32[]{:S(2)}, u32[]{:S(2)}) %collective-permute-start.4) | collective-permute-done | bytes 49184 | tf_op jit(solution)/shard_map/ppermute | solution.py:417
  90.4 2.0 %collective-permute-start.8 = (f32[16,768]{1,0:T(8,128)S(1)}, f32[16,768]{1,0:T(8,128)S(1)}, u32[]{:S(2)}, u32[]{:S(2)}) collective-permute-start(f32[16,768]{1,0:T(8,128)S(1)} %add_add_fusion.1), channel_id=1, source_target_pairs={{0,64},{32,96},{64,0},{96,32},{1,65},{33,97},{65,1},{97,33},{2,66}... | collective-permute-start | bytes 147464 | tf_op jit(solution)/shard_map/ppermute | solution.py:417
  93.8 3.6 %token_grads.1 = bf16[3136,768]{1,0:T(8,128)(2,1)} custom-call(bf16[4,16,784]{2,1,0:T(8,128)(2,1)S(1)} %get-tuple-element.29.gl_ref, bf16[4,64,768]{2,1,0:T(8,128)(2,1)S(1)} %get-tuple-element.30.slots_ref, f32[4,16,784]{2,1,0:T(8,128)S(1)} %get-tuple-element.27.disp_ref, bf16[16,768]{1,0:T(8,128)(2,1)S(1)} %bitcast.14), custom_call_target="tpu_custom_call" | custom-call | tf_op jit(solution)/shard_map/token_grads/pallas_call | solution.py:400
  98.8 2.8 %collective-permute-start.10 = (f32[16,768]{1,0:T(8,128)}, f32[16,768]{1,0:T(8,128)}, u32[]{:S(2)}, u32[]{:S(2)}) collective-permute-start(f32[16,768]{1,0:T(8,128)} %add_add_fusion), channel_id=1, source_target_pairs={{0,16},{16,0},{1,17},{17,1},{2,18},{18,2},{3,19},{19,3},{4,20},{20... | collective-permute-start | bytes 147464 | tf_op jit(solution)/shard_map/ppermute | solution.py:417
  102.5 4.1 %all-to-all-start.2 = ((bf16[4,96,768]{2,1,0:T(8,128)(2,1)}), bf16[4,96,768]{2,1,0:T(8,128)(2,1)S(1)}, u32[]{:S(2)}, u32[]{:S(2)}) async-start(bf16[4,96,768]{2,1,0:T(8,128)(2,1)} %add_convert_fusion), calls=%async_computation.2 | async-start | bytes 1179648 | tf_op jit(solution)/shard_map/all_to_all | solution.py:463
  106.6 6.5 %collective-permute-done.10 = f32[16,768]{1,0:T(8,128)} collective-permute-done((f32[16,768]{1,0:T(8,128)}, f32[16,768]{1,0:T(8,128)}, u32[]{:S(2)}, u32[]{:S(2)}) %collective-permute-start.10) | collective-permute-done | bytes 49184 | tf_op jit(solution)/shard_map/ppermute | solution.py:417
  113.1 1.4 %add_bitcast_fusion.1 = f32[768,16]{0,1:T(8,128)} fusion(f32[16,768]{1,0:T(8,128)} %add_add_fusion, f32[16,768]{1,0:T(8,128)} %collective-permute-done.10), kind=kLoop, calls=%fused_computation.2 | loop fusion | flops 12288 | bytes 147456 | tf_op jit(solution)/shard_map/transpose | solution.py:466
  (51 shorter events, 13.0 us)
Async XLA Ops:
  0.6 32.0 %slice-start = ((s8[4718592]{0:T(1024)(128)(4,1)}), s8[4194304]{0:T(1024)(128)(4,1)S(1)}, s32[]{:S(2)}) async-start(s8[4718592]{0:T(1024)(128)(4,1)} %bitcast.7), calls=%async_computation.3 | async-start | bytes 8388608
  1.5 31.1 %slice-start.1 = ((s8[4718592]{0:T(1024)(128)(4,1)}), s8[524288]{0:T(1024)(128)(4,1)S(1)}, s32[]{:S(2)}) async-start(s8[4718592]{0:T(1024)(128)(4,1)} %bitcast.7), calls=%async_computation.4 | async-start | bytes 1048576
  1.5 31.1 %copy-start = (bf16[1,3072,768]{2,1,0:T(8,128)(2,1)S(1)}, bf16[1,3072,768]{2,1,0:T(8,128)(2,1)}, u32[]{:S(2)}) copy-start(bf16[1,3072,768]{2,1,0:T(8,128)(2,1)} %refs_3_.3) | copy-start | bytes 14155780
  9.4 29.6 %copy-start.5 = (f32[4,16,784]{2,1,0:T(8,128)}, f32[4,16,784]{2,1,0:T(8,128)S(1)}, u32[]{:S(2)}) copy-start(f32[4,16,784]{2,1,0:T(8,128)S(1)} %get-tuple-element.28.comb_ref) | copy-start | bytes 602116
  29.4 20.2 %collective-permute-start = (bf16[256,1536]{1,0:T(8,128)(2,1)S(1)}, bf16[256,1536]{1,0:T(8,128)(2,1)S(1)}, u32[]{:S(2)}, u32[]{:S(2)}) collective-permute-start(bf16[256,1536]{1,0:T(8,128)(2,1)S(1)} %bitcast.9), channel_id=1, source_target_pairs={{0,32},{32,64},{64,96},{96,0},{1,33},{33,65},{65,97},{97,1},{2,34}... | collective-permute-start | bytes 2359304 | tf_op jit(solution)/shard_map/ppermute | solution.py:417
  30.9 19.7 %collective-permute-start.1 = (bf16[256,1536]{1,0:T(8,128)(2,1)S(1)}, bf16[256,1536]{1,0:T(8,128)(2,1)S(1)}, u32[]{:S(2)}, u32[]{:S(2)}) collective-permute-start(bf16[256,1536]{1,0:T(8,128)(2,1)S(1)} %bitcast.10), channel_id=1, source_target_pairs={{0,96},{32,0},{64,32},{96,64},{1,97},{33,1},{65,33},{97,65},{2,98}... | collective-permute-start | bytes 2359304 | tf_op jit(solution)/shard_map/ppermute | solution.py:417
  39.1 26.4 %all-to-all-start.1 = ((bf16[16,16,1536]{2,1,0:T(8,128)(2,1)}), bf16[16,16,1536]{2,1,0:T(8,128)(2,1)S(1)}, u32[]{:S(2)}, u32[]{:S(2)}) async-start(bf16[16,16,1536]{2,1,0:T(8,128)(2,1)} %bitcast.2), calls=%async_computation.1 | async-start | bytes 1572864 | tf_op jit(solution)/shard_map/all_to_all | solution.py:438
  50.4 24.9 %collective-permute-start.11 = (bf16[128,1536]{1,0:T(8,128)(2,1)}, bf16[128,1536]{1,0:T(8,128)(2,1)}, u32[]{:S(2)}, u32[]{:S(2)}) collective-permute-start(bf16[128,1536]{1,0:T(8,128)(2,1)} %slice.8), channel_id=1, source_target_pairs={{0,32},{32,64},{64,96},{96,0},{1,33},{33,65},{65,97},{97,1},{2,34}... | collective-permute-start | bytes 1179656 | tf_op jit(solution)/shard_map/ppermute | solution.py:417
  51.5 23.7 %collective-permute-start.12 = (bf16[128,1536]{1,0:T(8,128)(2,1)}, bf16[128,1536]{1,0:T(8,128)(2,1)}, u32[]{:S(2)}, u32[]{:S(2)}) collective-permute-start(bf16[128,1536]{1,0:T(8,128)(2,1)} %slice.9), channel_id=1, source_target_pairs={{0,96},{32,0},{64,32},{96,64},{1,97},{33,1},{65,33},{97,65},{2,98}... | collective-permute-start | bytes 1179656 | tf_op jit(solution)/shard_map/ppermute | solution.py:417
  65.5 9.7 %copy-start.2 = (f32[768,768]{1,0:T(8,128)S(1)}, f32[768,768]{1,0:T(8,128)}, u32[]{:S(2)}) copy-start(f32[768,768]{1,0:T(8,128)} %copy-done.1) | copy-start | bytes 7077892
  65.5 9.7 %copy-start.4 = (f32[768,768]{1,0:T(8,128)S(1)}, f32[768,768]{1,0:T(8,128)}, u32[]{:S(2)}) copy-start(f32[768,768]{1,0:T(8,128)} %copy-done.3) | copy-start | bytes 7077892
  72.4 1.3 %collective-permute-start.2 = (f32[16,768]{1,0:T(8,128)S(1)}, f32[16,768]{1,0:T(8,128)S(1)}, u32[]{:S(2)}, u32[]{:S(2)}) collective-permute-start(f32[16,768]{1,0:T(8,128)S(1)} %get-tuple-element.31), channel_id=1, source_target_pairs={{0,1},{1,0},{2,3},{3,2},{4,5},{5,4},{6,7},{7,6},{8,9},{9,8},{10,11... | collective-permute-start | bytes 147464 | tf_op jit(solution)/shard_map/ppermute | solution.py:417
  73.7 20.0 %copy-start.8 = (bf16[768,16]{0,1:T(8,128)(2,1)S(1)}, bf16[768,16]{0,1:T(8,128)(2,1)}, u32[]{:S(2)}) copy-start(bf16[768,16]{0,1:T(8,128)(2,1)} %param.6) | copy-start | bytes 73732
  73.7 9.8 %collective-permute-start.3 = (f32[16,768]{1,0:T(8,128)S(1)}, f32[16,768]{1,0:T(8,128)S(1)}, u32[]{:S(2)}, u32[]{:S(2)}) collective-permute-start(f32[16,768]{1,0:T(8,128)S(1)} %add.33), channel_id=1, source_target_pairs={{0,2},{2,0},{1,3},{3,1},{4,6},{6,4},{5,7},{7,5},{8,10},{10,8},{9,1... | collective-permute-start | bytes 147464 | tf_op jit(solution)/shard_map/ppermute | solution.py:417
  80.7 20.8 %collective-permute-start.13 = (bf16[4,96,768]{2,1,0:T(8,128)(2,1)S(1)}, bf16[4,96,768]{2,1,0:T(8,128)(2,1)S(1)}, u32[]{:S(2)}, u32[]{:S(2)}) collective-permute-start(bf16[4,96,768]{2,1,0:T(8,128)(2,1)S(1)} %get-tuple-element.35), channel_id=1, source_target_pairs={{0,16},{16,0},{1,17},{17,1},{2,18},{18,2},{3,19},{19,3},{4,20},{20... | collective-permute-start | bytes 1769480 | tf_op jit(solution)/shard_map/ppermute | solution.py:417
  83.6 5.4 %collective-permute-start.4 = (f32[16,768]{1,0:T(8,128)S(1)}, f32[16,768]{1,0:T(8,128)S(1)}, u32[]{:S(2)}, u32[]{:S(2)}) collective-permute-start(f32[16,768]{1,0:T(8,128)S(1)} %add.34), channel_id=1, source_target_pairs={{0,4},{4,8},{8,12},{12,0},{1,5},{5,9},{9,13},{13,1},{2,6},{6,10},{... | collective-permute-start | bytes 147464 | tf_op jit(solution)/shard_map/ppermute | solution.py:417
  83.7 5.9 %collective-permute-start.5 = (f32[16,768]{1,0:T(8,128)S(1)}, f32[16,768]{1,0:T(8,128)S(1)}, u32[]{:S(2)}, u32[]{:S(2)}) collective-permute-start(f32[16,768]{1,0:T(8,128)S(1)} %add.34), channel_id=1, source_target_pairs={{0,8},{4,12},{8,0},{12,4},{1,9},{5,13},{9,1},{13,5},{2,10},{6,14},... | collective-permute-start | bytes 147464 | tf_op jit(solution)/shard_map/ppermute | solution.py:417
  85.7 4.6 %collective-permute-start.6 = (f32[16,768]{1,0:T(8,128)S(1)}, f32[16,768]{1,0:T(8,128)S(1)}, u32[]{:S(2)}, u32[]{:S(2)}) collective-permute-start(f32[16,768]{1,0:T(8,128)S(1)} %add.34), channel_id=1, source_target_pairs={{0,12},{4,0},{8,4},{12,8},{1,13},{5,1},{9,5},{13,9},{2,14},{6,2},{... | collective-permute-start | bytes 147464 | tf_op jit(solution)/shard_map/ppermute | solution.py:417
  90.3 7.8 %collective-permute-start.7 = (f32[16,768]{1,0:T(8,128)S(1)}, f32[16,768]{1,0:T(8,128)S(1)}, u32[]{:S(2)}, u32[]{:S(2)}) collective-permute-start(f32[16,768]{1,0:T(8,128)S(1)} %add_add_fusion.1), channel_id=1, source_target_pairs={{0,32},{32,64},{64,96},{96,0},{1,33},{33,65},{65,97},{97,1},{2,34}... | collective-permute-start | bytes 147464 | tf_op jit(solution)/shard_map/ppermute | solution.py:417
  90.4 7.7 %collective-permute-start.8 = (f32[16,768]{1,0:T(8,128)S(1)}, f32[16,768]{1,0:T(8,128)S(1)}, u32[]{:S(2)}, u32[]{:S(2)}) collective-permute-start(f32[16,768]{1,0:T(8,128)S(1)} %add_add_fusion.1), channel_id=1, source_target_pairs={{0,64},{32,96},{64,0},{96,32},{1,65},{33,97},{65,1},{97,33},{2,66}... | collective-permute-start | bytes 147464 | tf_op jit(solution)/shard_map/ppermute | solution.py:417
  92.4 5.7 %collective-permute-start.9 = (f32[16,768]{1,0:T(8,128)S(1)}, f32[16,768]{1,0:T(8,128)S(1)}, u32[]{:S(2)}, u32[]{:S(2)}) collective-permute-start(f32[16,768]{1,0:T(8,128)S(1)} %add_add_fusion.1), channel_id=1, source_target_pairs={{0,96},{32,0},{64,32},{96,64},{1,97},{33,1},{65,33},{97,65},{2,98}... | collective-permute-start | bytes 147464 | tf_op jit(solution)/shard_map/ppermute | solution.py:417
  97.4 17.2 %collective-permute-start.14 = (bf16[384,768]{1,0:T(8,128)(2,1)S(1)}, bf16[384,768]{1,0:T(8,128)(2,1)S(1)}, u32[]{:S(2)}, u32[]{:S(2)}) collective-permute-start(bf16[384,768]{1,0:T(8,128)(2,1)S(1)} %get-tuple-element.37), channel_id=1, source_target_pairs={{0,16},{16,0},{1,17},{17,1},{2,18},{18,2},{3,19},{19,3},{4,20},{20... | collective-permute-start | bytes 1769480 | tf_op jit(solution)/shard_map/ppermute | solution.py:417
  98.8 14.3 %collective-permute-start.10 = (f32[16,768]{1,0:T(8,128)}, f32[16,768]{1,0:T(8,128)}, u32[]{:S(2)}, u32[]{:S(2)}) collective-permute-start(f32[16,768]{1,0:T(8,128)} %add_add_fusion), channel_id=1, source_target_pairs={{0,16},{16,0},{1,17},{17,1},{2,18},{18,2},{3,19},{19,3},{4,20},{20... | collective-permute-start | bytes 147464 | tf_op jit(solution)/shard_map/ppermute | solution.py:417
  102.5 13.1 %all-to-all-start.2 = ((bf16[4,96,768]{2,1,0:T(8,128)(2,1)}), bf16[4,96,768]{2,1,0:T(8,128)(2,1)S(1)}, u32[]{:S(2)}, u32[]{:S(2)}) async-start(bf16[4,96,768]{2,1,0:T(8,128)(2,1)} %add_convert_fusion), calls=%async_computation.2 | async-start | bytes 1179648 | tf_op jit(solution)/shard_map/all_to_all | solution.py:463
  (4 other events, 11.5 us)

commit v3 on v2

--- a/solution.py
+++ b/solution.py
@@ -89,7 +89,8 @@
 
 
 def token_forward_body(
-    rt_ref, x_hbm, g_hbm, slots_ref, disp_ref, comb_ref, x_ref, g_ref, acc, x_sem, g_sem
+    rt_hbm, x_hbm, g_hbm, slots_ref, disp_ref, comb_ref,
+    rt_ref, x_ref, g_ref, acc, rt_sem, x_sem, g_sem
 ):
     experts, images, double = slots_ref.shape
     feat = double // 2
@@ -100,8 +101,10 @@
 
     x_copies = block_copies(x_hbm, x_ref, x_sem)
     g_copies = block_copies(g_hbm, g_ref, g_sem)
-    for copy in x_copies + g_copies:
+    rt_copy = pltpu.make_async_copy(rt_hbm, rt_ref, rt_sem)
+    for copy in [rt_copy] + x_copies + g_copies:
         copy.start()
+    rt_copy.wait()
     image = lane_images(width)
     rt = rt_ref[...]
     spread = []
@@ -140,7 +143,7 @@
     steps = rows // width
     return pl.pallas_call(
         token_forward_body,
-        in_specs=[IN_VMEM, IN_PLACE, IN_PLACE],
+        in_specs=[IN_PLACE] * 3,
         out_specs=[IN_VMEM, IN_VMEM, IN_VMEM],
         out_shape=[
             jax.ShapeDtypeStruct((experts, images, 2 * feat), bf16),
@@ -148,15 +151,17 @@
             jax.ShapeDtypeStruct((steps, experts, width), f32),
         ],
         scratch_shapes=[
+            pltpu.VMEM((experts, feat), bf16),
             pltpu.VMEM((rows, feat), bf16),
             pltpu.VMEM((rows, feat), bf16),
             pltpu.VMEM((experts * images, 2 * feat), bf16),
+            pltpu.SemaphoreType.DMA(()),
             pltpu.SemaphoreType.DMA((steps,)),
             pltpu.SemaphoreType.DMA((steps,)),
         ],
         compiler_params=params(20),
         name="token_forward",
-    )(rt, pinned(tokens), pinned(g_outputs))
+    )(pinned(rt), pinned(tokens), pinned(g_outputs))
 
 
 def expert_body(rows_ref, w1_ref, w2_ref, out_ref):
@@ -190,58 +195,88 @@
     )(rows, w_in, w_out)
 
 
-def slice_grads(piece_refs, w1_hbm, w2_hbm, low, tile, both, act_all, pre_all, w1, w2, sem):
-    feat = w1.shape[0]
-    low = pl.multiple_of(low, tile)
-    first = pltpu.make_async_copy(w1_hbm.at[0, :, pl.ds(low, tile)], w1, sem.at[0])
-    second = pltpu.make_async_copy(w2_hbm.at[0, pl.ds(low, tile), :], w2, sem.at[1])
-    first.start()
-    second.start()
+def slice_copies(w1_hbm, w2_hbm, w1, w2, sem):
+    tile = w1.shape[1]
+    low = pl.multiple_of(lax.axis_index("y") * tile, tile)
+    return (
+        pltpu.make_async_copy(w1_hbm.at[0, :, pl.ds(low, tile)], w1, sem.at[0]),
+        pltpu.make_async_copy(w2_hbm.at[0, pl.ds(low, tile), :], w2, sem.at[1]),
+    )
+
+
+def gather_pieces(piece_refs, both):
     at = 0
     for piece in piece_refs:
         both[at : at + piece.shape[0], :] = piece[...]
         at += piece.shape[0]
+
+
+def slice_terms(both, w1, w2, act_all, pre_all, loads):
+    feat = w1.shape[0]
     rows = both[:, :feat]
     grads = both[:, feat:]
-    first.wait()
+    loads[0].wait()
     act, slope = gelu_parts(jnp.dot(rows, w1[...], preferred_element_type=f32))
     act_all[...] = act.astype(bf16)
-    second.wait()
+    loads[1].wait()
     pre_all[...] = (contract(grads, w2[...], 1, 1) * slope).astype(bf16)
-    return contract(rows, pre_all[...], 0, 0), contract(act_all[...], grads, 0, 0)
-
-
-def grads_body(count, first, *refs):
-    pieces, (w1_ref, w2_ref) = refs[:count], refs[count : count + 2]
-    refs = refs[count + 2 :]
-    sums, refs = (None, refs) if first else (refs[:2], refs[2:])
-    out_in, out_out, *scratch = refs
-    tile = out_in.shape[1]
-    low = lax.axis_index("y") * tile
-    part_in, part_out = slice_grads(pieces, w1_ref, w2_ref, low, tile, *scratch)
-    out_in[...] = part_in if first else sums[0][...] + part_in
-    out_out[...] = part_out if first else sums[1][...] + part_out
-
-
-def last_grads_body(count, *refs):
-    pieces, (w1_ref, w2_ref, sum_in, sum_out) = refs[:count], refs[count : count + 4]
-    keep_in, send_in, keep_out, send_out, acc_in, acc_out, *scratch = refs[count + 4 :]
-    tile = sum_in.shape[1]
-    low = lax.axis_index("y") * tile
+
+
+def near_grads_body(count, *refs):
+    pieces, (w1_hbm, w2_hbm) = refs[:count], refs[count : count + 2]
+    in_hbm, out_hbm, sum_in, sum_out, out_sem, both, act_all, pre_all, w1, w2, sem = refs[count + 2 :]
+    feat = w1.shape[0]
+    loads = slice_copies(w1_hbm, w2_hbm, w1, w2, sem)
+    for load in loads:
+        load.start()
+    gather_pieces(pieces, both)
+    slice_terms(both, w1, w2, act_all, pre_all, loads)
+    stores = (
+        pltpu.make_async_copy(sum_out, out_hbm, out_sem.at[0]),
+        pltpu.make_async_copy(sum_in, in_hbm, out_sem.at[1]),
+    )
+    sum_out[...] = contract(act_all[...], both[:, feat:], 0, 0)
+    stores[0].start()
+    sum_in[...] = contract(both[:, :feat], pre_all[...], 0, 0)
+    stores[1].start()
+    for store in stores:
+        store.wait()
+
+
+def far_grads_body(count, *refs):
+    pieces, (w1_hbm, w2_hbm, in_hbm, out_hbm) = refs[:count], refs[count : count + 4]
+    keep_in, send_in, keep_out, send_out, *refs = refs[count + 4 :]
+    acc_in, acc_out, sum_in, sum_out, in_sem, both, act_all, pre_all, w1, w2, sem = refs
+    feat = w1.shape[0]
     xh = lax.axis_index("xh")
-    part_in, part_out = slice_grads(pieces, w1_ref, w2_ref, low, tile, *scratch)
+    loads = slice_copies(w1_hbm, w2_hbm, w1, w2, sem)
+    sums = (
+        pltpu.make_async_copy(in_hbm, sum_in, in_sem.at[0]),
+        pltpu.make_async_copy(out_hbm, sum_out, in_sem.at[1]),
+    )
+    for load in loads + sums:
+        load.start()
+    gather_pieces(pieces, both)
+    slice_terms(both, w1, w2, act_all, pre_all, loads)
+    part_in = contract(both[:, :feat], pre_all[...], 0, 0)
+    sums[0].wait()
     acc_in[...] = (sum_in[...] + part_in).reshape(acc_in.shape)
+    send_in[...] = acc_in[:, pl.ds(1 - xh, 1)].reshape(send_in.shape).astype(bf16)
+    keep_in[...] = acc_in[:, pl.ds(xh, 1)].reshape(keep_in.shape)
+    part_out = contract(act_all[...], both[:, feat:], 0, 0)
+    sums[1].wait()
     acc_out[...] = (sum_out[...] + part_out).reshape(acc_out.shape)
-    keep_in[...] = acc_in[:, pl.ds(xh, 1)].reshape(keep_in.shape)
-    send_in[...] = acc_in[:, pl.ds(1 - xh, 1)].reshape(send_in.shape).astype(bf16)
+    send_out[...] = acc_out[1 - xh].astype(bf16)
     keep_out[...] = acc_out[xh]
-    send_out[...] = acc_out[1 - xh].astype(bf16)
 
 
 def piece_scratch(pieces, tile):
     count = sum(p.shape[0] for p in pieces)
     feat = pieces[0].shape[1] // 2
     return [
+        pltpu.VMEM((feat, tile), f32),
+        pltpu.VMEM((tile, feat), f32),
+        pltpu.SemaphoreType.DMA((2,)),
         pltpu.VMEM((count, 2 * feat), bf16),
         pltpu.VMEM((count, tile), bf16),
         pltpu.VMEM((count, tile), bf16),
@@ -251,32 +286,30 @@
     ]
 
 
-def weight_grads(pieces, w_in, w_out, sums, parts, name):
+def near_grads(pieces, w_in, w_out, parts):
     feat, hidden = w_in.shape[1:]
     tile = hidden // parts
-    count = sum(p.shape[0] for p in pieces)
-    return pl.pallas_call(
-        functools.partial(grads_body, len(pieces), not sums),
-        in_specs=[IN_VMEM] * len(pieces) + [IN_PLACE] * 2 + [IN_VMEM] * len(sums),
-        out_specs=[IN_VMEM] * 2,
+    return pl.pallas_call(
+        functools.partial(near_grads_body, len(pieces)),
+        in_specs=[IN_VMEM] * len(pieces) + [IN_PLACE] * 2,
+        out_specs=[IN_PLACE] * 2,
         out_shape=[
-            jax.ShapeDtypeStruct((feat, tile), f32),
-            jax.ShapeDtypeStruct((tile, feat), f32),
+            pltpu.HBM((feat, tile), f32),
+            pltpu.HBM((tile, feat), f32),
         ],
         scratch_shapes=piece_scratch(pieces, tile),
-        compiler_params=params(16),
-        name=name,
-    )(*pieces, pinned(w_in), pinned(w_out), *sums)
-
-
-def last_weight_grads(pieces, w_in, w_out, sums, parts):
+        compiler_params=params(20),
+        name="near_grads",
+    )(*pieces, pinned(w_in), pinned(w_out))
+
+
+def far_grads(pieces, w_in, w_out, sums, parts):
     feat, hidden = w_in.shape[1:]
     tile = hidden // parts
     own = feat // (parts * XH)
-    count = sum(p.shape[0] for p in pieces)
-    return pl.pallas_call(
-        functools.partial(last_grads_body, len(pieces)),
-        in_specs=[IN_VMEM] * len(pieces) + [IN_PLACE] * 2 + [IN_VMEM] * 2,
+    return pl.pallas_call(
+        functools.partial(far_grads_body, len(pieces)),
+        in_specs=[IN_VMEM] * len(pieces) + [IN_PLACE] * 4,
         out_specs=[IN_VMEM] * 4,
         out_shape=[
             jax.ShapeDtypeStruct((parts, own, tile), f32),
@@ -289,9 +322,9 @@
             pltpu.VMEM((XH, tile // XH, feat), f32),
         ]
         + piece_scratch(pieces, tile),
-        compiler_params=params(20),
+        compiler_params=params(24),
         name="far_grads",
-    )(*pieces, pinned(w_in), pinned(w_out), *sums)
+    )(*pieces, pinned(w_in), pinned(w_out), *[pinned(v) for v in sums])
 
 
 def widen_body(in_ref, out_ref):
@@ -417,22 +450,18 @@
     return lax.ppermute(value, axis, [(i, (i + by) % count) for i in range(count)])
 
 
-def everywhere_sum(value, sizes):
-    for axis, count in sizes:
-        value = sum([shift(value, axis, by, count) for by in range(1, count)], value)
-    return value
+def axis_sum(value, axis, count):
+    return sum([shift(value, axis, by, count) for by in range(1, count)], value)
 
 
 def solution(mesh):
     dp, experts = mesh.shape["dp"], mesh.shape["expert"]
-    ny = dp // XH
-    inner = (("core", 2), ("xl", 2), ("z", experts // 4))
+    ny, nz = dp // XH, experts // 4
     fine = Mesh(
-        mesh.devices.reshape(ny, XH, experts // 4, 2, 2), ("y", "xh", "z", "xl", "core")
+        mesh.devices.reshape(ny, XH, nz, 2, 2), ("y", "xh", "z", "xl", "core")
     )
     dp_axes = ("y", "xh")
     ex_axes = ("z", "xl", "core")
-    sizes = inner + (("y", ny), ("xh", XH))
 
     def over_experts(value):
         return lax.all_to_all(value, ex_axes, split_axis=0, concat_axis=0, tiled=True)
@@ -442,28 +471,36 @@
         slots, dispatch, combine = token_forward(tokens, rt, g_outputs)
         rows = over_experts(slots).reshape(-1, slots.shape[2])
         mid = rows.shape[0] // 2
-        right = shift(rows, "y", 1, ny)
-        left = shift(rows, "y", ny - 1, ny)
+        low, high = [
+            pltpu.with_memory_space_constraint(v, pltpu.VMEM) for v in (rows[:mid], rows[mid:])
+        ]
+        right_low = shift(low, "y", 1, ny)
+        left_high = shift(high, "y", ny - 1, ny)
+        right_high = shift(high, "y", 1, ny)
+        left_low = shift(low, "y", ny - 1, ny)
+        far_low = shift(right_low, "y", 1, ny)
+        far_high = shift(left_high, "y", ny - 1, ny)
         results = expert_rows(rows, w_in, w_out)
         back = over_experts(results.reshape(slots.shape))
-        own_sums = weight_grads((rows,), w_in, w_out, (), ny, "own_grads")
-        far_a = shift(right[:mid], "y", 1, ny)
-        far_b = shift(left[mid:], "y", ny - 1, ny)
-        near_sums = weight_grads((right, left), w_in, w_out, tuple(own_sums), ny, "near_grads")
-        back, near_sums = lax.optimization_barrier((back, tuple(near_sums)))
+        sums = near_grads(
+            (rows, right_low, left_high, right_high, left_low), w_in, w_out, ny
+        )
+        back, sums = lax.optimization_barrier((back, tuple(sums)))
         grad_logits, slot_grads, router_term = token_logits(
             back, tokens, g_outputs, dispatch, combine
         )
-        keep_in, send_in, keep_out, send_out = last_weight_grads(
-            (far_a, far_b), w_in, w_out, near_sums, ny
-        )
+        keep_in, send_in, keep_out, send_out = far_grads((far_low, far_high), w_in, w_out, sums, ny)
         came_in = shift(send_in, "xh", 1, XH)
         came_out = shift(send_out, "xh", 1, XH)
+        total = axis_sum(axis_sum(router_term, "core", 2), "z", nz)
+        total, came_in = lax.optimization_barrier((total, came_in))
         part_in = (keep_in + came_in.astype(f32)).astype(bf16)
         spread = lax.all_to_all(part_in, "y", split_axis=0, concat_axis=0, tiled=True)
+        total = axis_sum(axis_sum(total, "y", ny), "xl", 2)
+        total, came_out, spread = lax.optimization_barrier((total, came_out, spread))
         grad_first = widen(spread)
+        grad_router = axis_sum(total, "xh", XH).T
         grad_second = keep_out + came_out.astype(f32)
-        grad_router = everywhere_sum(router_term, sizes).T
         grad_tok = token_grads(grad_logits, slot_grads, dispatch, rt)
         return grad_tok, grad_router, grad_first, grad_second[None]
 

time: 117 us -> 122 us (1.043)
  waiting for transfers between devices: 17.7 us -> 22.6 us
  local copies, waits for them, and re-layouts: 5.29 us -> 0.96 us
  starting transfers between devices: 29.1 us -> 32.2 us
  Pallas kernels: 39.7 us -> 42.7 us
  other arithmetic: 4.18 us -> 2.74 us
    ppermute x15 -> x17, waiting for transfers between devices: 17.7 us -> 22.6 us  [shift(): lax.ppermute(value, axis, [(i, (i + by) % count) for i in range(count)])]
    unnamed x22 -> x12, local copies, waits for them, and re-layouts: 3.73 us -> 0.03 us
    ppermute x15 -> x17, starting transfers between devices: 21.4 us -> 25 us  [shift(): lax.ppermute(value, axis, [(i, (i + by) % count) for i in range(count)])]
    pallas_call x4 -> x3, Pallas kernels: 21.6 us -> 24.8 us  [the longest x1 9.28 us: token_forward(): pl.pallas_call(token_forward_body, in_specs=[IN_PLACE] * 3, out_specs=[IN...]
  transfers between devices with their start and end apart: 17 -> 19, of which waited for: 6 -> 9; matrix products, arithmetic and copies ran while one was open for 5% -> 2% of each run, Pallas kernels for 26% -> 21%
where the time goes in v3:
time: 122 us
  Pallas kernels  42.7 us (35%)
  starting transfers between devices  32.2 us (26%)
  waiting for transfers between devices  22.6 us (19%)
  blocking collectives  19.9 us (16%)
  other arithmetic  2.74 us (2%)
    ppermute x17, starting transfers between devices, shift(): lax.ppermute(value, axis, [(i, (i + by) % count) for i in range(count)])  25 us
    ppermute x17, waiting for transfers between devices, shift(): lax.ppermute(value, axis, [(i, (i + by) % count) for i in range(count)])  22.6 us
    all_to_all x1, blocking collectives, over_experts(): lax.all_to_all(value, ex_axes, split_axis=0, concat_axis=0, tiled=True)  19.9 us
    pallas_call x1, Pallas kernels, token_forward(): pl.pallas_call(token_forward_body, in_specs=[IN_PLACE] * 3, out_specs=[IN...  9.28 us
    pallas_call x1, Pallas kernels, near_grads(): pl.pallas_call(functools.partial(near_grads_body, len(pieces)), in_specs=...  7.92 us
    pallas_call x1, Pallas kernels, far_grads(): pl.pallas_call(functools.partial(far_grads_body, len(pieces)), in_specs=[...  7.55 us
    pallas_call x1, Pallas kernels, token_logits(): pl.pallas_call(token_logits_body, in_specs=[IN_VMEM, IN_PLACE, IN_PLACE,...  6.78 us
    pallas_call x1, Pallas kernels, expert_rows(): pl.pallas_call(expert_body, in_specs=[IN_VMEM] * 3, out_specs=IN_VMEM, ou...  6.48 us
  transfers between devices with their start and end apart: 19, of which 9 were waited for; matrix products, arithmetic and copies ran while one was open for 2% of the time, Pallas kernels for 21%

profile of v3, /device:TPU:0, one launch (start us, length us, event | category | flops | bytes accessed | tf_op | source)
XLA Modules:
  0.0 122.0 jit_solution(5647360701715629482)
XLA Ops:
  0.7 9.3 %token_forward.1 = (bf16[16,16,1536]{2,1,0:T(8,128)(2,1)S(1)}, f32[4,16,784]{2,1,0:T(8,128)S(1)}, f32[4,16,784]{2,1,0:T(8,128)S(1)}) custom-call(bf16[16,768]{1,0:T(8,128)(2,1)} %bitcast.13, bf16[3136,768]{1,0:T(8,128)(2,1)} %x_hbm.3, bf16[3136,768]{1,0:T(8,128)(2,1)} %g_hbm.3), custom_call_target="tpu_custom_call" | custom-call | tf_op jit(solution)/shard_map/token_forward/pallas_call | solution.py:144
  10.0 19.9 %all_to_all.15 = bf16[16,16,1536]{2,1,0:T(8,128)(2,1)S(1)} all-to-all(bf16[16,16,1536]{2,1,0:T(8,128)(2,1)S(1)} %get-tuple-element.24), channel_id=1, replica_groups=mesh['y'=4,'xh'=2,'z'=4,'xl'=2,'core'=2] {'z','xl','core'}, dimensions={0} | all-to-all | bytes 1572864 | tf_op jit(solution)/shard_map/all_to_all | solution.py:467
  30.8 1.6 %collective-permute-start = (bf16[128,1536]{1,0:T(8,128)(2,1)}, bf16[128,1536]{1,0:T(8,128)(2,1)S(1)}, u32[]{:S(2)}, u32[]{:S(2)}) collective-permute-start(bf16[128,1536]{1,0:T(8,128)(2,1)} %bitcast.3), channel_id=1, source_target_pairs={{0,32},{32,64},{64,96},{96,0},{1,33},{33,65},{65,97},{97,1},{2,34}... | collective-permute-start | bytes 1179656 | tf_op jit(solution)/shard_map/ppermute | solution.py:450
  32.4 1.7 %collective-permute-start.1 = (bf16[128,1536]{1,0:T(8,128)(2,1)}, bf16[128,1536]{1,0:T(8,128)(2,1)S(1)}, u32[]{:S(2)}, u32[]{:S(2)}) collective-permute-start(bf16[128,1536]{1,0:T(8,128)(2,1)} %bitcast.4), channel_id=1, source_target_pairs={{0,96},{32,0},{64,32},{96,64},{1,97},{33,1},{65,33},{97,65},{2,98}... | collective-permute-start | bytes 1179656 | tf_op jit(solution)/shard_map/ppermute | solution.py:450
  34.0 6.5 %expert_rows.1 = bf16[256,1536]{1,0:T(8,128)(2,1)} custom-call(bf16[256,1536]{1,0:T(8,128)(2,1)S(1)} %bitcast.11, bf16[1,768,3072]{2,1,0:T(8,128)(2,1)S(1)} %bitcast.10, bf16[1,3072,768]{2,1,0:T(8,128)(2,1)S(1)} %copy-done), custom_call_target="tpu_custom_call" | custom-call | tf_op jit(solution)/shard_map/expert_rows/pallas_call | solution.py:188
  40.5 3.6 %all-to-all-start.1 = ((bf16[16,16,1536]{2,1,0:T(8,128)(2,1)}), bf16[16,16,1536]{2,1,0:T(8,128)(2,1)S(1)}, u32[]{:S(2)}, u32[]{:S(2)}) async-start(bf16[16,16,1536]{2,1,0:T(8,128)(2,1)} %bitcast.2), calls=%async_computation.1 | async-start | bytes 1572864 | tf_op jit(solution)/shard_map/all_to_all | solution.py:467
  44.1 1.9 %collective-permute-start.3 = (bf16[128,1536]{1,0:T(8,128)(2,1)}, bf16[128,1536]{1,0:T(8,128)(2,1)S(1)}, u32[]{:S(2)}, u32[]{:S(2)}) collective-permute-start(bf16[128,1536]{1,0:T(8,128)(2,1)} %bitcast.3), channel_id=1, source_target_pairs={{0,96},{32,0},{64,32},{96,64},{1,97},{33,1},{65,33},{97,65},{2,98}... | collective-permute-start | bytes 1179656 | tf_op jit(solution)/shard_map/ppermute | solution.py:450
  46.6 2.9 %collective-permute-start.9 = (bf16[128,1536]{1,0:T(8,128)(2,1)S(1)}, bf16[128,1536]{1,0:T(8,128)(2,1)}, u32[]{:S(2)}, u32[]{:S(2)}) collective-permute-start(bf16[128,1536]{1,0:T(8,128)(2,1)S(1)} %collective-permute-done.1.refs_2_), channel_id=1, source_target_pairs={{0,96},{32,0},{64,32},{96,64},{1,97},{33,1},{65,33},{97,65},{2,98}... | collective-permute-start | bytes 1179656 | tf_op jit(solution)/shard_map/ppermute | solution.py:450
  49.5 6.9 %collective-permute-done.3.refs_4_ = bf16[128,1536]{1,0:T(8,128)(2,1)S(1)} collective-permute-done((bf16[128,1536]{1,0:T(8,128)(2,1)}, bf16[128,1536]{1,0:T(8,128)(2,1)S(1)}, u32[]{:S(2)}, u32[]{:S(2)}) %collective-permute-start.3) | collective-permute-done | bytes 393248 | tf_op jit(solution)/shard_map/ppermute | solution.py:450
  56.4 3.0 %collective-permute-done.2.refs_3_ = bf16[128,1536]{1,0:T(8,128)(2,1)S(1)} collective-permute-done((bf16[128,1536]{1,0:T(8,128)(2,1)}, bf16[128,1536]{1,0:T(8,128)(2,1)S(1)}, u32[]{:S(2)}, u32[]{:S(2)}) %collective-permute-start.2) | collective-permute-done | bytes 393248 | tf_op jit(solution)/shard_map/ppermute | solution.py:450
  59.4 7.9 %near_grads.1 = (f32[768,768]{1,0:T(8,128)}, f32[768,768]{1,0:T(8,128)}) custom-call(bf16[256,1536]{1,0:T(8,128)(2,1)S(1)} %bitcast.12, bf16[128,1536]{1,0:T(8,128)(2,1)S(1)} %collective-permute-done.refs_1_, bf16[128,1536]{1,0:T(8,128)(2,1)S(1)} %collective-permute-done.1.refs_2_, bf16[128,1536]{1,0:T(8,128)(2,1)S(1)} %collective-permute-done.2.refs_3_, ...), custom_call_target="tpu_custom_call" | custom-call | tf_op jit(solution)/shard_map/near_grads/pallas_call | solution.py:292
  67.4 7.6 %far_grads.1 = (f32[4,96,768]{2,1,0:T(8,128)S(1)}, bf16[4,96,768]{2,1,0:T(8,128)(2,1)S(1)}, f32[384,768]{1,0:T(8,128)S(1)}, bf16[384,768]{1,0:T(8,128)(2,1)}) custom-call(bf16[128,1536]{1,0:T(8,128)(2,1)S(1)} %collective-permute-done.8.refs_0_, bf16[128,1536]{1,0:T(8,128)(2,1)} %collective-permute-done.9.refs_1_, bf16[1,768,3072]{2,1,0:T(8,128)(2,1)} %refs_2_.1, ...), custom_call_target="tpu_custom_call" | custom-call | tf_op jit(solution)/shard_map/far_grads/pallas_call | solution.py:310
  75.0 2.8 %collective-permute-start.10 = (bf16[4,96,768]{2,1,0:T(8,128)(2,1)S(1)}, bf16[4,96,768]{2,1,0:T(8,128)(2,1)S(1)}, u32[]{:S(2)}, u32[]{:S(2)}) collective-permute-start(bf16[4,96,768]{2,1,0:T(8,128)(2,1)S(1)} %get-tuple-element.35), channel_id=1, source_target_pairs={{0,16},{16,0},{1,17},{17,1},{2,18},{18,2},{3,19},{19,3},{4,20},{20... | collective-permute-start | bytes 1769480 | tf_op jit(solution)/shard_map/ppermute | solution.py:450
  77.8 6.8 %token_logits.1 = (bf16[4,16,784]{2,1,0:T(8,128)(2,1)S(1)}, bf16[4,64,768]{2,1,0:T(8,128)(2,1)S(1)}, f32[16,768]{1,0:T(8,128)S(1)}) custom-call(bf16[16,16,1536]{2,1,0:T(8,128)(2,1)S(1)} %all-to-all-done.1.back_ref, bf16[3136,768]{1,0:T(8,128)(2,1)} %x_hbm.3, bf16[3136,768]{1,0:T(8,128)(2,1)} %g_hbm.3, f32[4,16,784]{2,1,0:T(8,128)S(1)} %get-tuple-element.28.disp_ref, ...), custom_call_target="tpu_custom_call" | custom-call | tf_op jit(solution)/shard_map/token_logits/pallas_call | solution.py:402
  84.7 1.2 collective-permute-done.4
  85.9 3.1 %collective-permute-start.7 = (f32[16,768]{1,0:T(8,128)S(1)}, f32[16,768]{1,0:T(8,128)S(1)}, u32[]{:S(2)}, u32[]{:S(2)}) collective-permute-start(f32[16,768]{1,0:T(8,128)S(1)} %add.33), channel_id=1, source_target_pairs={{0,12},{4,0},{8,4},{12,8},{1,13},{5,1},{9,5},{13,9},{2,14},{6,2},{... | collective-permute-start | bytes 147464 | tf_op jit(solution)/shard_map/ppermute | solution.py:450
  91.5 3.1 %collective-permute-done.6 = f32[16,768]{1,0:T(8,128)S(1)} collective-permute-done((f32[16,768]{1,0:T(8,128)S(1)}, f32[16,768]{1,0:T(8,128)S(1)}, u32[]{:S(2)}, u32[]{:S(2)}) %collective-permute-start.6) | collective-permute-done | bytes 49184 | tf_op jit(solution)/shard_map/ppermute | solution.py:450
  96.1 3.6 %all-to-all-start.2 = ((bf16[4,96,768]{2,1,0:T(8,128)(2,1)}), bf16[4,96,768]{2,1,0:T(8,128)(2,1)S(1)}, u32[]{:S(2)}, u32[]{:S(2)}) async-start(bf16[4,96,768]{2,1,0:T(8,128)(2,1)} %add_convert_fusion), calls=%async_computation.2 | async-start | bytes 1179648 | tf_op jit(solution)/shard_map/all_to_all | solution.py:498
  99.7 3.2 %collective-permute-start.13 = (f32[16,768]{1,0:T(8,128)S(1)}, f32[16,768]{1,0:T(8,128)S(1)}, u32[]{:S(2)}, u32[]{:S(2)}) collective-permute-start(f32[16,768]{1,0:T(8,128)S(1)} %add_add_fusion.1), channel_id=1, source_target_pairs={{0,96},{32,0},{64,32},{96,64},{1,97},{33,1},{65,33},{97,65},{2,98}... | collective-permute-start | bytes 147464 | tf_op jit(solution)/shard_map/ppermute | solution.py:450
  104.6 4.4 %collective-permute-done.13 = f32[16,768]{1,0:T(8,128)S(1)} collective-permute-done((f32[16,768]{1,0:T(8,128)S(1)}, f32[16,768]{1,0:T(8,128)S(1)}, u32[]{:S(2)}, u32[]{:S(2)}) %collective-permute-start.13) | collective-permute-done | bytes 49184 | tf_op jit(solution)/shard_map/ppermute | solution.py:450
  109.0 1.6 %collective-permute-done.12 = f32[16,768]{1,0:T(8,128)S(1)} collective-permute-done((f32[16,768]{1,0:T(8,128)S(1)}, f32[16,768]{1,0:T(8,128)S(1)}, u32[]{:S(2)}, u32[]{:S(2)}) %collective-permute-start.12) | collective-permute-done | bytes 49184 | tf_op jit(solution)/shard_map/ppermute | solution.py:450
  112.0 3.6 %token_grads.1 = bf16[3136,768]{1,0:T(8,128)(2,1)} custom-call(bf16[4,16,784]{2,1,0:T(8,128)(2,1)S(1)} %get-tuple-element.30.gl_ref, bf16[4,64,768]{2,1,0:T(8,128)(2,1)S(1)} %get-tuple-element.31.slots_ref, f32[4,16,784]{2,1,0:T(8,128)S(1)} %get-tuple-element.28.disp_ref, bf16[16,768]{1,0:T(8,128)(2,1)S(1)} %bitcast.14), custom_call_target="tpu_custom_call" | custom-call | tf_op jit(solution)/shard_map/token_grads/pallas_call | solution.py:433
  115.7 2.1 %collective-permute-start.16 = (f32[16,768]{1,0:T(8,128)S(1)}, f32[16,768]{1,0:T(8,128)S(1)}, u32[]{:S(2)}, u32[]{:S(2)}) collective-permute-start(f32[16,768]{1,0:T(8,128)S(1)} %add.40), channel_id=1, source_target_pairs={{0,16},{16,0},{1,17},{17,1},{2,18},{18,2},{3,19},{19,3},{4,20},{20... | collective-permute-start | bytes 147464 | tf_op jit(solution)/shard_map/ppermute | solution.py:450
  120.0 1.4 %collective-permute-done.16 = f32[16,768]{1,0:T(8,128)S(1)} collective-permute-done((f32[16,768]{1,0:T(8,128)S(1)}, f32[16,768]{1,0:T(8,128)S(1)}, u32[]{:S(2)}, u32[]{:S(2)}) %collective-permute-start.16) | collective-permute-done | bytes 49184 | tf_op jit(solution)/shard_map/ppermute | solution.py:450
  (43 shorter events, 11.6 us)
Async XLA Ops:
  0.6 33.4 %slice-start = ((s8[4718592]{0:T(1024)(128)(4,1)}), s8[4194304]{0:T(1024)(128)(4,1)S(1)}, s32[]{:S(2)}) async-start(s8[4718592]{0:T(1024)(128)(4,1)} %bitcast.9), calls=%async_computation.3 | async-start | bytes 8388608
  0.6 33.4 %slice-start.1 = ((s8[4718592]{0:T(1024)(128)(4,1)}), s8[524288]{0:T(1024)(128)(4,1)S(1)}, s32[]{:S(2)}) async-start(s8[4718592]{0:T(1024)(128)(4,1)} %bitcast.9), calls=%async_computation.4 | async-start | bytes 1048576
  0.7 33.4 %copy-start = (bf16[1,3072,768]{2,1,0:T(8,128)(2,1)S(1)}, bf16[1,3072,768]{2,1,0:T(8,128)(2,1)}, u32[]{:S(2)}) copy-start(bf16[1,3072,768]{2,1,0:T(8,128)(2,1)} %refs_3_.1) | copy-start | bytes 14155780
  10.0 20.8 %copy-start.1 = (f32[4,16,784]{2,1,0:T(8,128)}, f32[4,16,784]{2,1,0:T(8,128)S(1)}, u32[]{:S(2)}) copy-start(f32[4,16,784]{2,1,0:T(8,128)S(1)} %get-tuple-element.29.comb_ref) | copy-start | bytes 602116
  30.8 15.4 %collective-permute-start = (bf16[128,1536]{1,0:T(8,128)(2,1)}, bf16[128,1536]{1,0:T(8,128)(2,1)S(1)}, u32[]{:S(2)}, u32[]{:S(2)}) collective-permute-start(bf16[128,1536]{1,0:T(8,128)(2,1)} %bitcast.3), channel_id=1, source_target_pairs={{0,32},{32,64},{64,96},{96,0},{1,33},{33,65},{65,97},{97,1},{2,34}... | collective-permute-start | bytes 1179656 | tf_op jit(solution)/shard_map/ppermute | solution.py:450
  32.4 14.2 %collective-permute-start.1 = (bf16[128,1536]{1,0:T(8,128)(2,1)}, bf16[128,1536]{1,0:T(8,128)(2,1)S(1)}, u32[]{:S(2)}, u32[]{:S(2)}) collective-permute-start(bf16[128,1536]{1,0:T(8,128)(2,1)} %bitcast.4), channel_id=1, source_target_pairs={{0,96},{32,0},{64,32},{96,64},{1,97},{33,1},{65,33},{97,65},{2,98}... | collective-permute-start | bytes 1179656 | tf_op jit(solution)/shard_map/ppermute | solution.py:450
  40.5 26.8 %all-to-all-start.1 = ((bf16[16,16,1536]{2,1,0:T(8,128)(2,1)}), bf16[16,16,1536]{2,1,0:T(8,128)(2,1)S(1)}, u32[]{:S(2)}, u32[]{:S(2)}) async-start(bf16[16,16,1536]{2,1,0:T(8,128)(2,1)} %bitcast.2), calls=%async_computation.1 | async-start | bytes 1572864 | tf_op jit(solution)/shard_map/all_to_all | solution.py:467
  44.1 12.2 %collective-permute-start.3 = (bf16[128,1536]{1,0:T(8,128)(2,1)}, bf16[128,1536]{1,0:T(8,128)(2,1)S(1)}, u32[]{:S(2)}, u32[]{:S(2)}) collective-permute-start(bf16[128,1536]{1,0:T(8,128)(2,1)} %bitcast.3), channel_id=1, source_target_pairs={{0,96},{32,0},{64,32},{96,64},{1,97},{33,1},{65,33},{97,65},{2,98}... | collective-permute-start | bytes 1179656 | tf_op jit(solution)/shard_map/ppermute | solution.py:450
  46.0 13.4 %collective-permute-start.2 = (bf16[128,1536]{1,0:T(8,128)(2,1)}, bf16[128,1536]{1,0:T(8,128)(2,1)S(1)}, u32[]{:S(2)}, u32[]{:S(2)}) collective-permute-start(bf16[128,1536]{1,0:T(8,128)(2,1)} %bitcast.4), channel_id=1, source_target_pairs={{0,32},{32,64},{64,96},{96,0},{1,33},{33,65},{65,97},{97,1},{2,34}... | collective-permute-start | bytes 1179656 | tf_op jit(solution)/shard_map/ppermute | solution.py:450
  46.2 21.1 %collective-permute-start.8 = (bf16[128,1536]{1,0:T(8,128)(2,1)S(1)}, bf16[128,1536]{1,0:T(8,128)(2,1)S(1)}, u32[]{:S(2)}, u32[]{:S(2)}) collective-permute-start(bf16[128,1536]{1,0:T(8,128)(2,1)S(1)} %collective-permute-done.refs_1_), channel_id=1, source_target_pairs={{0,32},{32,64},{64,96},{96,0},{1,33},{33,65},{65,97},{97,1},{2,34}... | collective-permute-start | bytes 1179656 | tf_op jit(solution)/shard_map/ppermute | solution.py:450
  46.6 20.8 %collective-permute-start.9 = (bf16[128,1536]{1,0:T(8,128)(2,1)S(1)}, bf16[128,1536]{1,0:T(8,128)(2,1)}, u32[]{:S(2)}, u32[]{:S(2)}) collective-permute-start(bf16[128,1536]{1,0:T(8,128)(2,1)S(1)} %collective-permute-done.1.refs_2_), channel_id=1, source_target_pairs={{0,96},{32,0},{64,32},{96,64},{1,97},{33,1},{65,33},{97,65},{2,98}... | collective-permute-start | bytes 1179656 | tf_op jit(solution)/shard_map/ppermute | solution.py:450
  75.0 20.2 %collective-permute-start.10 = (bf16[4,96,768]{2,1,0:T(8,128)(2,1)S(1)}, bf16[4,96,768]{2,1,0:T(8,128)(2,1)S(1)}, u32[]{:S(2)}, u32[]{:S(2)}) collective-permute-start(bf16[4,96,768]{2,1,0:T(8,128)(2,1)S(1)} %get-tuple-element.35), channel_id=1, source_target_pairs={{0,16},{16,0},{1,17},{17,1},{2,18},{18,2},{3,19},{19,3},{4,20},{20... | collective-permute-start | bytes 1769480 | tf_op jit(solution)/shard_map/ppermute | solution.py:450
  84.6 1.3 %collective-permute-start.4 = (f32[16,768]{1,0:T(8,128)S(1)}, f32[16,768]{1,0:T(8,128)S(1)}, u32[]{:S(2)}, u32[]{:S(2)}) collective-permute-start(f32[16,768]{1,0:T(8,128)S(1)} %get-tuple-element.32), channel_id=1, source_target_pairs={{0,1},{1,0},{2,3},{3,2},{4,5},{5,4},{6,7},{7,6},{8,9},{9,8},{10,11... | collective-permute-start | bytes 147464 | tf_op jit(solution)/shard_map/ppermute | solution.py:450
  85.9 5.6 %collective-permute-start.7 = (f32[16,768]{1,0:T(8,128)S(1)}, f32[16,768]{1,0:T(8,128)S(1)}, u32[]{:S(2)}, u32[]{:S(2)}) collective-permute-start(f32[16,768]{1,0:T(8,128)S(1)} %add.33), channel_id=1, source_target_pairs={{0,12},{4,0},{8,4},{12,8},{1,13},{5,1},{9,5},{13,9},{2,14},{6,2},{... | collective-permute-start | bytes 147464 | tf_op jit(solution)/shard_map/ppermute | solution.py:450
  89.0 5.6 %collective-permute-start.6 = (f32[16,768]{1,0:T(8,128)S(1)}, f32[16,768]{1,0:T(8,128)S(1)}, u32[]{:S(2)}, u32[]{:S(2)}) collective-permute-start(f32[16,768]{1,0:T(8,128)S(1)} %add.33), channel_id=1, source_target_pairs={{0,8},{4,12},{8,0},{12,4},{1,9},{5,13},{9,1},{13,5},{2,10},{6,14},... | collective-permute-start | bytes 147464 | tf_op jit(solution)/shard_map/ppermute | solution.py:450
  89.8 5.3 %collective-permute-start.5 = (f32[16,768]{1,0:T(8,128)S(1)}, f32[16,768]{1,0:T(8,128)S(1)}, u32[]{:S(2)}, u32[]{:S(2)}) collective-permute-start(f32[16,768]{1,0:T(8,128)S(1)} %add.33), channel_id=1, source_target_pairs={{0,4},{4,8},{8,12},{12,0},{1,5},{5,9},{9,13},{13,1},{2,6},{6,10},{... | collective-permute-start | bytes 147464 | tf_op jit(solution)/shard_map/ppermute | solution.py:450
  90.7 25.0 %collective-permute-start.15 = (bf16[384,768]{1,0:T(8,128)(2,1)}, bf16[384,768]{1,0:T(8,128)(2,1)S(1)}, u32[]{:S(2)}, u32[]{:S(2)}) collective-permute-start(bf16[384,768]{1,0:T(8,128)(2,1)} %get-tuple-element.37), channel_id=1, source_target_pairs={{0,16},{16,0},{1,17},{17,1},{2,18},{18,2},{3,19},{19,3},{4,20},{20... | collective-permute-start | bytes 1769480 | tf_op jit(solution)/shard_map/ppermute | solution.py:450
  96.1 16.0 %copy-start.3 = (bf16[768,16]{0,1:T(8,128)(2,1)S(1)}, bf16[768,16]{0,1:T(8,128)(2,1)}, u32[]{:S(2)}) copy-start(bf16[768,16]{0,1:T(8,128)(2,1)} %param.6) | copy-start | bytes 73732
  96.1 19.6 %all-to-all-start.2 = ((bf16[4,96,768]{2,1,0:T(8,128)(2,1)}), bf16[4,96,768]{2,1,0:T(8,128)(2,1)S(1)}, u32[]{:S(2)}, u32[]{:S(2)}) async-start(bf16[4,96,768]{2,1,0:T(8,128)(2,1)} %add_convert_fusion), calls=%async_computation.2 | async-start | bytes 1179648 | tf_op jit(solution)/shard_map/all_to_all | solution.py:498
  99.7 9.3 %collective-permute-start.13 = (f32[16,768]{1,0:T(8,128)S(1)}, f32[16,768]{1,0:T(8,128)S(1)}, u32[]{:S(2)}, u32[]{:S(2)}) collective-permute-start(f32[16,768]{1,0:T(8,128)S(1)} %add_add_fusion.1), channel_id=1, source_target_pairs={{0,96},{32,0},{64,32},{96,64},{1,97},{33,1},{65,33},{97,65},{2,98}... | collective-permute-start | bytes 147464 | tf_op jit(solution)/shard_map/ppermute | solution.py:450
  102.9 7.7 %collective-permute-start.12 = (f32[16,768]{1,0:T(8,128)S(1)}, f32[16,768]{1,0:T(8,128)S(1)}, u32[]{:S(2)}, u32[]{:S(2)}) collective-permute-start(f32[16,768]{1,0:T(8,128)S(1)} %add_add_fusion.1), channel_id=1, source_target_pairs={{0,64},{32,96},{64,0},{96,32},{1,65},{33,97},{65,1},{97,33},{2,66}... | collective-permute-start | bytes 147464 | tf_op jit(solution)/shard_map/ppermute | solution.py:450
  103.7 7.3 %collective-permute-start.11 = (f32[16,768]{1,0:T(8,128)S(1)}, f32[16,768]{1,0:T(8,128)S(1)}, u32[]{:S(2)}, u32[]{:S(2)}) collective-permute-start(f32[16,768]{1,0:T(8,128)S(1)} %add_add_fusion.1), channel_id=1, source_target_pairs={{0,32},{32,64},{64,96},{96,0},{1,33},{33,65},{65,97},{97,1},{2,34}... | collective-permute-start | bytes 147464 | tf_op jit(solution)/shard_map/ppermute | solution.py:450
  111.1 4.6 %collective-permute-start.14 = (f32[16,768]{1,0:T(8,128)S(1)}, f32[16,768]{1,0:T(8,128)S(1)}, u32[]{:S(2)}, u32[]{:S(2)}) collective-permute-start(f32[16,768]{1,0:T(8,128)S(1)} %add_add_fusion), channel_id=1, source_target_pairs={{0,2},{2,0},{1,3},{3,1},{4,6},{6,4},{5,7},{7,5},{8,10},{10,8},{9,1... | collective-permute-start | bytes 147464 | tf_op jit(solution)/shard_map/ppermute | solution.py:450
  115.7 5.7 %collective-permute-start.16 = (f32[16,768]{1,0:T(8,128)S(1)}, f32[16,768]{1,0:T(8,128)S(1)}, u32[]{:S(2)}, u32[]{:S(2)}) collective-permute-start(f32[16,768]{1,0:T(8,128)S(1)} %add.40), channel_id=1, source_target_pairs={{0,16},{16,0},{1,17},{17,1},{2,18},{18,2},{3,19},{19,3},{4,20},{20... | collective-permute-start | bytes 147464 | tf_op jit(solution)/shard_map/ppermute | solution.py:450
  (1 other events, 10.4 us)

commit v4 on v3

v4 whole, which is shorter than its diff:
```python
import functools

import jax
import jax.numpy as jnp
from jax import lax
from jax.experimental import pallas as pl
from jax.experimental.pallas import tpu as pltpu
from jax.sharding import Mesh, PartitionSpec as P

PATCHES = 196
GROUP = 4
XH = 2
MIB = 1024 * 1024
GELU_C = 0.7978845608028654
GELU_A = 0.044715

f32 = jnp.float32
bf16 = jnp.bfloat16


def contract(left, right, left_dim, right_dim):
    return lax.dot_general(
        left, right, (((left_dim,), (right_dim,)), ((), ())), preferred_element_type=f32
    )


def params(mib):
    return pltpu.CompilerParams(vmem_limit_bytes=mib * MIB)


def pinned(value):
    return pltpu.with_memory_space_constraint(value, pltpu.HBM)


IN_VMEM = pl.BlockSpec(memory_space=pltpu.VMEM)
IN_PLACE = pl.BlockSpec(memory_space=pltpu.HBM)


def gelu_parts(x):
    x2 = x * x
    th = jnp.tanh(GELU_C * x * (1.0 + GELU_A * x2))
    cdf = 0.5 + 0.5 * th
    slope = cdf + (0.5 * GELU_C) * x * (1.0 - th * th) * (1.0 + (3.0 * GELU_A) * x2)
    return x * cdf, slope


def lane_images(width):
    lane = lax.broadcasted_iota(jnp.int32, (1, width), 1)
    image = jnp.zeros_like(lane)
    for i in range(1, width // PATCHES):
        image = image + (lane >= i * PATCHES).astype(jnp.int32)
    return image


def per_image(values, image, reduce, start):
    width = values.shape[1]
    out = jnp.zeros_like(values)
    for i in range(GROUP):
        low = i * PATCHES // 128 * 128
        high = min(-(-(i + 1) * PATCHES // 128) * 128, width)
        part = jnp.where(image[:, low:high] == i, values[:, low:high], start)
        own = reduce(part, axis=1, keepdims=True)
        out = jnp.where(image == i, own, out)
    return out


def inverse_sum(values, axis, keepdims):
    return 1.0 / jnp.sum(values, axis=axis, keepdims=keepdims)


def per_slot_rows(weights, image):
    return jnp.concatenate(
        [jnp.where(image == i, weights, 0.0) for i in range(GROUP)], axis=0
    ).astype(bf16)


def swap_matrix(total, inner):
    outer = total // inner
    out_row = lax.broadcasted_iota(jnp.int32, (total, total), 0)
    in_row = lax.broadcasted_iota(jnp.int32, (total, total), 1)
    wanted = (out_row % outer) * inner + out_row // outer
    return (in_row == wanted).astype(f32).astype(bf16)


def block_copies(src, dst, sem):
    width = GROUP * PATCHES
    return [
        pltpu.make_async_copy(
            src.at[pl.ds(b * width, width)], dst.at[pl.ds(b * width, width)], sem.at[b]
        )
        for b in range(src.shape[0] // width)
    ]


def token_forward_body(
    rt_hbm, x_hbm, g_hbm, slots_ref, disp_hbm, comb_hbm,
    rt_ref, disp_ref, comb_ref, x_ref, g_ref, acc, x_sem, g_sem, rt_sem, disp_sem, comb_sem
):
    experts, images, double = slots_ref.shape
    feat = double // 2
    width = GROUP * PATCHES
    steps = images // GROUP
    rows = GROUP * experts
    total = experts * images

    x_copies = block_copies(x_hbm, x_ref, x_sem)
    g_copies = block_copies(g_hbm, g_ref, g_sem)
    rt_copy = pltpu.make_async_copy(rt_hbm, rt_ref, rt_sem)
    for copy in [rt_copy] + x_copies + g_copies:
        copy.start()
    weight_copies = [
        pltpu.make_async_copy(disp_ref, disp_hbm, disp_sem),
        pltpu.make_async_copy(comb_ref, comb_hbm, comb_sem),
    ]
    image = lane_images(width)
    rt_copy.wait()
    rt = rt_ref[...]
    spread = {}
    for first in range(0, steps, 2):
        pair = (first, first + 1)
        logits, own = {}, {}
        for b in pair:
            x_copies[b].wait()
        for b in pair:
            logits[b] = contract(rt, x_ref[b * width : (b + 1) * width, :], 1, 1)
        for b in pair:
            top = per_image(logits[b], image, jnp.max, -jnp.inf)
            raised = jnp.exp(logits[b] - top)
            dispatch = raised * per_image(raised, image, inverse_sum, 0.0)
            raised_e = jnp.exp(logits[b] - jnp.max(logits[b], axis=0, keepdims=True))
            combine = raised_e * inverse_sum(raised_e, axis=0, keepdims=True)
            disp_ref[b] = dispatch
            comb_ref[b] = combine
            spread[b] = per_slot_rows(combine, image)
            own[b] = per_slot_rows(dispatch, image)
        for b in pair:
            acc[b * rows : (b + 1) * rows, :feat] = jnp.dot(
                own[b], x_ref[b * width : (b + 1) * width, :], preferred_element_type=f32
            ).astype(bf16)
    for copy in weight_copies:
        copy.start()
    for b in range(steps):
        g_copies[b].wait()
    for b in range(steps):
        acc[b * rows : (b + 1) * rows, feat:] = jnp.dot(
            spread[b], g_ref[b * width : (b + 1) * width, :], preferred_element_type=f32
        ).astype(bf16)
    slots_ref[...] = (
        jnp.dot(swap_matrix(total, experts), acc[...], preferred_element_type=f32)
        .astype(bf16)
        .reshape(experts, images, double)
    )
    for copy in weight_copies:
        copy.wait()


def token_forward(tokens, rt, g_outputs):
    rows, feat = tokens.shape
    experts = rt.shape[0]
    images = rows // PATCHES
    width = GROUP * PATCHES
    steps = rows // width
    return pl.pallas_call(
        token_forward_body,
        in_specs=[IN_PLACE] * 3,
        out_specs=[IN_VMEM, IN_PLACE, IN_PLACE],
        out_shape=[
            jax.ShapeDtypeStruct((experts, images, 2 * feat), bf16),
            pltpu.HBM((steps, experts, width), f32),
            pltpu.HBM((steps, experts, width), f32),
        ],
        scratch_shapes=[
            pltpu.VMEM((experts, feat), bf16),
            pltpu.VMEM((steps, experts, width), f32),
            pltpu.VMEM((steps, experts, width), f32),
            pltpu.VMEM((rows, feat), bf16),
            pltpu.VMEM((rows, feat), bf16),
            pltpu.VMEM((experts * images, 2 * feat), bf16),
            pltpu.SemaphoreType.DMA((steps,)),
            pltpu.SemaphoreType.DMA((steps,)),
            pltpu.SemaphoreType.DMA(()),
            pltpu.SemaphoreType.DMA(()),
            pltpu.SemaphoreType.DMA(()),
        ],
        compiler_params=params(20),
        name="token_forward",
    )(pinned(rt), pinned(tokens), pinned(g_outputs))


def hidden_terms(rows, grads, w1, w2):
    act, slope = gelu_parts(jnp.dot(rows, w1, preferred_element_type=f32))
    return act.astype(bf16), (contract(grads, w2, 1, 1) * slope).astype(bf16)


def expert_body(
    rows_ref, w1_ref, w2_ref, out_hbm, act_hbm, pre_hbm, out_ref, act_ref, pre_ref, sem
):
    feat = w1_ref.shape[1]
    hidden = w1_ref.shape[2]
    tile = act_ref.shape[1]
    part_at = lax.axis_index("y")
    rows = rows_ref[:, :feat]
    grads = rows_ref[:, feat:]
    made, back = None, None
    stores = [
        pltpu.make_async_copy(src, dst, sem.at[k])
        for k, (src, dst) in enumerate(
            ((act_ref, act_hbm), (pre_ref, pre_hbm), (out_ref, out_hbm))
        )
    ]
    for i in range(hidden // tile):
        w1 = w1_ref[0, :, i * tile : (i + 1) * tile]
        w2 = w2_ref[0, i * tile : (i + 1) * tile, :]
        act, grad_pre = hidden_terms(rows, grads, w1, w2)

        @pl.when(part_at == i)
        def _():
            act_ref[...] = act
            pre_ref[...] = grad_pre

        if i == hidden // tile - 1:
            stores[0].start()
            stores[1].start()
        part = jnp.dot(act, w2, preferred_element_type=f32)
        made = part if made is None else made + part
        part = contract(grad_pre, w1, 1, 1)
        back = part if back is None else back + part
    out_ref[:, :feat] = made.astype(bf16)
    out_ref[:, feat:] = back.astype(bf16)
    stores[2].start()
    for store in stores:
        store.wait()


def expert_rows(rows, w_in, w_out, parts):
    tile = w_in.shape[2] // parts
    shapes = [rows.shape, (rows.shape[0], tile), (rows.shape[0], tile)]
    return pl.pallas_call(
        expert_body,
        in_specs=[IN_VMEM] * 3,
        out_specs=[IN_PLACE] * 3,
        out_shape=[pltpu.HBM(shape, bf16) for shape in shapes],
        scratch_shapes=[pltpu.VMEM(shape, bf16) for shape in shapes]
        + [pltpu.SemaphoreType.DMA((3,))],
        compiler_params=params(12),
        name="expert_rows",
    )(rows, w_in, w_out)


def slice_copies(w1_hbm, w2_hbm, w1, w2, sem):
    tile = w1.shape[1]
    low = pl.multiple_of(lax.axis_index("y") * tile, tile)
    return (
        pltpu.make_async_copy(w1_hbm.at[0, :, pl.ds(low, tile)], w1, sem.at[0]),
        pltpu.make_async_copy(w2_hbm.at[0, pl.ds(low, tile), :], w2, sem.at[1]),
    )


def stacked_copies(sources, out, sem):
    copies, at = [], 0
    for k, source in enumerate(sources):
        rows = source.shape[0]
        copies.append(pltpu.make_async_copy(source, out.at[pl.ds(at, rows)], sem.at[k]))
        at += rows
    return copies


def join(pieces, low, high, out):
    at = 0
    for piece in pieces:
        out[at : at + piece.shape[0], :] = piece[:, low:high]
        at += piece.shape[0]


def near_terms_body(
    right_ref, left_ref, w1_hbm, w2_hbm, act_hbm, pre_hbm, act, pre, both, w1, w2, sem, out_sem
):
    feat = w1.shape[0]
    loads = slice_copies(w1_hbm, w2_hbm, w1, w2, sem)
    for load in loads:
        load.start()
    join((right_ref, left_ref), 0, 2 * feat, both)
    for load in loads:
        load.wait()
    act[...], pre[...] = hidden_terms(both[:, :feat], both[:, feat:], w1[...], w2[...])
    stores = (
        pltpu.make_async_copy(act, act_hbm, out_sem.at[0]),
        pltpu.make_async_copy(pre, pre_hbm, out_sem.at[1]),
    )
    for store in stores:
        store.start()
    for store in stores:
        store.wait()


def near_terms(right, left, w_in, w_out, parts):
    feat, hidden = w_in.shape[1:]
    tile = hidden // parts
    count = right.shape[0] + left.shape[0]
    return pl.pallas_call(
        near_terms_body,
        in_specs=[IN_VMEM] * 2 + [IN_PLACE] * 2,
        out_specs=[IN_PLACE] * 2,
        out_shape=[pltpu.HBM((count, tile), bf16)] * 2,
        scratch_shapes=[
            pltpu.VMEM((count, tile), bf16),
            pltpu.VMEM((count, tile), bf16),
            pltpu.VMEM((count, 2 * feat), bf16),
            pltpu.VMEM((feat, tile), bf16),
            pltpu.VMEM((tile, feat), bf16),
            pltpu.SemaphoreType.DMA((2,)),
            pltpu.SemaphoreType.DMA((2,)),
        ],
        compiler_params=params(16),
        name="near_terms",
    )(right, left, pinned(w_in), pinned(w_out))


def first_grads_body(
    own_ref, right_ref, left_ref, far_a, far_b, pre_own, pre_near, w1_hbm, w2_hbm,
    keep_ref, send_ref, act_far, rows, pre, far, acc, w1, w2, sem, pre_sem
):
    feat = w1.shape[0]
    xh = lax.axis_index("xh")
    loads = slice_copies(w1_hbm, w2_hbm, w1, w2, sem)
    terms = stacked_copies((pre_own, pre_near), pre, pre_sem)
    for load in terms + list(loads):
        load.start()
    join((own_ref, right_ref, left_ref), 0, feat, rows)
    join((far_a, far_b), 0, 2 * feat, far)
    for load in terms:
        load.wait()
    total = contract(rows[...], pre[...], 0, 0)
    for load in loads:
        load.wait()
    act, pre_far = hidden_terms(far[:, :feat], far[:, feat:], w1[...], w2[...])
    act_far[...] = act
    acc[...] = (total + contract(far[:, :feat], pre_far, 0, 0)).reshape(acc.shape)
    send_ref[...] = acc[:, pl.ds(1 - xh, 1)].reshape(send_ref.shape).astype(bf16)
    keep_ref[...] = acc[:, pl.ds(xh, 1)].reshape(keep_ref.shape)


def first_grads(pieces, pre_own, pre_near, w_in, w_out, parts):
    feat, hidden = w_in.shape[1:]
    tile = hidden // parts
    own = feat // (parts * XH)
    near_count = sum(p.shape[0] for p in pieces[:3])
    far_count = sum(p.shape[0] for p in pieces[3:])
    return pl.pallas_call(
        first_grads_body,
        in_specs=[IN_VMEM] * 5 + [IN_PLACE] * 4,
        out_specs=[IN_VMEM] * 3,
        out_shape=[
            jax.ShapeDtypeStruct((parts, own, tile), f32),
            jax.ShapeDtypeStruct((parts, own, tile), bf16),
            jax.ShapeDtypeStruct((far_count, tile), bf16),
        ],
        scratch_shapes=[
            pltpu.VMEM((near_count, feat), bf16),
            pltpu.VMEM((near_count, tile), bf16),
            pltpu.VMEM((far_count, 2 * feat), bf16),
            pltpu.VMEM((parts, XH, own, tile), f32),
            pltpu.VMEM((feat, tile), bf16),
            pltpu.VMEM((tile, feat), bf16),
            pltpu.SemaphoreType.DMA((2,)),
            pltpu.SemaphoreType.DMA((2,)),
        ],
        compiler_params=params(20),
        name="first_grads",
    )(*pieces, pinned(pre_own), pinned(pre_near), pinned(w_in), pinned(w_out))


def second_grads_body(
    own_ref, right_ref, left_ref, far_a, far_b, act_own, act_near, act_far,
    keep_ref, send_ref, grads, act, sem
):
    feat = grads.shape[1]
    tile = keep_ref.shape[0]
    xh = lax.axis_index("xh")
    terms = stacked_copies((act_own, act_near), act, sem)
    for load in terms:
        load.start()
    join((own_ref, right_ref, left_ref, far_a, far_b), feat, 2 * feat, grads)
    act[act.shape[0] - act_far.shape[0] :, :] = act_far[...]
    for load in terms:
        load.wait()

    def rows_of(part):
        low = pl.multiple_of(part * tile, tile)
        return contract(act[:, pl.ds(low, tile)], grads[...], 0, 0)

    send_ref[...] = rows_of(1 - xh).astype(bf16)
    keep_ref[...] = rows_of(xh)


def second_grads(pieces, acts):
    feat = pieces[0].shape[1] // 2
    count = sum(p.shape[0] for p in pieces)
    width = acts[0].shape[1]
    tile = width // XH
    return pl.pallas_call(
        second_grads_body,
        in_specs=[IN_VMEM] * 5 + [IN_PLACE] * 2 + [IN_VMEM],
        out_specs=[IN_VMEM] * 2,
        out_shape=[
            jax.ShapeDtypeStruct((tile, feat), f32),
            jax.ShapeDtypeStruct((tile, feat), bf16),
        ],
        scratch_shapes=[
            pltpu.VMEM((count, feat), bf16),
            pltpu.VMEM((count, width), bf16),
            pltpu.SemaphoreType.DMA((2,)),
        ],
        compiler_params=params(12),
        name="second_grads",
    )(*pieces, pinned(acts[0]), pinned(acts[1]), acts[2])


def widen_body(in_ref, out_ref):
    parts, _, tile = in_ref.shape
    for i in range(parts):
        out_ref[0, :, i * tile : (i + 1) * tile] = in_ref[i].astype(f32)


def widen(spread):
    parts, own, tile = spread.shape
    return pl.pallas_call(
        widen_body,
        in_specs=[IN_VMEM],
        out_specs=IN_VMEM,
        out_shape=jax.ShapeDtypeStruct((1, own, parts * tile), f32),
        compiler_params=params(4),
        name="widen",
    )(spread)


def token_logits_body(
    back_ref, x_hbm, g_hbm, disp_hbm, comb_hbm, gl_ref, slots_ref, router_ref,
    mix, disp_ref, comb_ref, x_ref, g_ref, x_sem, g_sem, weight_sem
):
    experts, images, double = back_ref.shape
    feat = double // 2
    width = GROUP * PATCHES
    rows = GROUP * experts
    total = experts * images
    x_copies = block_copies(x_hbm, x_ref, x_sem)
    g_copies = block_copies(g_hbm, g_ref, g_sem)
    for x_copy, g_copy in zip(x_copies, g_copies):
        g_copy.start()
        x_copy.start()
    weight_copies = [
        pltpu.make_async_copy(disp_hbm, disp_ref, weight_sem.at[0]),
        pltpu.make_async_copy(comb_hbm, comb_ref, weight_sem.at[1]),
    ]
    for copy in weight_copies:
        copy.start()
    mix[...] = jnp.dot(
        swap_matrix(total, images),
        back_ref[...].reshape(total, double),
        preferred_element_type=f32,
    ).astype(bf16)
    image = lane_images(width)

    def picked(both):
        out = both[:experts]
        for i in range(1, GROUP):
            out = jnp.where(image == i, both[i * experts : (i + 1) * experts], out)
        return out

    for copy in weight_copies:
        copy.wait()
    router_sum = None
    for first in range(0, images // GROUP, 2):
        pair = (first, first + 1)
        grad_comb, grad_disp, grad_logits = {}, {}, {}
        for b in pair:
            g_copies[b].wait()
            x_copies[b].wait()
        for b in pair:
            block = mix[b * rows : (b + 1) * rows, :]
            slots_ref[b] = block[:, feat:]
            g = g_ref[b * width : (b + 1) * width, :]
            grad_comb[b] = picked(contract(block[:, :feat], g, 1, 1))
            x = x_ref[b * width : (b + 1) * width, :]
            grad_disp[b] = picked(contract(block[:, feat:], x, 1, 1))
        for b in pair:
            both = comb_ref[b] * grad_comb[b]
            comb_part = both - comb_ref[b] * jnp.sum(both, axis=0, keepdims=True)
            both = disp_ref[b] * grad_disp[b]
            disp_part = both - disp_ref[b] * per_image(both, image, jnp.sum, 0.0)
            grad_logits[b] = (comb_part + disp_part).astype(bf16)
            gl_ref[b] = grad_logits[b]
        for b in pair:
            part = jnp.dot(
                grad_logits[b], x_ref[b * width : (b + 1) * width, :], preferred_element_type=f32
            )
            router_sum = part if router_sum is None else router_sum + part
    router_ref[...] = router_sum


def token_logits(back, tokens, g_outputs, dispatch, combine):
    experts, images, double = back.shape
    rows, feat = tokens.shape
    steps, _, width = dispatch.shape
    return pl.pallas_call(
        token_logits_body,
        in_specs=[IN_VMEM] + [IN_PLACE] * 4,
        out_specs=[IN_VMEM] * 3,
        out_shape=[
            jax.ShapeDtypeStruct((steps, experts, width), bf16),
            jax.ShapeDtypeStruct((steps, GROUP * experts, feat), bf16),
            jax.ShapeDtypeStruct((experts, feat), f32),
        ],
        scratch_shapes=[
            pltpu.VMEM((experts * images, double), bf16),
            pltpu.VMEM(dispatch.shape, f32),
            pltpu.VMEM(combine.shape, f32),
            pltpu.VMEM((rows, feat), bf16),
            pltpu.VMEM((rows, feat), bf16),
            pltpu.SemaphoreType.DMA((steps,)),
            pltpu.SemaphoreType.DMA((steps,)),
            pltpu.SemaphoreType.DMA((2,)),
        ],
        compiler_params=params(20),
        name="token_logits",
    )(back, *[pinned(v) for v in (tokens, g_outputs, dispatch, combine)])


def token_grads_body(gl_ref, slots_ref, disp_ref, rt_ref, out_ref):
    image = lane_images(gl_ref.shape[2])
    left = jnp.concatenate([per_slot_rows(disp_ref[0], image), gl_ref[0]], axis=0)
    right = jnp.concatenate([slots_ref[0], rt_ref[...]], axis=0)
    out_ref[...] = contract(left, right, 0, 0).astype(bf16)


def token_grads(grad_logits, slots, dispatch, rt):
    steps, experts, width = grad_logits.shape
    feat = slots.shape[2]
    return pl.pallas_call(
        token_grads_body,
        grid=(steps,),
        in_specs=[
            pl.BlockSpec((1, experts, width), lambda i: (i, 0, 0)),
            pl.BlockSpec((1, GROUP * experts, feat), lambda i: (i, 0, 0)),
            pl.BlockSpec((1, experts, width), lambda i: (i, 0, 0)),
            pl.BlockSpec((experts, feat), lambda i: (0, 0)),
        ],
        out_specs=pl.BlockSpec((width, feat), lambda i: (i, 0)),
        out_shape=jax.ShapeDtypeStruct((steps * width, feat), bf16),
        compiler_params=params(12),
        name="token_grads",
    )(grad_logits, slots, dispatch, rt)


def shift(value, axis, by, count):
    return lax.ppermute(value, axis, [(i, (i + by) % count) for i in range(count)])


def axis_sum(value, axis, count):
    return sum([shift(value, axis, by, count) for by in range(1, count)], value)


def solution(mesh):
    dp, experts = mesh.shape["dp"], mesh.shape["expert"]
    ny, nz = dp // XH, experts // 4
    fine = Mesh(
        mesh.devices.reshape(ny, XH, nz, 2, 2), ("y", "xh", "z", "xl", "core")
    )
    dp_axes = ("y", "xh")
    ex_axes = ("z", "xl", "core")

    def over_experts(value):
        return lax.all_to_all(value, ex_axes, split_axis=0, concat_axis=0, tiled=True)

    def on_device(tokens, router, w_in, w_out, g_outputs):
        rt = router.T
        slots, dispatch, combine = token_forward(tokens, rt, g_outputs)
        rows = over_experts(slots).reshape(-1, slots.shape[2])
        mid = rows.shape[0] // 2
        right = shift(rows, "y", 1, ny)
        left = shift(rows, "y", ny - 1, ny)
        results, act_own, pre_own = expert_rows(rows, w_in, w_out, ny)
        back = over_experts(results.reshape(slots.shape))
        far_a = shift(right[:mid], "y", 1, ny)
        far_b = shift(left[mid:], "y", ny - 1, ny)
        act_near, pre_near = near_terms(right, left, w_in, w_out, ny)
        back, act_near, pre_near = lax.optimization_barrier((back, act_near, pre_near))
        grad_logits, slot_grads, router_term = token_logits(
            back, tokens, g_outputs, dispatch, combine
        )
        pieces = (rows, right, left, far_a, far_b)
        keep_in, send_in, act_far = first_grads(pieces, pre_own, pre_near, w_in, w_out, ny)
        keep_out, send_out = second_grads(pieces, (act_own, act_near, act_far))
        came_in = shift(send_in, "xh", 1, XH)
        came_out = shift(send_out, "xh", 1, XH)
        total = axis_sum(router_term, ("xh", "xl"), 2 * XH)
        total, keep_out = lax.optimization_barrier((total, keep_out))
        total = axis_sum(axis_sum(total, "core", 2), "y", ny)
        total, came_in = lax.optimization_barrier((total, came_in))
        part_in = (keep_in + came_in.astype(f32)).astype(bf16)
        spread = lax.all_to_all(part_in, "y", split_axis=0, concat_axis=0, tiled=True)
        grad_router = axis_sum(total, "z", nz).T
        grad_second = keep_out + came_out.astype(f32)
        grad_first = widen(spread)
        grad_tok = token_grads(grad_logits, slot_grads, dispatch, rt)
        return grad_tok, grad_router, grad_first, grad_second[None]

    return jax.shard_map(
        on_device,
        mesh=fine,
        in_specs=(
            P(dp_axes + ex_axes, None),
            P(),
            P(ex_axes, None, None),
            P(ex_axes, None, None),
            P(dp_axes + ex_axes, None),
        ),
        out_specs=(
            P(dp_axes + ex_axes, None),
            P(),
            P(ex_axes, dp_axes, None),
            P(ex_axes, dp_axes, None),
        ),
        check_vma=False,
    )
```

time: 122 us -> 110 us (0.902)
  waiting for transfers between devices: 22.6 us -> 14.8 us
  Pallas kernels: 42.7 us -> 39.4 us
  starting transfers between devices: 32.2 us -> 30.1 us
    ppermute x17 -> x16, waiting for transfers between devices: 22.6 us -> 9.16 us  [shift(): lax.ppermute(value, axis, [(i, (i + by) % count) for i in range(count)])]
    all_to_all x1, waiting for transfers between devices: 0.01 us -> 5.59 us  [on_device(): lax.all_to_all(part_in, 'y', split_axis=0, concat_axis=0, tiled=True)]
    ppermute x17 -> x16, starting transfers between devices: 25 us -> 21.8 us  [shift(): lax.ppermute(value, axis, [(i, (i + by) % count) for i in range(count)])]
    pallas_call x1, Pallas kernels: 9.28 us -> 7.11 us  [token_forward(): pl.pallas_call(token_forward_body, in_specs=[IN_PLACE] * 3, out_specs=[IN...]
    pallas_call x4 -> x5, Pallas kernels: 28.7 us -> 27.6 us  [the longest x1 7.12 us: expert_rows(): pl.pallas_call(expert_body, in_specs=[IN_VMEM] * 3, out_specs=[IN_PLACE]...]
  transfers between devices with their start and end apart: 19 -> 18, of which waited for: 9 -> 6; matrix products, arithmetic and copies ran while one was open for 2% -> 4% of each run, Pallas kernels for 21% -> 29%
where the time goes in v4:
time: 110 us; the launch traced here: 109 us
  Pallas kernels  39.4 us (36%)
  starting transfers between devices  30.1 us (27%)
  blocking collectives  19.9 us (18%)
  waiting for transfers between devices  14.8 us (13%)
  other arithmetic  2.71 us (2%)
  local copies, waits for them, and re-layouts  1.58 us (1%)
    ppermute x16, starting transfers between devices, shift(): lax.ppermute(value, axis, [(i, (i + by) % count) for i in range(count)])  21.8 us
    all_to_all x1, blocking collectives, over_experts(): lax.all_to_all(value, ex_axes, split_axis=0, concat_axis=0, tiled=True)  19.9 us
    ppermute x16, waiting for transfers between devices, shift(): lax.ppermute(value, axis, [(i, (i + by) % count) for i in range(count)])  9.16 us
    pallas_call x1, Pallas kernels, expert_rows(): pl.pallas_call(expert_body, in_specs=[IN_VMEM] * 3, out_specs=[IN_PLACE]...  7.12 us
    pallas_call x1, Pallas kernels, token_forward(): pl.pallas_call(token_forward_body, in_specs=[IN_PLACE] * 3, out_specs=[IN...  7.11 us
    pallas_call x1, Pallas kernels, token_logits(): pl.pallas_call(token_logits_body, in_specs=[IN_VMEM] + [IN_PLACE] * 4, ou...  6.68 us
    pallas_call x1, Pallas kernels, first_grads(): pl.pallas_call(first_grads_body, in_specs=[IN_VMEM] * 5 + [IN_PLACE] * 4,...  5.75 us
    all_to_all x1, waiting for transfers between devices, on_device(): lax.all_to_all(part_in, 'y', split_axis=0, concat_axis=0, tiled=True)  5.59 us
  transfers between devices with their start and end apart: 18, of which 6 were waited for; matrix products, arithmetic and copies ran while one was open for 4% of the time, Pallas kernels for 29%

profile of v4, /device:TPU:0, one launch (start us, length us, event | category | flops | bytes accessed | tf_op | source)
XLA Modules:
  0.0 109.2 jit_solution(9207598286621630114)
XLA Ops:
  0.7 7.1 %token_forward.1 = (bf16[16,16,1536]{2,1,0:T(8,128)(2,1)S(1)}, f32[4,16,784]{2,1,0:T(8,128)}, f32[4,16,784]{2,1,0:T(8,128)}) custom-call(bf16[16,768]{1,0:T(8,128)(2,1)} %bitcast.14, bf16[3136,768]{1,0:T(8,128)(2,1)} %x_hbm.3, bf16[3136,768]{1,0:T(8,128)(2,1)} %g_hbm.3), custom_call_target="tpu_custom_call" | custom-call | tf_op jit(solution)/shard_map/token_forward/pallas_call | solution.py:163
  7.8 19.9 %all_to_all.15 = bf16[16,16,1536]{2,1,0:T(8,128)(2,1)S(1)} all-to-all(bf16[16,16,1536]{2,1,0:T(8,128)(2,1)S(1)} %get-tuple-element.27), channel_id=1, replica_groups=mesh['y'=4,'xh'=2,'z'=4,'xl'=2,'core'=2] {'z','xl','core'}, dimensions={0} | all-to-all | bytes 1572864 | tf_op jit(solution)/shard_map/all_to_all | solution.py:573
  27.7 3.0 %collective-permute-start.1 = (bf16[256,1536]{1,0:T(8,128)(2,1)S(1)}, bf16[256,1536]{1,0:T(8,128)(2,1)S(1)}, u32[]{:S(2)}, u32[]{:S(2)}) collective-permute-start(bf16[256,1536]{1,0:T(8,128)(2,1)S(1)} %bitcast.9), channel_id=1, source_target_pairs={{0,96},{32,0},{64,32},{96,64},{1,97},{33,1},{65,33},{97,65},{2,98}... | collective-permute-start | bytes 2359304 | tf_op jit(solution)/shard_map/ppermute | solution.py:556
  30.7 7.1 %expert_rows.1 = (bf16[256,1536]{1,0:T(8,128)(2,1)}, bf16[256,768]{1,0:T(8,128)(2,1)}, bf16[256,768]{1,0:T(8,128)(2,1)}) custom-call(bf16[256,1536]{1,0:T(8,128)(2,1)S(1)} %bitcast.11, bf16[1,768,3072]{2,1,0:T(8,128)(2,1)S(1)} %bitcast.8, bf16[1,3072,768]{2,1,0:T(8,128)(2,1)S(1)} %copy-done), custom_call_target="tpu_custom_call" | custom-call | tf_op jit(solution)/shard_map/expert_rows/pallas_call | solution.py:238
  37.9 3.6 %all-to-all-start.1 = ((bf16[16,16,1536]{2,1,0:T(8,128)(2,1)}), bf16[16,16,1536]{2,1,0:T(8,128)(2,1)S(1)}, u32[]{:S(2)}, u32[]{:S(2)}) async-start(bf16[16,16,1536]{2,1,0:T(8,128)(2,1)} %bitcast.16), calls=%async_computation.1 | async-start | bytes 1572864 | tf_op jit(solution)/shard_map/all_to_all | solution.py:573
  41.5 5.7 %collective-permute-done.1.left_ref = bf16[256,1536]{1,0:T(8,128)(2,1)S(1)} collective-permute-done((bf16[256,1536]{1,0:T(8,128)(2,1)S(1)}, bf16[256,1536]{1,0:T(8,128)(2,1)S(1)}, u32[]{:S(2)}, u32[]{:S(2)}) %collective-permute-start.1) | collective-permute-done | bytes 786464 | tf_op jit(solution)/shard_map/ppermute | solution.py:556
  48.0 3.7 %collective-permute-start.6 = (bf16[128,1536]{1,0:T(8,128)(2,1)}, bf16[128,1536]{1,0:T(8,128)(2,1)S(1)}, u32[]{:S(2)}, u32[]{:S(2)}) collective-permute-start(bf16[128,1536]{1,0:T(8,128)(2,1)} %slice.9), channel_id=1, source_target_pairs={{0,96},{32,0},{64,32},{96,64},{1,97},{33,1},{65,33},{97,65},{2,98}... | collective-permute-start | bytes 1179656 | tf_op jit(solution)/shard_map/ppermute | solution.py:556
  52.4 4.3 %near_terms.1 = (bf16[512,768]{1,0:T(8,128)(2,1)}, bf16[512,768]{1,0:T(8,128)(2,1)}) custom-call(bf16[256,1536]{1,0:T(8,128)(2,1)S(1)} %collective-permute-done.right_ref, bf16[256,1536]{1,0:T(8,128)(2,1)S(1)} %collective-permute-done.1.left_ref, bf16[1,768,3072]{2,1,0:T(8,128)(2,1)} %w1_hbm.3, bf16[1,3072,768]{2,1,0:T(8,128)(2,1)} %w2_hbm.3), custom_call_target="tpu_custom_call" | custom-call | tf_op jit(solution)/shard_map/near_terms/pallas_call | solution.py:300
  56.7 6.7 %token_logits.1 = (bf16[4,16,784]{2,1,0:T(8,128)(2,1)S(1)}, bf16[4,64,768]{2,1,0:T(8,128)(2,1)S(1)}, f32[16,768]{1,0:T(8,128)S(1)}) custom-call(bf16[16,16,1536]{2,1,0:T(8,128)(2,1)S(1)} %all-to-all-done.1.back_ref, bf16[3136,768]{1,0:T(8,128)(2,1)} %x_hbm.3, bf16[3136,768]{1,0:T(8,128)(2,1)} %g_hbm.3, f32[4,16,784]{2,1,0:T(8,128)} %get-tuple-element.32.disp_hbm.disp_ref, ...), custom_call_target="tpu_custom_call" | custom-call | tf_op jit(solution)/shard_map/token_logits/pallas_call | solution.py:505
  63.4 2.7 %collective-permute-start.4 = (f32[16,768]{1,0:T(8,128)S(1)}, f32[16,768]{1,0:T(8,128)S(1)}, u32[]{:S(2)}, u32[]{:S(2)}) collective-permute-start(f32[16,768]{1,0:T(8,128)S(1)} %get-tuple-element.36), channel_id=1, source_target_pairs={{0,18},{2,0},{16,2},{18,16},{1,19},{3,1},{17,3},{19,17},{4,22},{6,... | collective-permute-start | bytes 147464 | tf_op jit(solution)/shard_map/ppermute | solution.py:556
  67.7 5.7 %first_grads.1 = (f32[4,96,768]{2,1,0:T(8,128)S(1)}, bf16[4,96,768]{2,1,0:T(8,128)(2,1)S(1)}, bf16[256,768]{1,0:T(8,128)(2,1)S(1)}) custom-call(bf16[256,1536]{1,0:T(8,128)(2,1)S(1)} %bitcast.12, bf16[256,1536]{1,0:T(8,128)(2,1)S(1)} %collective-permute-done.right_ref, bf16[256,1536]{1,0:T(8,128)(2,1)S(1)} %collective-permute-done.1.left_ref, ...), custom_call_target="tpu_custom_call" | custom-call | tf_op jit(solution)/shard_map/first_grads/pallas_call | solution.py:349
  73.4 2.1 %collective-permute-start.11 = (bf16[4,96,768]{2,1,0:T(8,128)(2,1)S(1)}, bf16[4,96,768]{2,1,0:T(8,128)(2,1)S(1)}, u32[]{:S(2)}, u32[]{:S(2)}) collective-permute-start(bf16[4,96,768]{2,1,0:T(8,128)(2,1)S(1)} %get-tuple-element.44), channel_id=1, source_target_pairs={{0,16},{16,0},{1,17},{17,1},{2,18},{18,2},{3,19},{19,3},{4,20},{20... | collective-permute-start | bytes 1769480 | tf_op jit(solution)/shard_map/ppermute | solution.py:556
  75.6 3.7 %second_grads.1 = (f32[384,768]{1,0:T(8,128)S(1)}, bf16[384,768]{1,0:T(8,128)(2,1)S(1)}) custom-call(bf16[256,1536]{1,0:T(8,128)(2,1)S(1)} %bitcast.13, bf16[256,1536]{1,0:T(8,128)(2,1)S(1)} %collective-permute-done.right_ref, bf16[256,1536]{1,0:T(8,128)(2,1)S(1)} %collective-permute-done.1.left_ref, bf16[128,1536]{1,0:T(8,128)(2,1)} %collective-permute-done.5.far_a, ...), custom_call_target="tpu_custom_call" | custom-call | tf_op jit(solution)/shard_map/second_grads/pallas_call | solution.py:401
  79.5 1.6 %collective-permute-start.15 = (bf16[384,768]{1,0:T(8,128)(2,1)S(1)}, bf16[384,768]{1,0:T(8,128)(2,1)S(1)}, u32[]{:S(2)}, u32[]{:S(2)}) collective-permute-start(bf16[384,768]{1,0:T(8,128)(2,1)S(1)} %get-tuple-element.49), channel_id=1, source_target_pairs={{0,16},{16,0},{1,17},{17,1},{2,18},{18,2},{3,19},{19,3},{4,20},{20... | collective-permute-start | bytes 1769480 | tf_op jit(solution)/shard_map/ppermute | solution.py:556
  81.0 3.3 %collective-permute-start.10 = (f32[16,768]{1,0:T(8,128)S(1)}, f32[16,768]{1,0:T(8,128)S(1)}, u32[]{:S(2)}, u32[]{:S(2)}) collective-permute-start(f32[16,768]{1,0:T(8,128)S(1)} %add.39), channel_id=1, source_target_pairs={{0,96},{32,0},{64,32},{96,64},{1,97},{33,1},{65,33},{97,65},{2,98}... | collective-permute-start | bytes 147464 | tf_op jit(solution)/shard_map/ppermute | solution.py:556
  85.3 3.6 %token_grads.1 = bf16[3136,768]{1,0:T(8,128)(2,1)} custom-call(bf16[4,16,784]{2,1,0:T(8,128)(2,1)S(1)} %get-tuple-element.34.gl_ref, bf16[4,64,768]{2,1,0:T(8,128)(2,1)S(1)} %get-tuple-element.35.slots_ref, f32[4,16,784]{2,1,0:T(8,128)S(1)} %copy-done.3, bf16[16,768]{1,0:T(8,128)(2,1)S(1)} %bitcast.15), custom_call_target="tpu_custom_call" | custom-call | tf_op jit(solution)/shard_map/token_grads/pallas_call | solution.py:539
  90.2 1.1 collective-permute-done.11
  91.3 1.2 %collective-permute-start.14 = (f32[16,768]{1,0:T(8,128)S(1)}, f32[16,768]{1,0:T(8,128)S(1)}, u32[]{:S(2)}, u32[]{:S(2)}) collective-permute-start(f32[16,768]{1,0:T(8,128)S(1)} %add_add_fusion), channel_id=1, source_target_pairs={{0,12},{4,0},{8,4},{12,8},{1,13},{5,1},{9,5},{13,9},{2,14},{6,2},{... | collective-permute-start | bytes 147464 | tf_op jit(solution)/shard_map/ppermute | solution.py:556
  92.4 1.5 %collective-permute-start.13 = (f32[16,768]{1,0:T(8,128)S(1)}, f32[16,768]{1,0:T(8,128)S(1)}, u32[]{:S(2)}, u32[]{:S(2)}) collective-permute-start(f32[16,768]{1,0:T(8,128)S(1)} %add_add_fusion), channel_id=1, source_target_pairs={{0,8},{4,12},{8,0},{12,4},{1,9},{5,13},{9,1},{13,5},{2,10},{6,14},... | collective-permute-start | bytes 147464 | tf_op jit(solution)/shard_map/ppermute | solution.py:556
  95.1 4.6 %all-to-all-start.2 = ((bf16[4,96,768]{2,1,0:T(8,128)(2,1)}), bf16[4,96,768]{2,1,0:T(8,128)(2,1)S(1)}, u32[]{:S(2)}, u32[]{:S(2)}) async-start(bf16[4,96,768]{2,1,0:T(8,128)(2,1)} %add_convert_fusion), calls=%async_computation.2 | async-start | bytes 1179648 | tf_op jit(solution)/shard_map/all_to_all | solution.py:601
  99.7 1.1 collective-permute-done.15
  100.8 1.1 %add_bitcast_fusion = f32[1,384,768]{2,1,0:T(8,128)} fusion(f32[384,768]{1,0:T(8,128)S(1)} %copy-done.2, bf16[384,768]{1,0:T(8,128)(2,1)S(1)} %collective-permute-done.15), kind=kLoop, calls=%fused_computation | loop fusion | flops 589824 | bytes 2949120 | tf_op jit(solution)/shard_map/broadcast_in_dim | solution.py:606
  102.5 5.6 %all-to-all-done.2.in_ref = bf16[4,96,768]{2,1,0:T(8,128)(2,1)S(1)} async-done(((bf16[4,96,768]{2,1,0:T(8,128)(2,1)}), bf16[4,96,768]{2,1,0:T(8,128)(2,1)S(1)}, u32[]{:S(2)}, u32[]{:S(2)}) %all-to-all-start.2) | async-done | bytes 589856 | tf_op jit(solution)/shard_map/all_to_all | solution.py:601
  108.1 1.1 widen.1
  (44 shorter events, 7.2 us)
Async XLA Ops:
  0.6 30.1 %slice-start = ((s8[4718592]{0:T(1024)(128)(4,1)}), s8[4194304]{0:T(1024)(128)(4,1)S(1)}, s32[]{:S(2)}) async-start(s8[4718592]{0:T(1024)(128)(4,1)} %bitcast.7), calls=%async_computation.3 | async-start | bytes 8388608
  0.6 30.1 %slice-start.1 = ((s8[4718592]{0:T(1024)(128)(4,1)}), s8[524288]{0:T(1024)(128)(4,1)S(1)}, s32[]{:S(2)}) async-start(s8[4718592]{0:T(1024)(128)(4,1)} %bitcast.7), calls=%async_computation.4 | async-start | bytes 1048576
  0.7 30.1 %copy-start = (bf16[1,3072,768]{2,1,0:T(8,128)(2,1)S(1)}, bf16[1,3072,768]{2,1,0:T(8,128)(2,1)}, u32[]{:S(2)}) copy-start(bf16[1,3072,768]{2,1,0:T(8,128)(2,1)} %w2_hbm.3) | copy-start | bytes 14155780
  27.7 19.5 %collective-permute-start.1 = (bf16[256,1536]{1,0:T(8,128)(2,1)S(1)}, bf16[256,1536]{1,0:T(8,128)(2,1)S(1)}, u32[]{:S(2)}, u32[]{:S(2)}) collective-permute-start(bf16[256,1536]{1,0:T(8,128)(2,1)S(1)} %bitcast.9), channel_id=1, source_target_pairs={{0,96},{32,0},{64,32},{96,64},{1,97},{33,1},{65,33},{97,65},{2,98}... | collective-permute-start | bytes 2359304 | tf_op jit(solution)/shard_map/ppermute | solution.py:556
  30.7 21.0 %collective-permute-start = (bf16[256,1536]{1,0:T(8,128)(2,1)S(1)}, bf16[256,1536]{1,0:T(8,128)(2,1)S(1)}, u32[]{:S(2)}, u32[]{:S(2)}) collective-permute-start(bf16[256,1536]{1,0:T(8,128)(2,1)S(1)} %bitcast.10), channel_id=1, source_target_pairs={{0,32},{32,64},{64,96},{96,0},{1,33},{33,65},{65,97},{97,1},{2,34}... | collective-permute-start | bytes 2359304 | tf_op jit(solution)/shard_map/ppermute | solution.py:556
  37.9 18.9 %all-to-all-start.1 = ((bf16[16,16,1536]{2,1,0:T(8,128)(2,1)}), bf16[16,16,1536]{2,1,0:T(8,128)(2,1)S(1)}, u32[]{:S(2)}, u32[]{:S(2)}) async-start(bf16[16,16,1536]{2,1,0:T(8,128)(2,1)} %bitcast.16), calls=%async_computation.1 | async-start | bytes 1572864 | tf_op jit(solution)/shard_map/all_to_all | solution.py:573
  48.0 19.7 %collective-permute-start.6 = (bf16[128,1536]{1,0:T(8,128)(2,1)}, bf16[128,1536]{1,0:T(8,128)(2,1)S(1)}, u32[]{:S(2)}, u32[]{:S(2)}) collective-permute-start(bf16[128,1536]{1,0:T(8,128)(2,1)} %slice.9), channel_id=1, source_target_pairs={{0,96},{32,0},{64,32},{96,64},{1,97},{33,1},{65,33},{97,65},{2,98}... | collective-permute-start | bytes 1179656 | tf_op jit(solution)/shard_map/ppermute | solution.py:556
  52.4 15.2 %collective-permute-start.5 = (bf16[128,1536]{1,0:T(8,128)(2,1)}, bf16[128,1536]{1,0:T(8,128)(2,1)}, u32[]{:S(2)}, u32[]{:S(2)}) collective-permute-start(bf16[128,1536]{1,0:T(8,128)(2,1)} %slice.8), channel_id=1, source_target_pairs={{0,32},{32,64},{64,96},{96,0},{1,33},{33,65},{65,97},{97,1},{2,34}... | collective-permute-start | bytes 1179656 | tf_op jit(solution)/shard_map/ppermute | solution.py:556
  63.4 12.1 %collective-permute-start.4 = (f32[16,768]{1,0:T(8,128)S(1)}, f32[16,768]{1,0:T(8,128)S(1)}, u32[]{:S(2)}, u32[]{:S(2)}) collective-permute-start(f32[16,768]{1,0:T(8,128)S(1)} %get-tuple-element.36), channel_id=1, source_target_pairs={{0,18},{2,0},{16,2},{18,16},{1,19},{3,1},{17,3},{19,17},{4,22},{6,... | collective-permute-start | bytes 147464 | tf_op jit(solution)/shard_map/ppermute | solution.py:556
  66.2 9.4 %collective-permute-start.3 = (f32[16,768]{1,0:T(8,128)S(1)}, f32[16,768]{1,0:T(8,128)S(1)}, u32[]{:S(2)}, u32[]{:S(2)}) collective-permute-start(f32[16,768]{1,0:T(8,128)S(1)} %get-tuple-element.36), channel_id=1, source_target_pairs={{0,16},{2,18},{16,0},{18,2},{1,17},{3,19},{17,1},{19,3},{4,20},{6,... | collective-permute-start | bytes 147464 | tf_op jit(solution)/shard_map/ppermute | solution.py:556
  67.0 8.6 %collective-permute-start.2 = (f32[16,768]{1,0:T(8,128)S(1)}, f32[16,768]{1,0:T(8,128)S(1)}, u32[]{:S(2)}, u32[]{:S(2)}) collective-permute-start(f32[16,768]{1,0:T(8,128)S(1)} %get-tuple-element.36), channel_id=1, source_target_pairs={{0,2},{2,16},{16,18},{18,0},{1,3},{3,17},{17,19},{19,1},{4,6},{6,2... | collective-permute-start | bytes 147464 | tf_op jit(solution)/shard_map/ppermute | solution.py:556
  73.4 17.9 %collective-permute-start.11 = (bf16[4,96,768]{2,1,0:T(8,128)(2,1)S(1)}, bf16[4,96,768]{2,1,0:T(8,128)(2,1)S(1)}, u32[]{:S(2)}, u32[]{:S(2)}) collective-permute-start(bf16[4,96,768]{2,1,0:T(8,128)(2,1)S(1)} %get-tuple-element.44), channel_id=1, source_target_pairs={{0,16},{16,0},{1,17},{17,1},{2,18},{18,2},{3,19},{19,3},{4,20},{20... | collective-permute-start | bytes 1769480 | tf_op jit(solution)/shard_map/ppermute | solution.py:556
  75.6 9.7 %copy-start.3 = (f32[4,16,784]{2,1,0:T(8,128)S(1)}, f32[4,16,784]{2,1,0:T(8,128)}, u32[]{:S(2)}) copy-start(f32[4,16,784]{2,1,0:T(8,128)} %get-tuple-element.32.disp_hbm.disp_ref) | copy-start | bytes 602116
  75.6 9.7 %copy-start.4 = (bf16[768,16]{0,1:T(8,128)(2,1)S(1)}, bf16[768,16]{0,1:T(8,128)(2,1)}, u32[]{:S(2)}) copy-start(bf16[768,16]{0,1:T(8,128)(2,1)} %param.6) | copy-start | bytes 73732
  79.3 9.6 %copy-start.1 = (f32[384,768]{1,0:T(8,128)}, f32[384,768]{1,0:T(8,128)S(1)}, u32[]{:S(2)}) copy-start(f32[384,768]{1,0:T(8,128)S(1)} %get-tuple-element.48) | copy-start | bytes 3538948
  79.4 1.7 %collective-permute-start.7 = (f32[16,768]{1,0:T(8,128)S(1)}, f32[16,768]{1,0:T(8,128)S(1)}, u32[]{:S(2)}, u32[]{:S(2)}) collective-permute-start(f32[16,768]{1,0:T(8,128)S(1)} %add_add_fusion.1), channel_id=1, source_target_pairs={{0,1},{1,0},{2,3},{3,2},{4,5},{5,4},{6,7},{7,6},{8,9},{9,8},{10,11... | collective-permute-start | bytes 147464 | tf_op jit(solution)/shard_map/ppermute | solution.py:556
  79.5 21.3 %collective-permute-start.15 = (bf16[384,768]{1,0:T(8,128)(2,1)S(1)}, bf16[384,768]{1,0:T(8,128)(2,1)S(1)}, u32[]{:S(2)}, u32[]{:S(2)}) collective-permute-start(bf16[384,768]{1,0:T(8,128)(2,1)S(1)} %get-tuple-element.49), channel_id=1, source_target_pairs={{0,16},{16,0},{1,17},{17,1},{2,18},{18,2},{3,19},{19,3},{4,20},{20... | collective-permute-start | bytes 1769480 | tf_op jit(solution)/shard_map/ppermute | solution.py:556
  81.0 7.9 %collective-permute-start.10 = (f32[16,768]{1,0:T(8,128)S(1)}, f32[16,768]{1,0:T(8,128)S(1)}, u32[]{:S(2)}, u32[]{:S(2)}) collective-permute-start(f32[16,768]{1,0:T(8,128)S(1)} %add.39), channel_id=1, source_target_pairs={{0,96},{32,0},{64,32},{96,64},{1,97},{33,1},{65,33},{97,65},{2,98}... | collective-permute-start | bytes 147464 | tf_op jit(solution)/shard_map/ppermute | solution.py:556
  84.3 5.6 %collective-permute-start.9 = (f32[16,768]{1,0:T(8,128)S(1)}, f32[16,768]{1,0:T(8,128)S(1)}, u32[]{:S(2)}, u32[]{:S(2)}) collective-permute-start(f32[16,768]{1,0:T(8,128)S(1)} %add.39), channel_id=1, source_target_pairs={{0,64},{32,96},{64,0},{96,32},{1,65},{33,97},{65,1},{97,33},{2,66}... | collective-permute-start | bytes 147464 | tf_op jit(solution)/shard_map/ppermute | solution.py:556
  84.3 5.8 %collective-permute-start.8 = (f32[16,768]{1,0:T(8,128)S(1)}, f32[16,768]{1,0:T(8,128)S(1)}, u32[]{:S(2)}, u32[]{:S(2)}) collective-permute-start(f32[16,768]{1,0:T(8,128)S(1)} %add.39), channel_id=1, source_target_pairs={{0,32},{32,64},{64,96},{96,0},{1,33},{33,65},{65,97},{97,1},{2,34}... | collective-permute-start | bytes 147464 | tf_op jit(solution)/shard_map/ppermute | solution.py:556
  91.3 10.6 %collective-permute-start.14 = (f32[16,768]{1,0:T(8,128)S(1)}, f32[16,768]{1,0:T(8,128)S(1)}, u32[]{:S(2)}, u32[]{:S(2)}) collective-permute-start(f32[16,768]{1,0:T(8,128)S(1)} %add_add_fusion), channel_id=1, source_target_pairs={{0,12},{4,0},{8,4},{12,8},{1,13},{5,1},{9,5},{13,9},{2,14},{6,2},{... | collective-permute-start | bytes 147464 | tf_op jit(solution)/shard_map/ppermute | solution.py:556
  92.4 9.5 %collective-permute-start.13 = (f32[16,768]{1,0:T(8,128)S(1)}, f32[16,768]{1,0:T(8,128)S(1)}, u32[]{:S(2)}, u32[]{:S(2)}) collective-permute-start(f32[16,768]{1,0:T(8,128)S(1)} %add_add_fusion), channel_id=1, source_target_pairs={{0,8},{4,12},{8,0},{12,4},{1,9},{5,13},{9,1},{13,5},{2,10},{6,14},... | collective-permute-start | bytes 147464 | tf_op jit(solution)/shard_map/ppermute | solution.py:556
  93.9 8.0 %collective-permute-start.12 = (f32[16,768]{1,0:T(8,128)S(1)}, f32[16,768]{1,0:T(8,128)S(1)}, u32[]{:S(2)}, u32[]{:S(2)}) collective-permute-start(f32[16,768]{1,0:T(8,128)S(1)} %add_add_fusion), channel_id=1, source_target_pairs={{0,4},{4,8},{8,12},{12,0},{1,5},{5,9},{9,13},{13,1},{2,6},{6,10},{... | collective-permute-start | bytes 147464 | tf_op jit(solution)/shard_map/ppermute | solution.py:556
  95.1 13.1 %all-to-all-start.2 = ((bf16[4,96,768]{2,1,0:T(8,128)(2,1)}), bf16[4,96,768]{2,1,0:T(8,128)(2,1)S(1)}, u32[]{:S(2)}, u32[]{:S(2)}) async-start(bf16[4,96,768]{2,1,0:T(8,128)(2,1)} %add_convert_fusion), calls=%async_computation.2 | async-start | bytes 1179648 | tf_op jit(solution)/shard_map/all_to_all | solution.py:601
  (1 other events, 5.7 us)

commit v5 on v4

--- a/solution.py
+++ b/solution.py
@@ -588,18 +588,22 @@
         grad_logits, slot_grads, router_term = token_logits(
             back, tokens, g_outputs, dispatch, combine
         )
+        far_a, far_b, router_term = lax.optimization_barrier((far_a, far_b, router_term))
         pieces = (rows, right, left, far_a, far_b)
         keep_in, send_in, act_far = first_grads(pieces, pre_own, pre_near, w_in, w_out, ny)
         keep_out, send_out = second_grads(pieces, (act_own, act_near, act_far))
+        total = axis_sum(router_term, "xh", XH)
+        total, send_in = lax.optimization_barrier((total, send_in))
         came_in = shift(send_in, "xh", 1, XH)
+        total = axis_sum(axis_sum(total, "core", 2), "y", ny)
+        total, keep_out, send_out = lax.optimization_barrier((total, keep_out, send_out))
+        total = axis_sum(total, "z", nz)
+        came_in, send_out = lax.optimization_barrier((came_in, send_out))
         came_out = shift(send_out, "xh", 1, XH)
-        total = axis_sum(router_term, ("xh", "xl"), 2 * XH)
-        total, keep_out = lax.optimization_barrier((total, keep_out))
-        total = axis_sum(axis_sum(total, "core", 2), "y", ny)
-        total, came_in = lax.optimization_barrier((total, came_in))
         part_in = (keep_in + came_in.astype(f32)).astype(bf16)
+        total, part_in, grad_logits = lax.optimization_barrier((total, part_in, grad_logits))
         spread = lax.all_to_all(part_in, "y", split_axis=0, concat_axis=0, tiled=True)
-        grad_router = axis_sum(total, "z", nz).T
+        grad_router = axis_sum(total, "xl", 2).T
         grad_second = keep_out + came_out.astype(f32)
         grad_first = widen(spread)
         grad_tok = token_grads(grad_logits, slot_grads, dispatch, rt)

time: 110 us -> 109 us (level)
  starting transfers between devices: 30.1 us -> 27.7 us
  waiting for transfers between devices: 14.8 us -> 16.6 us
    ppermute x16 -> x15, waiting for transfers between devices: 9.16 us -> 16.6 us  [shift(): lax.ppermute(value, axis, [(i, (i + by) % count) for i in range(count)])]
    all_to_all x1, waiting for transfers between devices: 5.59 us -> 0.01 us  [on_device(): lax.all_to_all(part_in, 'y', split_axis=0, concat_axis=0, tiled=True)]
    ppermute x16 -> x15, starting transfers between devices: 21.8 us -> 20.4 us  [shift(): lax.ppermute(value, axis, [(i, (i + by) % count) for i in range(count)])]
  transfers between devices with their start and end apart: 18 -> 17, of which waited for: 6 -> 8; matrix products, arithmetic and copies ran while one was open for 4% -> 3% of each run, Pallas kernels for 29% -> 30%
where the time goes in v5:
time: 109 us
  Pallas kernels  39.4 us (36%)
  starting transfers between devices  27.7 us (25%)
  blocking collectives  19.9 us (18%)
  waiting for transfers between devices  16.6 us (15%)
  other arithmetic  2.71 us (2%)
  local copies, waits for them, and re-layouts  1.59 us (1%)
    ppermute x15, starting transfers between devices, shift(): lax.ppermute(value, axis, [(i, (i + by) % count) for i in range(count)])  20.4 us
    all_to_all x1, blocking collectives, over_experts(): lax.all_to_all(value, ex_axes, split_axis=0, concat_axis=0, tiled=True)  19.9 us
    ppermute x15, waiting for transfers between devices, shift(): lax.ppermute(value, axis, [(i, (i + by) % count) for i in range(count)])  16.6 us
    pallas_call x1, Pallas kernels, expert_rows(): pl.pallas_call(expert_body, in_specs=[IN_VMEM] * 3, out_specs=[IN_PLACE]...  7.12 us
    pallas_call x1, Pallas kernels, token_forward(): pl.pallas_call(token_forward_body, in_specs=[IN_PLACE] * 3, out_specs=[IN...  7.11 us
    pallas_call x1, Pallas kernels, token_logits(): pl.pallas_call(token_logits_body, in_specs=[IN_VMEM] + [IN_PLACE] * 4, ou...  6.68 us
    pallas_call x1, Pallas kernels, first_grads(): pl.pallas_call(first_grads_body, in_specs=[IN_VMEM] * 5 + [IN_PLACE] * 4,...  5.75 us
    pallas_call x1, Pallas kernels, near_terms(): pl.pallas_call(near_terms_body, in_specs=[IN_VMEM] * 2 + [IN_PLACE] * 2,...  4.29 us
  transfers between devices with their start and end apart: 17, of which 8 were waited for; matrix products, arithmetic and copies ran while one was open for 3% of the time, Pallas kernels for 30%

profile of v5, /device:TPU:0, one launch (start us, length us, event | category | flops | bytes accessed | tf_op | source)
XLA Modules:
  0.0 108.8 jit_solution(11808161026079293560)
XLA Ops:
  0.7 7.1 %token_forward.1 = (bf16[16,16,1536]{2,1,0:T(8,128)(2,1)S(1)}, f32[4,16,784]{2,1,0:T(8,128)}, f32[4,16,784]{2,1,0:T(8,128)}) custom-call(bf16[16,768]{1,0:T(8,128)(2,1)} %bitcast.14, bf16[3136,768]{1,0:T(8,128)(2,1)} %x_hbm.3, bf16[3136,768]{1,0:T(8,128)(2,1)} %g_hbm.3), custom_call_target="tpu_custom_call" | custom-call | tf_op jit(solution)/shard_map/token_forward/pallas_call | solution.py:163
  7.8 19.9 %all_to_all.15 = bf16[16,16,1536]{2,1,0:T(8,128)(2,1)S(1)} all-to-all(bf16[16,16,1536]{2,1,0:T(8,128)(2,1)S(1)} %get-tuple-element.36), channel_id=1, replica_groups=mesh['y'=4,'xh'=2,'z'=4,'xl'=2,'core'=2] {'z','xl','core'}, dimensions={0} | all-to-all | bytes 1572864 | tf_op jit(solution)/shard_map/all_to_all | solution.py:573
  27.7 3.0 %collective-permute-start.2 = (bf16[256,1536]{1,0:T(8,128)(2,1)S(1)}, bf16[256,1536]{1,0:T(8,128)(2,1)S(1)}, u32[]{:S(2)}, u32[]{:S(2)}) collective-permute-start(bf16[256,1536]{1,0:T(8,128)(2,1)S(1)} %bitcast.9), channel_id=1, source_target_pairs={{0,96},{32,0},{64,32},{96,64},{1,97},{33,1},{65,33},{97,65},{2,98}... | collective-permute-start | bytes 2359304 | tf_op jit(solution)/shard_map/ppermute | solution.py:556
  30.7 7.1 %expert_rows.1 = (bf16[256,1536]{1,0:T(8,128)(2,1)}, bf16[256,768]{1,0:T(8,128)(2,1)}, bf16[256,768]{1,0:T(8,128)(2,1)}) custom-call(bf16[256,1536]{1,0:T(8,128)(2,1)S(1)} %bitcast.11, bf16[1,768,3072]{2,1,0:T(8,128)(2,1)S(1)} %bitcast.8, bf16[1,3072,768]{2,1,0:T(8,128)(2,1)S(1)} %copy-done), custom_call_target="tpu_custom_call" | custom-call | tf_op jit(solution)/shard_map/expert_rows/pallas_call | solution.py:238
  37.9 3.6 %all-to-all-start.1 = ((bf16[16,16,1536]{2,1,0:T(8,128)(2,1)}), bf16[16,16,1536]{2,1,0:T(8,128)(2,1)S(1)}, u32[]{:S(2)}, u32[]{:S(2)}) async-start(bf16[16,16,1536]{2,1,0:T(8,128)(2,1)} %bitcast.16), calls=%async_computation.1 | async-start | bytes 1572864 | tf_op jit(solution)/shard_map/all_to_all | solution.py:573
  41.5 5.7 %collective-permute-done.2.left_ref = bf16[256,1536]{1,0:T(8,128)(2,1)S(1)} collective-permute-done((bf16[256,1536]{1,0:T(8,128)(2,1)S(1)}, bf16[256,1536]{1,0:T(8,128)(2,1)S(1)}, u32[]{:S(2)}, u32[]{:S(2)}) %collective-permute-start.2) | collective-permute-done | bytes 786464 | tf_op jit(solution)/shard_map/ppermute | solution.py:556
  48.0 3.7 %collective-permute-start.3 = (bf16[128,1536]{1,0:T(8,128)(2,1)}, bf16[128,1536]{1,0:T(8,128)(2,1)S(1)}, u32[]{:S(2)}, u32[]{:S(2)}) collective-permute-start(bf16[128,1536]{1,0:T(8,128)(2,1)} %slice.9), channel_id=1, source_target_pairs={{0,96},{32,0},{64,32},{96,64},{1,97},{33,1},{65,33},{97,65},{2,98}... | collective-permute-start | bytes 1179656 | tf_op jit(solution)/shard_map/ppermute | solution.py:556
  52.4 4.3 %near_terms.1 = (bf16[512,768]{1,0:T(8,128)(2,1)}, bf16[512,768]{1,0:T(8,128)(2,1)}) custom-call(bf16[256,1536]{1,0:T(8,128)(2,1)S(1)} %collective-permute-done.right_ref, bf16[256,1536]{1,0:T(8,128)(2,1)S(1)} %collective-permute-done.2.left_ref, bf16[1,768,3072]{2,1,0:T(8,128)(2,1)} %w1_hbm.3, bf16[1,3072,768]{2,1,0:T(8,128)(2,1)} %w2_hbm.3), custom_call_target="tpu_custom_call" | custom-call | tf_op jit(solution)/shard_map/near_terms/pallas_call | solution.py:300
  56.7 6.7 %token_logits.1 = (bf16[4,16,784]{2,1,0:T(8,128)(2,1)S(1)}, bf16[4,64,768]{2,1,0:T(8,128)(2,1)S(1)}, f32[16,768]{1,0:T(8,128)S(1)}) custom-call(bf16[16,16,1536]{2,1,0:T(8,128)(2,1)S(1)} %all-to-all-done.1.back_ref, bf16[3136,768]{1,0:T(8,128)(2,1)} %x_hbm.3, bf16[3136,768]{1,0:T(8,128)(2,1)} %g_hbm.3, f32[4,16,784]{2,1,0:T(8,128)} %get-tuple-element.41.disp_hbm.disp_ref, ...), custom_call_target="tpu_custom_call" | custom-call | tf_op jit(solution)/shard_map/token_logits/pallas_call | solution.py:505
  63.5 2.8 %collective-permute-start.4 = (f32[16,768]{1,0:T(8,128)S(1)}, f32[16,768]{1,0:T(8,128)S(1)}, u32[]{:S(2)}, u32[]{:S(2)}) collective-permute-start(f32[16,768]{1,0:T(8,128)S(1)} %get-tuple-element.44), channel_id=1, source_target_pairs={{0,16},{16,0},{1,17},{17,1},{2,18},{18,2},{3,19},{19,3},{4,20},{20... | collective-permute-start | bytes 147464 | tf_op jit(solution)/shard_map/ppermute | solution.py:556
  66.3 5.7 %first_grads.1 = (f32[4,96,768]{2,1,0:T(8,128)S(1)}, bf16[4,96,768]{2,1,0:T(8,128)(2,1)S(1)}, bf16[256,768]{1,0:T(8,128)(2,1)S(1)}) custom-call(bf16[256,1536]{1,0:T(8,128)(2,1)S(1)} %bitcast.12, bf16[256,1536]{1,0:T(8,128)(2,1)S(1)} %collective-permute-done.right_ref, bf16[256,1536]{1,0:T(8,128)(2,1)S(1)} %collective-permute-done.2.left_ref, ...), custom_call_target="tpu_custom_call" | custom-call | tf_op jit(solution)/shard_map/first_grads/pallas_call | solution.py:349
  73.4 3.3 %collective-permute-start.8 = (f32[16,768]{1,0:T(8,128)S(1)}, f32[16,768]{1,0:T(8,128)S(1)}, u32[]{:S(2)}, u32[]{:S(2)}) collective-permute-start(f32[16,768]{1,0:T(8,128)S(1)} %add.34), channel_id=1, source_target_pairs={{0,96},{32,0},{64,32},{96,64},{1,97},{33,1},{65,33},{97,65},{2,98}... | collective-permute-start | bytes 147464 | tf_op jit(solution)/shard_map/ppermute | solution.py:556
  77.6 3.7 %second_grads.1 = (f32[384,768]{1,0:T(8,128)S(1)}, bf16[384,768]{1,0:T(8,128)(2,1)S(1)}) custom-call(bf16[256,1536]{1,0:T(8,128)(2,1)S(1)} %bitcast.13, bf16[256,1536]{1,0:T(8,128)(2,1)S(1)} %collective-permute-done.right_ref, bf16[256,1536]{1,0:T(8,128)(2,1)S(1)} %collective-permute-done.2.left_ref, bf16[128,1536]{1,0:T(8,128)(2,1)} %collective-permute-done.1.far_a, ...), custom_call_target="tpu_custom_call" | custom-call | tf_op jit(solution)/shard_map/second_grads/pallas_call | solution.py:401
  82.5 1.2 %collective-permute-start.11 = (f32[16,768]{1,0:T(8,128)S(1)}, f32[16,768]{1,0:T(8,128)S(1)}, u32[]{:S(2)}, u32[]{:S(2)}) collective-permute-start(f32[16,768]{1,0:T(8,128)S(1)} %add_add_fusion.1), channel_id=1, source_target_pairs={{0,12},{4,0},{8,4},{12,8},{1,13},{5,1},{9,5},{13,9},{2,14},{6,2},{... | collective-permute-start | bytes 147464 | tf_op jit(solution)/shard_map/ppermute | solution.py:556
  83.8 1.5 %collective-permute-start.10 = (f32[16,768]{1,0:T(8,128)S(1)}, f32[16,768]{1,0:T(8,128)S(1)}, u32[]{:S(2)}, u32[]{:S(2)}) collective-permute-start(f32[16,768]{1,0:T(8,128)S(1)} %add_add_fusion.1), channel_id=1, source_target_pairs={{0,8},{4,12},{8,0},{12,4},{1,9},{5,13},{9,1},{13,5},{2,10},{6,14},... | collective-permute-start | bytes 147464 | tf_op jit(solution)/shard_map/ppermute | solution.py:556
  85.5 1.2 %collective-permute-done.11 = f32[16,768]{1,0:T(8,128)S(1)} collective-permute-done((f32[16,768]{1,0:T(8,128)S(1)}, f32[16,768]{1,0:T(8,128)S(1)}, u32[]{:S(2)}, u32[]{:S(2)}) %collective-permute-start.11) | collective-permute-done | bytes 49184 | tf_op jit(solution)/shard_map/ppermute | solution.py:556
  86.7 2.7 %collective-permute-done.10 = f32[16,768]{1,0:T(8,128)S(1)} collective-permute-done((f32[16,768]{1,0:T(8,128)S(1)}, f32[16,768]{1,0:T(8,128)S(1)}, u32[]{:S(2)}, u32[]{:S(2)}) %collective-permute-start.10) | collective-permute-done | bytes 49184 | tf_op jit(solution)/shard_map/ppermute | solution.py:556
  89.4 1.2 %collective-permute-done.9 = f32[16,768]{1,0:T(8,128)S(1)} collective-permute-done((f32[16,768]{1,0:T(8,128)S(1)}, f32[16,768]{1,0:T(8,128)S(1)}, u32[]{:S(2)}, u32[]{:S(2)}) %collective-permute-start.9) | collective-permute-done | bytes 49184 | tf_op jit(solution)/shard_map/ppermute | solution.py:556
  90.6 2.5 %collective-permute-start.14 = (bf16[384,768]{1,0:T(8,128)(2,1)S(1)}, bf16[384,768]{1,0:T(8,128)(2,1)S(1)}, u32[]{:S(2)}, u32[]{:S(2)}) collective-permute-start(bf16[384,768]{1,0:T(8,128)(2,1)S(1)} %get-tuple-element.67), channel_id=1, source_target_pairs={{0,16},{16,0},{1,17},{17,1},{2,18},{18,2},{3,19},{19,3},{4,20},{20... | collective-permute-start | bytes 1769480 | tf_op jit(solution)/shard_map/ppermute | solution.py:556
  94.0 3.6 %all-to-all-start.2 = ((bf16[4,96,768]{2,1,0:T(8,128)(2,1)}), bf16[4,96,768]{2,1,0:T(8,128)(2,1)S(1)}, u32[]{:S(2)}, u32[]{:S(2)}) async-start(bf16[4,96,768]{2,1,0:T(8,128)(2,1)} %add_convert_fusion), calls=%async_computation.2 | async-start | bytes 1179648 | tf_op jit(solution)/shard_map/all_to_all | solution.py:605
  97.9 3.6 %token_grads.1 = bf16[3136,768]{1,0:T(8,128)(2,1)} custom-call(bf16[4,16,784]{2,1,0:T(8,128)(2,1)S(1)} %copy-done.7, bf16[4,64,768]{2,1,0:T(8,128)(2,1)S(1)} %copy-done.5, f32[4,16,784]{2,1,0:T(8,128)S(1)} %copy-done.3, bf16[16,768]{1,0:T(8,128)(2,1)S(1)} %bitcast.15), custom_call_target="tpu_custom_call" | custom-call | tf_op jit(solution)/shard_map/token_grads/pallas_call | solution.py:539
  101.6 4.4 %collective-permute-done.13 = f32[16,768]{1,0:T(8,128)S(1)} collective-permute-done((f32[16,768]{1,0:T(8,128)S(1)}, f32[16,768]{1,0:T(8,128)S(1)}, u32[]{:S(2)}, u32[]{:S(2)}) %collective-permute-start.13) | collective-permute-done | bytes 49184 | tf_op jit(solution)/shard_map/ppermute | solution.py:556
  106.6 1.1 %widen.1 = f32[1,96,3072]{2,1,0:T(8,128)} custom-call(bf16[4,96,768]{2,1,0:T(8,128)(2,1)S(1)} %all-to-all-done.2.in_ref), custom_call_target="tpu_custom_call" | custom-call | tf_op jit(solution)/shard_map/widen/pallas_call | solution.py:427
  107.7 1.1 %add_bitcast_fusion = f32[1,384,768]{2,1,0:T(8,128)} fusion(f32[384,768]{1,0:T(8,128)S(1)} %copy-done.2, bf16[384,768]{1,0:T(8,128)(2,1)S(1)} %collective-permute-done.14), kind=kLoop, calls=%fused_computation | loop fusion | flops 589824 | bytes 2949120 | tf_op jit(solution)/shard_map/broadcast_in_dim | solution.py:610
  (51 shorter events, 7.1 us)
Async XLA Ops:
  0.6 30.1 %slice-start = ((s8[4718592]{0:T(1024)(128)(4,1)}), s8[4194304]{0:T(1024)(128)(4,1)S(1)}, s32[]{:S(2)}) async-start(s8[4718592]{0:T(1024)(128)(4,1)} %bitcast.7), calls=%async_computation.3 | async-start | bytes 8388608
  0.6 30.1 %slice-start.1 = ((s8[4718592]{0:T(1024)(128)(4,1)}), s8[524288]{0:T(1024)(128)(4,1)S(1)}, s32[]{:S(2)}) async-start(s8[4718592]{0:T(1024)(128)(4,1)} %bitcast.7), calls=%async_computation.4 | async-start | bytes 1048576
  0.7 30.1 %copy-start = (bf16[1,3072,768]{2,1,0:T(8,128)(2,1)S(1)}, bf16[1,3072,768]{2,1,0:T(8,128)(2,1)}, u32[]{:S(2)}) copy-start(bf16[1,3072,768]{2,1,0:T(8,128)(2,1)} %w2_hbm.3) | copy-start | bytes 14155780
  27.7 19.5 %collective-permute-start.2 = (bf16[256,1536]{1,0:T(8,128)(2,1)S(1)}, bf16[256,1536]{1,0:T(8,128)(2,1)S(1)}, u32[]{:S(2)}, u32[]{:S(2)}) collective-permute-start(bf16[256,1536]{1,0:T(8,128)(2,1)S(1)} %bitcast.9), channel_id=1, source_target_pairs={{0,96},{32,0},{64,32},{96,64},{1,97},{33,1},{65,33},{97,65},{2,98}... | collective-permute-start | bytes 2359304 | tf_op jit(solution)/shard_map/ppermute | solution.py:556
  30.7 21.0 %collective-permute-start = (bf16[256,1536]{1,0:T(8,128)(2,1)S(1)}, bf16[256,1536]{1,0:T(8,128)(2,1)S(1)}, u32[]{:S(2)}, u32[]{:S(2)}) collective-permute-start(bf16[256,1536]{1,0:T(8,128)(2,1)S(1)} %bitcast.10), channel_id=1, source_target_pairs={{0,32},{32,64},{64,96},{96,0},{1,33},{33,65},{65,97},{97,1},{2,34}... | collective-permute-start | bytes 2359304 | tf_op jit(solution)/shard_map/ppermute | solution.py:556
  37.9 18.9 %all-to-all-start.1 = ((bf16[16,16,1536]{2,1,0:T(8,128)(2,1)}), bf16[16,16,1536]{2,1,0:T(8,128)(2,1)S(1)}, u32[]{:S(2)}, u32[]{:S(2)}) async-start(bf16[16,16,1536]{2,1,0:T(8,128)(2,1)} %bitcast.16), calls=%async_computation.1 | async-start | bytes 1572864 | tf_op jit(solution)/shard_map/all_to_all | solution.py:573
  48.0 15.5 %collective-permute-start.3 = (bf16[128,1536]{1,0:T(8,128)(2,1)}, bf16[128,1536]{1,0:T(8,128)(2,1)S(1)}, u32[]{:S(2)}, u32[]{:S(2)}) collective-permute-start(bf16[128,1536]{1,0:T(8,128)(2,1)} %slice.9), channel_id=1, source_target_pairs={{0,96},{32,0},{64,32},{96,64},{1,97},{33,1},{65,33},{97,65},{2,98}... | collective-permute-start | bytes 1179656 | tf_op jit(solution)/shard_map/ppermute | solution.py:556
  52.4 11.0 %collective-permute-start.1 = (bf16[128,1536]{1,0:T(8,128)(2,1)}, bf16[128,1536]{1,0:T(8,128)(2,1)}, u32[]{:S(2)}, u32[]{:S(2)}) collective-permute-start(bf16[128,1536]{1,0:T(8,128)(2,1)} %slice.8), channel_id=1, source_target_pairs={{0,32},{32,64},{64,96},{96,0},{1,33},{33,65},{65,97},{97,1},{2,34}... | collective-permute-start | bytes 1179656 | tf_op jit(solution)/shard_map/ppermute | solution.py:556
  63.4 8.6 %copy-start.4 = (bf16[4,64,768]{2,1,0:T(8,128)(2,1)}, bf16[4,64,768]{2,1,0:T(8,128)(2,1)S(1)}, u32[]{:S(2)}) copy-start(bf16[4,64,768]{2,1,0:T(8,128)(2,1)S(1)} %get-tuple-element.63.slots_ref) | copy-start | bytes 1179652
  63.4 8.6 %copy-start.6 = (bf16[4,16,784]{2,1,0:T(8,128)(2,1)}, bf16[4,16,784]{2,1,0:T(8,128)(2,1)S(1)}, u32[]{:S(2)}) copy-start(bf16[4,16,784]{2,1,0:T(8,128)(2,1)S(1)} %get-tuple-element.62.gl_ref) | copy-start | bytes 301060
  63.5 8.6 %collective-permute-start.4 = (f32[16,768]{1,0:T(8,128)S(1)}, f32[16,768]{1,0:T(8,128)S(1)}, u32[]{:S(2)}, u32[]{:S(2)}) collective-permute-start(f32[16,768]{1,0:T(8,128)S(1)} %get-tuple-element.44), channel_id=1, source_target_pairs={{0,16},{16,0},{1,17},{17,1},{2,18},{18,2},{3,19},{19,3},{4,20},{20... | collective-permute-start | bytes 147464 | tf_op jit(solution)/shard_map/ppermute | solution.py:556
  72.1 1.3 %collective-permute-start.5 = (f32[16,768]{1,0:T(8,128)S(1)}, f32[16,768]{1,0:T(8,128)S(1)}, u32[]{:S(2)}, u32[]{:S(2)}) collective-permute-start(f32[16,768]{1,0:T(8,128)S(1)} %add.33), channel_id=1, source_target_pairs={{0,1},{1,0},{2,3},{3,2},{4,5},{5,4},{6,7},{7,6},{8,9},{9,8},{10,11... | collective-permute-start | bytes 147464 | tf_op jit(solution)/shard_map/ppermute | solution.py:556
  72.2 18.4 %collective-permute-start.12 = (bf16[4,96,768]{2,1,0:T(8,128)(2,1)S(1)}, bf16[4,96,768]{2,1,0:T(8,128)(2,1)S(1)}, u32[]{:S(2)}, u32[]{:S(2)}) collective-permute-start(bf16[4,96,768]{2,1,0:T(8,128)(2,1)S(1)} %get-tuple-element.58), channel_id=1, source_target_pairs={{0,16},{16,0},{1,17},{17,1},{2,18},{18,2},{3,19},{19,3},{4,20},{20... | collective-permute-start | bytes 1769480 | tf_op jit(solution)/shard_map/ppermute | solution.py:556
  73.4 8.0 %collective-permute-start.8 = (f32[16,768]{1,0:T(8,128)S(1)}, f32[16,768]{1,0:T(8,128)S(1)}, u32[]{:S(2)}, u32[]{:S(2)}) collective-permute-start(f32[16,768]{1,0:T(8,128)S(1)} %add.34), channel_id=1, source_target_pairs={{0,96},{32,0},{64,32},{96,64},{1,97},{33,1},{65,33},{97,65},{2,98}... | collective-permute-start | bytes 147464 | tf_op jit(solution)/shard_map/ppermute | solution.py:556
  76.7 5.6 %collective-permute-start.7 = (f32[16,768]{1,0:T(8,128)S(1)}, f32[16,768]{1,0:T(8,128)S(1)}, u32[]{:S(2)}, u32[]{:S(2)}) collective-permute-start(f32[16,768]{1,0:T(8,128)S(1)} %add.34), channel_id=1, source_target_pairs={{0,64},{32,96},{64,0},{96,32},{1,65},{33,97},{65,1},{97,33},{2,66}... | collective-permute-start | bytes 147464 | tf_op jit(solution)/shard_map/ppermute | solution.py:556
  76.7 5.8 %collective-permute-start.6 = (f32[16,768]{1,0:T(8,128)S(1)}, f32[16,768]{1,0:T(8,128)S(1)}, u32[]{:S(2)}, u32[]{:S(2)}) collective-permute-start(f32[16,768]{1,0:T(8,128)S(1)} %add.34), channel_id=1, source_target_pairs={{0,32},{32,64},{64,96},{96,0},{1,33},{33,65},{65,97},{97,1},{2,34}... | collective-permute-start | bytes 147464 | tf_op jit(solution)/shard_map/ppermute | solution.py:556
  81.4 12.6 %copy-start.1 = (f32[384,768]{1,0:T(8,128)}, f32[384,768]{1,0:T(8,128)S(1)}, u32[]{:S(2)}) copy-start(f32[384,768]{1,0:T(8,128)S(1)} %get-tuple-element.66) | copy-start | bytes 3538948
  82.5 4.2 %collective-permute-start.11 = (f32[16,768]{1,0:T(8,128)S(1)}, f32[16,768]{1,0:T(8,128)S(1)}, u32[]{:S(2)}, u32[]{:S(2)}) collective-permute-start(f32[16,768]{1,0:T(8,128)S(1)} %add_add_fusion.1), channel_id=1, source_target_pairs={{0,12},{4,0},{8,4},{12,8},{1,13},{5,1},{9,5},{13,9},{2,14},{6,2},{... | collective-permute-start | bytes 147464 | tf_op jit(solution)/shard_map/ppermute | solution.py:556
  83.8 5.6 %collective-permute-start.10 = (f32[16,768]{1,0:T(8,128)S(1)}, f32[16,768]{1,0:T(8,128)S(1)}, u32[]{:S(2)}, u32[]{:S(2)}) collective-permute-start(f32[16,768]{1,0:T(8,128)S(1)} %add_add_fusion.1), channel_id=1, source_target_pairs={{0,8},{4,12},{8,0},{12,4},{1,9},{5,13},{9,1},{13,5},{2,10},{6,14},... | collective-permute-start | bytes 147464 | tf_op jit(solution)/shard_map/ppermute | solution.py:556
  85.3 5.3 %collective-permute-start.9 = (f32[16,768]{1,0:T(8,128)S(1)}, f32[16,768]{1,0:T(8,128)S(1)}, u32[]{:S(2)}, u32[]{:S(2)}) collective-permute-start(f32[16,768]{1,0:T(8,128)S(1)} %add_add_fusion.1), channel_id=1, source_target_pairs={{0,4},{4,8},{8,12},{12,0},{1,5},{5,9},{9,13},{13,1},{2,6},{6,10},{... | collective-permute-start | bytes 147464 | tf_op jit(solution)/shard_map/ppermute | solution.py:556
  90.6 17.1 %collective-permute-start.14 = (bf16[384,768]{1,0:T(8,128)(2,1)S(1)}, bf16[384,768]{1,0:T(8,128)(2,1)S(1)}, u32[]{:S(2)}, u32[]{:S(2)}) collective-permute-start(bf16[384,768]{1,0:T(8,128)(2,1)S(1)} %get-tuple-element.67), channel_id=1, source_target_pairs={{0,16},{16,0},{1,17},{17,1},{2,18},{18,2},{3,19},{19,3},{4,20},{20... | collective-permute-start | bytes 1769480 | tf_op jit(solution)/shard_map/ppermute | solution.py:556
  94.0 12.6 %all-to-all-start.2 = ((bf16[4,96,768]{2,1,0:T(8,128)(2,1)}), bf16[4,96,768]{2,1,0:T(8,128)(2,1)S(1)}, u32[]{:S(2)}, u32[]{:S(2)}) async-start(bf16[4,96,768]{2,1,0:T(8,128)(2,1)} %add_convert_fusion), calls=%async_computation.2 | async-start | bytes 1179648 | tf_op jit(solution)/shard_map/all_to_all | solution.py:605
  97.6 8.3 %collective-permute-start.13 = (f32[16,768]{1,0:T(8,128)S(1)}, f32[16,768]{1,0:T(8,128)S(1)}, u32[]{:S(2)}, u32[]{:S(2)}) collective-permute-start(f32[16,768]{1,0:T(8,128)S(1)} %add_add_fusion), channel_id=1, source_target_pairs={{0,2},{2,0},{1,3},{3,1},{4,6},{6,4},{5,7},{7,5},{8,10},{10,8},{9,1... | collective-permute-start | bytes 147464 | tf_op jit(solution)/shard_map/ppermute | solution.py:556
  101.6 6.1 %copy-start.2 = (f32[384,768]{1,0:T(8,128)S(1)}, f32[384,768]{1,0:T(8,128)}, u32[]{:S(2)}) copy-start(f32[384,768]{1,0:T(8,128)} %copy-done.1) | copy-start | bytes 3538948
  (4 other events, 15.7 us)

commit v6 on v4

--- a/solution.py
+++ b/solution.py
@@ -106,7 +106,7 @@
     x_copies = block_copies(x_hbm, x_ref, x_sem)
     g_copies = block_copies(g_hbm, g_ref, g_sem)
     rt_copy = pltpu.make_async_copy(rt_hbm, rt_ref, rt_sem)
-    for copy in [rt_copy] + x_copies + g_copies:
+    for copy in [rt_copy] + x_copies:
         copy.start()
     weight_copies = [
         pltpu.make_async_copy(disp_ref, disp_hbm, disp_sem),
@@ -121,6 +121,8 @@
         logits, own = {}, {}
         for b in pair:
             x_copies[b].wait()
+        for b in pair:
+            g_copies[b].start()
         for b in pair:
             logits[b] = contract(rt, x_ref[b * width : (b + 1) * width, :], 1, 1)
         for b in pair:
@@ -317,27 +319,32 @@
 
 
 def first_grads_body(
-    own_ref, right_ref, left_ref, far_a, far_b, pre_own, pre_near, w1_hbm, w2_hbm,
-    keep_ref, send_ref, act_far, rows, pre, far, acc, w1, w2, sem, pre_sem
+    own_ref, right_ref, left_ref, far_ref, pre_own, pre_near, w1_hbm, w2_hbm,
+    terms_hbm, act_hbm, terms_ref, act_far, rows, pre, w1, w2, sem, pre_sem, out_sem
 ):
     feat = w1.shape[0]
-    xh = lax.axis_index("xh")
     loads = slice_copies(w1_hbm, w2_hbm, w1, w2, sem)
     terms = stacked_copies((pre_own, pre_near), pre, pre_sem)
     for load in terms + list(loads):
         load.start()
     join((own_ref, right_ref, left_ref), 0, feat, rows)
-    join((far_a, far_b), 0, 2 * feat, far)
     for load in terms:
         load.wait()
     total = contract(rows[...], pre[...], 0, 0)
     for load in loads:
         load.wait()
-    act, pre_far = hidden_terms(far[:, :feat], far[:, feat:], w1[...], w2[...])
+    act, pre_far = hidden_terms(far_ref[:, :feat], far_ref[:, feat:], w1[...], w2[...])
     act_far[...] = act
-    acc[...] = (total + contract(far[:, :feat], pre_far, 0, 0)).reshape(acc.shape)
-    send_ref[...] = acc[:, pl.ds(1 - xh, 1)].reshape(send_ref.shape).astype(bf16)
-    keep_ref[...] = acc[:, pl.ds(xh, 1)].reshape(keep_ref.shape)
+    stores = [
+        pltpu.make_async_copy(act_far, act_hbm, out_sem.at[0]),
+        pltpu.make_async_copy(terms_ref, terms_hbm, out_sem.at[1]),
+    ]
+    stores[0].start()
+    total = total + contract(far_ref[:, :feat], pre_far, 0, 0)
+    terms_ref[...] = total.astype(bf16).reshape(terms_ref.shape)
+    stores[1].start()
+    for store in stores:
+        store.wait()
 
 
 def first_grads(pieces, pre_own, pre_near, w_in, w_out, parts):
@@ -345,25 +352,24 @@
     tile = hidden // parts
     own = feat // (parts * XH)
     near_count = sum(p.shape[0] for p in pieces[:3])
-    far_count = sum(p.shape[0] for p in pieces[3:])
     return pl.pallas_call(
         first_grads_body,
-        in_specs=[IN_VMEM] * 5 + [IN_PLACE] * 4,
-        out_specs=[IN_VMEM] * 3,
+        in_specs=[IN_VMEM] * 4 + [IN_PLACE] * 4,
+        out_specs=[IN_PLACE] * 2,
         out_shape=[
-            jax.ShapeDtypeStruct((parts, own, tile), f32),
-            jax.ShapeDtypeStruct((parts, own, tile), bf16),
-            jax.ShapeDtypeStruct((far_count, tile), bf16),
+            pltpu.HBM((parts * XH, own, tile), bf16),
+            pltpu.HBM((pieces[3].shape[0], tile), bf16),
         ],
         scratch_shapes=[
+            pltpu.VMEM((parts * XH, own, tile), bf16),
+            pltpu.VMEM((pieces[3].shape[0], tile), bf16),
             pltpu.VMEM((near_count, feat), bf16),
             pltpu.VMEM((near_count, tile), bf16),
-            pltpu.VMEM((far_count, 2 * feat), bf16),
-            pltpu.VMEM((parts, XH, own, tile), f32),
             pltpu.VMEM((feat, tile), bf16),
             pltpu.VMEM((tile, feat), bf16),
             pltpu.SemaphoreType.DMA((2,)),
             pltpu.SemaphoreType.DMA((2,)),
+            pltpu.SemaphoreType.DMA((2,)),
         ],
         compiler_params=params(20),
         name="first_grads",
@@ -371,17 +377,22 @@
 
 
 def second_grads_body(
-    own_ref, right_ref, left_ref, far_a, far_b, act_own, act_near, act_far,
+    own_ref, right_ref, left_ref, far_hbm, act_own, act_near, act_far,
     keep_ref, send_ref, grads, act, sem
 ):
     feat = grads.shape[1]
     tile = keep_ref.shape[0]
     xh = lax.axis_index("xh")
-    terms = stacked_copies((act_own, act_near), act, sem)
+    terms = stacked_copies((act_own, act_near, act_far), act, sem)
+    far = far_hbm.shape[0]
+    terms.append(
+        pltpu.make_async_copy(
+            far_hbm.at[:, pl.ds(feat, feat)], grads.at[pl.ds(grads.shape[0] - far, far)], sem.at[3]
+        )
+    )
     for load in terms:
         load.start()
-    join((own_ref, right_ref, left_ref, far_a, far_b), feat, 2 * feat, grads)
-    act[act.shape[0] - act_far.shape[0] :, :] = act_far[...]
+    join((own_ref, right_ref, left_ref), feat, 2 * feat, grads)
     for load in terms:
         load.wait()
 
@@ -400,7 +411,7 @@
     tile = width // XH
     return pl.pallas_call(
         second_grads_body,
-        in_specs=[IN_VMEM] * 5 + [IN_PLACE] * 2 + [IN_VMEM],
+        in_specs=[IN_VMEM] * 3 + [IN_PLACE] * 4,
         out_specs=[IN_VMEM] * 2,
         out_shape=[
             jax.ShapeDtypeStruct((tile, feat), f32),
@@ -409,28 +420,29 @@
         scratch_shapes=[
             pltpu.VMEM((count, feat), bf16),
             pltpu.VMEM((count, width), bf16),
-            pltpu.SemaphoreType.DMA((2,)),
+            pltpu.SemaphoreType.DMA((4,)),
         ],
         compiler_params=params(12),
         name="second_grads",
-    )(*pieces, pinned(acts[0]), pinned(acts[1]), acts[2])
-
-
-def widen_body(in_ref, out_ref):
-    parts, _, tile = in_ref.shape
-    for i in range(parts):
-        out_ref[0, :, i * tile : (i + 1) * tile] = in_ref[i].astype(f32)
-
-
-def widen(spread):
-    parts, own, tile = spread.shape
-    return pl.pallas_call(
-        widen_body,
+    )(*pieces[:3], *[pinned(v) for v in (pieces[3],) + tuple(acts)])
+
+
+def sum_pairs_body(in_ref, out_ref):
+    count, _, tile = in_ref.shape
+    for i in range(count // XH):
+        terms = [in_ref[XH * i + k].astype(f32) for k in range(XH)]
+        out_ref[0, :, i * tile : (i + 1) * tile] = sum(terms[1:], terms[0])
+
+
+def sum_pairs(spread):
+    count, own, tile = spread.shape
+    return pl.pallas_call(
+        sum_pairs_body,
         in_specs=[IN_VMEM],
         out_specs=IN_VMEM,
-        out_shape=jax.ShapeDtypeStruct((1, own, parts * tile), f32),
+        out_shape=jax.ShapeDtypeStruct((1, own, count // XH * tile), f32),
         compiler_params=params(4),
-        name="widen",
+        name="sum_pairs",
     )(spread)
 
 
@@ -445,14 +457,11 @@
     total = experts * images
     x_copies = block_copies(x_hbm, x_ref, x_sem)
     g_copies = block_copies(g_hbm, g_ref, g_sem)
-    for x_copy, g_copy in zip(x_copies, g_copies):
-        g_copy.start()
-        x_copy.start()
     weight_copies = [
         pltpu.make_async_copy(disp_hbm, disp_ref, weight_sem.at[0]),
         pltpu.make_async_copy(comb_hbm, comb_ref, weight_sem.at[1]),
     ]
-    for copy in weight_copies:
+    for copy in g_copies[:2] + x_copies[:2] + weight_copies:
         copy.start()
     mix[...] = jnp.dot(
         swap_matrix(total, images),
@@ -476,6 +485,9 @@
         for b in pair:
             g_copies[b].wait()
             x_copies[b].wait()
+        if first == 0:
+            for copy in g_copies[2:] + x_copies[2:]:
+                copy.start()
         for b in pair:
             block = mix[b * rows : (b + 1) * rows, :]
             slots_ref[b] = block[:, feat:]
@@ -576,32 +588,31 @@
         rt = router.T
         slots, dispatch, combine = token_forward(tokens, rt, g_outputs)
         rows = over_experts(slots).reshape(-1, slots.shape[2])
-        mid = rows.shape[0] // 2
         right = shift(rows, "y", 1, ny)
         left = shift(rows, "y", ny - 1, ny)
         results, act_own, pre_own = expert_rows(rows, w_in, w_out, ny)
+        rows, results = lax.optimization_barrier((rows, results))
+        far = shift(rows, "y", ny // 2, ny)
         back = over_experts(results.reshape(slots.shape))
-        far_a = shift(right[:mid], "y", 1, ny)
-        far_b = shift(left[mid:], "y", ny - 1, ny)
         act_near, pre_near = near_terms(right, left, w_in, w_out, ny)
         back, act_near, pre_near = lax.optimization_barrier((back, act_near, pre_near))
         grad_logits, slot_grads, router_term = token_logits(
             back, tokens, g_outputs, dispatch, combine
         )
-        pieces = (rows, right, left, far_a, far_b)
-        keep_in, send_in, act_far = first_grads(pieces, pre_own, pre_near, w_in, w_out, ny)
+        far, router_term = lax.optimization_barrier((far, router_term))
+        pieces = (rows, right, left, far)
+        terms_in, act_far = first_grads(pieces, pre_own, pre_near, w_in, w_out, ny)
+        total = axis_sum(router_term, "xh", XH)
+        total, terms_in = lax.optimization_barrier((total, terms_in))
+        spread = lax.all_to_all(terms_in, dp_axes, split_axis=0, concat_axis=0, tiled=True)
         keep_out, send_out = second_grads(pieces, (act_own, act_near, act_far))
-        came_in = shift(send_in, "xh", 1, XH)
         came_out = shift(send_out, "xh", 1, XH)
-        total = axis_sum(router_term, ("xh", "xl"), 2 * XH)
-        total, keep_out = lax.optimization_barrier((total, keep_out))
-        total = axis_sum(axis_sum(total, "core", 2), "y", ny)
-        total, came_in = lax.optimization_barrier((total, came_in))
-        part_in = (keep_in + came_in.astype(f32)).astype(bf16)
-        spread = lax.all_to_all(part_in, "y", split_axis=0, concat_axis=0, tiled=True)
-        grad_router = axis_sum(total, "z", nz).T
+        total = axis_sum(axis_sum(total, "core", 2), "z", nz)
+        total, keep_out, send_out = lax.optimization_barrier((total, keep_out, send_out))
+        total, spread = lax.optimization_barrier((axis_sum(total, "y", ny), spread))
+        grad_first = sum_pairs(spread)
+        grad_router = axis_sum(total, "xl", 2).T
         grad_second = keep_out + came_out.astype(f32)
-        grad_first = widen(spread)
         grad_tok = token_grads(grad_logits, slot_grads, dispatch, rt)
         return grad_tok, grad_router, grad_first, grad_second[None]
 

time: 110 us -> 124 us (1.13)
  waiting for transfers between devices: 14.8 us -> 30.4 us
  starting transfers between devices: 30.1 us -> 27.2 us
    ppermute x16 -> x13, waiting for transfers between devices: 9.16 us -> 30.4 us  [shift(): lax.ppermute(value, axis, [(i, (i + by) % count) for i in range(count)])]
    all_to_all x1, waiting for transfers between devices: 5.59 us -> 0.01 us  [on_device(): lax.all_to_all(terms_in, dp_axes, split_axis=0, concat_axis=0, tiled=True)]
    ppermute x16 -> x13, starting transfers between devices: 21.8 us -> 19.2 us  [shift(): lax.ppermute(value, axis, [(i, (i + by) % count) for i in range(count)])]
    slice x2 -> x0, local copies, waits for them, and re-layouts: 1.54 us -> none  [the longest x1 0.77 us: on_device(): far_b = shift(left[mid:], 'y', ny - 1, ny)]
    pallas_call x1, Pallas kernels: 6.68 us -> 8.04 us  [token_logits(): pl.pallas_call(token_logits_body, in_specs=[IN_VMEM] + [IN_PLACE] * 4, ou...]
  transfers between devices with their start and end apart: 18 -> 15, of which waited for: 6 -> 8; matrix products, arithmetic and copies ran while one was open for 4% -> 1% of each run, Pallas kernels for 29% -> 27%
where the time goes in v6:
time: 124 us; the launch traced here: 122 us
  Pallas kernels  40.3 us (32%)
  waiting for transfers between devices  30.4 us (25%)
  starting transfers between devices  27.2 us (22%)
  blocking collectives  19.9 us (16%)
  other arithmetic  2.4 us (2%)
    ppermute x13, waiting for transfers between devices, shift(): lax.ppermute(value, axis, [(i, (i + by) % count) for i in range(count)])  30.4 us
    all_to_all x1, blocking collectives, over_experts(): lax.all_to_all(value, ex_axes, split_axis=0, concat_axis=0, tiled=True)  19.9 us
    ppermute x13, starting transfers between devices, shift(): lax.ppermute(value, axis, [(i, (i + by) % count) for i in range(count)])  19.2 us
    pallas_call x1, Pallas kernels, token_logits(): pl.pallas_call(token_logits_body, in_specs=[IN_VMEM] + [IN_PLACE] * 4, ou...  8.04 us
    pallas_call x1, Pallas kernels, token_forward(): pl.pallas_call(token_forward_body, in_specs=[IN_PLACE] * 3, out_specs=[IN...  7.44 us
    pallas_call x1, Pallas kernels, expert_rows(): pl.pallas_call(expert_body, in_specs=[IN_VMEM] * 3, out_specs=[IN_PLACE]...  7.12 us
    pallas_call x1, Pallas kernels, first_grads(): pl.pallas_call(first_grads_body, in_specs=[IN_VMEM] * 4 + [IN_PLACE] * 4,...  5.18 us
    all_to_all x1, starting transfers between devices, over_experts(): lax.all_to_all(value, ex_axes, split_axis=0, concat_axis=0, tiled=True)  4.47 us
  transfers between devices with their start and end apart: 15, of which 8 were waited for; matrix products, arithmetic and copies ran while one was open for 1% of the time, Pallas kernels for 27%

profile of v6, /device:TPU:0, one launch (start us, length us, event | category | flops | bytes accessed | tf_op | source)
XLA Modules:
  0.0 122.1 jit_solution(17000601704935806007)
XLA Ops:
  0.7 7.4 %token_forward.1 = (bf16[16,16,1536]{2,1,0:T(8,128)(2,1)S(1)}, f32[4,16,784]{2,1,0:T(8,128)}, f32[4,16,784]{2,1,0:T(8,128)}) custom-call(bf16[16,768]{1,0:T(8,128)(2,1)} %bitcast.15, bf16[3136,768]{1,0:T(8,128)(2,1)} %x_hbm.3, bf16[3136,768]{1,0:T(8,128)(2,1)} %g_hbm.3), custom_call_target="tpu_custom_call" | custom-call | tf_op jit(solution)/shard_map/token_forward/pallas_call | solution.py:165
  8.1 19.9 %all_to_all.15 = bf16[16,16,1536]{2,1,0:T(8,128)(2,1)S(1)} all-to-all(bf16[16,16,1536]{2,1,0:T(8,128)(2,1)S(1)} %get-tuple-element.32), channel_id=1, replica_groups=mesh['y'=4,'xh'=2,'z'=4,'xl'=2,'core'=2] {'z','xl','core'}, dimensions={0} | all-to-all | bytes 1572864 | tf_op jit(solution)/shard_map/all_to_all | solution.py:585
  28.0 3.0 %collective-permute-start.1 = (bf16[256,1536]{1,0:T(8,128)(2,1)S(1)}, bf16[256,1536]{1,0:T(8,128)(2,1)S(1)}, u32[]{:S(2)}, u32[]{:S(2)}) collective-permute-start(bf16[256,1536]{1,0:T(8,128)(2,1)S(1)} %bitcast.9), channel_id=1, source_target_pairs={{0,96},{32,0},{64,32},{96,64},{1,97},{33,1},{65,33},{97,65},{2,98}... | collective-permute-start | bytes 2359304 | tf_op jit(solution)/shard_map/ppermute | solution.py:568
  31.1 7.1 %expert_rows.1 = (bf16[256,1536]{1,0:T(8,128)(2,1)}, bf16[256,768]{1,0:T(8,128)(2,1)}, bf16[256,768]{1,0:T(8,128)(2,1)}) custom-call(bf16[256,1536]{1,0:T(8,128)(2,1)S(1)} %bitcast.11, bf16[1,768,3072]{2,1,0:T(8,128)(2,1)S(1)} %bitcast.8, bf16[1,3072,768]{2,1,0:T(8,128)(2,1)S(1)} %copy-done), custom_call_target="tpu_custom_call" | custom-call | tf_op jit(solution)/shard_map/expert_rows/pallas_call | solution.py:240
  38.2 2.3 %collective-permute-start.2 = (bf16[256,1536]{1,0:T(8,128)(2,1)S(1)}, bf16[256,1536]{1,0:T(8,128)(2,1)S(1)}, u32[]{:S(2)}, u32[]{:S(2)}) collective-permute-start(bf16[256,1536]{1,0:T(8,128)(2,1)S(1)} %bitcast.12), channel_id=1, source_target_pairs={{0,64},{32,96},{64,0},{96,32},{1,65},{33,97},{65,1},{97,33},{2,66}... | collective-permute-start | bytes 2359304 | tf_op jit(solution)/shard_map/ppermute | solution.py:568
  40.5 4.5 %all-to-all-start.1 = ((bf16[16,16,1536]{2,1,0:T(8,128)(2,1)}), bf16[16,16,1536]{2,1,0:T(8,128)(2,1)}, u32[]{:S(2)}, u32[]{:S(2)}) async-start(bf16[16,16,1536]{2,1,0:T(8,128)(2,1)} %bitcast.17), calls=%async_computation.1 | async-start | bytes 1572864 | tf_op jit(solution)/shard_map/all_to_all | solution.py:585
  44.9 19.4 %collective-permute-done.1.left_ref = bf16[256,1536]{1,0:T(8,128)(2,1)S(1)} collective-permute-done((bf16[256,1536]{1,0:T(8,128)(2,1)S(1)}, bf16[256,1536]{1,0:T(8,128)(2,1)S(1)}, u32[]{:S(2)}, u32[]{:S(2)}) %collective-permute-start.1) | collective-permute-done | bytes 786464 | tf_op jit(solution)/shard_map/ppermute | solution.py:568
  64.4 3.4 %collective-permute-done.right_ref = bf16[256,1536]{1,0:T(8,128)(2,1)S(1)} collective-permute-done((bf16[256,1536]{1,0:T(8,128)(2,1)S(1)}, bf16[256,1536]{1,0:T(8,128)(2,1)S(1)}, u32[]{:S(2)}, u32[]{:S(2)}) %collective-permute-start) | collective-permute-done | bytes 786464 | tf_op jit(solution)/shard_map/ppermute | solution.py:568
  67.8 4.3 %near_terms.1 = (bf16[512,768]{1,0:T(8,128)(2,1)}, bf16[512,768]{1,0:T(8,128)(2,1)}) custom-call(bf16[256,1536]{1,0:T(8,128)(2,1)S(1)} %collective-permute-done.right_ref, bf16[256,1536]{1,0:T(8,128)(2,1)S(1)} %collective-permute-done.1.left_ref, bf16[1,768,3072]{2,1,0:T(8,128)(2,1)} %w1_hbm.3, bf16[1,3072,768]{2,1,0:T(8,128)(2,1)} %w2_hbm.3), custom_call_target="tpu_custom_call" | custom-call | tf_op jit(solution)/shard_map/near_terms/pallas_call | solution.py:302
  72.1 8.0 %token_logits.1 = (bf16[4,16,784]{2,1,0:T(8,128)(2,1)S(1)}, bf16[4,64,768]{2,1,0:T(8,128)(2,1)S(1)}, f32[16,768]{1,0:T(8,128)S(1)}) custom-call(bf16[16,16,1536]{2,1,0:T(8,128)(2,1)} %all-to-all-done.1.back_ref, bf16[3136,768]{1,0:T(8,128)(2,1)} %x_hbm.3, bf16[3136,768]{1,0:T(8,128)(2,1)} %g_hbm.3, f32[4,16,784]{2,1,0:T(8,128)} %get-tuple-element.38.disp_hbm.disp_ref, ...), custom_call_target="tpu_custom_call" | custom-call | tf_op jit(solution)/shard_map/token_logits/pallas_call | solution.py:517
  80.2 2.8 %collective-permute-start.3 = (f32[16,768]{1,0:T(8,128)S(1)}, f32[16,768]{1,0:T(8,128)S(1)}, u32[]{:S(2)}, u32[]{:S(2)}) collective-permute-start(f32[16,768]{1,0:T(8,128)S(1)} %get-tuple-element.44), channel_id=1, source_target_pairs={{0,16},{16,0},{1,17},{17,1},{2,18},{18,2},{3,19},{19,3},{4,20},{20... | collective-permute-start | bytes 147464 | tf_op jit(solution)/shard_map/ppermute | solution.py:568
  83.0 5.2 %first_grads.1 = (bf16[8,96,768]{2,1,0:T(8,128)(2,1)}, bf16[256,768]{1,0:T(8,128)(2,1)}) custom-call(bf16[256,1536]{1,0:T(8,128)(2,1)S(1)} %bitcast.13, bf16[256,1536]{1,0:T(8,128)(2,1)S(1)} %collective-permute-done.right_ref, bf16[256,1536]{1,0:T(8,128)(2,1)S(1)} %collective-permute-done.1.left_ref, ...), custom_call_target="tpu_custom_call" | custom-call | tf_op jit(solution)/shard_map/first_grads/pallas_call | solution.py:355
  88.9 3.6 %all-to-all-start.2 = ((bf16[8,96,768]{2,1,0:T(8,128)(2,1)}), bf16[8,96,768]{2,1,0:T(8,128)(2,1)S(1)}, u32[]{:S(2)}, u32[]{:S(2)}) async-start(bf16[8,96,768]{2,1,0:T(8,128)(2,1)} %get-tuple-element.56), calls=%async_computation.2 | async-start | bytes 2359296 | tf_op jit(solution)/shard_map/all_to_all | solution.py:607
  92.6 3.4 %second_grads.1 = (f32[384,768]{1,0:T(8,128)S(1)}, bf16[384,768]{1,0:T(8,128)(2,1)}) custom-call(bf16[256,1536]{1,0:T(8,128)(2,1)S(1)} %bitcast.14, bf16[256,1536]{1,0:T(8,128)(2,1)S(1)} %collective-permute-done.right_ref, bf16[256,1536]{1,0:T(8,128)(2,1)S(1)} %collective-permute-done.1.left_ref, bf16[256,1536]{1,0:T(8,128)(2,1)} %copy-done.1, ...), custom_call_target="tpu_custom_call" | custom-call | tf_op jit(solution)/shard_map/second_grads/pallas_call | solution.py:412
  97.0 3.3 %collective-permute-start.12 = (bf16[384,768]{1,0:T(8,128)(2,1)}, bf16[384,768]{1,0:T(8,128)(2,1)S(1)}, u32[]{:S(2)}, u32[]{:S(2)}) collective-permute-start(bf16[384,768]{1,0:T(8,128)(2,1)} %get-tuple-element.54), channel_id=1, source_target_pairs={{0,16},{16,0},{1,17},{17,1},{2,18},{18,2},{3,19},{19,3},{4,20},{20... | collective-permute-start | bytes 1769480 | tf_op jit(solution)/shard_map/ppermute | solution.py:568
  100.4 1.2 %collective-permute-start.7 = (f32[16,768]{1,0:T(8,128)S(1)}, f32[16,768]{1,0:T(8,128)S(1)}, u32[]{:S(2)}, u32[]{:S(2)}) collective-permute-start(f32[16,768]{1,0:T(8,128)S(1)} %add.31), channel_id=1, source_target_pairs={{0,12},{4,0},{8,4},{12,8},{1,13},{5,1},{9,5},{13,9},{2,14},{6,2},{... | collective-permute-start | bytes 147464 | tf_op jit(solution)/shard_map/ppermute | solution.py:568
  101.6 1.5 %collective-permute-start.6 = (f32[16,768]{1,0:T(8,128)S(1)}, f32[16,768]{1,0:T(8,128)S(1)}, u32[]{:S(2)}, u32[]{:S(2)}) collective-permute-start(f32[16,768]{1,0:T(8,128)S(1)} %add.31), channel_id=1, source_target_pairs={{0,8},{4,12},{8,0},{12,4},{1,9},{5,13},{9,1},{13,5},{2,10},{6,14},... | collective-permute-start | bytes 147464 | tf_op jit(solution)/shard_map/ppermute | solution.py:568
  103.3 1.5 %collective-permute-done.7 = f32[16,768]{1,0:T(8,128)S(1)} collective-permute-done((f32[16,768]{1,0:T(8,128)S(1)}, f32[16,768]{1,0:T(8,128)S(1)}, u32[]{:S(2)}, u32[]{:S(2)}) %collective-permute-start.7) | collective-permute-done | bytes 49184 | tf_op jit(solution)/shard_map/ppermute | solution.py:568
  104.8 2.7 %collective-permute-done.6 = f32[16,768]{1,0:T(8,128)S(1)} collective-permute-done((f32[16,768]{1,0:T(8,128)S(1)}, f32[16,768]{1,0:T(8,128)S(1)}, u32[]{:S(2)}, u32[]{:S(2)}) %collective-permute-start.6) | collective-permute-done | bytes 49184 | tf_op jit(solution)/shard_map/ppermute | solution.py:568
  108.4 2.8 %collective-permute-start.10 = (f32[16,768]{1,0:T(8,128)S(1)}, f32[16,768]{1,0:T(8,128)S(1)}, u32[]{:S(2)}, u32[]{:S(2)}) collective-permute-start(f32[16,768]{1,0:T(8,128)S(1)} %add_add_fusion.1), channel_id=1, source_target_pairs={{0,96},{32,0},{64,32},{96,64},{1,97},{33,1},{65,33},{97,65},{2,98}... | collective-permute-start | bytes 147464 | tf_op jit(solution)/shard_map/ppermute | solution.py:568
  112.9 3.6 %token_grads.1 = bf16[3136,768]{1,0:T(8,128)(2,1)} custom-call(bf16[4,16,784]{2,1,0:T(8,128)(2,1)S(1)} %copy-done.8, bf16[4,64,768]{2,1,0:T(8,128)(2,1)S(1)} %copy-done.6, f32[4,16,784]{2,1,0:T(8,128)S(1)} %copy-done.4, bf16[16,768]{1,0:T(8,128)(2,1)S(1)} %bitcast.16), custom_call_target="tpu_custom_call" | custom-call | tf_op jit(solution)/shard_map/token_grads/pallas_call | solution.py:551
  117.6 1.1 add_bitcast_fusion
  118.7 1.1 sum_pairs.1
  119.9 1.7 %collective-permute-done.11 = f32[16,768]{1,0:T(8,128)S(1)} collective-permute-done((f32[16,768]{1,0:T(8,128)S(1)}, f32[16,768]{1,0:T(8,128)S(1)}, u32[]{:S(2)}, u32[]{:S(2)}) %collective-permute-start.11) | collective-permute-done | bytes 49184 | tf_op jit(solution)/shard_map/ppermute | solution.py:568
  (48 shorter events, 6.2 us)
Async XLA Ops:
  0.6 30.4 %slice-start = ((s8[4718592]{0:T(1024)(128)(4,1)}), s8[4194304]{0:T(1024)(128)(4,1)S(1)}, s32[]{:S(2)}) async-start(s8[4718592]{0:T(1024)(128)(4,1)} %bitcast.7), calls=%async_computation.3 | async-start | bytes 8388608
  0.6 30.4 %slice-start.1 = ((s8[4718592]{0:T(1024)(128)(4,1)}), s8[524288]{0:T(1024)(128)(4,1)S(1)}, s32[]{:S(2)}) async-start(s8[4718592]{0:T(1024)(128)(4,1)} %bitcast.7), calls=%async_computation.4 | async-start | bytes 1048576
  0.7 30.4 %copy-start = (bf16[1,3072,768]{2,1,0:T(8,128)(2,1)S(1)}, bf16[1,3072,768]{2,1,0:T(8,128)(2,1)}, u32[]{:S(2)}) copy-start(bf16[1,3072,768]{2,1,0:T(8,128)(2,1)} %w2_hbm.3) | copy-start | bytes 14155780
  28.0 36.4 %collective-permute-start.1 = (bf16[256,1536]{1,0:T(8,128)(2,1)S(1)}, bf16[256,1536]{1,0:T(8,128)(2,1)S(1)}, u32[]{:S(2)}, u32[]{:S(2)}) collective-permute-start(bf16[256,1536]{1,0:T(8,128)(2,1)S(1)} %bitcast.9), channel_id=1, source_target_pairs={{0,96},{32,0},{64,32},{96,64},{1,97},{33,1},{65,33},{97,65},{2,98}... | collective-permute-start | bytes 2359304 | tf_op jit(solution)/shard_map/ppermute | solution.py:568
  31.0 36.8 %collective-permute-start = (bf16[256,1536]{1,0:T(8,128)(2,1)S(1)}, bf16[256,1536]{1,0:T(8,128)(2,1)S(1)}, u32[]{:S(2)}, u32[]{:S(2)}) collective-permute-start(bf16[256,1536]{1,0:T(8,128)(2,1)S(1)} %bitcast.10), channel_id=1, source_target_pairs={{0,32},{32,64},{64,96},{96,0},{1,33},{33,65},{65,97},{97,1},{2,34}... | collective-permute-start | bytes 2359304 | tf_op jit(solution)/shard_map/ppermute | solution.py:568
  38.2 42.0 %collective-permute-start.2 = (bf16[256,1536]{1,0:T(8,128)(2,1)S(1)}, bf16[256,1536]{1,0:T(8,128)(2,1)S(1)}, u32[]{:S(2)}, u32[]{:S(2)}) collective-permute-start(bf16[256,1536]{1,0:T(8,128)(2,1)S(1)} %bitcast.12), channel_id=1, source_target_pairs={{0,64},{32,96},{64,0},{96,32},{1,65},{33,97},{65,1},{97,33},{2,66}... | collective-permute-start | bytes 2359304 | tf_op jit(solution)/shard_map/ppermute | solution.py:568
  40.5 31.6 %all-to-all-start.1 = ((bf16[16,16,1536]{2,1,0:T(8,128)(2,1)}), bf16[16,16,1536]{2,1,0:T(8,128)(2,1)}, u32[]{:S(2)}, u32[]{:S(2)}) async-start(bf16[16,16,1536]{2,1,0:T(8,128)(2,1)} %bitcast.17), calls=%async_computation.1 | async-start | bytes 1572864 | tf_op jit(solution)/shard_map/all_to_all | solution.py:585
  80.1 8.0 %copy-start.5 = (bf16[4,64,768]{2,1,0:T(8,128)(2,1)}, bf16[4,64,768]{2,1,0:T(8,128)(2,1)S(1)}, u32[]{:S(2)}) copy-start(bf16[4,64,768]{2,1,0:T(8,128)(2,1)S(1)} %get-tuple-element.41.slots_ref) | copy-start | bytes 1179652
  80.2 8.0 %copy-start.7 = (bf16[4,16,784]{2,1,0:T(8,128)(2,1)}, bf16[4,16,784]{2,1,0:T(8,128)(2,1)S(1)}, u32[]{:S(2)}) copy-start(bf16[4,16,784]{2,1,0:T(8,128)(2,1)S(1)} %get-tuple-element.40.gl_ref) | copy-start | bytes 301060
  80.2 8.0 %collective-permute-start.3 = (f32[16,768]{1,0:T(8,128)S(1)}, f32[16,768]{1,0:T(8,128)S(1)}, u32[]{:S(2)}, u32[]{:S(2)}) collective-permute-start(f32[16,768]{1,0:T(8,128)S(1)} %get-tuple-element.44), channel_id=1, source_target_pairs={{0,16},{16,0},{1,17},{17,1},{2,18},{18,2},{3,19},{19,3},{4,20},{20... | collective-permute-start | bytes 147464 | tf_op jit(solution)/shard_map/ppermute | solution.py:568
  88.9 28.5 %all-to-all-start.2 = ((bf16[8,96,768]{2,1,0:T(8,128)(2,1)}), bf16[8,96,768]{2,1,0:T(8,128)(2,1)S(1)}, u32[]{:S(2)}, u32[]{:S(2)}) async-start(bf16[8,96,768]{2,1,0:T(8,128)(2,1)} %get-tuple-element.56), calls=%async_computation.2 | async-start | bytes 2359296 | tf_op jit(solution)/shard_map/all_to_all | solution.py:607
  92.4 7.9 %collective-permute-start.4 = (f32[16,768]{1,0:T(8,128)}, f32[16,768]{1,0:T(8,128)S(1)}, u32[]{:S(2)}, u32[]{:S(2)}) collective-permute-start(f32[16,768]{1,0:T(8,128)} %add.30), channel_id=1, source_target_pairs={{0,1},{1,0},{2,3},{3,2},{4,5},{5,4},{6,7},{7,6},{8,9},{9,8},{10,11... | collective-permute-start | bytes 147464 | tf_op jit(solution)/shard_map/ppermute | solution.py:568
  92.5 20.4 %copy-start.4 = (f32[4,16,784]{2,1,0:T(8,128)S(1)}, f32[4,16,784]{2,1,0:T(8,128)}, u32[]{:S(2)}) copy-start(f32[4,16,784]{2,1,0:T(8,128)} %get-tuple-element.38.disp_hbm.disp_ref) | copy-start | bytes 602116
  92.5 20.4 %copy-start.6 = (bf16[4,64,768]{2,1,0:T(8,128)(2,1)S(1)}, bf16[4,64,768]{2,1,0:T(8,128)(2,1)}, u32[]{:S(2)}) copy-start(bf16[4,64,768]{2,1,0:T(8,128)(2,1)} %copy-done.5) | copy-start | bytes 1179652
  92.5 20.4 %copy-start.8 = (bf16[4,16,784]{2,1,0:T(8,128)(2,1)S(1)}, bf16[4,16,784]{2,1,0:T(8,128)(2,1)}, u32[]{:S(2)}) copy-start(bf16[4,16,784]{2,1,0:T(8,128)(2,1)} %copy-done.7) | copy-start | bytes 301060
  92.6 20.3 %copy-start.9 = (bf16[768,16]{0,1:T(8,128)(2,1)S(1)}, bf16[768,16]{0,1:T(8,128)(2,1)}, u32[]{:S(2)}) copy-start(bf16[768,16]{0,1:T(8,128)(2,1)} %param.6) | copy-start | bytes 73732
  97.0 20.6 %collective-permute-start.12 = (bf16[384,768]{1,0:T(8,128)(2,1)}, bf16[384,768]{1,0:T(8,128)(2,1)S(1)}, u32[]{:S(2)}, u32[]{:S(2)}) collective-permute-start(bf16[384,768]{1,0:T(8,128)(2,1)} %get-tuple-element.54), channel_id=1, source_target_pairs={{0,16},{16,0},{1,17},{17,1},{2,18},{18,2},{3,19},{19,3},{4,20},{20... | collective-permute-start | bytes 1769480 | tf_op jit(solution)/shard_map/ppermute | solution.py:568
  100.4 4.5 %collective-permute-start.7 = (f32[16,768]{1,0:T(8,128)S(1)}, f32[16,768]{1,0:T(8,128)S(1)}, u32[]{:S(2)}, u32[]{:S(2)}) collective-permute-start(f32[16,768]{1,0:T(8,128)S(1)} %add.31), channel_id=1, source_target_pairs={{0,12},{4,0},{8,4},{12,8},{1,13},{5,1},{9,5},{13,9},{2,14},{6,2},{... | collective-permute-start | bytes 147464 | tf_op jit(solution)/shard_map/ppermute | solution.py:568
  101.6 6.0 %collective-permute-start.6 = (f32[16,768]{1,0:T(8,128)S(1)}, f32[16,768]{1,0:T(8,128)S(1)}, u32[]{:S(2)}, u32[]{:S(2)}) collective-permute-start(f32[16,768]{1,0:T(8,128)S(1)} %add.31), channel_id=1, source_target_pairs={{0,8},{4,12},{8,0},{12,4},{1,9},{5,13},{9,1},{13,5},{2,10},{6,14},... | collective-permute-start | bytes 147464 | tf_op jit(solution)/shard_map/ppermute | solution.py:568
  103.1 5.3 %collective-permute-start.5 = (f32[16,768]{1,0:T(8,128)S(1)}, f32[16,768]{1,0:T(8,128)S(1)}, u32[]{:S(2)}, u32[]{:S(2)}) collective-permute-start(f32[16,768]{1,0:T(8,128)S(1)} %add.31), channel_id=1, source_target_pairs={{0,4},{4,8},{8,12},{12,0},{1,5},{5,9},{9,13},{13,1},{2,6},{6,10},{... | collective-permute-start | bytes 147464 | tf_op jit(solution)/shard_map/ppermute | solution.py:568
  108.4 8.1 %collective-permute-start.10 = (f32[16,768]{1,0:T(8,128)S(1)}, f32[16,768]{1,0:T(8,128)S(1)}, u32[]{:S(2)}, u32[]{:S(2)}) collective-permute-start(f32[16,768]{1,0:T(8,128)S(1)} %add_add_fusion.1), channel_id=1, source_target_pairs={{0,96},{32,0},{64,32},{96,64},{1,97},{33,1},{65,33},{97,65},{2,98}... | collective-permute-start | bytes 147464 | tf_op jit(solution)/shard_map/ppermute | solution.py:568
  111.2 5.6 %collective-permute-start.9 = (f32[16,768]{1,0:T(8,128)S(1)}, f32[16,768]{1,0:T(8,128)S(1)}, u32[]{:S(2)}, u32[]{:S(2)}) collective-permute-start(f32[16,768]{1,0:T(8,128)S(1)} %add_add_fusion.1), channel_id=1, source_target_pairs={{0,64},{32,96},{64,0},{96,32},{1,65},{33,97},{65,1},{97,33},{2,66}... | collective-permute-start | bytes 147464 | tf_op jit(solution)/shard_map/ppermute | solution.py:568
  112.0 5.3 %collective-permute-start.8 = (f32[16,768]{1,0:T(8,128)S(1)}, f32[16,768]{1,0:T(8,128)S(1)}, u32[]{:S(2)}, u32[]{:S(2)}) collective-permute-start(f32[16,768]{1,0:T(8,128)S(1)} %add_add_fusion.1), channel_id=1, source_target_pairs={{0,32},{32,64},{64,96},{96,0},{1,33},{33,65},{65,97},{97,1},{2,34}... | collective-permute-start | bytes 147464 | tf_op jit(solution)/shard_map/ppermute | solution.py:568
  117.3 4.2 %collective-permute-start.11 = (f32[16,768]{1,0:T(8,128)S(1)}, f32[16,768]{1,0:T(8,128)S(1)}, u32[]{:S(2)}, u32[]{:S(2)}) collective-permute-start(f32[16,768]{1,0:T(8,128)S(1)} %add_add_fusion), channel_id=1, source_target_pairs={{0,2},{2,0},{1,3},{3,1},{4,6},{6,4},{5,7},{7,5},{8,10},{10,8},{9,1... | collective-permute-start | bytes 147464 | tf_op jit(solution)/shard_map/ppermute | solution.py:568
  (4 other events, 21.6 us)

commit v7 on v5

--- a/solution.py
+++ b/solution.py
@@ -318,7 +318,7 @@
 
 def first_grads_body(
     own_ref, right_ref, left_ref, far_a, far_b, pre_own, pre_near, w1_hbm, w2_hbm,
-    keep_ref, send_ref, act_far, rows, pre, far, acc, w1, w2, sem, pre_sem
+    keep_ref, send_ref, act_far, rows, pre, far, w1, w2, sem, pre_sem
 ):
     feat = w1.shape[0]
     xh = lax.axis_index("xh")
@@ -335,9 +335,13 @@
         load.wait()
     act, pre_far = hidden_terms(far[:, :feat], far[:, feat:], w1[...], w2[...])
     act_far[...] = act
-    acc[...] = (total + contract(far[:, :feat], pre_far, 0, 0)).reshape(acc.shape)
-    send_ref[...] = acc[:, pl.ds(1 - xh, 1)].reshape(send_ref.shape).astype(bf16)
-    keep_ref[...] = acc[:, pl.ds(xh, 1)].reshape(keep_ref.shape)
+    total = total + contract(far[:, :feat], pre_far, 0, 0)
+    parts, own, _ = keep_ref.shape
+    for i in range(parts):
+        low = total[XH * i * own : (XH * i + 1) * own]
+        high = total[(XH * i + 1) * own : XH * (i + 1) * own]
+        send_ref[i] = jnp.where(xh == 0, high, low).astype(bf16)
+        keep_ref[i] = jnp.where(xh == 0, low, high)
 
 
 def first_grads(pieces, pre_own, pre_near, w_in, w_out, parts):
@@ -359,7 +363,6 @@
             pltpu.VMEM((near_count, feat), bf16),
             pltpu.VMEM((near_count, tile), bf16),
             pltpu.VMEM((far_count, 2 * feat), bf16),
-            pltpu.VMEM((parts, XH, own, tile), f32),
             pltpu.VMEM((feat, tile), bf16),
             pltpu.VMEM((tile, feat), bf16),
             pltpu.SemaphoreType.DMA((2,)),
@@ -416,22 +419,26 @@
     )(*pieces, pinned(acts[0]), pinned(acts[1]), acts[2])
 
 
-def widen_body(in_ref, out_ref):
-    parts, _, tile = in_ref.shape
+def finish_body(spread_ref, keep_ref, came_ref, first_ref, second_ref):
+    parts, _, tile = spread_ref.shape
     for i in range(parts):
-        out_ref[0, :, i * tile : (i + 1) * tile] = in_ref[i].astype(f32)
-
-
-def widen(spread):
+        first_ref[0, :, i * tile : (i + 1) * tile] = spread_ref[i].astype(f32)
+    second_ref[0] = keep_ref[...] + came_ref[...].astype(f32)
+
+
+def finish(spread, keep, came):
     parts, own, tile = spread.shape
     return pl.pallas_call(
-        widen_body,
-        in_specs=[IN_VMEM],
-        out_specs=IN_VMEM,
-        out_shape=jax.ShapeDtypeStruct((1, own, parts * tile), f32),
-        compiler_params=params(4),
-        name="widen",
-    )(spread)
+        finish_body,
+        in_specs=[IN_VMEM] * 3,
+        out_specs=[IN_VMEM] * 2,
+        out_shape=[
+            jax.ShapeDtypeStruct((1, own, parts * tile), f32),
+            jax.ShapeDtypeStruct((1,) + keep.shape, f32),
+        ],
+        compiler_params=params(8),
+        name="finish",
+    )(spread, keep, came)
 
 
 def token_logits_body(
@@ -595,19 +602,18 @@
         total = axis_sum(router_term, "xh", XH)
         total, send_in = lax.optimization_barrier((total, send_in))
         came_in = shift(send_in, "xh", 1, XH)
-        total = axis_sum(axis_sum(total, "core", 2), "y", ny)
+        total = axis_sum(axis_sum(total, "core", 2), "xl", 2)
         total, keep_out, send_out = lax.optimization_barrier((total, keep_out, send_out))
-        total = axis_sum(total, "z", nz)
+        total = axis_sum(total, "y", ny)
         came_in, send_out = lax.optimization_barrier((came_in, send_out))
         came_out = shift(send_out, "xh", 1, XH)
         part_in = (keep_in + came_in.astype(f32)).astype(bf16)
         total, part_in, grad_logits = lax.optimization_barrier((total, part_in, grad_logits))
         spread = lax.all_to_all(part_in, "y", split_axis=0, concat_axis=0, tiled=True)
-        grad_router = axis_sum(total, "xl", 2).T
-        grad_second = keep_out + came_out.astype(f32)
-        grad_first = widen(spread)
+        grad_router = axis_sum(total, "z", nz).T
+        grad_first, grad_second = finish(spread, keep_out, came_out)
         grad_tok = token_grads(grad_logits, slot_grads, dispatch, rt)
-        return grad_tok, grad_router, grad_first, grad_second[None]
+        return grad_tok, grad_router, grad_first, grad_second
 
     return jax.shard_map(
         on_device,

time: 109 us -> 114 us (1.046)
  waiting for transfers between devices: 16.6 us -> 20.4 us
  starting transfers between devices: 27.7 us -> 29.1 us
    ppermute x15, waiting for transfers between devices: 16.6 us -> 20.4 us  [shift(): lax.ppermute(value, axis, [(i, (i + by) % count) for i in range(count)])]
    ppermute x15, starting transfers between devices: 20.4 us -> 21.9 us  [shift(): lax.ppermute(value, axis, [(i, (i + by) % count) for i in range(count)])]
  transfers between devices with their start and end apart: 17 -> 17, of which waited for: 8 -> 8; matrix products, arithmetic and copies ran while one was open for 3% -> 3% of each run, Pallas kernels for 30% -> 27%
where the time goes in v7:
time: 114 us; the launch traced here: 113 us
  Pallas kernels  39.7 us (35%)
  starting transfers between devices  29.1 us (26%)
  waiting for transfers between devices  20.4 us (18%)
  blocking collectives  19.9 us (17%)
  local copies, waits for them, and re-layouts  1.61 us (1%)
  other arithmetic  1.6 us (1%)
    ppermute x15, starting transfers between devices, shift(): lax.ppermute(value, axis, [(i, (i + by) % count) for i in range(count)])  21.9 us
    ppermute x15, waiting for transfers between devices, shift(): lax.ppermute(value, axis, [(i, (i + by) % count) for i in range(count)])  20.4 us
    all_to_all x1, blocking collectives, over_experts(): lax.all_to_all(value, ex_axes, split_axis=0, concat_axis=0, tiled=True)  19.9 us
    pallas_call x1, Pallas kernels, expert_rows(): pl.pallas_call(expert_body, in_specs=[IN_VMEM] * 3, out_specs=[IN_PLACE]...  7.12 us
    pallas_call x1, Pallas kernels, token_forward(): pl.pallas_call(token_forward_body, in_specs=[IN_PLACE] * 3, out_specs=[IN...  7.11 us
    pallas_call x1, Pallas kernels, token_logits(): pl.pallas_call(token_logits_body, in_specs=[IN_VMEM] + [IN_PLACE] * 4, ou...  6.68 us
    pallas_call x1, Pallas kernels, first_grads(): pl.pallas_call(first_grads_body, in_specs=[IN_VMEM] * 5 + [IN_PLACE] * 4,...  5.17 us
    pallas_call x1, Pallas kernels, near_terms(): pl.pallas_call(near_terms_body, in_specs=[IN_VMEM] * 2 + [IN_PLACE] * 2,...  4.29 us
  transfers between devices with their start and end apart: 17, of which 8 were waited for; matrix products, arithmetic and copies ran while one was open for 3% of the time, Pallas kernels for 27%

profile of v7, /device:TPU:0, one launch (start us, length us, event | category | flops | bytes accessed | tf_op | source)
XLA Modules:
  0.0 113.2 jit_solution(7801679928373068390)
XLA Ops:
  0.7 7.1 %token_forward.1 = (bf16[16,16,1536]{2,1,0:T(8,128)(2,1)S(1)}, f32[4,16,784]{2,1,0:T(8,128)}, f32[4,16,784]{2,1,0:T(8,128)}) custom-call(bf16[16,768]{1,0:T(8,128)(2,1)} %bitcast.12, bf16[3136,768]{1,0:T(8,128)(2,1)} %x_hbm.3, bf16[3136,768]{1,0:T(8,128)(2,1)} %g_hbm.3), custom_call_target="tpu_custom_call" | custom-call | tf_op jit(solution)/shard_map/token_forward/pallas_call | solution.py:163
  7.8 19.9 %all_to_all.15 = bf16[16,16,1536]{2,1,0:T(8,128)(2,1)S(1)} all-to-all(bf16[16,16,1536]{2,1,0:T(8,128)(2,1)S(1)} %get-tuple-element.38), channel_id=1, replica_groups=mesh['y'=4,'xh'=2,'z'=4,'xl'=2,'core'=2] {'z','xl','core'}, dimensions={0} | all-to-all | bytes 1572864 | tf_op jit(solution)/shard_map/all_to_all | solution.py:580
  27.7 3.0 %collective-permute-start.2 = (bf16[256,1536]{1,0:T(8,128)(2,1)S(1)}, bf16[256,1536]{1,0:T(8,128)(2,1)S(1)}, u32[]{:S(2)}, u32[]{:S(2)}) collective-permute-start(bf16[256,1536]{1,0:T(8,128)(2,1)S(1)} %bitcast.7), channel_id=1, source_target_pairs={{0,96},{32,0},{64,32},{96,64},{1,97},{33,1},{65,33},{97,65},{2,98}... | collective-permute-start | bytes 2359304 | tf_op jit(solution)/shard_map/ppermute | solution.py:563
  30.7 7.1 %expert_rows.1 = (bf16[256,1536]{1,0:T(8,128)(2,1)}, bf16[256,768]{1,0:T(8,128)(2,1)}, bf16[256,768]{1,0:T(8,128)(2,1)}) custom-call(bf16[256,1536]{1,0:T(8,128)(2,1)S(1)} %bitcast.9, bf16[1,768,3072]{2,1,0:T(8,128)(2,1)S(1)} %bitcast.6, bf16[1,3072,768]{2,1,0:T(8,128)(2,1)S(1)} %copy-done), custom_call_target="tpu_custom_call" | custom-call | tf_op jit(solution)/shard_map/expert_rows/pallas_call | solution.py:238
  37.9 3.6 %all-to-all-start.1 = ((bf16[16,16,1536]{2,1,0:T(8,128)(2,1)}), bf16[16,16,1536]{2,1,0:T(8,128)(2,1)S(1)}, u32[]{:S(2)}, u32[]{:S(2)}) async-start(bf16[16,16,1536]{2,1,0:T(8,128)(2,1)} %bitcast.14), calls=%async_computation.1 | async-start | bytes 1572864 | tf_op jit(solution)/shard_map/all_to_all | solution.py:580
  41.5 5.7 %collective-permute-done.2.left_ref = bf16[256,1536]{1,0:T(8,128)(2,1)S(1)} collective-permute-done((bf16[256,1536]{1,0:T(8,128)(2,1)S(1)}, bf16[256,1536]{1,0:T(8,128)(2,1)S(1)}, u32[]{:S(2)}, u32[]{:S(2)}) %collective-permute-start.2) | collective-permute-done | bytes 786464 | tf_op jit(solution)/shard_map/ppermute | solution.py:563
  48.0 3.7 %collective-permute-start.3 = (bf16[128,1536]{1,0:T(8,128)(2,1)}, bf16[128,1536]{1,0:T(8,128)(2,1)S(1)}, u32[]{:S(2)}, u32[]{:S(2)}) collective-permute-start(bf16[128,1536]{1,0:T(8,128)(2,1)} %slice.9), channel_id=1, source_target_pairs={{0,96},{32,0},{64,32},{96,64},{1,97},{33,1},{65,33},{97,65},{2,98}... | collective-permute-start | bytes 1179656 | tf_op jit(solution)/shard_map/ppermute | solution.py:563
  52.4 4.3 %near_terms.1 = (bf16[512,768]{1,0:T(8,128)(2,1)}, bf16[512,768]{1,0:T(8,128)(2,1)}) custom-call(bf16[256,1536]{1,0:T(8,128)(2,1)S(1)} %collective-permute-done.right_ref, bf16[256,1536]{1,0:T(8,128)(2,1)S(1)} %collective-permute-done.2.left_ref, bf16[1,768,3072]{2,1,0:T(8,128)(2,1)} %w1_hbm.3, bf16[1,3072,768]{2,1,0:T(8,128)(2,1)} %w2_hbm.3), custom_call_target="tpu_custom_call" | custom-call | tf_op jit(solution)/shard_map/near_terms/pallas_call | solution.py:300
  56.8 6.7 %token_logits.1 = (bf16[4,16,784]{2,1,0:T(8,128)(2,1)S(1)}, bf16[4,64,768]{2,1,0:T(8,128)(2,1)S(1)}, f32[16,768]{1,0:T(8,128)S(1)}) custom-call(bf16[16,16,1536]{2,1,0:T(8,128)(2,1)S(1)} %all-to-all-done.1.back_ref, bf16[3136,768]{1,0:T(8,128)(2,1)} %x_hbm.3, bf16[3136,768]{1,0:T(8,128)(2,1)} %g_hbm.3, f32[4,16,784]{2,1,0:T(8,128)} %get-tuple-element.43.disp_hbm.disp_ref, ...), custom_call_target="tpu_custom_call" | custom-call | tf_op jit(solution)/shard_map/token_logits/pallas_call | solution.py:512
  63.5 2.8 %collective-permute-start.4 = (f32[16,768]{1,0:T(8,128)S(1)}, f32[16,768]{1,0:T(8,128)S(1)}, u32[]{:S(2)}, u32[]{:S(2)}) collective-permute-start(f32[16,768]{1,0:T(8,128)S(1)} %get-tuple-element.46), channel_id=1, source_target_pairs={{0,16},{16,0},{1,17},{17,1},{2,18},{18,2},{3,19},{19,3},{4,20},{20... | collective-permute-start | bytes 147464 | tf_op jit(solution)/shard_map/ppermute | solution.py:563
  66.3 5.2 %first_grads.1 = (f32[4,96,768]{2,1,0:T(8,128)S(1)}, bf16[4,96,768]{2,1,0:T(8,128)(2,1)S(1)}, bf16[256,768]{1,0:T(8,128)(2,1)S(1)}) custom-call(bf16[256,1536]{1,0:T(8,128)(2,1)S(1)} %bitcast.10, bf16[256,1536]{1,0:T(8,128)(2,1)S(1)} %collective-permute-done.right_ref, bf16[256,1536]{1,0:T(8,128)(2,1)S(1)} %collective-permute-done.2.left_ref, ...), custom_call_target="tpu_custom_call" | custom-call | tf_op jit(solution)/shard_map/first_grads/pallas_call | solution.py:353
  72.4 1.2 %collective-permute-done.5 = f32[16,768]{1,0:T(8,128)S(1)} collective-permute-done((f32[16,768]{1,0:T(8,128)S(1)}, f32[16,768]{1,0:T(8,128)S(1)}, u32[]{:S(2)}, u32[]{:S(2)}) %collective-permute-start.5) | collective-permute-done | bytes 49184 | tf_op jit(solution)/shard_map/ppermute | solution.py:563
  73.6 1.9 %collective-permute-start.6 = (f32[16,768]{1,0:T(8,128)S(1)}, f32[16,768]{1,0:T(8,128)S(1)}, u32[]{:S(2)}, u32[]{:S(2)}) collective-permute-start(f32[16,768]{1,0:T(8,128)S(1)} %add.31), channel_id=1, source_target_pairs={{0,2},{2,0},{1,3},{3,1},{4,6},{6,4},{5,7},{7,5},{8,10},{10,8},{9,1... | collective-permute-start | bytes 147464 | tf_op jit(solution)/shard_map/ppermute | solution.py:563
  75.5 4.1 %second_grads.1 = (f32[384,768]{1,0:T(8,128)S(1)}, bf16[384,768]{1,0:T(8,128)(2,1)}) custom-call(bf16[256,1536]{1,0:T(8,128)(2,1)S(1)} %bitcast.11, bf16[256,1536]{1,0:T(8,128)(2,1)S(1)} %collective-permute-done.right_ref, bf16[256,1536]{1,0:T(8,128)(2,1)S(1)} %collective-permute-done.2.left_ref, bf16[128,1536]{1,0:T(8,128)(2,1)} %collective-permute-done.1.far_a, ...), custom_call_target="tpu_custom_call" | custom-call | tf_op jit(solution)/shard_map/second_grads/pallas_call | solution.py:404
  79.7 7.1 %collective-permute-done.6 = f32[16,768]{1,0:T(8,128)S(1)} collective-permute-done((f32[16,768]{1,0:T(8,128)S(1)}, f32[16,768]{1,0:T(8,128)S(1)}, u32[]{:S(2)}, u32[]{:S(2)}) %collective-permute-start.6) | collective-permute-done | bytes 49184 | tf_op jit(solution)/shard_map/ppermute | solution.py:563
  86.8 3.0 %collective-permute-start.9 = (f32[16,768]{1,0:T(8,128)S(1)}, f32[16,768]{1,0:T(8,128)S(1)}, u32[]{:S(2)}, u32[]{:S(2)}) collective-permute-start(f32[16,768]{1,0:T(8,128)S(1)} %add.32), channel_id=1, source_target_pairs={{0,96},{32,0},{64,32},{96,64},{1,97},{33,1},{65,33},{97,65},{2,98}... | collective-permute-start | bytes 147464 | tf_op jit(solution)/shard_map/ppermute | solution.py:563
  89.8 0.9 collective-permute-start.7
  91.5 3.9 %collective-permute-done.8 = f32[16,768]{1,0:T(8,128)S(1)} collective-permute-done((f32[16,768]{1,0:T(8,128)S(1)}, f32[16,768]{1,0:T(8,128)S(1)}, u32[]{:S(2)}, u32[]{:S(2)}) %collective-permute-start.8) | collective-permute-done | bytes 49184 | tf_op jit(solution)/shard_map/ppermute | solution.py:563
  95.7 2.8 %collective-permute-start.14 = (bf16[384,768]{1,0:T(8,128)(2,1)}, bf16[384,768]{1,0:T(8,128)(2,1)S(1)}, u32[]{:S(2)}, u32[]{:S(2)}) collective-permute-start(bf16[384,768]{1,0:T(8,128)(2,1)} %get-tuple-element.69), channel_id=1, source_target_pairs={{0,16},{16,0},{1,17},{17,1},{2,18},{18,2},{3,19},{19,3},{4,20},{20... | collective-permute-start | bytes 1769480 | tf_op jit(solution)/shard_map/ppermute | solution.py:563
  99.4 3.6 %all-to-all-start.2 = ((bf16[4,96,768]{2,1,0:T(8,128)(2,1)}), bf16[4,96,768]{2,1,0:T(8,128)(2,1)S(1)}, u32[]{:S(2)}, u32[]{:S(2)}) async-start(bf16[4,96,768]{2,1,0:T(8,128)(2,1)} %add_convert_fusion), calls=%async_computation.2 | async-start | bytes 1179648 | tf_op jit(solution)/shard_map/all_to_all | solution.py:612
  104.0 1.8 %collective-permute-start.12 = (f32[16,768]{1,0:T(8,128)S(1)}, f32[16,768]{1,0:T(8,128)S(1)}, u32[]{:S(2)}, u32[]{:S(2)}) collective-permute-start(f32[16,768]{1,0:T(8,128)S(1)} %add_add_fusion), channel_id=1, source_target_pairs={{0,8},{4,12},{8,0},{12,4},{1,9},{5,13},{9,1},{13,5},{2,10},{6,14},... | collective-permute-start | bytes 147464 | tf_op jit(solution)/shard_map/ppermute | solution.py:563
  105.9 3.6 %token_grads.1 = bf16[3136,768]{1,0:T(8,128)(2,1)} custom-call(bf16[4,16,784]{2,1,0:T(8,128)(2,1)S(1)} %copy-done.7, bf16[4,64,768]{2,1,0:T(8,128)(2,1)S(1)} %copy-done.5, f32[4,16,784]{2,1,0:T(8,128)S(1)} %copy-done.3, bf16[16,768]{1,0:T(8,128)(2,1)S(1)} %bitcast.13), custom_call_target="tpu_custom_call" | custom-call | tf_op jit(solution)/shard_map/token_grads/pallas_call | solution.py:546
  109.6 1.5 %collective-permute-done.11 = f32[16,768]{1,0:T(8,128)S(1)} collective-permute-done((f32[16,768]{1,0:T(8,128)S(1)}, f32[16,768]{1,0:T(8,128)S(1)}, u32[]{:S(2)}, u32[]{:S(2)}) %collective-permute-start.11) | collective-permute-done | bytes 49184 | tf_op jit(solution)/shard_map/ppermute | solution.py:563
  111.7 1.6 %finish.1 = (f32[1,96,3072]{2,1,0:T(8,128)}, f32[1,384,768]{2,1,0:T(8,128)}) custom-call(bf16[4,96,768]{2,1,0:T(8,128)(2,1)S(1)} %all-to-all-done.2.spread_ref, f32[384,768]{1,0:T(8,128)S(1)} %copy-done.2, bf16[384,768]{1,0:T(8,128)(2,1)S(1)} %collective-permute-done.14.came_ref), custom_call_target="tpu_custom_call" | custom-call | tf_op jit(solution)/shard_map/finish/pallas_call | solution.py:431
  (50 shorter events, 6.2 us)
Async XLA Ops:
  0.6 30.1 %slice-start = ((s8[4718592]{0:T(1024)(128)(4,1)}), s8[4194304]{0:T(1024)(128)(4,1)S(1)}, s32[]{:S(2)}) async-start(s8[4718592]{0:T(1024)(128)(4,1)} %bitcast.5), calls=%async_computation.3 | async-start | bytes 8388608
  0.6 30.1 %slice-start.1 = ((s8[4718592]{0:T(1024)(128)(4,1)}), s8[524288]{0:T(1024)(128)(4,1)S(1)}, s32[]{:S(2)}) async-start(s8[4718592]{0:T(1024)(128)(4,1)} %bitcast.5), calls=%async_computation.4 | async-start | bytes 1048576
  0.7 30.1 %copy-start = (bf16[1,3072,768]{2,1,0:T(8,128)(2,1)S(1)}, bf16[1,3072,768]{2,1,0:T(8,128)(2,1)}, u32[]{:S(2)}) copy-start(bf16[1,3072,768]{2,1,0:T(8,128)(2,1)} %w2_hbm.3) | copy-start | bytes 14155780
  27.7 19.5 %collective-permute-start.2 = (bf16[256,1536]{1,0:T(8,128)(2,1)S(1)}, bf16[256,1536]{1,0:T(8,128)(2,1)S(1)}, u32[]{:S(2)}, u32[]{:S(2)}) collective-permute-start(bf16[256,1536]{1,0:T(8,128)(2,1)S(1)} %bitcast.7), channel_id=1, source_target_pairs={{0,96},{32,0},{64,32},{96,64},{1,97},{33,1},{65,33},{97,65},{2,98}... | collective-permute-start | bytes 2359304 | tf_op jit(solution)/shard_map/ppermute | solution.py:563
  30.7 21.0 %collective-permute-start = (bf16[256,1536]{1,0:T(8,128)(2,1)S(1)}, bf16[256,1536]{1,0:T(8,128)(2,1)S(1)}, u32[]{:S(2)}, u32[]{:S(2)}) collective-permute-start(bf16[256,1536]{1,0:T(8,128)(2,1)S(1)} %bitcast.8), channel_id=1, source_target_pairs={{0,32},{32,64},{64,96},{96,0},{1,33},{33,65},{65,97},{97,1},{2,34}... | collective-permute-start | bytes 2359304 | tf_op jit(solution)/shard_map/ppermute | solution.py:563
  37.9 18.9 %all-to-all-start.1 = ((bf16[16,16,1536]{2,1,0:T(8,128)(2,1)}), bf16[16,16,1536]{2,1,0:T(8,128)(2,1)S(1)}, u32[]{:S(2)}, u32[]{:S(2)}) async-start(bf16[16,16,1536]{2,1,0:T(8,128)(2,1)} %bitcast.14), calls=%async_computation.1 | async-start | bytes 1572864 | tf_op jit(solution)/shard_map/all_to_all | solution.py:580
  48.0 15.5 %collective-permute-start.3 = (bf16[128,1536]{1,0:T(8,128)(2,1)}, bf16[128,1536]{1,0:T(8,128)(2,1)S(1)}, u32[]{:S(2)}, u32[]{:S(2)}) collective-permute-start(bf16[128,1536]{1,0:T(8,128)(2,1)} %slice.9), channel_id=1, source_target_pairs={{0,96},{32,0},{64,32},{96,64},{1,97},{33,1},{65,33},{97,65},{2,98}... | collective-permute-start | bytes 1179656 | tf_op jit(solution)/shard_map/ppermute | solution.py:563
  52.4 11.0 %collective-permute-start.1 = (bf16[128,1536]{1,0:T(8,128)(2,1)}, bf16[128,1536]{1,0:T(8,128)(2,1)}, u32[]{:S(2)}, u32[]{:S(2)}) collective-permute-start(bf16[128,1536]{1,0:T(8,128)(2,1)} %slice.8), channel_id=1, source_target_pairs={{0,32},{32,64},{64,96},{96,0},{1,33},{33,65},{65,97},{97,1},{2,34}... | collective-permute-start | bytes 1179656 | tf_op jit(solution)/shard_map/ppermute | solution.py:563
  63.4 8.0 %copy-start.4 = (bf16[4,64,768]{2,1,0:T(8,128)(2,1)}, bf16[4,64,768]{2,1,0:T(8,128)(2,1)S(1)}, u32[]{:S(2)}) copy-start(bf16[4,64,768]{2,1,0:T(8,128)(2,1)S(1)} %get-tuple-element.65.slots_ref) | copy-start | bytes 1179652
  63.5 8.0 %copy-start.6 = (bf16[4,16,784]{2,1,0:T(8,128)(2,1)}, bf16[4,16,784]{2,1,0:T(8,128)(2,1)S(1)}, u32[]{:S(2)}) copy-start(bf16[4,16,784]{2,1,0:T(8,128)(2,1)S(1)} %get-tuple-element.64.gl_ref) | copy-start | bytes 301060
  63.5 8.0 %collective-permute-start.4 = (f32[16,768]{1,0:T(8,128)S(1)}, f32[16,768]{1,0:T(8,128)S(1)}, u32[]{:S(2)}, u32[]{:S(2)}) collective-permute-start(f32[16,768]{1,0:T(8,128)S(1)} %get-tuple-element.46), channel_id=1, source_target_pairs={{0,16},{16,0},{1,17},{17,1},{2,18},{18,2},{3,19},{19,3},{4,20},{20... | collective-permute-start | bytes 147464 | tf_op jit(solution)/shard_map/ppermute | solution.py:563
  71.5 24.1 %collective-permute-start.10 = (bf16[4,96,768]{2,1,0:T(8,128)(2,1)S(1)}, bf16[4,96,768]{2,1,0:T(8,128)(2,1)S(1)}, u32[]{:S(2)}, u32[]{:S(2)}) collective-permute-start(bf16[4,96,768]{2,1,0:T(8,128)(2,1)S(1)} %get-tuple-element.60), channel_id=1, source_target_pairs={{0,16},{16,0},{1,17},{17,1},{2,18},{18,2},{3,19},{19,3},{4,20},{20... | collective-permute-start | bytes 1769480 | tf_op jit(solution)/shard_map/ppermute | solution.py:563
  72.4 1.2 %collective-permute-start.5 = (f32[16,768]{1,0:T(8,128)S(1)}, f32[16,768]{1,0:T(8,128)S(1)}, u32[]{:S(2)}, u32[]{:S(2)}) collective-permute-start(f32[16,768]{1,0:T(8,128)S(1)} %add.30), channel_id=1, source_target_pairs={{0,1},{1,0},{2,3},{3,2},{4,5},{5,4},{6,7},{7,6},{8,9},{9,8},{10,11... | collective-permute-start | bytes 147464 | tf_op jit(solution)/shard_map/ppermute | solution.py:563
  73.6 13.1 %collective-permute-start.6 = (f32[16,768]{1,0:T(8,128)S(1)}, f32[16,768]{1,0:T(8,128)S(1)}, u32[]{:S(2)}, u32[]{:S(2)}) collective-permute-start(f32[16,768]{1,0:T(8,128)S(1)} %add.31), channel_id=1, source_target_pairs={{0,2},{2,0},{1,3},{3,1},{4,6},{6,4},{5,7},{7,5},{8,10},{10,8},{9,1... | collective-permute-start | bytes 147464 | tf_op jit(solution)/shard_map/ppermute | solution.py:563
  79.7 19.7 %copy-start.1 = (f32[384,768]{1,0:T(8,128)}, f32[384,768]{1,0:T(8,128)S(1)}, u32[]{:S(2)}) copy-start(f32[384,768]{1,0:T(8,128)S(1)} %get-tuple-element.68.keep_ref) | copy-start | bytes 3538948
  86.8 4.8 %collective-permute-start.9 = (f32[16,768]{1,0:T(8,128)S(1)}, f32[16,768]{1,0:T(8,128)S(1)}, u32[]{:S(2)}, u32[]{:S(2)}) collective-permute-start(f32[16,768]{1,0:T(8,128)S(1)} %add.32), channel_id=1, source_target_pairs={{0,96},{32,0},{64,32},{96,64},{1,97},{33,1},{65,33},{97,65},{2,98}... | collective-permute-start | bytes 147464 | tf_op jit(solution)/shard_map/ppermute | solution.py:563
  89.8 5.7 %collective-permute-start.8 = (f32[16,768]{1,0:T(8,128)S(1)}, f32[16,768]{1,0:T(8,128)S(1)}, u32[]{:S(2)}, u32[]{:S(2)}) collective-permute-start(f32[16,768]{1,0:T(8,128)S(1)} %add.32), channel_id=1, source_target_pairs={{0,64},{32,96},{64,0},{96,32},{1,65},{33,97},{65,1},{97,33},{2,66}... | collective-permute-start | bytes 147464 | tf_op jit(solution)/shard_map/ppermute | solution.py:563
  89.8 5.8 %collective-permute-start.7 = (f32[16,768]{1,0:T(8,128)S(1)}, f32[16,768]{1,0:T(8,128)S(1)}, u32[]{:S(2)}, u32[]{:S(2)}) collective-permute-start(f32[16,768]{1,0:T(8,128)S(1)} %add.32), channel_id=1, source_target_pairs={{0,32},{32,64},{64,96},{96,0},{1,33},{33,65},{65,97},{97,1},{2,34}... | collective-permute-start | bytes 147464 | tf_op jit(solution)/shard_map/ppermute | solution.py:563
  95.7 16.0 %collective-permute-start.14 = (bf16[384,768]{1,0:T(8,128)(2,1)}, bf16[384,768]{1,0:T(8,128)(2,1)S(1)}, u32[]{:S(2)}, u32[]{:S(2)}) collective-permute-start(bf16[384,768]{1,0:T(8,128)(2,1)} %get-tuple-element.69), channel_id=1, source_target_pairs={{0,16},{16,0},{1,17},{17,1},{2,18},{18,2},{3,19},{19,3},{4,20},{20... | collective-permute-start | bytes 1769480 | tf_op jit(solution)/shard_map/ppermute | solution.py:563
  99.4 6.5 %copy-start.7 = (bf16[4,16,784]{2,1,0:T(8,128)(2,1)S(1)}, bf16[4,16,784]{2,1,0:T(8,128)(2,1)}, u32[]{:S(2)}) copy-start(bf16[4,16,784]{2,1,0:T(8,128)(2,1)} %copy-done.6) | copy-start | bytes 301060
  99.4 12.3 %all-to-all-start.2 = ((bf16[4,96,768]{2,1,0:T(8,128)(2,1)}), bf16[4,96,768]{2,1,0:T(8,128)(2,1)S(1)}, u32[]{:S(2)}, u32[]{:S(2)}) async-start(bf16[4,96,768]{2,1,0:T(8,128)(2,1)} %add_convert_fusion), calls=%async_computation.2 | async-start | bytes 1179648 | tf_op jit(solution)/shard_map/all_to_all | solution.py:612
  103.0 6.5 %collective-permute-start.13 = (f32[16,768]{1,0:T(8,128)S(1)}, f32[16,768]{1,0:T(8,128)S(1)}, u32[]{:S(2)}, u32[]{:S(2)}) collective-permute-start(f32[16,768]{1,0:T(8,128)S(1)} %add_add_fusion), channel_id=1, source_target_pairs={{0,12},{4,0},{8,4},{12,8},{1,13},{5,1},{9,5},{13,9},{2,14},{6,2},{... | collective-permute-start | bytes 147464 | tf_op jit(solution)/shard_map/ppermute | solution.py:563
  104.0 5.6 %collective-permute-start.12 = (f32[16,768]{1,0:T(8,128)S(1)}, f32[16,768]{1,0:T(8,128)S(1)}, u32[]{:S(2)}, u32[]{:S(2)}) collective-permute-start(f32[16,768]{1,0:T(8,128)S(1)} %add_add_fusion), channel_id=1, source_target_pairs={{0,8},{4,12},{8,0},{12,4},{1,9},{5,13},{9,1},{13,5},{2,10},{6,14},... | collective-permute-start | bytes 147464 | tf_op jit(solution)/shard_map/ppermute | solution.py:563
  105.7 5.3 %collective-permute-start.11 = (f32[16,768]{1,0:T(8,128)S(1)}, f32[16,768]{1,0:T(8,128)S(1)}, u32[]{:S(2)}, u32[]{:S(2)}) collective-permute-start(f32[16,768]{1,0:T(8,128)S(1)} %add_add_fusion), channel_id=1, source_target_pairs={{0,4},{4,8},{8,12},{12,0},{1,5},{5,9},{9,13},{13,1},{2,6},{6,10},{... | collective-permute-start | bytes 147464 | tf_op jit(solution)/shard_map/ppermute | solution.py:563
  (4 other events, 25.2 us)

commit v8 on v7

--- a/solution.py
+++ b/solution.py
@@ -599,14 +599,11 @@
         pieces = (rows, right, left, far_a, far_b)
         keep_in, send_in, act_far = first_grads(pieces, pre_own, pre_near, w_in, w_out, ny)
         keep_out, send_out = second_grads(pieces, (act_own, act_near, act_far))
-        total = axis_sum(router_term, "xh", XH)
-        total, send_in = lax.optimization_barrier((total, send_in))
         came_in = shift(send_in, "xh", 1, XH)
-        total = axis_sum(axis_sum(total, "core", 2), "xl", 2)
-        total, keep_out, send_out = lax.optimization_barrier((total, keep_out, send_out))
-        total = axis_sum(total, "y", ny)
-        came_in, send_out = lax.optimization_barrier((came_in, send_out))
         came_out = shift(send_out, "xh", 1, XH)
+        total = axis_sum(router_term, ("xh", "xl"), 2 * XH)
+        total, keep_out = lax.optimization_barrier((total, keep_out))
+        total = axis_sum(axis_sum(total, "core", 2), "y", ny)
         part_in = (keep_in + came_in.astype(f32)).astype(bf16)
         total, part_in, grad_logits = lax.optimization_barrier((total, part_in, grad_logits))
         spread = lax.all_to_all(part_in, "y", split_axis=0, concat_axis=0, tiled=True)

time: 114 us -> 107 us (0.939)
  waiting for transfers between devices: 20.4 us -> 10.9 us
  starting transfers between devices: 29.1 us -> 31.4 us
    ppermute x15 -> x16, waiting for transfers between devices: 20.4 us -> 10.9 us  [shift(): lax.ppermute(value, axis, [(i, (i + by) % count) for i in range(count)])]
    ppermute x15 -> x16, starting transfers between devices: 21.9 us -> 24.1 us  [shift(): lax.ppermute(value, axis, [(i, (i + by) % count) for i in range(count)])]
  transfers between devices with their start and end apart: 17 -> 18, of which waited for: 8 -> 5; matrix products, arithmetic and copies ran while one was open for 3% -> 3% of each run, Pallas kernels for 27% -> 29%
where the time goes in v8:
time: 107 us; the launch traced here: 106 us
  Pallas kernels  39.7 us (37%)
  starting transfers between devices  31.4 us (29%)
  blocking collectives  19.9 us (19%)
  waiting for transfers between devices  10.9 us (10%)
  local copies, waits for them, and re-layouts  1.62 us (2%)
  other arithmetic  1.6 us (1%)
    ppermute x16, starting transfers between devices, shift(): lax.ppermute(value, axis, [(i, (i + by) % count) for i in range(count)])  24.1 us
    all_to_all x1, blocking collectives, over_experts(): lax.all_to_all(value, ex_axes, split_axis=0, concat_axis=0, tiled=True)  19.9 us
    ppermute x16, waiting for transfers between devices, shift(): lax.ppermute(value, axis, [(i, (i + by) % count) for i in range(count)])  10.9 us
    pallas_call x1, Pallas kernels, expert_rows(): pl.pallas_call(expert_body, in_specs=[IN_VMEM] * 3, out_specs=[IN_PLACE]...  7.12 us
    pallas_call x1, Pallas kernels, token_forward(): pl.pallas_call(token_forward_body, in_specs=[IN_PLACE] * 3, out_specs=[IN...  7.11 us
    pallas_call x1, Pallas kernels, token_logits(): pl.pallas_call(token_logits_body, in_specs=[IN_VMEM] + [IN_PLACE] * 4, ou...  6.68 us
    pallas_call x1, Pallas kernels, first_grads(): pl.pallas_call(first_grads_body, in_specs=[IN_VMEM] * 5 + [IN_PLACE] * 4,...  5.18 us
    pallas_call x1, Pallas kernels, near_terms(): pl.pallas_call(near_terms_body, in_specs=[IN_VMEM] * 2 + [IN_PLACE] * 2,...  4.29 us
  transfers between devices with their start and end apart: 18, of which 5 were waited for; matrix products, arithmetic and copies ran while one was open for 3% of the time, Pallas kernels for 29%

profile of v8, /device:TPU:0, one launch (start us, length us, event | category | flops | bytes accessed | tf_op | source)
XLA Modules:
  0.0 106.0 jit_solution(13610976912627720050)
XLA Ops:
  0.7 7.1 %token_forward.1 = (bf16[16,16,1536]{2,1,0:T(8,128)(2,1)S(1)}, f32[4,16,784]{2,1,0:T(8,128)}, f32[4,16,784]{2,1,0:T(8,128)}) custom-call(bf16[16,768]{1,0:T(8,128)(2,1)} %bitcast.12, bf16[3136,768]{1,0:T(8,128)(2,1)} %x_hbm.3, bf16[3136,768]{1,0:T(8,128)(2,1)} %g_hbm.3), custom_call_target="tpu_custom_call" | custom-call | tf_op jit(solution)/shard_map/token_forward/pallas_call | solution.py:163
  7.8 19.9 %all_to_all.15 = bf16[16,16,1536]{2,1,0:T(8,128)(2,1)S(1)} all-to-all(bf16[16,16,1536]{2,1,0:T(8,128)(2,1)S(1)} %get-tuple-element.33), channel_id=1, replica_groups=mesh['y'=4,'xh'=2,'z'=4,'xl'=2,'core'=2] {'z','xl','core'}, dimensions={0} | all-to-all | bytes 1572864 | tf_op jit(solution)/shard_map/all_to_all | solution.py:580
  27.7 1.6 %collective-permute-start = (bf16[256,1536]{1,0:T(8,128)(2,1)S(1)}, bf16[256,1536]{1,0:T(8,128)(2,1)S(1)}, u32[]{:S(2)}, u32[]{:S(2)}) collective-permute-start(bf16[256,1536]{1,0:T(8,128)(2,1)S(1)} %bitcast.7), channel_id=1, source_target_pairs={{0,32},{32,64},{64,96},{96,0},{1,33},{33,65},{65,97},{97,1},{2,34}... | collective-permute-start | bytes 2359304 | tf_op jit(solution)/shard_map/ppermute | solution.py:563
  29.3 1.7 %collective-permute-start.2 = (bf16[256,1536]{1,0:T(8,128)(2,1)S(1)}, bf16[256,1536]{1,0:T(8,128)(2,1)S(1)}, u32[]{:S(2)}, u32[]{:S(2)}) collective-permute-start(bf16[256,1536]{1,0:T(8,128)(2,1)S(1)} %bitcast.8), channel_id=1, source_target_pairs={{0,96},{32,0},{64,32},{96,64},{1,97},{33,1},{65,33},{97,65},{2,98}... | collective-permute-start | bytes 2359304 | tf_op jit(solution)/shard_map/ppermute | solution.py:563
  30.9 7.1 %expert_rows.1 = (bf16[256,1536]{1,0:T(8,128)(2,1)}, bf16[256,768]{1,0:T(8,128)(2,1)}, bf16[256,768]{1,0:T(8,128)(2,1)}) custom-call(bf16[256,1536]{1,0:T(8,128)(2,1)S(1)} %bitcast.9, bf16[1,768,3072]{2,1,0:T(8,128)(2,1)S(1)} %bitcast.6, bf16[1,3072,768]{2,1,0:T(8,128)(2,1)S(1)} %copy-done), custom_call_target="tpu_custom_call" | custom-call | tf_op jit(solution)/shard_map/expert_rows/pallas_call | solution.py:238
  38.1 3.6 %all-to-all-start.1 = ((bf16[16,16,1536]{2,1,0:T(8,128)(2,1)}), bf16[16,16,1536]{2,1,0:T(8,128)(2,1)S(1)}, u32[]{:S(2)}, u32[]{:S(2)}) async-start(bf16[16,16,1536]{2,1,0:T(8,128)(2,1)} %bitcast.14), calls=%async_computation.1 | async-start | bytes 1572864 | tf_op jit(solution)/shard_map/all_to_all | solution.py:580
  41.7 6.2 %collective-permute-done.right_ref = bf16[256,1536]{1,0:T(8,128)(2,1)S(1)} collective-permute-done((bf16[256,1536]{1,0:T(8,128)(2,1)S(1)}, bf16[256,1536]{1,0:T(8,128)(2,1)S(1)}, u32[]{:S(2)}, u32[]{:S(2)}) %collective-permute-start) | collective-permute-done | bytes 786464 | tf_op jit(solution)/shard_map/ppermute | solution.py:563
  49.8 2.9 %collective-permute-start.3 = (bf16[128,1536]{1,0:T(8,128)(2,1)}, bf16[128,1536]{1,0:T(8,128)(2,1)}, u32[]{:S(2)}, u32[]{:S(2)}) collective-permute-start(bf16[128,1536]{1,0:T(8,128)(2,1)} %slice.9), channel_id=1, source_target_pairs={{0,96},{32,0},{64,32},{96,64},{1,97},{33,1},{65,33},{97,65},{2,98}... | collective-permute-start | bytes 1179656 | tf_op jit(solution)/shard_map/ppermute | solution.py:563
  52.7 4.3 %near_terms.1 = (bf16[512,768]{1,0:T(8,128)(2,1)}, bf16[512,768]{1,0:T(8,128)(2,1)}) custom-call(bf16[256,1536]{1,0:T(8,128)(2,1)S(1)} %collective-permute-done.right_ref, bf16[256,1536]{1,0:T(8,128)(2,1)S(1)} %collective-permute-done.2.left_ref, bf16[1,768,3072]{2,1,0:T(8,128)(2,1)} %w1_hbm.3, bf16[1,3072,768]{2,1,0:T(8,128)(2,1)} %w2_hbm.3), custom_call_target="tpu_custom_call" | custom-call | tf_op jit(solution)/shard_map/near_terms/pallas_call | solution.py:300
  57.0 6.7 %token_logits.1 = (bf16[4,16,784]{2,1,0:T(8,128)(2,1)S(1)}, bf16[4,64,768]{2,1,0:T(8,128)(2,1)S(1)}, f32[16,768]{1,0:T(8,128)S(1)}) custom-call(bf16[16,16,1536]{2,1,0:T(8,128)(2,1)S(1)} %all-to-all-done.1.back_ref, bf16[3136,768]{1,0:T(8,128)(2,1)} %x_hbm.3, bf16[3136,768]{1,0:T(8,128)(2,1)} %g_hbm.3, f32[4,16,784]{2,1,0:T(8,128)} %get-tuple-element.38.disp_hbm.disp_ref, ...), custom_call_target="tpu_custom_call" | custom-call | tf_op jit(solution)/shard_map/token_logits/pallas_call | solution.py:512
  63.8 1.5 %collective-permute-start.4 = (f32[16,768]{1,0:T(8,128)S(1)}, f32[16,768]{1,0:T(8,128)S(1)}, u32[]{:S(2)}, u32[]{:S(2)}) collective-permute-start(f32[16,768]{1,0:T(8,128)S(1)} %get-tuple-element.41), channel_id=1, source_target_pairs={{0,2},{2,16},{16,18},{18,0},{1,3},{3,17},{17,19},{19,1},{4,6},{6,2... | collective-permute-start | bytes 147464 | tf_op jit(solution)/shard_map/ppermute | solution.py:563
  65.2 2.7 %collective-permute-start.5 = (f32[16,768]{1,0:T(8,128)S(1)}, f32[16,768]{1,0:T(8,128)S(1)}, u32[]{:S(2)}, u32[]{:S(2)}) collective-permute-start(f32[16,768]{1,0:T(8,128)S(1)} %get-tuple-element.41), channel_id=1, source_target_pairs={{0,16},{2,18},{16,0},{18,2},{1,17},{3,19},{17,1},{19,3},{4,20},{6,... | collective-permute-start | bytes 147464 | tf_op jit(solution)/shard_map/ppermute | solution.py:563
  68.0 1.2 %collective-permute-start.6 = (f32[16,768]{1,0:T(8,128)S(1)}, f32[16,768]{1,0:T(8,128)S(1)}, u32[]{:S(2)}, u32[]{:S(2)}) collective-permute-start(f32[16,768]{1,0:T(8,128)S(1)} %get-tuple-element.41), channel_id=1, source_target_pairs={{0,18},{2,0},{16,2},{18,16},{1,19},{3,1},{17,3},{19,17},{4,22},{6,... | collective-permute-start | bytes 147464 | tf_op jit(solution)/shard_map/ppermute | solution.py:563
  69.2 5.2 %first_grads.1 = (f32[4,96,768]{2,1,0:T(8,128)S(1)}, bf16[4,96,768]{2,1,0:T(8,128)(2,1)S(1)}, bf16[256,768]{1,0:T(8,128)(2,1)S(1)}) custom-call(bf16[256,1536]{1,0:T(8,128)(2,1)S(1)} %bitcast.10, bf16[256,1536]{1,0:T(8,128)(2,1)S(1)} %collective-permute-done.right_ref, bf16[256,1536]{1,0:T(8,128)(2,1)S(1)} %collective-permute-done.2.left_ref, ...), custom_call_target="tpu_custom_call" | custom-call | tf_op jit(solution)/shard_map/first_grads/pallas_call | solution.py:353
  75.3 4.1 %second_grads.1 = (f32[384,768]{1,0:T(8,128)S(1)}, bf16[384,768]{1,0:T(8,128)(2,1)}) custom-call(bf16[256,1536]{1,0:T(8,128)(2,1)S(1)} %bitcast.11, bf16[256,1536]{1,0:T(8,128)(2,1)S(1)} %collective-permute-done.right_ref, bf16[256,1536]{1,0:T(8,128)(2,1)S(1)} %collective-permute-done.2.left_ref, bf16[128,1536]{1,0:T(8,128)(2,1)S(1)} %collective-permute-done.1.far_a, ...), custom_call_target="tpu_custom_call" | custom-call | tf_op jit(solution)/shard_map/second_grads/pallas_call | solution.py:404
  81.4 1.5 %collective-permute-start.8 = (f32[16,768]{1,0:T(8,128)S(1)}, f32[16,768]{1,0:T(8,128)S(1)}, u32[]{:S(2)}, u32[]{:S(2)}) collective-permute-start(f32[16,768]{1,0:T(8,128)S(1)} %add.36), channel_id=1, source_target_pairs={{0,32},{32,64},{64,96},{96,0},{1,33},{33,65},{65,97},{97,1},{2,34}... | collective-permute-start | bytes 147464 | tf_op jit(solution)/shard_map/ppermute | solution.py:563
  83.6 2.7 %collective-permute-start.15 = (bf16[384,768]{1,0:T(8,128)(2,1)}, bf16[384,768]{1,0:T(8,128)(2,1)S(1)}, u32[]{:S(2)}, u32[]{:S(2)}) collective-permute-start(bf16[384,768]{1,0:T(8,128)(2,1)} %get-tuple-element.59), channel_id=1, source_target_pairs={{0,16},{16,0},{1,17},{17,1},{2,18},{18,2},{3,19},{19,3},{4,20},{20... | collective-permute-start | bytes 1769480 | tf_op jit(solution)/shard_map/ppermute | solution.py:563
  87.2 1.3 %collective-permute-done.9 = f32[16,768]{1,0:T(8,128)S(1)} collective-permute-done((f32[16,768]{1,0:T(8,128)S(1)}, f32[16,768]{1,0:T(8,128)S(1)}, u32[]{:S(2)}, u32[]{:S(2)}) %collective-permute-start.9) | collective-permute-done | bytes 49184 | tf_op jit(solution)/shard_map/ppermute | solution.py:563
  88.5 1.2 %collective-permute-done.11 = bf16[4,96,768]{2,1,0:T(8,128)(2,1)S(1)} collective-permute-done((bf16[4,96,768]{2,1,0:T(8,128)(2,1)S(1)}, bf16[4,96,768]{2,1,0:T(8,128)(2,1)S(1)}, u32[]{:S(2)}, u32[]{:S(2)}) %collective-permute-start.11) | collective-permute-done | bytes 589856 | tf_op jit(solution)/shard_map/ppermute | solution.py:563
  90.7 3.6 %all-to-all-start.2 = ((bf16[4,96,768]{2,1,0:T(8,128)(2,1)}), bf16[4,96,768]{2,1,0:T(8,128)(2,1)S(1)}, u32[]{:S(2)}, u32[]{:S(2)}) async-start(bf16[4,96,768]{2,1,0:T(8,128)(2,1)} %add_convert_fusion), calls=%async_computation.2 | async-start | bytes 1179648 | tf_op jit(solution)/shard_map/all_to_all | solution.py:609
  94.4 3.0 %collective-permute-start.12 = (f32[16,768]{1,0:T(8,128)S(1)}, f32[16,768]{1,0:T(8,128)S(1)}, u32[]{:S(2)}, u32[]{:S(2)}) collective-permute-start(f32[16,768]{1,0:T(8,128)S(1)} %add_add_fusion), channel_id=1, source_target_pairs={{0,4},{4,8},{8,12},{12,0},{1,5},{5,9},{9,13},{13,1},{2,6},{6,10},{... | collective-permute-start | bytes 147464 | tf_op jit(solution)/shard_map/ppermute | solution.py:563
  97.8 2.3 %collective-permute-start.14 = (f32[16,768]{1,0:T(8,128)S(1)}, f32[16,768]{1,0:T(8,128)S(1)}, u32[]{:S(2)}, u32[]{:S(2)}) collective-permute-start(f32[16,768]{1,0:T(8,128)S(1)} %add_add_fusion), channel_id=1, source_target_pairs={{0,12},{4,0},{8,4},{12,8},{1,13},{5,1},{9,5},{13,9},{2,14},{6,2},{... | collective-permute-start | bytes 147464 | tf_op jit(solution)/shard_map/ppermute | solution.py:563
  100.1 3.6 %token_grads.1 = bf16[3136,768]{1,0:T(8,128)(2,1)} custom-call(bf16[4,16,784]{2,1,0:T(8,128)(2,1)S(1)} %copy-done.7, bf16[4,64,768]{2,1,0:T(8,128)(2,1)S(1)} %copy-done.5, f32[4,16,784]{2,1,0:T(8,128)S(1)} %copy-done.3, bf16[16,768]{1,0:T(8,128)(2,1)S(1)} %bitcast.13), custom_call_target="tpu_custom_call" | custom-call | tf_op jit(solution)/shard_map/token_grads/pallas_call | solution.py:546
  104.4 1.6 %finish.1 = (f32[1,96,3072]{2,1,0:T(8,128)}, f32[1,384,768]{2,1,0:T(8,128)}) custom-call(bf16[4,96,768]{2,1,0:T(8,128)(2,1)S(1)} %all-to-all-done.2.spread_ref, f32[384,768]{1,0:T(8,128)S(1)} %copy-done.2, bf16[384,768]{1,0:T(8,128)(2,1)S(1)} %collective-permute-done.15.came_ref), custom_call_target="tpu_custom_call" | custom-call | tf_op jit(solution)/shard_map/finish/pallas_call | solution.py:431
  (51 shorter events, 8.4 us)
Async XLA Ops:
  0.6 30.3 %slice-start = ((s8[4718592]{0:T(1024)(128)(4,1)}), s8[4194304]{0:T(1024)(128)(4,1)S(1)}, s32[]{:S(2)}) async-start(s8[4718592]{0:T(1024)(128)(4,1)} %bitcast.5), calls=%async_computation.3 | async-start | bytes 8388608
  0.6 30.3 %slice-start.1 = ((s8[4718592]{0:T(1024)(128)(4,1)}), s8[524288]{0:T(1024)(128)(4,1)S(1)}, s32[]{:S(2)}) async-start(s8[4718592]{0:T(1024)(128)(4,1)} %bitcast.5), calls=%async_computation.4 | async-start | bytes 1048576
  0.7 30.3 %copy-start = (bf16[1,3072,768]{2,1,0:T(8,128)(2,1)S(1)}, bf16[1,3072,768]{2,1,0:T(8,128)(2,1)}, u32[]{:S(2)}) copy-start(bf16[1,3072,768]{2,1,0:T(8,128)(2,1)} %w2_hbm.3) | copy-start | bytes 14155780
  27.7 20.2 %collective-permute-start = (bf16[256,1536]{1,0:T(8,128)(2,1)S(1)}, bf16[256,1536]{1,0:T(8,128)(2,1)S(1)}, u32[]{:S(2)}, u32[]{:S(2)}) collective-permute-start(bf16[256,1536]{1,0:T(8,128)(2,1)S(1)} %bitcast.7), channel_id=1, source_target_pairs={{0,32},{32,64},{64,96},{96,0},{1,33},{33,65},{65,97},{97,1},{2,34}... | collective-permute-start | bytes 2359304 | tf_op jit(solution)/shard_map/ppermute | solution.py:563
  29.3 19.7 %collective-permute-start.2 = (bf16[256,1536]{1,0:T(8,128)(2,1)S(1)}, bf16[256,1536]{1,0:T(8,128)(2,1)S(1)}, u32[]{:S(2)}, u32[]{:S(2)}) collective-permute-start(bf16[256,1536]{1,0:T(8,128)(2,1)S(1)} %bitcast.8), channel_id=1, source_target_pairs={{0,96},{32,0},{64,32},{96,64},{1,97},{33,1},{65,33},{97,65},{2,98}... | collective-permute-start | bytes 2359304 | tf_op jit(solution)/shard_map/ppermute | solution.py:563
  38.1 19.0 %all-to-all-start.1 = ((bf16[16,16,1536]{2,1,0:T(8,128)(2,1)}), bf16[16,16,1536]{2,1,0:T(8,128)(2,1)S(1)}, u32[]{:S(2)}, u32[]{:S(2)}) async-start(bf16[16,16,1536]{2,1,0:T(8,128)(2,1)} %bitcast.14), calls=%async_computation.1 | async-start | bytes 1572864 | tf_op jit(solution)/shard_map/all_to_all | solution.py:580
  48.7 15.1 %collective-permute-start.1 = (bf16[128,1536]{1,0:T(8,128)(2,1)}, bf16[128,1536]{1,0:T(8,128)(2,1)S(1)}, u32[]{:S(2)}, u32[]{:S(2)}) collective-permute-start(bf16[128,1536]{1,0:T(8,128)(2,1)} %slice.8), channel_id=1, source_target_pairs={{0,32},{32,64},{64,96},{96,0},{1,33},{33,65},{65,97},{97,1},{2,34}... | collective-permute-start | bytes 1179656 | tf_op jit(solution)/shard_map/ppermute | solution.py:563
  49.8 14.0 %collective-permute-start.3 = (bf16[128,1536]{1,0:T(8,128)(2,1)}, bf16[128,1536]{1,0:T(8,128)(2,1)}, u32[]{:S(2)}, u32[]{:S(2)}) collective-permute-start(bf16[128,1536]{1,0:T(8,128)(2,1)} %slice.9), channel_id=1, source_target_pairs={{0,96},{32,0},{64,32},{96,64},{1,97},{33,1},{65,33},{97,65},{2,98}... | collective-permute-start | bytes 1179656 | tf_op jit(solution)/shard_map/ppermute | solution.py:563
  63.7 10.7 %copy-start.4 = (bf16[4,64,768]{2,1,0:T(8,128)(2,1)}, bf16[4,64,768]{2,1,0:T(8,128)(2,1)S(1)}, u32[]{:S(2)}) copy-start(bf16[4,64,768]{2,1,0:T(8,128)(2,1)S(1)} %get-tuple-element.55.slots_ref) | copy-start | bytes 1179652
  63.7 10.7 %copy-start.6 = (bf16[4,16,784]{2,1,0:T(8,128)(2,1)}, bf16[4,16,784]{2,1,0:T(8,128)(2,1)S(1)}, u32[]{:S(2)}) copy-start(bf16[4,16,784]{2,1,0:T(8,128)(2,1)S(1)} %get-tuple-element.54.gl_ref) | copy-start | bytes 301060
  63.8 15.7 %collective-permute-start.4 = (f32[16,768]{1,0:T(8,128)S(1)}, f32[16,768]{1,0:T(8,128)S(1)}, u32[]{:S(2)}, u32[]{:S(2)}) collective-permute-start(f32[16,768]{1,0:T(8,128)S(1)} %get-tuple-element.41), channel_id=1, source_target_pairs={{0,2},{2,16},{16,18},{18,0},{1,3},{3,17},{17,19},{19,1},{4,6},{6,2... | collective-permute-start | bytes 147464 | tf_op jit(solution)/shard_map/ppermute | solution.py:563
  65.2 14.2 %collective-permute-start.5 = (f32[16,768]{1,0:T(8,128)S(1)}, f32[16,768]{1,0:T(8,128)S(1)}, u32[]{:S(2)}, u32[]{:S(2)}) collective-permute-start(f32[16,768]{1,0:T(8,128)S(1)} %get-tuple-element.41), channel_id=1, source_target_pairs={{0,16},{2,18},{16,0},{18,2},{1,17},{3,19},{17,1},{19,3},{4,20},{6,... | collective-permute-start | bytes 147464 | tf_op jit(solution)/shard_map/ppermute | solution.py:563
  68.0 11.5 %collective-permute-start.6 = (f32[16,768]{1,0:T(8,128)S(1)}, f32[16,768]{1,0:T(8,128)S(1)}, u32[]{:S(2)}, u32[]{:S(2)}) collective-permute-start(f32[16,768]{1,0:T(8,128)S(1)} %get-tuple-element.41), channel_id=1, source_target_pairs={{0,18},{2,0},{16,2},{18,16},{1,19},{3,1},{17,3},{19,17},{4,22},{6,... | collective-permute-start | bytes 147464 | tf_op jit(solution)/shard_map/ppermute | solution.py:563
  74.4 15.3 %collective-permute-start.11 = (bf16[4,96,768]{2,1,0:T(8,128)(2,1)S(1)}, bf16[4,96,768]{2,1,0:T(8,128)(2,1)S(1)}, u32[]{:S(2)}, u32[]{:S(2)}) collective-permute-start(bf16[4,96,768]{2,1,0:T(8,128)(2,1)S(1)} %get-tuple-element.52), channel_id=1, source_target_pairs={{0,16},{16,0},{1,17},{17,1},{2,18},{18,2},{3,19},{19,3},{4,20},{20... | collective-permute-start | bytes 1769480 | tf_op jit(solution)/shard_map/ppermute | solution.py:563
  79.4 11.3 %copy-start.1 = (f32[384,768]{1,0:T(8,128)}, f32[384,768]{1,0:T(8,128)S(1)}, u32[]{:S(2)}) copy-start(f32[384,768]{1,0:T(8,128)S(1)} %get-tuple-element.58.keep_ref) | copy-start | bytes 3538948
  79.5 1.3 %collective-permute-start.7 = (f32[16,768]{1,0:T(8,128)S(1)}, f32[16,768]{1,0:T(8,128)S(1)}, u32[]{:S(2)}, u32[]{:S(2)}) collective-permute-start(f32[16,768]{1,0:T(8,128)S(1)} %add_add_fusion.1), channel_id=1, source_target_pairs={{0,1},{1,0},{2,3},{3,2},{4,5},{5,4},{6,7},{7,6},{8,9},{9,8},{10,11... | collective-permute-start | bytes 147464 | tf_op jit(solution)/shard_map/ppermute | solution.py:563
  80.8 5.5 %collective-permute-start.10 = (f32[16,768]{1,0:T(8,128)S(1)}, f32[16,768]{1,0:T(8,128)S(1)}, u32[]{:S(2)}, u32[]{:S(2)}) collective-permute-start(f32[16,768]{1,0:T(8,128)S(1)} %add.36), channel_id=1, source_target_pairs={{0,96},{32,0},{64,32},{96,64},{1,97},{33,1},{65,33},{97,65},{2,98}... | collective-permute-start | bytes 147464 | tf_op jit(solution)/shard_map/ppermute | solution.py:563
  81.4 5.8 %collective-permute-start.8 = (f32[16,768]{1,0:T(8,128)S(1)}, f32[16,768]{1,0:T(8,128)S(1)}, u32[]{:S(2)}, u32[]{:S(2)}) collective-permute-start(f32[16,768]{1,0:T(8,128)S(1)} %add.36), channel_id=1, source_target_pairs={{0,32},{32,64},{64,96},{96,0},{1,33},{33,65},{65,97},{97,1},{2,34}... | collective-permute-start | bytes 147464 | tf_op jit(solution)/shard_map/ppermute | solution.py:563
  82.9 5.6 %collective-permute-start.9 = (f32[16,768]{1,0:T(8,128)S(1)}, f32[16,768]{1,0:T(8,128)S(1)}, u32[]{:S(2)}, u32[]{:S(2)}) collective-permute-start(f32[16,768]{1,0:T(8,128)S(1)} %add.36), channel_id=1, source_target_pairs={{0,64},{32,96},{64,0},{96,32},{1,65},{33,97},{65,1},{97,33},{2,66}... | collective-permute-start | bytes 147464 | tf_op jit(solution)/shard_map/ppermute | solution.py:563
  83.6 20.8 %collective-permute-start.15 = (bf16[384,768]{1,0:T(8,128)(2,1)}, bf16[384,768]{1,0:T(8,128)(2,1)S(1)}, u32[]{:S(2)}, u32[]{:S(2)}) collective-permute-start(bf16[384,768]{1,0:T(8,128)(2,1)} %get-tuple-element.59), channel_id=1, source_target_pairs={{0,16},{16,0},{1,17},{17,1},{2,18},{18,2},{3,19},{19,3},{4,20},{20... | collective-permute-start | bytes 1769480 | tf_op jit(solution)/shard_map/ppermute | solution.py:563
  90.7 13.7 %all-to-all-start.2 = ((bf16[4,96,768]{2,1,0:T(8,128)(2,1)}), bf16[4,96,768]{2,1,0:T(8,128)(2,1)S(1)}, u32[]{:S(2)}, u32[]{:S(2)}) async-start(bf16[4,96,768]{2,1,0:T(8,128)(2,1)} %add_convert_fusion), calls=%async_computation.2 | async-start | bytes 1179648 | tf_op jit(solution)/shard_map/all_to_all | solution.py:609
  94.4 9.4 %collective-permute-start.12 = (f32[16,768]{1,0:T(8,128)S(1)}, f32[16,768]{1,0:T(8,128)S(1)}, u32[]{:S(2)}, u32[]{:S(2)}) collective-permute-start(f32[16,768]{1,0:T(8,128)S(1)} %add_add_fusion), channel_id=1, source_target_pairs={{0,4},{4,8},{8,12},{12,0},{1,5},{5,9},{9,13},{13,1},{2,6},{6,10},{... | collective-permute-start | bytes 147464 | tf_op jit(solution)/shard_map/ppermute | solution.py:563
  97.3 6.4 %collective-permute-start.13 = (f32[16,768]{1,0:T(8,128)S(1)}, f32[16,768]{1,0:T(8,128)S(1)}, u32[]{:S(2)}, u32[]{:S(2)}) collective-permute-start(f32[16,768]{1,0:T(8,128)S(1)} %add_add_fusion), channel_id=1, source_target_pairs={{0,8},{4,12},{8,0},{12,4},{1,9},{5,13},{9,1},{13,5},{2,10},{6,14},... | collective-permute-start | bytes 147464 | tf_op jit(solution)/shard_map/ppermute | solution.py:563
  97.8 6.0 %collective-permute-start.14 = (f32[16,768]{1,0:T(8,128)S(1)}, f32[16,768]{1,0:T(8,128)S(1)}, u32[]{:S(2)}, u32[]{:S(2)}) collective-permute-start(f32[16,768]{1,0:T(8,128)S(1)} %add_add_fusion), channel_id=1, source_target_pairs={{0,12},{4,0},{8,4},{12,8},{1,13},{5,1},{9,5},{13,9},{2,14},{6,2},{... | collective-permute-start | bytes 147464 | tf_op jit(solution)/shard_map/ppermute | solution.py:563
  (5 other events, 41.8 us)

commit v9 on v8

--- a/solution.py
+++ b/solution.py
@@ -205,7 +205,12 @@
     stores = [
         pltpu.make_async_copy(src, dst, sem.at[k])
         for k, (src, dst) in enumerate(
-            ((act_ref, act_hbm), (pre_ref, pre_hbm), (out_ref, out_hbm))
+            (
+                (act_ref, act_hbm),
+                (pre_ref, pre_hbm),
+                (out_ref.at[:, pl.ds(0, feat)], out_hbm.at[:, pl.ds(0, feat)]),
+                (out_ref.at[:, pl.ds(feat, feat)], out_hbm.at[:, pl.ds(feat, feat)]),
+            )
         )
     ]
     for i in range(hidden // tile):
@@ -223,11 +228,13 @@
             stores[1].start()
         part = jnp.dot(act, w2, preferred_element_type=f32)
         made = part if made is None else made + part
+        if i == hidden // tile - 1:
+            out_ref[:, :feat] = made.astype(bf16)
+            stores[2].start()
         part = contract(grad_pre, w1, 1, 1)
         back = part if back is None else back + part
-    out_ref[:, :feat] = made.astype(bf16)
     out_ref[:, feat:] = back.astype(bf16)
-    stores[2].start()
+    stores[3].start()
     for store in stores:
         store.wait()
 
@@ -241,7 +248,7 @@
         out_specs=[IN_PLACE] * 3,
         out_shape=[pltpu.HBM(shape, bf16) for shape in shapes],
         scratch_shapes=[pltpu.VMEM(shape, bf16) for shape in shapes]
-        + [pltpu.SemaphoreType.DMA((3,))],
+        + [pltpu.SemaphoreType.DMA((4,))],
         compiler_params=params(12),
         name="expert_rows",
     )(rows, w_in, w_out)
@@ -533,27 +540,30 @@
     )(back, *[pinned(v) for v in (tokens, g_outputs, dispatch, combine)])
 
 
-def token_grads_body(gl_ref, slots_ref, disp_ref, rt_ref, out_ref):
-    image = lane_images(gl_ref.shape[2])
-    left = jnp.concatenate([per_slot_rows(disp_ref[0], image), gl_ref[0]], axis=0)
-    right = jnp.concatenate([slots_ref[0], rt_ref[...]], axis=0)
-    out_ref[...] = contract(left, right, 0, 0).astype(bf16)
+def token_grads_body(gl_ref, slots_ref, disp_ref, rt_ref, out_hbm, out, sem):
+    steps, _, width = gl_ref.shape
+    image = lane_images(width)
+    stores = []
+    for b in range(steps):
+        left = jnp.concatenate([per_slot_rows(disp_ref[b], image), gl_ref[b]], axis=0)
+        right = jnp.concatenate([slots_ref[b], rt_ref[...]], axis=0)
+        out[b * width : (b + 1) * width, :] = contract(left, right, 0, 0).astype(bf16)
+        at = pl.ds(b * width, width)
+        stores.append(pltpu.make_async_copy(out.at[at], out_hbm.at[at], sem.at[b]))
+        stores[b].start()
+    for store in stores:
+        store.wait()
 
 
 def token_grads(grad_logits, slots, dispatch, rt):
-    steps, experts, width = grad_logits.shape
-    feat = slots.shape[2]
+    steps, _, width = grad_logits.shape
+    shape = (steps * width, slots.shape[2])
     return pl.pallas_call(
         token_grads_body,
-        grid=(steps,),
-        in_specs=[
-            pl.BlockSpec((1, experts, width), lambda i: (i, 0, 0)),
-            pl.BlockSpec((1, GROUP * experts, feat), lambda i: (i, 0, 0)),
-            pl.BlockSpec((1, experts, width), lambda i: (i, 0, 0)),
-            pl.BlockSpec((experts, feat), lambda i: (0, 0)),
-        ],
-        out_specs=pl.BlockSpec((width, feat), lambda i: (i, 0)),
-        out_shape=jax.ShapeDtypeStruct((steps * width, feat), bf16),
+        in_specs=[IN_VMEM] * 4,
+        out_specs=IN_PLACE,
+        out_shape=pltpu.HBM(shape, bf16),
+        scratch_shapes=[pltpu.VMEM(shape, bf16), pltpu.SemaphoreType.DMA((steps,))],
         compiler_params=params(12),
         name="token_grads",
     )(grad_logits, slots, dispatch, rt)
@@ -605,11 +615,11 @@
         total, keep_out = lax.optimization_barrier((total, keep_out))
         total = axis_sum(axis_sum(total, "core", 2), "y", ny)
         part_in = (keep_in + came_in.astype(f32)).astype(bf16)
-        total, part_in, grad_logits = lax.optimization_barrier((total, part_in, grad_logits))
+        grad_tok = token_grads(grad_logits, slot_grads, dispatch, rt)
+        total, part_in, grad_tok = lax.optimization_barrier((total, part_in, grad_tok))
         spread = lax.all_to_all(part_in, "y", split_axis=0, concat_axis=0, tiled=True)
         grad_router = axis_sum(total, "z", nz).T
         grad_first, grad_second = finish(spread, keep_out, came_out)
-        grad_tok = token_grads(grad_logits, slot_grads, dispatch, rt)
         return grad_tok, grad_router, grad_first, grad_second
 
     return jax.shard_map(

time: 107 us -> 106 us (level)
  waiting for transfers between devices: 10.9 us -> 13.6 us
  starting transfers between devices: 31.4 us -> 29.2 us
  Pallas kernels: 39.7 us -> 38.4 us
    ppermute x16, waiting for transfers between devices: 10.9 us -> 13.6 us  [shift(): lax.ppermute(value, axis, [(i, (i + by) % count) for i in range(count)])]
    ppermute x16, starting transfers between devices: 24.1 us -> 22 us  [shift(): lax.ppermute(value, axis, [(i, (i + by) % count) for i in range(count)])]
  transfers between devices with their start and end apart: 18 -> 18, of which waited for: 5 -> 8; matrix products, arithmetic and copies ran while one was open for 3% -> 3% of each run, Pallas kernels for 29% -> 28%
where the time goes in v9:
time: 106 us; the launch traced here: 105 us
  Pallas kernels  38.4 us (36%)
  starting transfers between devices  29.2 us (28%)
  blocking collectives  19.9 us (19%)
  waiting for transfers between devices  13.6 us (13%)
  other arithmetic  1.6 us (2%)
  local copies, waits for them, and re-layouts  1.57 us (1%)
    ppermute x16, starting transfers between devices, shift(): lax.ppermute(value, axis, [(i, (i + by) % count) for i in range(count)])  22 us
    all_to_all x1, blocking collectives, over_experts(): lax.all_to_all(value, ex_axes, split_axis=0, concat_axis=0, tiled=True)  19.9 us
    ppermute x16, waiting for transfers between devices, shift(): lax.ppermute(value, axis, [(i, (i + by) % count) for i in range(count)])  13.6 us
    pallas_call x1, Pallas kernels, token_forward(): pl.pallas_call(token_forward_body, in_specs=[IN_PLACE] * 3, out_specs=[IN...  7.11 us
    pallas_call x1, Pallas kernels, expert_rows(): pl.pallas_call(expert_body, in_specs=[IN_VMEM] * 3, out_specs=[IN_PLACE]...  7 us
    pallas_call x1, Pallas kernels, token_logits(): pl.pallas_call(token_logits_body, in_specs=[IN_VMEM] + [IN_PLACE] * 4, ou...  6.68 us
    pallas_call x1, Pallas kernels, first_grads(): pl.pallas_call(first_grads_body, in_specs=[IN_VMEM] * 5 + [IN_PLACE] * 4,...  5.18 us
    pallas_call x1, Pallas kernels, near_terms(): pl.pallas_call(near_terms_body, in_specs=[IN_VMEM] * 2 + [IN_PLACE] * 2,...  4.29 us
  transfers between devices with their start and end apart: 18, of which 8 were waited for; matrix products, arithmetic and copies ran while one was open for 3% of the time, Pallas kernels for 28%

profile of v9, /device:TPU:0, one launch (start us, length us, event | category | flops | bytes accessed | tf_op | source)
XLA Modules:
  0.0 105.1 jit_solution(5222626869306013404)
XLA Ops:
  0.7 7.1 %token_forward.1 = (bf16[16,16,1536]{2,1,0:T(8,128)(2,1)S(1)}, f32[4,16,784]{2,1,0:T(8,128)}, f32[4,16,784]{2,1,0:T(8,128)}) custom-call(bf16[16,768]{1,0:T(8,128)(2,1)} %bitcast.12, bf16[3136,768]{1,0:T(8,128)(2,1)} %x_hbm.3, bf16[3136,768]{1,0:T(8,128)(2,1)} %g_hbm.3), custom_call_target="tpu_custom_call" | custom-call | tf_op jit(solution)/shard_map/token_forward/pallas_call | solution.py:163
  7.8 19.9 %all_to_all.15 = bf16[16,16,1536]{2,1,0:T(8,128)(2,1)S(1)} all-to-all(bf16[16,16,1536]{2,1,0:T(8,128)(2,1)S(1)} %get-tuple-element.33), channel_id=1, replica_groups=mesh['y'=4,'xh'=2,'z'=4,'xl'=2,'core'=2] {'z','xl','core'}, dimensions={0} | all-to-all | bytes 1572864 | tf_op jit(solution)/shard_map/all_to_all | solution.py:590
  27.7 3.0 %collective-permute-start.2 = (bf16[256,1536]{1,0:T(8,128)(2,1)S(1)}, bf16[256,1536]{1,0:T(8,128)(2,1)S(1)}, u32[]{:S(2)}, u32[]{:S(2)}) collective-permute-start(bf16[256,1536]{1,0:T(8,128)(2,1)S(1)} %bitcast.7), channel_id=1, source_target_pairs={{0,96},{32,0},{64,32},{96,64},{1,97},{33,1},{65,33},{97,65},{2,98}... | collective-permute-start | bytes 2359304 | tf_op jit(solution)/shard_map/ppermute | solution.py:573
  30.7 7.0 %expert_rows.1 = (bf16[256,1536]{1,0:T(8,128)(2,1)}, bf16[256,768]{1,0:T(8,128)(2,1)}, bf16[256,768]{1,0:T(8,128)(2,1)}) custom-call(bf16[256,1536]{1,0:T(8,128)(2,1)S(1)} %bitcast.9, bf16[1,768,3072]{2,1,0:T(8,128)(2,1)S(1)} %bitcast.6, bf16[1,3072,768]{2,1,0:T(8,128)(2,1)S(1)} %copy-done), custom_call_target="tpu_custom_call" | custom-call | tf_op jit(solution)/shard_map/expert_rows/pallas_call | solution.py:245
  37.7 3.6 %all-to-all-start.1 = ((bf16[16,16,1536]{2,1,0:T(8,128)(2,1)}), bf16[16,16,1536]{2,1,0:T(8,128)(2,1)S(1)}, u32[]{:S(2)}, u32[]{:S(2)}) async-start(bf16[16,16,1536]{2,1,0:T(8,128)(2,1)} %bitcast.14), calls=%async_computation.1 | async-start | bytes 1572864 | tf_op jit(solution)/shard_map/all_to_all | solution.py:590
  41.4 5.8 %collective-permute-done.2.left_ref = bf16[256,1536]{1,0:T(8,128)(2,1)S(1)} collective-permute-done((bf16[256,1536]{1,0:T(8,128)(2,1)S(1)}, bf16[256,1536]{1,0:T(8,128)(2,1)S(1)}, u32[]{:S(2)}, u32[]{:S(2)}) %collective-permute-start.2) | collective-permute-done | bytes 786464 | tf_op jit(solution)/shard_map/ppermute | solution.py:573
  48.0 3.7 %collective-permute-start.3 = (bf16[128,1536]{1,0:T(8,128)(2,1)}, bf16[128,1536]{1,0:T(8,128)(2,1)S(1)}, u32[]{:S(2)}, u32[]{:S(2)}) collective-permute-start(bf16[128,1536]{1,0:T(8,128)(2,1)} %slice.9), channel_id=1, source_target_pairs={{0,96},{32,0},{64,32},{96,64},{1,97},{33,1},{65,33},{97,65},{2,98}... | collective-permute-start | bytes 1179656 | tf_op jit(solution)/shard_map/ppermute | solution.py:573
  52.4 4.3 %near_terms.1 = (bf16[512,768]{1,0:T(8,128)(2,1)}, bf16[512,768]{1,0:T(8,128)(2,1)}) custom-call(bf16[256,1536]{1,0:T(8,128)(2,1)S(1)} %collective-permute-done.right_ref, bf16[256,1536]{1,0:T(8,128)(2,1)S(1)} %collective-permute-done.2.left_ref, bf16[1,768,3072]{2,1,0:T(8,128)(2,1)} %w1_hbm.3, bf16[1,3072,768]{2,1,0:T(8,128)(2,1)} %w2_hbm.3), custom_call_target="tpu_custom_call" | custom-call | tf_op jit(solution)/shard_map/near_terms/pallas_call | solution.py:307
  56.7 6.7 %token_logits.1 = (bf16[4,16,784]{2,1,0:T(8,128)(2,1)S(1)}, bf16[4,64,768]{2,1,0:T(8,128)(2,1)S(1)}, f32[16,768]{1,0:T(8,128)S(1)}) custom-call(bf16[16,16,1536]{2,1,0:T(8,128)(2,1)S(1)} %all-to-all-done.1.back_ref, bf16[3136,768]{1,0:T(8,128)(2,1)} %x_hbm.3, bf16[3136,768]{1,0:T(8,128)(2,1)} %g_hbm.3, f32[4,16,784]{2,1,0:T(8,128)} %get-tuple-element.38.disp_hbm.disp_ref, ...), custom_call_target="tpu_custom_call" | custom-call | tf_op jit(solution)/shard_map/token_logits/pallas_call | solution.py:519
  63.4 3.2 %collective-permute-start.6 = (f32[16,768]{1,0:T(8,128)S(1)}, f32[16,768]{1,0:T(8,128)S(1)}, u32[]{:S(2)}, u32[]{:S(2)}) collective-permute-start(f32[16,768]{1,0:T(8,128)S(1)} %get-tuple-element.41), channel_id=1, source_target_pairs={{0,18},{2,0},{16,2},{18,16},{1,19},{3,1},{17,3},{19,17},{4,22},{6,... | collective-permute-start | bytes 147464 | tf_op jit(solution)/shard_map/ppermute | solution.py:573
  67.7 5.2 %first_grads.1 = (f32[4,96,768]{2,1,0:T(8,128)S(1)}, bf16[4,96,768]{2,1,0:T(8,128)(2,1)S(1)}, bf16[256,768]{1,0:T(8,128)(2,1)S(1)}) custom-call(bf16[256,1536]{1,0:T(8,128)(2,1)S(1)} %bitcast.10, bf16[256,1536]{1,0:T(8,128)(2,1)S(1)} %collective-permute-done.right_ref, bf16[256,1536]{1,0:T(8,128)(2,1)S(1)} %collective-permute-done.2.left_ref, ...), custom_call_target="tpu_custom_call" | custom-call | tf_op jit(solution)/shard_map/first_grads/pallas_call | solution.py:360
  72.9 2.6 %collective-permute-start.11 = (bf16[4,96,768]{2,1,0:T(8,128)(2,1)S(1)}, bf16[4,96,768]{2,1,0:T(8,128)(2,1)S(1)}, u32[]{:S(2)}, u32[]{:S(2)}) collective-permute-start(bf16[4,96,768]{2,1,0:T(8,128)(2,1)S(1)} %get-tuple-element.52), channel_id=1, source_target_pairs={{0,16},{16,0},{1,17},{17,1},{2,18},{18,2},{3,19},{19,3},{4,20},{20... | collective-permute-start | bytes 1769480 | tf_op jit(solution)/shard_map/ppermute | solution.py:573
  75.4 3.7 %second_grads.1 = (f32[384,768]{1,0:T(8,128)S(1)}, bf16[384,768]{1,0:T(8,128)(2,1)S(1)}) custom-call(bf16[256,1536]{1,0:T(8,128)(2,1)S(1)} %bitcast.11, bf16[256,1536]{1,0:T(8,128)(2,1)S(1)} %collective-permute-done.right_ref, bf16[256,1536]{1,0:T(8,128)(2,1)S(1)} %collective-permute-done.2.left_ref, bf16[128,1536]{1,0:T(8,128)(2,1)} %collective-permute-done.1.far_a, ...), custom_call_target="tpu_custom_call" | custom-call | tf_op jit(solution)/shard_map/second_grads/pallas_call | solution.py:411
  79.3 1.2 %collective-permute-done.7 = f32[16,768]{1,0:T(8,128)S(1)} collective-permute-done((f32[16,768]{1,0:T(8,128)S(1)}, f32[16,768]{1,0:T(8,128)S(1)}, u32[]{:S(2)}, u32[]{:S(2)}) %collective-permute-start.7) | collective-permute-done | bytes 49184 | tf_op jit(solution)/shard_map/ppermute | solution.py:573
  80.6 2.8 %collective-permute-start.10 = (f32[16,768]{1,0:T(8,128)S(1)}, f32[16,768]{1,0:T(8,128)S(1)}, u32[]{:S(2)}, u32[]{:S(2)}) collective-permute-start(f32[16,768]{1,0:T(8,128)S(1)} %add.36), channel_id=1, source_target_pairs={{0,96},{32,0},{64,32},{96,64},{1,97},{33,1},{65,33},{97,65},{2,98}... | collective-permute-start | bytes 147464 | tf_op jit(solution)/shard_map/ppermute | solution.py:573
  84.4 2.9 %token_grads.1 = bf16[3136,768]{1,0:T(8,128)(2,1)} custom-call(bf16[4,16,784]{2,1,0:T(8,128)(2,1)S(1)} %get-tuple-element.53.gl_ref, bf16[4,64,768]{2,1,0:T(8,128)(2,1)S(1)} %get-tuple-element.54.slots_ref, f32[4,16,784]{2,1,0:T(8,128)S(1)} %copy-done.3, bf16[16,768]{1,0:T(8,128)(2,1)S(1)} %bitcast.13), custom_call_target="tpu_custom_call" | custom-call | tf_op jit(solution)/shard_map/token_grads/pallas_call | solution.py:561
  87.2 1.6 %collective-permute-start.15 = (bf16[384,768]{1,0:T(8,128)(2,1)S(1)}, bf16[384,768]{1,0:T(8,128)(2,1)S(1)}, u32[]{:S(2)}, u32[]{:S(2)}) collective-permute-start(bf16[384,768]{1,0:T(8,128)(2,1)S(1)} %get-tuple-element.59), channel_id=1, source_target_pairs={{0,16},{16,0},{1,17},{17,1},{2,18},{18,2},{3,19},{19,3},{4,20},{20... | collective-permute-start | bytes 1769480 | tf_op jit(solution)/shard_map/ppermute | solution.py:573
  90.2 3.6 %all-to-all-start.2 = ((bf16[4,96,768]{2,1,0:T(8,128)(2,1)}), bf16[4,96,768]{2,1,0:T(8,128)(2,1)S(1)}, u32[]{:S(2)}, u32[]{:S(2)}) async-start(bf16[4,96,768]{2,1,0:T(8,128)(2,1)} %add_convert_fusion), calls=%async_computation.2 | async-start | bytes 1179648 | tf_op jit(solution)/shard_map/all_to_all | solution.py:620
  93.8 1.2 %collective-permute-start.14 = (f32[16,768]{1,0:T(8,128)S(1)}, f32[16,768]{1,0:T(8,128)S(1)}, u32[]{:S(2)}, u32[]{:S(2)}) collective-permute-start(f32[16,768]{1,0:T(8,128)S(1)} %add_add_fusion), channel_id=1, source_target_pairs={{0,12},{4,0},{8,4},{12,8},{1,13},{5,1},{9,5},{13,9},{2,14},{6,2},{... | collective-permute-start | bytes 147464 | tf_op jit(solution)/shard_map/ppermute | solution.py:573
  95.0 1.8 %collective-permute-start.13 = (f32[16,768]{1,0:T(8,128)S(1)}, f32[16,768]{1,0:T(8,128)S(1)}, u32[]{:S(2)}, u32[]{:S(2)}) collective-permute-start(f32[16,768]{1,0:T(8,128)S(1)} %add_add_fusion), channel_id=1, source_target_pairs={{0,8},{4,12},{8,0},{12,4},{1,9},{5,13},{9,1},{13,5},{2,10},{6,14},... | collective-permute-start | bytes 147464 | tf_op jit(solution)/shard_map/ppermute | solution.py:573
  96.8 1.1 %collective-permute-done.14 = f32[16,768]{1,0:T(8,128)S(1)} collective-permute-done((f32[16,768]{1,0:T(8,128)S(1)}, f32[16,768]{1,0:T(8,128)S(1)}, u32[]{:S(2)}, u32[]{:S(2)}) %collective-permute-start.14) | collective-permute-done | bytes 49184 | tf_op jit(solution)/shard_map/ppermute | solution.py:573
  98.0 2.7 %collective-permute-done.13 = f32[16,768]{1,0:T(8,128)S(1)} collective-permute-done((f32[16,768]{1,0:T(8,128)S(1)}, f32[16,768]{1,0:T(8,128)S(1)}, u32[]{:S(2)}, u32[]{:S(2)}) %collective-permute-start.13) | collective-permute-done | bytes 49184 | tf_op jit(solution)/shard_map/ppermute | solution.py:573
  100.6 1.5 %collective-permute-done.12 = f32[16,768]{1,0:T(8,128)S(1)} collective-permute-done((f32[16,768]{1,0:T(8,128)S(1)}, f32[16,768]{1,0:T(8,128)S(1)}, u32[]{:S(2)}, u32[]{:S(2)}) %collective-permute-start.12) | collective-permute-done | bytes 49184 | tf_op jit(solution)/shard_map/ppermute | solution.py:573
  103.6 1.6 %finish.1 = (f32[1,96,3072]{2,1,0:T(8,128)}, f32[1,384,768]{2,1,0:T(8,128)}) custom-call(bf16[4,96,768]{2,1,0:T(8,128)(2,1)S(1)} %all-to-all-done.2.spread_ref, f32[384,768]{1,0:T(8,128)S(1)} %copy-done.2, bf16[384,768]{1,0:T(8,128)(2,1)S(1)} %collective-permute-done.15.came_ref), custom_call_target="tpu_custom_call" | custom-call | tf_op jit(solution)/shard_map/finish/pallas_call | solution.py:438
  (43 shorter events, 6.5 us)
Async XLA Ops:
  0.6 30.1 %slice-start = ((s8[4718592]{0:T(1024)(128)(4,1)}), s8[4194304]{0:T(1024)(128)(4,1)S(1)}, s32[]{:S(2)}) async-start(s8[4718592]{0:T(1024)(128)(4,1)} %bitcast.5), calls=%async_computation.3 | async-start | bytes 8388608
  0.6 30.1 %slice-start.1 = ((s8[4718592]{0:T(1024)(128)(4,1)}), s8[524288]{0:T(1024)(128)(4,1)S(1)}, s32[]{:S(2)}) async-start(s8[4718592]{0:T(1024)(128)(4,1)} %bitcast.5), calls=%async_computation.4 | async-start | bytes 1048576
  0.7 30.1 %copy-start = (bf16[1,3072,768]{2,1,0:T(8,128)(2,1)S(1)}, bf16[1,3072,768]{2,1,0:T(8,128)(2,1)}, u32[]{:S(2)}) copy-start(bf16[1,3072,768]{2,1,0:T(8,128)(2,1)} %w2_hbm.3) | copy-start | bytes 14155780
  27.7 19.5 %collective-permute-start.2 = (bf16[256,1536]{1,0:T(8,128)(2,1)S(1)}, bf16[256,1536]{1,0:T(8,128)(2,1)S(1)}, u32[]{:S(2)}, u32[]{:S(2)}) collective-permute-start(bf16[256,1536]{1,0:T(8,128)(2,1)S(1)} %bitcast.7), channel_id=1, source_target_pairs={{0,96},{32,0},{64,32},{96,64},{1,97},{33,1},{65,33},{97,65},{2,98}... | collective-permute-start | bytes 2359304 | tf_op jit(solution)/shard_map/ppermute | solution.py:573
  30.7 21.0 %collective-permute-start = (bf16[256,1536]{1,0:T(8,128)(2,1)S(1)}, bf16[256,1536]{1,0:T(8,128)(2,1)S(1)}, u32[]{:S(2)}, u32[]{:S(2)}) collective-permute-start(bf16[256,1536]{1,0:T(8,128)(2,1)S(1)} %bitcast.8), channel_id=1, source_target_pairs={{0,32},{32,64},{64,96},{96,0},{1,33},{33,65},{65,97},{97,1},{2,34}... | collective-permute-start | bytes 2359304 | tf_op jit(solution)/shard_map/ppermute | solution.py:573
  37.7 19.0 %all-to-all-start.1 = ((bf16[16,16,1536]{2,1,0:T(8,128)(2,1)}), bf16[16,16,1536]{2,1,0:T(8,128)(2,1)S(1)}, u32[]{:S(2)}, u32[]{:S(2)}) async-start(bf16[16,16,1536]{2,1,0:T(8,128)(2,1)} %bitcast.14), calls=%async_computation.1 | async-start | bytes 1572864 | tf_op jit(solution)/shard_map/all_to_all | solution.py:590
  48.0 15.5 %collective-permute-start.3 = (bf16[128,1536]{1,0:T(8,128)(2,1)}, bf16[128,1536]{1,0:T(8,128)(2,1)S(1)}, u32[]{:S(2)}, u32[]{:S(2)}) collective-permute-start(bf16[128,1536]{1,0:T(8,128)(2,1)} %slice.9), channel_id=1, source_target_pairs={{0,96},{32,0},{64,32},{96,64},{1,97},{33,1},{65,33},{97,65},{2,98}... | collective-permute-start | bytes 1179656 | tf_op jit(solution)/shard_map/ppermute | solution.py:573
  52.4 11.0 %collective-permute-start.1 = (bf16[128,1536]{1,0:T(8,128)(2,1)}, bf16[128,1536]{1,0:T(8,128)(2,1)}, u32[]{:S(2)}, u32[]{:S(2)}) collective-permute-start(bf16[128,1536]{1,0:T(8,128)(2,1)} %slice.8), channel_id=1, source_target_pairs={{0,32},{32,64},{64,96},{96,0},{1,33},{33,65},{65,97},{97,1},{2,34}... | collective-permute-start | bytes 1179656 | tf_op jit(solution)/shard_map/ppermute | solution.py:573
  63.4 15.8 %collective-permute-start.6 = (f32[16,768]{1,0:T(8,128)S(1)}, f32[16,768]{1,0:T(8,128)S(1)}, u32[]{:S(2)}, u32[]{:S(2)}) collective-permute-start(f32[16,768]{1,0:T(8,128)S(1)} %get-tuple-element.41), channel_id=1, source_target_pairs={{0,18},{2,0},{16,2},{18,16},{1,19},{3,1},{17,3},{19,17},{4,22},{6,... | collective-permute-start | bytes 147464 | tf_op jit(solution)/shard_map/ppermute | solution.py:573
  66.6 12.6 %collective-permute-start.5 = (f32[16,768]{1,0:T(8,128)S(1)}, f32[16,768]{1,0:T(8,128)S(1)}, u32[]{:S(2)}, u32[]{:S(2)}) collective-permute-start(f32[16,768]{1,0:T(8,128)S(1)} %get-tuple-element.41), channel_id=1, source_target_pairs={{0,16},{2,18},{16,0},{18,2},{1,17},{3,19},{17,1},{19,3},{4,20},{6,... | collective-permute-start | bytes 147464 | tf_op jit(solution)/shard_map/ppermute | solution.py:573
  67.4 11.8 %collective-permute-start.4 = (f32[16,768]{1,0:T(8,128)S(1)}, f32[16,768]{1,0:T(8,128)S(1)}, u32[]{:S(2)}, u32[]{:S(2)}) collective-permute-start(f32[16,768]{1,0:T(8,128)S(1)} %get-tuple-element.41), channel_id=1, source_target_pairs={{0,2},{2,16},{16,18},{18,0},{1,3},{3,17},{17,19},{19,1},{4,6},{6,2... | collective-permute-start | bytes 147464 | tf_op jit(solution)/shard_map/ppermute | solution.py:573
  72.9 16.4 %collective-permute-start.11 = (bf16[4,96,768]{2,1,0:T(8,128)(2,1)S(1)}, bf16[4,96,768]{2,1,0:T(8,128)(2,1)S(1)}, u32[]{:S(2)}, u32[]{:S(2)}) collective-permute-start(bf16[4,96,768]{2,1,0:T(8,128)(2,1)S(1)} %get-tuple-element.52), channel_id=1, source_target_pairs={{0,16},{16,0},{1,17},{17,1},{2,18},{18,2},{3,19},{19,3},{4,20},{20... | collective-permute-start | bytes 1769480 | tf_op jit(solution)/shard_map/ppermute | solution.py:573
  75.4 8.9 %copy-start.3 = (f32[4,16,784]{2,1,0:T(8,128)S(1)}, f32[4,16,784]{2,1,0:T(8,128)}, u32[]{:S(2)}) copy-start(f32[4,16,784]{2,1,0:T(8,128)} %get-tuple-element.38.disp_hbm.disp_ref) | copy-start | bytes 602116
  75.4 8.9 %copy-start.4 = (bf16[768,16]{0,1:T(8,128)(2,1)S(1)}, bf16[768,16]{0,1:T(8,128)(2,1)}, u32[]{:S(2)}) copy-start(bf16[768,16]{0,1:T(8,128)(2,1)} %param.6) | copy-start | bytes 73732
  79.3 1.3 %collective-permute-start.7 = (f32[16,768]{1,0:T(8,128)S(1)}, f32[16,768]{1,0:T(8,128)S(1)}, u32[]{:S(2)}, u32[]{:S(2)}) collective-permute-start(f32[16,768]{1,0:T(8,128)S(1)} %add_add_fusion.1), channel_id=1, source_target_pairs={{0,1},{1,0},{2,3},{3,2},{4,5},{5,4},{6,7},{7,6},{8,9},{9,8},{10,11... | collective-permute-start | bytes 147464 | tf_op jit(solution)/shard_map/ppermute | solution.py:573
  80.6 8.2 %collective-permute-start.10 = (f32[16,768]{1,0:T(8,128)S(1)}, f32[16,768]{1,0:T(8,128)S(1)}, u32[]{:S(2)}, u32[]{:S(2)}) collective-permute-start(f32[16,768]{1,0:T(8,128)S(1)} %add.36), channel_id=1, source_target_pairs={{0,96},{32,0},{64,32},{96,64},{1,97},{33,1},{65,33},{97,65},{2,98}... | collective-permute-start | bytes 147464 | tf_op jit(solution)/shard_map/ppermute | solution.py:573
  83.4 5.6 %collective-permute-start.9 = (f32[16,768]{1,0:T(8,128)S(1)}, f32[16,768]{1,0:T(8,128)S(1)}, u32[]{:S(2)}, u32[]{:S(2)}) collective-permute-start(f32[16,768]{1,0:T(8,128)S(1)} %add.36), channel_id=1, source_target_pairs={{0,64},{32,96},{64,0},{96,32},{1,65},{33,97},{65,1},{97,33},{2,66}... | collective-permute-start | bytes 147464 | tf_op jit(solution)/shard_map/ppermute | solution.py:573
  83.4 5.8 %collective-permute-start.8 = (f32[16,768]{1,0:T(8,128)S(1)}, f32[16,768]{1,0:T(8,128)S(1)}, u32[]{:S(2)}, u32[]{:S(2)}) collective-permute-start(f32[16,768]{1,0:T(8,128)S(1)} %add.36), channel_id=1, source_target_pairs={{0,32},{32,64},{64,96},{96,0},{1,33},{33,65},{65,97},{97,1},{2,34}... | collective-permute-start | bytes 147464 | tf_op jit(solution)/shard_map/ppermute | solution.py:573
  87.2 16.3 %collective-permute-start.15 = (bf16[384,768]{1,0:T(8,128)(2,1)S(1)}, bf16[384,768]{1,0:T(8,128)(2,1)S(1)}, u32[]{:S(2)}, u32[]{:S(2)}) collective-permute-start(bf16[384,768]{1,0:T(8,128)(2,1)S(1)} %get-tuple-element.59), channel_id=1, source_target_pairs={{0,16},{16,0},{1,17},{17,1},{2,18},{18,2},{3,19},{19,3},{4,20},{20... | collective-permute-start | bytes 1769480 | tf_op jit(solution)/shard_map/ppermute | solution.py:573
  90.2 13.4 %copy-start.2 = (f32[384,768]{1,0:T(8,128)S(1)}, f32[384,768]{1,0:T(8,128)}, u32[]{:S(2)}) copy-start(f32[384,768]{1,0:T(8,128)} %copy-done.1) | copy-start | bytes 3538948
  90.2 13.4 %all-to-all-start.2 = ((bf16[4,96,768]{2,1,0:T(8,128)(2,1)}), bf16[4,96,768]{2,1,0:T(8,128)(2,1)S(1)}, u32[]{:S(2)}, u32[]{:S(2)}) async-start(bf16[4,96,768]{2,1,0:T(8,128)(2,1)} %add_convert_fusion), calls=%async_computation.2 | async-start | bytes 1179648 | tf_op jit(solution)/shard_map/all_to_all | solution.py:620
  93.8 4.2 %collective-permute-start.14 = (f32[16,768]{1,0:T(8,128)S(1)}, f32[16,768]{1,0:T(8,128)S(1)}, u32[]{:S(2)}, u32[]{:S(2)}) collective-permute-start(f32[16,768]{1,0:T(8,128)S(1)} %add_add_fusion), channel_id=1, source_target_pairs={{0,12},{4,0},{8,4},{12,8},{1,13},{5,1},{9,5},{13,9},{2,14},{6,2},{... | collective-permute-start | bytes 147464 | tf_op jit(solution)/shard_map/ppermute | solution.py:573
  95.0 5.6 %collective-permute-start.13 = (f32[16,768]{1,0:T(8,128)S(1)}, f32[16,768]{1,0:T(8,128)S(1)}, u32[]{:S(2)}, u32[]{:S(2)}) collective-permute-start(f32[16,768]{1,0:T(8,128)S(1)} %add_add_fusion), channel_id=1, source_target_pairs={{0,8},{4,12},{8,0},{12,4},{1,9},{5,13},{9,1},{13,5},{2,10},{6,14},... | collective-permute-start | bytes 147464 | tf_op jit(solution)/shard_map/ppermute | solution.py:573
  96.8 5.3 %collective-permute-start.12 = (f32[16,768]{1,0:T(8,128)S(1)}, f32[16,768]{1,0:T(8,128)S(1)}, u32[]{:S(2)}, u32[]{:S(2)}) collective-permute-start(f32[16,768]{1,0:T(8,128)S(1)} %add_add_fusion), channel_id=1, source_target_pairs={{0,4},{4,8},{8,12},{12,0},{1,5},{5,9},{9,13},{13,1},{2,6},{6,10},{... | collective-permute-start | bytes 147464 | tf_op jit(solution)/shard_map/ppermute | solution.py:573
  (1 other events, 8.0 us)

commit v10 on v9

--- a/solution.py
+++ b/solution.py
@@ -577,6 +577,10 @@
     return sum([shift(value, axis, by, count) for by in range(1, count)], value)
 
 
+def pair_sum(value, axis, count, by):
+    return value + lax.ppermute(value, axis, [(i, i ^ by) for i in range(count)])
+
+
 def solution(mesh):
     dp, experts = mesh.shape["dp"], mesh.shape["expert"]
     ny, nz = dp // XH, experts // 4
@@ -609,13 +613,16 @@
         pieces = (rows, right, left, far_a, far_b)
         keep_in, send_in, act_far = first_grads(pieces, pre_own, pre_near, w_in, w_out, ny)
         keep_out, send_out = second_grads(pieces, (act_own, act_near, act_far))
+        total = axis_sum(router_term, ("xh", "xl"), 2 * XH)
+        total, send_in = lax.optimization_barrier((total, send_in))
         came_in = shift(send_in, "xh", 1, XH)
         came_out = shift(send_out, "xh", 1, XH)
-        total = axis_sum(router_term, ("xh", "xl"), 2 * XH)
         total, keep_out = lax.optimization_barrier((total, keep_out))
-        total = axis_sum(axis_sum(total, "core", 2), "y", ny)
+        total = pair_sum(axis_sum(total, "core", 2), "y", ny, 1)
         part_in = (keep_in + came_in.astype(f32)).astype(bf16)
         grad_tok = token_grads(grad_logits, slot_grads, dispatch, rt)
+        total, grad_tok = lax.optimization_barrier((total, grad_tok))
+        total = pair_sum(total, "y", ny, 2)
         total, part_in, grad_tok = lax.optimization_barrier((total, part_in, grad_tok))
         spread = lax.all_to_all(part_in, "y", split_axis=0, concat_axis=0, tiled=True)
         grad_router = axis_sum(total, "z", nz).T

time: 106 us -> 107 us (level)
  waiting for transfers between devices: 13.6 us -> 14.8 us
    ppermute x16 -> x13, starting transfers between devices: 22 us -> 17.9 us  [shift(): lax.ppermute(value, axis, [(i, (i + by) % count) for i in range(count)])]
    ppermute x0 -> x2, starting transfers between devices: none -> 3.21 us  [pair_sum(): lax.ppermute(value, axis, [(i, i ^ by) for i in range(count)])]
    ppermute x0 -> x2, waiting for transfers between devices: none -> 2.24 us  [pair_sum(): lax.ppermute(value, axis, [(i, i ^ by) for i in range(count)])]
    ppermute x16 -> x13, waiting for transfers between devices: 13.6 us -> 12.1 us  [shift(): lax.ppermute(value, axis, [(i, (i + by) % count) for i in range(count)])]
  transfers between devices with their start and end apart: 18 -> 17, of which waited for: 8 -> 8; matrix products, arithmetic and copies ran while one was open for 3% -> 3% of each run, Pallas kernels for 28% -> 28%
where the time goes in v10:
time: 107 us; the launch traced here: 106 us
  Pallas kernels  38.4 us (36%)
  starting transfers between devices  29.2 us (27%)
  blocking collectives  19.9 us (19%)
  waiting for transfers between devices  14.8 us (14%)
  other arithmetic  1.6 us (1%)
  local copies, waits for them, and re-layouts  1.58 us (1%)
    all_to_all x1, blocking collectives, over_experts(): lax.all_to_all(value, ex_axes, split_axis=0, concat_axis=0, tiled=True)  19.9 us
    ppermute x13, starting transfers between devices, shift(): lax.ppermute(value, axis, [(i, (i + by) % count) for i in range(count)])  17.9 us
    ppermute x13, waiting for transfers between devices, shift(): lax.ppermute(value, axis, [(i, (i + by) % count) for i in range(count)])  12.1 us
    pallas_call x1, Pallas kernels, token_forward(): pl.pallas_call(token_forward_body, in_specs=[IN_PLACE] * 3, out_specs=[IN...  7.11 us
    pallas_call x1, Pallas kernels, expert_rows(): pl.pallas_call(expert_body, in_specs=[IN_VMEM] * 3, out_specs=[IN_PLACE]...  7 us
    pallas_call x1, Pallas kernels, token_logits(): pl.pallas_call(token_logits_body, in_specs=[IN_VMEM] + [IN_PLACE] * 4, ou...  6.68 us
    pallas_call x1, Pallas kernels, first_grads(): pl.pallas_call(first_grads_body, in_specs=[IN_VMEM] * 5 + [IN_PLACE] * 4,...  5.17 us
    all_to_all x1, starting transfers between devices, on_device(): lax.all_to_all(part_in, 'y', split_axis=0, concat_axis=0, tiled=True)  4.46 us
  transfers between devices with their start and end apart: 17, of which 8 were waited for; matrix products, arithmetic and copies ran while one was open for 3% of the time, Pallas kernels for 28%

profile of v10, /device:TPU:0, one launch (start us, length us, event | category | flops | bytes accessed | tf_op | source)
XLA Modules:
  0.0 106.4 jit_solution(16525203606078027146)
XLA Ops:
  0.7 7.1 %token_forward.1 = (bf16[16,16,1536]{2,1,0:T(8,128)(2,1)S(1)}, f32[4,16,784]{2,1,0:T(8,128)}, f32[4,16,784]{2,1,0:T(8,128)}) custom-call(bf16[16,768]{1,0:T(8,128)(2,1)} %bitcast.12, bf16[3136,768]{1,0:T(8,128)(2,1)} %x_hbm.3, bf16[3136,768]{1,0:T(8,128)(2,1)} %g_hbm.3), custom_call_target="tpu_custom_call" | custom-call | tf_op jit(solution)/shard_map/token_forward/pallas_call | solution.py:163
  7.8 19.9 %all_to_all.15 = bf16[16,16,1536]{2,1,0:T(8,128)(2,1)S(1)} all-to-all(bf16[16,16,1536]{2,1,0:T(8,128)(2,1)S(1)} %get-tuple-element.37), channel_id=1, replica_groups=mesh['y'=4,'xh'=2,'z'=4,'xl'=2,'core'=2] {'z','xl','core'}, dimensions={0} | all-to-all | bytes 1572864 | tf_op jit(solution)/shard_map/all_to_all | solution.py:594
  27.7 3.0 %collective-permute-start.2 = (bf16[256,1536]{1,0:T(8,128)(2,1)S(1)}, bf16[256,1536]{1,0:T(8,128)(2,1)S(1)}, u32[]{:S(2)}, u32[]{:S(2)}) collective-permute-start(bf16[256,1536]{1,0:T(8,128)(2,1)S(1)} %bitcast.7), channel_id=1, source_target_pairs={{0,96},{32,0},{64,32},{96,64},{1,97},{33,1},{65,33},{97,65},{2,98}... | collective-permute-start | bytes 2359304 | tf_op jit(solution)/shard_map/ppermute | solution.py:573
  30.7 7.0 %expert_rows.1 = (bf16[256,1536]{1,0:T(8,128)(2,1)}, bf16[256,768]{1,0:T(8,128)(2,1)}, bf16[256,768]{1,0:T(8,128)(2,1)}) custom-call(bf16[256,1536]{1,0:T(8,128)(2,1)S(1)} %bitcast.9, bf16[1,768,3072]{2,1,0:T(8,128)(2,1)S(1)} %bitcast.6, bf16[1,3072,768]{2,1,0:T(8,128)(2,1)S(1)} %copy-done), custom_call_target="tpu_custom_call" | custom-call | tf_op jit(solution)/shard_map/expert_rows/pallas_call | solution.py:245
  37.7 3.6 %all-to-all-start.1 = ((bf16[16,16,1536]{2,1,0:T(8,128)(2,1)}), bf16[16,16,1536]{2,1,0:T(8,128)(2,1)S(1)}, u32[]{:S(2)}, u32[]{:S(2)}) async-start(bf16[16,16,1536]{2,1,0:T(8,128)(2,1)} %bitcast.14), calls=%async_computation.1 | async-start | bytes 1572864 | tf_op jit(solution)/shard_map/all_to_all | solution.py:594
  41.4 5.8 %collective-permute-done.2.left_ref = bf16[256,1536]{1,0:T(8,128)(2,1)S(1)} collective-permute-done((bf16[256,1536]{1,0:T(8,128)(2,1)S(1)}, bf16[256,1536]{1,0:T(8,128)(2,1)S(1)}, u32[]{:S(2)}, u32[]{:S(2)}) %collective-permute-start.2) | collective-permute-done | bytes 786464 | tf_op jit(solution)/shard_map/ppermute | solution.py:573
  48.0 3.7 %collective-permute-start.3 = (bf16[128,1536]{1,0:T(8,128)(2,1)}, bf16[128,1536]{1,0:T(8,128)(2,1)S(1)}, u32[]{:S(2)}, u32[]{:S(2)}) collective-permute-start(bf16[128,1536]{1,0:T(8,128)(2,1)} %slice.9), channel_id=1, source_target_pairs={{0,96},{32,0},{64,32},{96,64},{1,97},{33,1},{65,33},{97,65},{2,98}... | collective-permute-start | bytes 1179656 | tf_op jit(solution)/shard_map/ppermute | solution.py:573
  52.4 4.3 %near_terms.1 = (bf16[512,768]{1,0:T(8,128)(2,1)}, bf16[512,768]{1,0:T(8,128)(2,1)}) custom-call(bf16[256,1536]{1,0:T(8,128)(2,1)S(1)} %collective-permute-done.right_ref, bf16[256,1536]{1,0:T(8,128)(2,1)S(1)} %collective-permute-done.2.left_ref, bf16[1,768,3072]{2,1,0:T(8,128)(2,1)} %w1_hbm.3, bf16[1,3072,768]{2,1,0:T(8,128)(2,1)} %w2_hbm.3), custom_call_target="tpu_custom_call" | custom-call | tf_op jit(solution)/shard_map/near_terms/pallas_call | solution.py:307
  56.7 6.7 %token_logits.1 = (bf16[4,16,784]{2,1,0:T(8,128)(2,1)S(1)}, bf16[4,64,768]{2,1,0:T(8,128)(2,1)S(1)}, f32[16,768]{1,0:T(8,128)S(1)}) custom-call(bf16[16,16,1536]{2,1,0:T(8,128)(2,1)S(1)} %all-to-all-done.1.back_ref, bf16[3136,768]{1,0:T(8,128)(2,1)} %x_hbm.3, bf16[3136,768]{1,0:T(8,128)(2,1)} %g_hbm.3, f32[4,16,784]{2,1,0:T(8,128)} %get-tuple-element.42.disp_hbm.disp_ref, ...), custom_call_target="tpu_custom_call" | custom-call | tf_op jit(solution)/shard_map/token_logits/pallas_call | solution.py:519
  63.5 3.2 %collective-permute-start.6 = (f32[16,768]{1,0:T(8,128)S(1)}, f32[16,768]{1,0:T(8,128)S(1)}, u32[]{:S(2)}, u32[]{:S(2)}) collective-permute-start(f32[16,768]{1,0:T(8,128)S(1)} %get-tuple-element.45), channel_id=1, source_target_pairs={{0,18},{2,0},{16,2},{18,16},{1,19},{3,1},{17,3},{19,17},{4,22},{6,... | collective-permute-start | bytes 147464 | tf_op jit(solution)/shard_map/ppermute | solution.py:573
  67.7 5.2 %first_grads.1 = (f32[4,96,768]{2,1,0:T(8,128)S(1)}, bf16[4,96,768]{2,1,0:T(8,128)(2,1)S(1)}, bf16[256,768]{1,0:T(8,128)(2,1)S(1)}) custom-call(bf16[256,1536]{1,0:T(8,128)(2,1)S(1)} %bitcast.10, bf16[256,1536]{1,0:T(8,128)(2,1)S(1)} %collective-permute-done.right_ref, bf16[256,1536]{1,0:T(8,128)(2,1)S(1)} %collective-permute-done.2.left_ref, ...), custom_call_target="tpu_custom_call" | custom-call | tf_op jit(solution)/shard_map/first_grads/pallas_call | solution.py:360
  72.9 2.6 %collective-permute-start.10 = (bf16[4,96,768]{2,1,0:T(8,128)(2,1)S(1)}, bf16[4,96,768]{2,1,0:T(8,128)(2,1)S(1)}, u32[]{:S(2)}, u32[]{:S(2)}) collective-permute-start(bf16[4,96,768]{2,1,0:T(8,128)(2,1)S(1)} %get-tuple-element.61), channel_id=1, source_target_pairs={{0,16},{16,0},{1,17},{17,1},{2,18},{18,2},{3,19},{19,3},{4,20},{20... | collective-permute-start | bytes 1769480 | tf_op jit(solution)/shard_map/ppermute | solution.py:573
  75.5 3.7 %second_grads.1 = (f32[384,768]{1,0:T(8,128)S(1)}, bf16[384,768]{1,0:T(8,128)(2,1)S(1)}) custom-call(bf16[256,1536]{1,0:T(8,128)(2,1)S(1)} %bitcast.11, bf16[256,1536]{1,0:T(8,128)(2,1)S(1)} %collective-permute-done.right_ref, bf16[256,1536]{1,0:T(8,128)(2,1)S(1)} %collective-permute-done.2.left_ref, bf16[128,1536]{1,0:T(8,128)(2,1)} %collective-permute-done.1.far_a, ...), custom_call_target="tpu_custom_call" | custom-call | tf_op jit(solution)/shard_map/second_grads/pallas_call | solution.py:411
  79.4 1.2 %collective-permute-done.7 = f32[16,768]{1,0:T(8,128)S(1)} collective-permute-done((f32[16,768]{1,0:T(8,128)S(1)}, f32[16,768]{1,0:T(8,128)S(1)}, u32[]{:S(2)}, u32[]{:S(2)}) %collective-permute-start.7) | collective-permute-done | bytes 49184 | tf_op jit(solution)/shard_map/ppermute | solution.py:573
  80.7 2.9 %token_grads.1 = bf16[3136,768]{1,0:T(8,128)(2,1)} custom-call(bf16[4,16,784]{2,1,0:T(8,128)(2,1)S(1)} %get-tuple-element.57.gl_ref, bf16[4,64,768]{2,1,0:T(8,128)(2,1)S(1)} %get-tuple-element.58.slots_ref, f32[4,16,784]{2,1,0:T(8,128)S(1)} %copy-done.3, bf16[16,768]{1,0:T(8,128)(2,1)S(1)} %bitcast.13), custom_call_target="tpu_custom_call" | custom-call | tf_op jit(solution)/shard_map/token_grads/pallas_call | solution.py:561
  83.6 1.2 %collective-permute-done.8 = f32[16,768]{1,0:T(8,128)S(1)} collective-permute-done((f32[16,768]{1,0:T(8,128)S(1)}, f32[16,768]{1,0:T(8,128)S(1)}, u32[]{:S(2)}, u32[]{:S(2)}) %collective-permute-start.8) | collective-permute-done | bytes 49184 | tf_op jit(solution)/shard_map/ppermute | solution.py:581
  84.7 3.1 %collective-permute-start.9 = (f32[16,768]{1,0:T(8,128)S(1)}, f32[16,768]{1,0:T(8,128)S(1)}, u32[]{:S(2)}, u32[]{:S(2)}) collective-permute-start(f32[16,768]{1,0:T(8,128)S(1)} %add.34), channel_id=1, source_target_pairs={{0,64},{32,96},{64,0},{96,32},{1,65},{33,97},{65,1},{97,33},{2,66}... | collective-permute-start | bytes 147464 | tf_op jit(solution)/shard_map/ppermute | solution.py:581
  87.9 1.5 %collective-permute-start.14 = (bf16[384,768]{1,0:T(8,128)(2,1)S(1)}, bf16[384,768]{1,0:T(8,128)(2,1)S(1)}, u32[]{:S(2)}, u32[]{:S(2)}) collective-permute-start(bf16[384,768]{1,0:T(8,128)(2,1)S(1)} %get-tuple-element.67), channel_id=1, source_target_pairs={{0,16},{16,0},{1,17},{17,1},{2,18},{18,2},{3,19},{19,3},{4,20},{20... | collective-permute-start | bytes 1769480 | tf_op jit(solution)/shard_map/ppermute | solution.py:573
  91.4 4.5 %all-to-all-start.2 = ((bf16[4,96,768]{2,1,0:T(8,128)(2,1)}), bf16[4,96,768]{2,1,0:T(8,128)(2,1)S(1)}, u32[]{:S(2)}, u32[]{:S(2)}) async-start(bf16[4,96,768]{2,1,0:T(8,128)(2,1)} %add_convert_fusion), calls=%async_computation.2 | async-start | bytes 1179648 | tf_op jit(solution)/shard_map/all_to_all | solution.py:627
  96.9 1.5 %collective-permute-start.12 = (f32[16,768]{1,0:T(8,128)S(1)}, f32[16,768]{1,0:T(8,128)S(1)}, u32[]{:S(2)}, u32[]{:S(2)}) collective-permute-start(f32[16,768]{1,0:T(8,128)S(1)} %add.35), channel_id=1, source_target_pairs={{0,8},{4,12},{8,0},{12,4},{1,9},{5,13},{9,1},{13,5},{2,10},{6,14},... | collective-permute-start | bytes 147464 | tf_op jit(solution)/shard_map/ppermute | solution.py:573
  98.6 1.3 %collective-permute-done.13 = f32[16,768]{1,0:T(8,128)S(1)} collective-permute-done((f32[16,768]{1,0:T(8,128)S(1)}, f32[16,768]{1,0:T(8,128)S(1)}, u32[]{:S(2)}, u32[]{:S(2)}) %collective-permute-start.13) | collective-permute-done | bytes 49184 | tf_op jit(solution)/shard_map/ppermute | solution.py:573
  99.9 2.6 %collective-permute-done.12 = f32[16,768]{1,0:T(8,128)S(1)} collective-permute-done((f32[16,768]{1,0:T(8,128)S(1)}, f32[16,768]{1,0:T(8,128)S(1)}, u32[]{:S(2)}, u32[]{:S(2)}) %collective-permute-start.12) | collective-permute-done | bytes 49184 | tf_op jit(solution)/shard_map/ppermute | solution.py:573
  102.5 1.2 %collective-permute-done.11 = f32[16,768]{1,0:T(8,128)S(1)} collective-permute-done((f32[16,768]{1,0:T(8,128)S(1)}, f32[16,768]{1,0:T(8,128)S(1)}, u32[]{:S(2)}, u32[]{:S(2)}) %collective-permute-start.11) | collective-permute-done | bytes 49184 | tf_op jit(solution)/shard_map/ppermute | solution.py:573
  104.8 1.6 %finish.1 = (f32[1,96,3072]{2,1,0:T(8,128)}, f32[1,384,768]{2,1,0:T(8,128)}) custom-call(bf16[4,96,768]{2,1,0:T(8,128)(2,1)S(1)} %all-to-all-done.2.spread_ref, f32[384,768]{1,0:T(8,128)S(1)} %copy-done.2, bf16[384,768]{1,0:T(8,128)(2,1)S(1)} %collective-permute-done.14.came_ref), custom_call_target="tpu_custom_call" | custom-call | tf_op jit(solution)/shard_map/finish/pallas_call | solution.py:438
  (42 shorter events, 7.3 us)
Async XLA Ops:
  0.6 30.1 %slice-start = ((s8[4718592]{0:T(1024)(128)(4,1)}), s8[4194304]{0:T(1024)(128)(4,1)S(1)}, s32[]{:S(2)}) async-start(s8[4718592]{0:T(1024)(128)(4,1)} %bitcast.5), calls=%async_computation.3 | async-start | bytes 8388608
  0.6 30.1 %slice-start.1 = ((s8[4718592]{0:T(1024)(128)(4,1)}), s8[524288]{0:T(1024)(128)(4,1)S(1)}, s32[]{:S(2)}) async-start(s8[4718592]{0:T(1024)(128)(4,1)} %bitcast.5), calls=%async_computation.4 | async-start | bytes 1048576
  0.7 30.1 %copy-start = (bf16[1,3072,768]{2,1,0:T(8,128)(2,1)S(1)}, bf16[1,3072,768]{2,1,0:T(8,128)(2,1)}, u32[]{:S(2)}) copy-start(bf16[1,3072,768]{2,1,0:T(8,128)(2,1)} %w2_hbm.3) | copy-start | bytes 14155780
  27.7 19.5 %collective-permute-start.2 = (bf16[256,1536]{1,0:T(8,128)(2,1)S(1)}, bf16[256,1536]{1,0:T(8,128)(2,1)S(1)}, u32[]{:S(2)}, u32[]{:S(2)}) collective-permute-start(bf16[256,1536]{1,0:T(8,128)(2,1)S(1)} %bitcast.7), channel_id=1, source_target_pairs={{0,96},{32,0},{64,32},{96,64},{1,97},{33,1},{65,33},{97,65},{2,98}... | collective-permute-start | bytes 2359304 | tf_op jit(solution)/shard_map/ppermute | solution.py:573
  30.7 21.0 %collective-permute-start = (bf16[256,1536]{1,0:T(8,128)(2,1)S(1)}, bf16[256,1536]{1,0:T(8,128)(2,1)S(1)}, u32[]{:S(2)}, u32[]{:S(2)}) collective-permute-start(bf16[256,1536]{1,0:T(8,128)(2,1)S(1)} %bitcast.8), channel_id=1, source_target_pairs={{0,32},{32,64},{64,96},{96,0},{1,33},{33,65},{65,97},{97,1},{2,34}... | collective-permute-start | bytes 2359304 | tf_op jit(solution)/shard_map/ppermute | solution.py:573
  37.7 19.0 %all-to-all-start.1 = ((bf16[16,16,1536]{2,1,0:T(8,128)(2,1)}), bf16[16,16,1536]{2,1,0:T(8,128)(2,1)S(1)}, u32[]{:S(2)}, u32[]{:S(2)}) async-start(bf16[16,16,1536]{2,1,0:T(8,128)(2,1)} %bitcast.14), calls=%async_computation.1 | async-start | bytes 1572864 | tf_op jit(solution)/shard_map/all_to_all | solution.py:594
  48.0 15.5 %collective-permute-start.3 = (bf16[128,1536]{1,0:T(8,128)(2,1)}, bf16[128,1536]{1,0:T(8,128)(2,1)S(1)}, u32[]{:S(2)}, u32[]{:S(2)}) collective-permute-start(bf16[128,1536]{1,0:T(8,128)(2,1)} %slice.9), channel_id=1, source_target_pairs={{0,96},{32,0},{64,32},{96,64},{1,97},{33,1},{65,33},{97,65},{2,98}... | collective-permute-start | bytes 1179656 | tf_op jit(solution)/shard_map/ppermute | solution.py:573
  52.4 11.0 %collective-permute-start.1 = (bf16[128,1536]{1,0:T(8,128)(2,1)}, bf16[128,1536]{1,0:T(8,128)(2,1)}, u32[]{:S(2)}, u32[]{:S(2)}) collective-permute-start(bf16[128,1536]{1,0:T(8,128)(2,1)} %slice.8), channel_id=1, source_target_pairs={{0,32},{32,64},{64,96},{96,0},{1,33},{33,65},{65,97},{97,1},{2,34}... | collective-permute-start | bytes 1179656 | tf_op jit(solution)/shard_map/ppermute | solution.py:573
  63.5 9.4 %collective-permute-start.6 = (f32[16,768]{1,0:T(8,128)S(1)}, f32[16,768]{1,0:T(8,128)S(1)}, u32[]{:S(2)}, u32[]{:S(2)}) collective-permute-start(f32[16,768]{1,0:T(8,128)S(1)} %get-tuple-element.45), channel_id=1, source_target_pairs={{0,18},{2,0},{16,2},{18,16},{1,19},{3,1},{17,3},{19,17},{4,22},{6,... | collective-permute-start | bytes 147464 | tf_op jit(solution)/shard_map/ppermute | solution.py:573
  66.6 6.2 %collective-permute-start.5 = (f32[16,768]{1,0:T(8,128)S(1)}, f32[16,768]{1,0:T(8,128)S(1)}, u32[]{:S(2)}, u32[]{:S(2)}) collective-permute-start(f32[16,768]{1,0:T(8,128)S(1)} %get-tuple-element.45), channel_id=1, source_target_pairs={{0,16},{2,18},{16,0},{18,2},{1,17},{3,19},{17,1},{19,3},{4,20},{6,... | collective-permute-start | bytes 147464 | tf_op jit(solution)/shard_map/ppermute | solution.py:573
  67.4 5.5 %collective-permute-start.4 = (f32[16,768]{1,0:T(8,128)S(1)}, f32[16,768]{1,0:T(8,128)S(1)}, u32[]{:S(2)}, u32[]{:S(2)}) collective-permute-start(f32[16,768]{1,0:T(8,128)S(1)} %get-tuple-element.45), channel_id=1, source_target_pairs={{0,2},{2,16},{16,18},{18,0},{1,3},{3,17},{17,19},{19,1},{4,6},{6,2... | collective-permute-start | bytes 147464 | tf_op jit(solution)/shard_map/ppermute | solution.py:573
  72.9 17.5 %collective-permute-start.10 = (bf16[4,96,768]{2,1,0:T(8,128)(2,1)S(1)}, bf16[4,96,768]{2,1,0:T(8,128)(2,1)S(1)}, u32[]{:S(2)}, u32[]{:S(2)}) collective-permute-start(bf16[4,96,768]{2,1,0:T(8,128)(2,1)S(1)} %get-tuple-element.61), channel_id=1, source_target_pairs={{0,16},{16,0},{1,17},{17,1},{2,18},{18,2},{3,19},{19,3},{4,20},{20... | collective-permute-start | bytes 1769480 | tf_op jit(solution)/shard_map/ppermute | solution.py:573
  75.5 5.2 %copy-start.3 = (f32[4,16,784]{2,1,0:T(8,128)S(1)}, f32[4,16,784]{2,1,0:T(8,128)}, u32[]{:S(2)}) copy-start(f32[4,16,784]{2,1,0:T(8,128)} %get-tuple-element.42.disp_hbm.disp_ref) | copy-start | bytes 602116
  75.5 5.2 %copy-start.4 = (bf16[768,16]{0,1:T(8,128)(2,1)S(1)}, bf16[768,16]{0,1:T(8,128)(2,1)}, u32[]{:S(2)}) copy-start(bf16[768,16]{0,1:T(8,128)(2,1)} %param.6) | copy-start | bytes 73732
  79.2 4.3 %copy-start.1 = (f32[384,768]{1,0:T(8,128)}, f32[384,768]{1,0:T(8,128)S(1)}, u32[]{:S(2)}) copy-start(f32[384,768]{1,0:T(8,128)S(1)} %get-tuple-element.66.keep_ref) | copy-start | bytes 3538948
  79.3 1.3 %collective-permute-start.7 = (f32[16,768]{1,0:T(8,128)S(1)}, f32[16,768]{1,0:T(8,128)S(1)}, u32[]{:S(2)}, u32[]{:S(2)}) collective-permute-start(f32[16,768]{1,0:T(8,128)S(1)} %add_add_fusion), channel_id=1, source_target_pairs={{0,1},{1,0},{2,3},{3,2},{4,5},{5,4},{6,7},{7,6},{8,9},{9,8},{10,11... | collective-permute-start | bytes 147464 | tf_op jit(solution)/shard_map/ppermute | solution.py:573
  80.6 4.2 %collective-permute-start.8 = (f32[16,768]{1,0:T(8,128)S(1)}, f32[16,768]{1,0:T(8,128)S(1)}, u32[]{:S(2)}, u32[]{:S(2)}) collective-permute-start(f32[16,768]{1,0:T(8,128)S(1)} %add.33), channel_id=1, source_target_pairs={{0,32},{32,0},{64,96},{96,64},{1,33},{33,1},{65,97},{97,65},{2,34}... | collective-permute-start | bytes 147464 | tf_op jit(solution)/shard_map/ppermute | solution.py:581
  84.7 5.7 %collective-permute-start.9 = (f32[16,768]{1,0:T(8,128)S(1)}, f32[16,768]{1,0:T(8,128)S(1)}, u32[]{:S(2)}, u32[]{:S(2)}) collective-permute-start(f32[16,768]{1,0:T(8,128)S(1)} %add.34), channel_id=1, source_target_pairs={{0,64},{32,96},{64,0},{96,32},{1,65},{33,97},{65,1},{97,33},{2,66}... | collective-permute-start | bytes 147464 | tf_op jit(solution)/shard_map/ppermute | solution.py:581
  87.9 16.5 %collective-permute-start.14 = (bf16[384,768]{1,0:T(8,128)(2,1)S(1)}, bf16[384,768]{1,0:T(8,128)(2,1)S(1)}, u32[]{:S(2)}, u32[]{:S(2)}) collective-permute-start(bf16[384,768]{1,0:T(8,128)(2,1)S(1)} %get-tuple-element.67), channel_id=1, source_target_pairs={{0,16},{16,0},{1,17},{17,1},{2,18},{18,2},{3,19},{19,3},{4,20},{20... | collective-permute-start | bytes 1769480 | tf_op jit(solution)/shard_map/ppermute | solution.py:573
  91.4 13.5 %copy-start.2 = (f32[384,768]{1,0:T(8,128)S(1)}, f32[384,768]{1,0:T(8,128)}, u32[]{:S(2)}) copy-start(f32[384,768]{1,0:T(8,128)} %copy-done.1) | copy-start | bytes 3538948
  91.4 13.5 %all-to-all-start.2 = ((bf16[4,96,768]{2,1,0:T(8,128)(2,1)}), bf16[4,96,768]{2,1,0:T(8,128)(2,1)S(1)}, u32[]{:S(2)}, u32[]{:S(2)}) async-start(bf16[4,96,768]{2,1,0:T(8,128)(2,1)} %add_convert_fusion), calls=%async_computation.2 | async-start | bytes 1179648 | tf_op jit(solution)/shard_map/all_to_all | solution.py:627
  95.8 4.1 %collective-permute-start.13 = (f32[16,768]{1,0:T(8,128)S(1)}, f32[16,768]{1,0:T(8,128)S(1)}, u32[]{:S(2)}, u32[]{:S(2)}) collective-permute-start(f32[16,768]{1,0:T(8,128)S(1)} %add.35), channel_id=1, source_target_pairs={{0,12},{4,0},{8,4},{12,8},{1,13},{5,1},{9,5},{13,9},{2,14},{6,2},{... | collective-permute-start | bytes 147464 | tf_op jit(solution)/shard_map/ppermute | solution.py:573
  96.9 5.6 %collective-permute-start.12 = (f32[16,768]{1,0:T(8,128)S(1)}, f32[16,768]{1,0:T(8,128)S(1)}, u32[]{:S(2)}, u32[]{:S(2)}) collective-permute-start(f32[16,768]{1,0:T(8,128)S(1)} %add.35), channel_id=1, source_target_pairs={{0,8},{4,12},{8,0},{12,4},{1,9},{5,13},{9,1},{13,5},{2,10},{6,14},... | collective-permute-start | bytes 147464 | tf_op jit(solution)/shard_map/ppermute | solution.py:573
  98.4 5.3 %collective-permute-start.11 = (f32[16,768]{1,0:T(8,128)S(1)}, f32[16,768]{1,0:T(8,128)S(1)}, u32[]{:S(2)}, u32[]{:S(2)}) collective-permute-start(f32[16,768]{1,0:T(8,128)S(1)} %add.35), channel_id=1, source_target_pairs={{0,4},{4,8},{8,12},{12,0},{1,5},{5,9},{9,13},{13,1},{2,6},{6,10},{... | collective-permute-start | bytes 147464 | tf_op jit(solution)/shard_map/ppermute | solution.py:573
